TPU v7x, 32 devices: a whole 2x2x4 slice. The times are simulated.
32 devices in a mesh: dp: 16 (over z, x, core), mp: 2 (over y).
Axes of the slice: x: 2, y: 2, z: 4, core: 2. Of those that a mesh axis runs over, the one named last changes fastest.
Arguments:
- layer_in: bfloat16 [35840, 1024], P(('dp', 'mp')), may hold values from -6 to 6
- patch_count: int32 [128], P('dp'), may hold values from 100 to 240, as said below
- attn_gain: bfloat16 [1024], replicated, may hold values from 0.5 to 1.5
- attn_shift: bfloat16 [1024], replicated, may hold values from -2 to 2
- query_weight: bfloat16 [1024, 1024], P(None, 'mp'), may hold values from -0.1875 to 0.1875
- query_bias: bfloat16 [1024], P('mp'), may hold values from -2 to 2
- key_weight: bfloat16 [1024, 1024], P(None, 'mp'), may hold values from -0.1875 to 0.1875
- value_weight: bfloat16 [1024, 1024], P(None, 'mp'), may hold values from -0.1875 to 0.1875
- value_bias: bfloat16 [1024], P('mp'), may hold values from -2 to 2
- out_weight: bfloat16 [1024, 1024], P('mp'), may hold values from -0.5 to 0.5
- out_bias: bfloat16 [1024], replicated, may hold values from -2 to 2
- mlp_gain: bfloat16 [1024], replicated, may hold values from 0.5 to 1.5
- mlp_shift: bfloat16 [1024], replicated, may hold values from -2 to 2
- up_weight: bfloat16 [1024, 4096], P(None, 'mp'), may hold values from -0.1875 to 0.1875
- up_bias: bfloat16 [4096], P('mp'), may hold values from -2 to 2
- down_weight: bfloat16 [4096, 1024], P('mp'), may hold values from -0.09375 to 0.09375
- down_bias: bfloat16 [1024], replicated, may hold values from -2 to 2
- layer_cot: bfloat16 [35840, 1024], P(('dp', 'mp')), may hold values from -6 to 6
Outputs:
- layer_out: bfloat16 [35840, 1024], P(('dp', 'mp'))
- grad_in: bfloat16 [35840, 1024], P(('dp', 'mp'))
- grad_attn_gain: float32 [1024], replicated
- grad_attn_shift: float32 [1024], replicated
- grad_query_weight: float32 [1024, 1024], P(None, 'mp')
- grad_query_bias: float32 [1024], P('mp')
- grad_key_weight: float32 [1024, 1024], P(None, 'mp')
- grad_value_weight: float32 [1024, 1024], P(None, 'mp')
- grad_value_bias: float32 [1024], P('mp')
- grad_out_weight: float32 [1024, 1024], P('mp')
- grad_out_bias: float32 [1024], replicated
- grad_mlp_gain: float32 [1024], replicated
- grad_mlp_shift: float32 [1024], replicated
- grad_up_weight: float32 [1024, 4096], P(None, 'mp')
- grad_up_bias: float32 [4096], P('mp')
- grad_down_weight: float32 [4096, 1024], P('mp')
- grad_down_bias: float32 [1024], replicated
Inputs may be any that keep to these rules, and one draw needn't show every extreme that they name: Patches of each pair; rows 40 + patch_count and later of a pair are padding.
All inputs are finite; a program needn't handle non-finite values.
Results may differ from a plain program's by a relative error of at most 0.02.
Values may be sent and summed in bfloat16 or wider, within the bound.
No kernel may reach another device: no remote copies, remote signals or barrier semaphores. Data moves between devices by JAX's collectives and lax.ppermute only.
A program may use at most 320 MiB of HBM per device.

v0:
```python
import jax
import jax.numpy as jnp
from jax import lax
from jax.sharding import PartitionSpec as P

HEAD_DIM = 64
TEXT = 40
SEQ = 280


EPS = 1e-05
SCALE = 0.125
NEGATIVE = -1e30


def layer_norm(values, gain, shift):
    center = values - jnp.mean(values, -1, keepdims=True)
    spread = jnp.mean(center * center, -1, keepdims=True)
    return center * lax.rsqrt(spread + EPS) * gain + shift


def exact_gelu(values):
    return jax.nn.gelu(values, approximate=False)


def matmul_rows(left, right):
    return jnp.dot(left, right, preferred_element_type=jnp.float32)


def contract_rows(left, right):
    return lax.dot_general(
        left, right, (((0,), (0,)), ((), ())), preferred_element_type=jnp.float32
    )


def contract_cols(left, right):
    return lax.dot_general(
        left, right, (((1,), (1,)), ((), ())), preferred_element_type=jnp.float32
    )


def column_sum(values):
    return jnp.sum(values.astype(jnp.float32), 0)


def body(
    layer_in,
    patch_count,
    attn_gain,
    attn_shift,
    query_weight,
    query_bias,
    key_weight,
    value_weight,
    value_bias,
    out_weight,
    out_bias,
    mlp_gain,
    mlp_shift,
    up_weight,
    up_bias,
    down_weight,
    down_bias,
    layer_cot,
):
    lowtype = jnp.bfloat16
    wide = jnp.float32
    rows_in = layer_in.astype(wide)
    gain_one = attn_gain.astype(wide)
    shift_one = attn_shift.astype(wide)
    gain_two = mlp_gain.astype(wide)
    shift_two = mlp_shift.astype(wide)
    normed_tok, norm_pull = jax.vjp(layer_norm, rows_in, gain_one, shift_one)
    group_rows = lax.all_gather(normed_tok.astype(lowtype), "mp", axis=0, tiled=True)
    query_rows = (matmul_rows(group_rows, query_weight) + query_bias.astype(wide)).astype(lowtype)
    key_rows = matmul_rows(group_rows, key_weight).astype(lowtype)
    value_rows = (matmul_rows(group_rows, value_weight) + value_bias.astype(wide)).astype(lowtype)
    pairs = patch_count.shape[0]
    local_width = query_weight.shape[1]
    local_heads = local_width // HEAD_DIM
    group_total = group_rows.shape[0]
    shape_four = (pairs, SEQ, local_heads, HEAD_DIM)
    query_blk = query_rows.reshape(shape_four)
    key_blk = key_rows.reshape(shape_four)
    value_blk = value_rows.reshape(shape_four)
    scores = jnp.einsum("pqhd,pkhd->phqk", query_blk, key_blk, preferred_element_type=wide) * SCALE
    valid = jnp.arange(SEQ)[None, :] < (TEXT + patch_count)[:, None]
    scores = jnp.where(valid[:, None, None, :], scores, NEGATIVE)
    probs = jax.nn.softmax(scores, axis=-1)
    probs_low = probs.astype(lowtype)
    context = jnp.einsum("phqk,pkhd->pqhd", probs_low, value_blk, preferred_element_type=wide)
    context = context.astype(lowtype).reshape(group_total, local_width)
    context_tok = lax.all_to_all(context, "mp", split_axis=0, concat_axis=1, tiled=True)
    out_full = lax.all_gather(out_weight, "mp", axis=0, tiled=True)
    attended = matmul_rows(context_tok, out_full) + out_bias.astype(wide)
    middle = rows_in + attended
    hidden_wide, mlp_pull = jax.vjp(layer_norm, middle, gain_two, shift_two)
    hidden_in = hidden_wide.astype(lowtype)
    cot_wide = layer_cot.astype(wide)
    up_full, bias_full, down_full = (
        lax.all_gather(up_weight, "mp", axis=1, tiled=True),
        lax.all_gather(up_bias, "mp", axis=0, tiled=True),
        lax.all_gather(down_weight, "mp", axis=0, tiled=True),
    )
    pre_act = matmul_rows(hidden_in, up_full) + bias_full.astype(wide)
    act_wide, gelu_pull = jax.vjp(exact_gelu, pre_act)
    act_low = act_wide.astype(lowtype)
    ffn_out = matmul_rows(act_low, down_full) + down_bias.astype(wide)
    whole_down = contract_rows(act_low, layer_cot)
    act_grad = contract_cols(layer_cot, down_full)
    pre_grad = gelu_pull(act_grad)[0].astype(lowtype)
    whole_up_bias = column_sum(pre_grad)
    whole_up = contract_rows(hidden_in, pre_grad)
    hidden_grad = contract_cols(pre_grad, up_full)
    grad_up_weight, grad_up_bias, grad_down_weight = (
        lax.psum_scatter(
            whole_up.astype(jnp.bfloat16), "mp", scatter_dimension=1, tiled=True
        ).astype(jnp.float32),
        lax.psum_scatter(
            whole_up_bias.astype(jnp.bfloat16), "mp", scatter_dimension=0, tiled=True
        ).astype(jnp.float32),
        lax.psum_scatter(
            whole_down.astype(jnp.bfloat16), "mp", scatter_dimension=0, tiled=True
        ).astype(jnp.float32),
    )
    layer_out = (middle + ffn_out).astype(lowtype)
    grad_down_bias = column_sum(layer_cot)
    middle_part, grad_gain_two, grad_shift_two = mlp_pull(hidden_grad)
    middle_grad = cot_wide + middle_part
    attn_grad = middle_grad.astype(lowtype)
    grad_out_bias = column_sum(attn_grad)
    grad_out_weight = lax.psum_scatter(
        contract_rows(context_tok, attn_grad).astype(jnp.bfloat16),
        "mp",
        scatter_dimension=0,
        tiled=True,
    ).astype(jnp.float32)
    context_grad_tok = contract_cols(attn_grad, out_full).astype(lowtype)
    context_grad = lax.all_to_all(
        context_grad_tok, "mp", split_axis=1, concat_axis=0, tiled=True
    ).reshape(shape_four)
    probs_grad = jnp.einsum("pqhd,pkhd->phqk", context_grad, value_blk, preferred_element_type=wide)
    value_grad = jnp.einsum("phqk,pqhd->pkhd", probs_low, context_grad, preferred_element_type=wide)
    value_grad = value_grad.astype(lowtype).reshape(group_total, local_width)
    score_grad = (probs * (probs_grad - jnp.sum(probs * probs_grad, -1, keepdims=True))).astype(
        lowtype
    )
    query_grad = (
        jnp.einsum("phqk,pkhd->pqhd", score_grad, key_blk, preferred_element_type=wide) * SCALE
    )
    query_grad = query_grad.astype(lowtype).reshape(group_total, local_width)
    key_grad = (
        jnp.einsum("phqk,pqhd->pkhd", score_grad, query_blk, preferred_element_type=wide) * SCALE
    )
    key_grad = key_grad.astype(lowtype).reshape(group_total, local_width)
    grad_query_weight = contract_rows(group_rows, query_grad)
    grad_key_weight = contract_rows(group_rows, key_grad)
    grad_value_weight = contract_rows(group_rows, value_grad)
    grad_query_bias = column_sum(query_grad)
    grad_value_bias = column_sum(value_grad)
    total = contract_cols(query_grad, query_weight)
    total = total + contract_cols(key_grad, key_weight)
    normed_grad = lax.psum_scatter(
        (total + contract_cols(value_grad, value_weight)).astype(jnp.bfloat16),
        "mp",
        scatter_dimension=0,
        tiled=True,
    ).astype(jnp.float32)
    input_part, grad_gain_one, grad_shift_one = norm_pull(normed_grad)
    grad_in = (middle_grad + input_part).astype(lowtype)
    (
        grad_query_weight,
        grad_query_bias,
        grad_key_weight,
        grad_value_weight,
        grad_value_bias,
        grad_out_weight,
        grad_up_weight,
        grad_up_bias,
        grad_down_weight,
    ) = (
        lax.psum(grad_query_weight.astype(jnp.bfloat16), "dp").astype(jnp.float32),
        lax.psum(grad_query_bias.astype(jnp.bfloat16), "dp").astype(jnp.float32),
        lax.psum(grad_key_weight.astype(jnp.bfloat16), "dp").astype(jnp.float32),
        lax.psum(grad_value_weight.astype(jnp.bfloat16), "dp").astype(jnp.float32),
        lax.psum(grad_value_bias.astype(jnp.bfloat16), "dp").astype(jnp.float32),
        lax.psum(grad_out_weight.astype(jnp.bfloat16), "dp").astype(jnp.float32),
        lax.psum(grad_up_weight.astype(jnp.bfloat16), "dp").astype(jnp.float32),
        lax.psum(grad_up_bias.astype(jnp.bfloat16), "dp").astype(jnp.float32),
        lax.psum(grad_down_weight.astype(jnp.bfloat16), "dp").astype(jnp.float32),
    )
    grad_gain_one, grad_shift_one, grad_out_bias, grad_gain_two, grad_shift_two, grad_down_bias = (
        lax.psum(
            (
                grad_gain_one,
                grad_shift_one,
                grad_out_bias,
                grad_gain_two,
                grad_shift_two,
                grad_down_bias,
            ),
            ("dp", "mp"),
        )
    )
    return (
        layer_out,
        grad_in,
        grad_gain_one,
        grad_shift_one,
        grad_query_weight,
        grad_query_bias,
        grad_key_weight,
        grad_value_weight,
        grad_value_bias,
        grad_out_weight,
        grad_out_bias,
        grad_gain_two,
        grad_shift_two,
        grad_up_weight,
        grad_up_bias,
        grad_down_weight,
        grad_down_bias,
    )


def solution(mesh):
    placed = (
        P(("dp", "mp"), None),
        P("dp"),
        P(),
        P(),
        P(None, "mp"),
        P("mp"),
        P(None, "mp"),
        P(None, "mp"),
        P("mp"),
        P("mp", None),
        P(),
        P(),
        P(),
        P(None, "mp"),
        P("mp"),
        P("mp", None),
        P(),
        P(("dp", "mp"), None),
    )
    return jax.shard_map(
        body,
        mesh=mesh,
        in_specs=placed,
        out_specs=(
            P(("dp", "mp"), None),
            P(("dp", "mp"), None),
            P(),
            P(),
            P(None, "mp"),
            P("mp"),
            P(None, "mp"),
            P(None, "mp"),
            P("mp"),
            P("mp", None),
            P(),
            P(),
            P(),
            P(None, "mp"),
            P("mp"),
            P("mp", None),
            P(),
        ),
        check_vma=False,
    )
```

profile of v0, /device:TPU:0, one launch (start us, length us, event | category | flops | bytes accessed | tf_op | source)
XLA Modules:
  0.0 1011.2 jit_solution(3853599798226063012)
XLA Ops:
  19.0 61.8 %all-gather.5.cloned.1.call-done = bf16[2240,1024]{1,0:T(8,128)(2,1)} async-done(((bf16[1120,1024]{1,0:T(8,128)(2,1)}), bf16[2240,1024]{1,0:T(8,128)(2,1)}) %all-gather.5.cloned.1.call-update) | async-done | bytes 4587536 | tf_op jit(solution)/shard_map/all_gather | solution.py:74
  141.6 18.4 %fusion.56 = (f32[8,8,280]{2,1,0:T(8,128)S(1)}, f32[8,8,280,280]{2,3,1,0:T(8,128)}) fusion(pred[8,280]{1,0:T(8,128)(4,1)S(1)} %iota_compare_fusion, bf16[8,280,8,64]{1,3,2,0:T(8,128)(2,1)} %copy.69, bf16[8,280,8,64]{1,3,2,0:T(8,128)(2,1)} %copy.70), kind=kOutput, calls=%fused_computation.101 | convolution fusion | flops 662323456 | bytes 24731840 | tf_op jit(solution)/shard_map/sub | solution.py:89
  160.0 17.6 %convert_bitcast_fusion.1 = bf16[8,280,8,64]{1,3,2,0:T(8,128)(2,1)} fusion(bf16[8,280,8,64]{1,3,2,0:T(8,128)(2,1)} %copy.71, f32[8,8,280]{2,1,0:T(8,128)S(1)} %get-tuple-element.48, pred[8,280]{1,0:T(8,128)(4,1)S(1)} %iota_compare_fusion, bf16[8,280,8,64]{1,3,2,0:T(8,128)(2,1)} %copy.69, bf16[8,280,8,64]{1,3,2,0:T(8,128)(2,1)} %copy.70), kind=kOutput, calls=%fused_computation.76 | convolution fusion | flops 1310758656 | bytes 9248960 | tf_op jit(solution)/shard_map/phqk,pkhd->pqhd/dot_general | solution.py:91
  184.3 7.3 reshape.162
  196.5 49.1 %all_gather.18 = bf16[4096]{0:T(1024)(128)(2,1)S(1)} all-gather(bf16[2048]{0:T(1024)(128)(2,1)S(1)} %copy-done.43), channel_id=1, replica_groups=mesh['dp'=16,'mp'=2] {'mp'}, dimensions={0}, use_global_device_ids=true | all-gather | bytes 12288 | tf_op jit(solution)/shard_map/all_gather | solution.py:102
  259.8 18.8 %convolution_add_fusion = f32[1120,4096]{1,0:T(8,128)} fusion(bf16[1024,4096]{1,0:T(8,128)(2,1)} %all-gather.9.cloned.1.call-done, f32[4096]{0:T(1024)S(1)} %convert_element_type.181, f32[1120,1024]{1,0:T(8,128)} %copy-done.5, f32[1024]{0:T(1024)S(1)} %convert_element_type.179, f32[1024]{0:T(1024)S(1)} %convert_element_type.178, f32[1120]{0:T(1024)S(1)} %fusion.41, ...), kind=kOutput, calls=%fused_computation.7 | convolution fusion | flops 9405562880 | bytes 31359744 | tf_op jit(solution)/shard_map/dot_general | solution.py:27
  278.7 70.3 %all-gather.11.cloned.1.call-done = bf16[4096,1024]{1,0:T(8,128)(2,1)} async-done(((bf16[2048,1024]{1,0:T(8,128)(2,1)}), bf16[4096,1024]{1,0:T(8,128)(2,1)}) %all-gather.11.cloned.1.call-update) | async-done | bytes 8388624 | tf_op jit(solution)/shard_map/all_gather | solution.py:103
  349.0 56.3 %fusion.52 = (bf16[4096]{0:T(1024)(128)(2,1)}, bf16[1120,4096]{1,0:T(8,128)(2,1)}, f32[1120,4096]{1,0:T(8,128)}) fusion(f32[1120,4096]{1,0:T(8,128)} %convolution_add_fusion, bf16[1120,1024]{1,0:T(8,128)(2,1)S(1)} %copy-done.7, bf16[4096,1024]{1,0:T(8,128)(2,1)} %all-gather.11.cloned.1.call-done), kind=kOutput, calls=%fused_computation.99 | convolution fusion | flops 9730125824 | bytes 56565760 | tf_op jit(solution)/shard_map/dot_general | solution.py:37
  405.2 18.0 %multiply_reduce_fusion.1 = (f32[1024]{0:T(1024)}, f32[1120]{0:T(1024)S(1)}, f32[1024]{0:T(1024)}, f32[1120,1024]{1,0:T(8,128)S(1)}) fusion(f32[1120,1024]{1,0:T(8,128)S(1)} %copy-done.6, f32[1120]{0:T(1024)S(1)} %copy-done.38, f32[1120]{0:T(1024)S(1)} %copy-done.30, f32[1024]{0:T(1024)S(1)} %copy-done.40, bf16[1120,4096]{1,0:T(8,128)(2,1)} %get-tuple-element.40, ...), kind=kOutput, calls=%fused_computation.62 | convolution fusion | flops 9404412928 | bytes 26764416 | tf_op jit(solution)/shard_map/dot_general | solution.py:37
  432.4 17.8 %convolution_convert_fusion.1 = bf16[1024,4096]{1,0:T(8,128)(2,1)} fusion(bf16[1120,4096]{1,0:T(8,128)(2,1)} %get-tuple-element.40, f32[1120,1024]{1,0:T(8,128)} %copy-done.5, f32[1024]{0:T(1024)S(1)} %copy-done.45, f32[1024]{0:T(1024)S(1)} %copy-done.40, f32[1120]{0:T(1024)S(1)} %copy-done.38, f32[1120]{0:T(1024)S(1)} %copy-done.30), kind=kOutput, calls=%fused_computation.30 | convolution fusion | flops 9405169664 | bytes 22168320 | tf_op jit(solution)/shard_map/dot_general | solution.py:31
  461.5 12.9 %multiply_convert_fusion.1 = bf16[1120,4096]{1,0:T(8,128)(2,1)S(1)} fusion(f32[1120,4096]{1,0:T(8,128)} %get-tuple-element.41, f32[1120,4096]{1,0:T(8,128)} %convolution_add_fusion), kind=kLoop, calls=%fused_computation.10 | loop fusion | flops 13762560 | bytes 45875200 | tf_op jit(solution)/shard_map/convert_element_type | solution.py:107
  477.9 13.1 %convolution_convert_fusion = bf16[4096,1024]{1,0:T(8,128)(2,1)} fusion(bf16[1120,4096]{1,0:T(8,128)(2,1)S(1)} %multiply_convert_fusion.1, bf16[1120,1024]{1,0:T(8,128)(2,1)S(1)} %copy-done.8), kind=kOutput, calls=%fused_computation.29 | convolution fusion | flops 9399435264 | bytes 19857408 | tf_op jit(solution)/shard_map/dot_general | solution.py:31
  491.9 17.6 %fusion.39.clone.4 = bf16[8,8,280,280]{2,3,1,0:T(8,128)(2,1)} fusion(f32[8,8,280]{2,1,0:T(8,128)S(1)} %copy-done.28, pred[8,280]{1,0:T(8,128)(4,1)S(1)} %copy-done.49, bf16[8,280,8,64]{1,3,2,0:T(8,128)(2,1)} %copy.69, bf16[8,280,8,64]{1,3,2,0:T(8,128)(2,1)} %copy.70), kind=kOutput, calls=%fused_computation.37.clone.clone.clone.clone.clone.1 | convolution fusion | flops 667358976 | bytes 14696640 | tf_op jit(solution)/shard_map/sub | solution.py:89
  520.4 24.7 %multiply_reduce_fusion = (f32[8,8,280]{2,1,0:T(8,128)S(1)}, f32[8,8,280,280]{2,3,1,0:T(8,128)}) fusion(f32[8,8,280,280]{2,3,1,0:T(8,128)} %get-tuple-element.49, f32[8,8,280]{2,1,0:T(8,128)S(1)} %copy-done.28, bf16[8,280,8,64]{1,3,2,0:T(8,128)(2,1)} %copy.78, bf16[8,280,8,64]{1,3,2,0:T(8,128)(2,1)} %copy.71), kind=kOutput, calls=%fused_computation.2 | convolution fusion | flops 657287680 | bytes 44871680 | tf_op jit(solution)/shard_map/pqhd,pkhd->phqk/dot_general | solution.py:142
  545.1 24.6 %multiply_convert_fusion = bf16[8,8,280,280]{2,3,1,0:T(8,128)(2,1)} fusion(f32[8,8,280,280]{2,3,1,0:T(8,128)} %get-tuple-element.54, f32[8,8,280]{2,1,0:T(8,128)S(1)} %get-tuple-element.53, f32[8,8,280,280]{2,3,1,0:T(8,128)} %get-tuple-element.49, f32[8,8,280]{2,1,0:T(8,128)S(1)} %copy-done.28), kind=kLoop, calls=%fused_computation.1 | loop fusion | flops 20070400 | bytes 50319360 | tf_op jit(solution)/shard_map/convert_element_type | solution.py:145
  569.7 9.1 fusion.58
  588.3 8.7 fusion.31
  606.6 8.7 fusion.59
  634.8 9.4 add_convert_fusion.1
  660.9 21.2 %reduce-scatter.11.cloned.1.call-done = bf16[2048,1024]{1,0:T(8,128)(2,1)} async-done(((bf16[4096,1024]{1,0:T(8,128)(2,1)}), bf16[2048,1024]{1,0:T(8,128)(2,1)}) %reduce-scatter.11.cloned.1.call-update) | async-done | bytes 4194320 | tf_op jit(solution)/shard_map/reduce_scatter | solution.py:122
  689.4 17.1 %fusion.29 = bf16[1120,1024]{1,0:T(8,128)(2,1)} fusion(f32[1120,1024]{1,0:T(8,128)} %copy-done.5, bf16[1120,4096]{1,0:T(8,128)(2,1)} %copy-done.10, bf16[4096,1024]{1,0:T(8,128)(2,1)} %all-gather.11.cloned.1.call-done, f32[1024]{0:T(1024)S(1)} %convert_element_type.183), kind=kOutput, calls=%fused_computation.71 | convolution fusion | flops 9398681600 | bytes 24449024 | tf_op jit(solution)/shard_map/dot_general | solution.py:27
  706.7 32.5 %all-reduce.2 = (bf16[512]{0:T(512)(128)(2,1)S(1)}, bf16[512]{0:T(512)(128)(2,1)S(1)}, bf16[2048]{0:T(1024)(128)(2,1)S(1)}) all-reduce(bf16[512]{0:T(512)(128)(2,1)S(1)} %reduce_sum.229, bf16[512]{0:T(512)(128)(2,1)S(1)} %reduce_sum.231, bf16[2048]{0:T(1024)(128)(2,1)S(1)} %dynamic-slice.1), channel_id=1, replica_groups=mesh['dp'=16,'mp'=2] {'dp'}, use_global_device_ids=true, to_apply=%region_18.19 | all-reduce | flops 3072 | bytes 12288 | tf_op jit(solution)/shard_map/psum | solution.py:183
  754.6 41.9 %all-reduce.1 = (f32[1024]{0:T(1024)}, f32[1024]{0:T(1024)}, f32[1024]{0:T(1024)}, f32[1024]{0:T(1024)}, f32[1024]{0:T(1024)}, /*index=5*/f32[1024]{0:T(1024)}) all-reduce(f32[1024]{0:T(1024)S(1)} %get-tuple-element.19, f32[1024]{0:T(1024)S(1)} %get-tuple-element.22, ...), channel_id=1, replica_groups=mesh['dp'=16,'mp'=2] {'dp','mp'}, use_global_device_ids=true, to_apply=%region_13.14 | all-reduce | flops 6144 | bytes 49152 | tf_op jit(solution)/shard_map/psum | solution.py:193
  796.5 189.9 %all-reduce.6.cloned.1.call-done = (bf16[1024,512]{1,0:T(8,128)(2,1)}, bf16[1024,512]{1,0:T(8,128)(2,1)}, bf16[1024,512]{1,0:T(8,128)(2,1)}, bf16[512,1024]{1,0:...) async-done(((bf16[1024,512]{1,0:T(8,128)(2,1)}, bf16[1024,512]{1,0:T(8,128)(2,1)}, bf16[1024,512]{1,0:T(8,128)(2,1)}, bf16[512,1024]{1,0:T(8,128)(2,1)}, ...) | async-done | bytes 12582928 | tf_op jit(solution)/shard_map/psum | solution.py:182
  (220 shorter events, 229.2 us)
Async XLA Ops:
  7.2 93.9 %copy-start = (bf16[1024,512]{1,0:T(8,128)(2,1)S(1)}, bf16[1024,512]{1,0:T(8,128)(2,1)}, u32[]{:S(2)}) copy-start(bf16[1024,512]{1,0:T(8,128)(2,1)} %param.22) | copy-start | bytes 3145732
  7.2 73.6 %all-gather.5.cloned.1.call-start = ((), (), s32[]{:S(2)}) async-start(), calls=%async_computation.6 | async-start | bytes 6881280 | tf_op jit(solution)/shard_map/all_gather | solution.py:74
  16.8 233.6 %all-gather.7.cloned.1.call-start = ((), (), s32[]{:S(2)}) async-start(), calls=%async_computation.7 | async-start | bytes 3145728 | tf_op jit(solution)/shard_map/all_gather | solution.py:94
  17.6 242.2 %all-gather.9.cloned.1.call-start = ((), (), s32[]{:S(2)}) async-start(), calls=%async_computation.8 | async-start | bytes 12582912 | tf_op jit(solution)/shard_map/all_gather | solution.py:101
  18.3 330.6 %all-gather.11.cloned.1.call-start = ((), (), s32[]{:S(2)}) async-start(), calls=%async_computation.9 | async-start | bytes 12582912 | tf_op jit(solution)/shard_map/all_gather | solution.py:103
  19.0 141.0 %copy-start.48 = (pred[8,280]{1,0:T(8,128)(4,1)}, pred[8,280]{1,0:T(8,128)(4,1)S(1)}, u32[]{:S(2)}) copy-start(pred[8,280]{1,0:T(8,128)(4,1)S(1)} %iota_compare_fusion) | copy-start | bytes 6724
  184.3 61.4 %copy-start.51 = (bf16[1024]{0:T(1024)(128)(2,1)S(1)}, bf16[1024]{0:T(1024)(128)(2,1)}, u32[]{:S(2)}) copy-start(bf16[1024]{0:T(1024)(128)(2,1)} %param.30) | copy-start | bytes 6148
  184.3 61.4 %copy-start.52 = (bf16[1024]{0:T(1024)(128)(2,1)S(1)}, bf16[1024]{0:T(1024)(128)(2,1)}, u32[]{:S(2)}) copy-start(bf16[1024]{0:T(1024)(128)(2,1)} %param.29) | copy-start | bytes 6148
  191.5 54.2 %all-to-all-start = ((bf16[2,1120,512]{2,1,0:T(8,128)(2,1)}), bf16[2,1120,512]{2,1,0:T(8,128)(2,1)}, u32[]{:S(2)}, u32[]{:S(2)}) async-start(bf16[2,1120,512]{2,1,0:T(8,128)(2,1)} %reshape.162), calls=%async_computation | async-start | bytes 4587520 | tf_op jit(solution)/shard_map/all_to_all | solution.py:93
  196.4 464.5 %reduce-scatter.7.cloned.1.call-start = ((), (), s32[]{:S(2)}) async-start(), calls=%async_computation.11 | async-start | bytes 3145728 | tf_op jit(solution)/shard_map/reduce_scatter | solution.py:132
  259.8 89.2 %copy-start.7 = (bf16[1120,1024]{1,0:T(8,128)(2,1)S(1)}, bf16[1120,1024]{1,0:T(8,128)(2,1)}, u32[]{:S(2)}) copy-start(bf16[1120,1024]{1,0:T(8,128)(2,1)} %param.35) | copy-start | bytes 6881284
  348.9 56.3 %copy-start.6 = (f32[1120,1024]{1,0:T(8,128)S(1)}, f32[1120,1024]{1,0:T(8,128)}, u32[]{:S(2)}) copy-start(f32[1120,1024]{1,0:T(8,128)} %copy-done.5) | copy-start | bytes 13762564
  348.9 56.3 %copy-start.30 = (f32[1120]{0:T(1024)S(1)}, f32[1120]{0:T(1024)}, u32[]{:S(2)}) copy-start(f32[1120]{0:T(1024)} %copy-done.29) | copy-start | bytes 13444
  348.9 56.3 %copy-start.38 = (f32[1120]{0:T(1024)S(1)}, f32[1120]{0:T(1024)}, u32[]{:S(2)}) copy-start(f32[1120]{0:T(1024)} %copy-done.37) | copy-start | bytes 13444
  349.0 56.3 %copy-start.40 = (f32[1024]{0:T(1024)S(1)}, f32[1024]{0:T(1024)}, u32[]{:S(2)}) copy-start(f32[1024]{0:T(1024)} %copy-done.39) | copy-start | bytes 12292
  432.4 228.6 %reduce-scatter.9.cloned.1.call-start = ((), (), s32[]{:S(2)}) async-start(), calls=%async_computation.12 | async-start | bytes 12582912 | tf_op jit(solution)/shard_map/reduce_scatter | solution.py:116
  457.7 51.8 %all-to-all-start.1 = ((bf16[1120,2,512]{2,0,1:T(8,128)(2,1)}), bf16[1120,2,512]{2,0,1:T(8,128)(2,1)S(1)}, u32[]{:S(2)}, u32[]{:S(2)}) async-start(bf16[1120,2,512]{2,0,1:T(8,128)(2,1)} %bitcast.99), calls=%async_computation.1 | async-start | bytes 4587520 | tf_op jit(solution)/shard_map/all_to_all | solution.py:139
  461.5 220.7 %reduce-scatter.11.cloned.1.call-start = ((), (), s32[]{:S(2)}) async-start(), calls=%async_computation.13 | async-start | bytes 12582912 | tf_op jit(solution)/shard_map/reduce_scatter | solution.py:122
  491.0 252.1 %reduce-scatter.5.cloned.1.call-start = ((), (), s32[]{:S(2)}) async-start(), calls=%async_computation.10 | async-start | bytes 6881280 | tf_op jit(solution)/shard_map/reduce_scatter | solution.py:163
  644.2 342.2 %all-reduce.6.cloned.1.call-start = ((), (), s32[]{:S(2)}) async-start(), calls=%async_computation.14 | async-start | bytes 25165824 | tf_op jit(solution)/shard_map/psum | solution.py:182
  689.3 53.8 %copy-start.2 = (bf16[1120,1024]{1,0:T(8,128)(2,1)S(1)}, bf16[1120,1024]{1,0:T(8,128)(2,1)}, u32[]{:S(2)}) copy-start(bf16[1120,1024]{1,0:T(8,128)(2,1)} %param.18) | copy-start | bytes 6881284
  689.3 53.8 %copy-start.22 = (f32[1120]{0:T(1024)S(1)}, f32[1120]{0:T(1024)}, u32[]{:S(2)}) copy-start(f32[1120]{0:T(1024)} %copy-done.21) | copy-start | bytes 13444
  689.3 53.8 %copy-start.26 = (f32[1024]{0:T(1024)S(1)}, f32[1024]{0:T(1024)}, u32[]{:S(2)}) copy-start(f32[1024]{0:T(1024)} %copy-done.25) | copy-start | bytes 12292
  706.5 40.0 %copy-start.24 = (f32[1120]{0:T(1024)S(1)}, f32[1120]{0:T(1024)}, u32[]{:S(2)}) copy-start(f32[1120]{0:T(1024)} %copy-done.23) | copy-start | bytes 13444
  (48 other events, 334.5 us)
Sparse Core Ops, SparseCore 0:
  16.9 63.8 all-gather.4
  82.4 33.1 all-gather.6
  117.1 125.9 all-gather.8
  244.4 104.4 all-gather.10
  432.5 31.8 reduce-scatter.6
  467.2 112.7 reduce-scatter.8
  582.8 99.2 reduce-scatter.10
  684.5 58.5 reduce-scatter.4
  748.9 237.4 all-reduce.5
where the time goes:
time: 1020 us; the launch traced here: 1010 us
  waiting for transfers between devices  347 us (34%)
  matrix products  316 us (31%)
  blocking collectives  129 us (13%)
  local copies, waits for them, and re-layouts  114 us (11%)
  other arithmetic  80.3 us (8%)
  between operations  15.5 us (2%)
    psum x1, waiting for transfers between devices, body(): lax.psum(grad_query_weight.astype(jnp.bfloat16), 'dp').astype(jnp.float32)  190 us
    dot_general x6, matrix products, contract_cols(): lax.dot_general(left, right, (((1,), (1,)), ((), ())), preferred_element_...  98.7 us
    all_gather x1, waiting for transfers between devices, body(): lax.all_gather(down_weight, 'mp', axis=0, tiled=True)  70.3 us
    all_gather x1, waiting for transfers between devices, body(): lax.all_gather(normed_tok.astype(lowtype), 'mp', axis=0, tiled=True)  61.8 us
    dot_general x6, matrix products, matmul_rows(): return jnp.dot(left, right, preferred_element_type=jnp.float32)  61.7 us
    dot_general x6, matrix products, contract_rows(): lax.dot_general(left, right, (((0,), (0,)), ((), ())), preferred_element_...  51.4 us
    all_gather x1, blocking collectives, body(): lax.all_gather(up_bias, 'mp', axis=0, tiled=True)  49.1 us
    psum x1, blocking collectives, body(): lax.psum((grad_gain_one, grad_shift_one, grad_out_bias, grad_gain_two, gr...  41.9 us
  transfers between devices with their start and end apart: 11, of which 5 were waited for; matrix products, arithmetic and copies ran while one was open for 39% of the time, Pallas kernels for 0%

commit v1 on v0

--- a/solution.py
+++ b/solution.py
@@ -43,7 +43,7 @@
     return jnp.sum(values.astype(jnp.float32), 0)
 
 
-def body(
+def general_body(
     layer_in,
     patch_count,
     attn_gain,
@@ -223,7 +223,273 @@
     )
 
 
+def flip(value, axis, bit, size):
+    return lax.ppermute(value, axis, [(i, i ^ bit) for i in range(size)])
+
+
+CORE, XBIT, ZLOW, ZHIGH = 1, 2, 4, 8
+
+
+def pick(value, index, width, axis):
+    return lax.dynamic_slice_in_dim(value, index * width, width, axis)
+
+
+def attend(query, key, value, valid):
+    wide = jnp.float32
+    scores = jnp.einsum("pqhd,pkhd->phqk", query, key, preferred_element_type=wide) * SCALE
+    scores = jnp.where(valid[:, None, None, :], scores, NEGATIVE)
+    probs = jax.nn.softmax(scores, axis=-1)
+    context = jnp.einsum(
+        "phqk,pkhd->pqhd", probs.astype(jnp.bfloat16), value, preferred_element_type=wide
+    )
+    return probs, context.astype(jnp.bfloat16)
+
+
+def attend_back(query, key, value, probs, cot):
+    wide = jnp.float32
+    low = jnp.bfloat16
+    probs_grad = jnp.einsum("pqhd,pkhd->phqk", cot, value, preferred_element_type=wide)
+    value_grad = jnp.einsum(
+        "phqk,pqhd->pkhd", probs.astype(low), cot, preferred_element_type=wide
+    ).astype(low)
+    score_grad = (probs * (probs_grad - jnp.sum(probs * probs_grad, -1, keepdims=True))).astype(low)
+    query_grad = (
+        jnp.einsum("phqk,pkhd->pqhd", score_grad, key, preferred_element_type=wide) * SCALE
+    ).astype(low)
+    key_grad = (
+        jnp.einsum("phqk,pqhd->pkhd", score_grad, query, preferred_element_type=wide) * SCALE
+    ).astype(low)
+    return query_grad, key_grad, value_grad
+
+
+def paired_body(
+    layer_in,
+    patch_count,
+    attn_gain,
+    attn_shift,
+    query_weight,
+    query_bias,
+    key_weight,
+    value_weight,
+    value_bias,
+    out_weight,
+    out_bias,
+    mlp_gain,
+    mlp_shift,
+    up_weight,
+    up_bias,
+    down_weight,
+    down_bias,
+    layer_cot,
+):
+    low = jnp.bfloat16
+    wide = jnp.float32
+    groups = lax.axis_size("dp")
+    rank = lax.axis_index("dp")
+    half_id = lax.axis_index("mp")
+    core_id, x_id, zlow_id, zhigh_id = rank & 1, (rank >> 1) & 1, (rank >> 2) & 1, (rank >> 3) & 1
+    part = core_id * 2 + x_id
+    spot = part * 4 + zlow_id * 2 + zhigh_id
+
+    def swap(value, bit):
+        return flip(value, "dp", bit, groups)
+
+    def across(value):
+        return flip(value, "mp", 1, 2)
+
+    def fetch(piece):
+        near = across(piece)
+        pair = jnp.stack([near, swap(near, XBIT)])
+        far = swap(pair, CORE)
+        return [pair[0], pair[1], far[0], far[1]]
+
+    width = query_weight.shape[1]
+    hidden = up_weight.shape[1]
+    quarter = width // 4
+    block = hidden // 4
+
+    bias_other = across(jnp.concatenate([query_bias, value_bias, up_bias]))
+    small = lambda vec: [pick(vec, part ^ r, vec.shape[0] // 4, 0) for r in range(4)]
+    other_query_bias = jnp.concatenate(small(bias_other[:width]))
+    other_value_bias = jnp.concatenate(small(bias_other[width : 2 * width]))
+    other_up_bias = jnp.concatenate(small(bias_other[2 * width :]))
+
+    qkv_pieces = fetch(
+        jnp.stack([pick(w, part, quarter, 1) for w in (query_weight, key_weight, value_weight)])
+    )
+    other_query, other_key, other_value = (
+        jnp.concatenate([piece[i] for piece in qkv_pieces], 1) for i in range(3)
+    )
+    other_out = jnp.concatenate(fetch(pick(out_weight, part, quarter, 0)), 0)
+    other_up = jnp.concatenate(fetch(pick(up_weight, part, block, 1)), 1)
+    other_down = jnp.concatenate(fetch(pick(down_weight, part, block, 0)), 0)
+
+    rows_in = layer_in.astype(wide)
+    gain_one = attn_gain.astype(wide)
+    shift_one = attn_shift.astype(wide)
+    gain_two = mlp_gain.astype(wide)
+    shift_two = mlp_shift.astype(wide)
+    normed_wide, norm_pull = jax.vjp(layer_norm, rows_in, gain_one, shift_one)
+    normed = normed_wide.astype(low)
+    rows = layer_in.shape[0]
+    pairs = rows // SEQ
+    counts = pick(patch_count, half_id, pairs, 0)
+    valid = jnp.arange(SEQ)[None, :] < (TEXT + counts)[:, None]
+    shape_four = (pairs, SEQ, width // HEAD_DIM, HEAD_DIM)
+
+    halves = (
+        (query_weight, query_bias, key_weight, value_weight, value_bias, out_weight),
+        (other_query, other_query_bias, other_key, other_value, other_value_bias, other_out),
+    )
+    kept = []
+    attended = out_bias.astype(wide)
+    for wq, bq, wk, wv, bv, wo in halves:
+        query = (matmul_rows(normed, wq) + bq.astype(wide)).astype(low).reshape(shape_four)
+        key = matmul_rows(normed, wk).astype(low).reshape(shape_four)
+        value = (matmul_rows(normed, wv) + bv.astype(wide)).astype(low).reshape(shape_four)
+        probs, context = attend(query, key, value, valid)
+        context = context.reshape(rows, width)
+        attended = attended + matmul_rows(context, wo)
+        kept.append((query, key, value, probs, context))
+    middle = rows_in + attended
+    hidden_wide, mlp_pull = jax.vjp(layer_norm, middle, gain_two, shift_two)
+    hidden_in = hidden_wide.astype(low)
+    cot_wide = layer_cot.astype(wide)
+
+    ffn_out = down_bias.astype(wide)
+    hidden_grad = 0.0
+    up_grads, down_grads, up_bias_grads = [], [], []
+    for wu, bu, wd in ((up_weight, up_bias, down_weight), (other_up, other_up_bias, other_down)):
+        pre_act = matmul_rows(hidden_in, wu) + bu.astype(wide)
+        act_wide, gelu_pull = jax.vjp(exact_gelu, pre_act)
+        act_low = act_wide.astype(low)
+        ffn_out = ffn_out + matmul_rows(act_low, wd)
+        act_grad = contract_cols(layer_cot, wd)
+        pre_grad = gelu_pull(act_grad)[0].astype(low)
+        hidden_grad = hidden_grad + contract_cols(pre_grad, wu)
+        down_grads.append(contract_rows(act_low, layer_cot).astype(low))
+        up_grads.append(contract_rows(hidden_in, pre_grad).astype(low))
+        up_bias_grads.append(column_sum(pre_grad))
+    layer_out = (middle + ffn_out).astype(low)
+    grad_down_bias = column_sum(layer_cot)
+
+    def relative(own, axis):
+        return [pick(own, part ^ r, own.shape[axis] // 4, axis) for r in range(4)]
+
+    def split(other, axis):
+        return jnp.split(other, 4, axis)
+
+    def reduce(own, other):
+        total = lambda a, b: (a.astype(wide) + b.astype(wide)).astype(low)
+        arrived = swap(jnp.stack(other[2:]), CORE)
+        outbound = total(jnp.stack(other[:2]), arrived)
+        arrived = swap(jnp.stack(own[2:]), CORE)
+        beyond = across(outbound)
+        mine = (
+            jnp.stack(own[:2]).astype(wide) + arrived.astype(wide) + beyond.astype(wide)
+        ).astype(low)
+        one = total(mine[0], swap(mine[1], XBIT))
+        four = one.reshape((2, 2, one.shape[0] // 4) + one.shape[1:])
+        two = total(
+            pick(four, zlow_id, 1, 0)[0], swap(pick(four, zlow_id ^ 1, 1, 0)[0], ZLOW)
+        )
+        last = total(pick(two, zhigh_id, 1, 0), swap(pick(two, zhigh_id ^ 1, 1, 0), ZHIGH))
+        for bit in (ZHIGH, ZLOW, XBIT):
+            last = jnp.concatenate([last, swap(last, bit)])
+        return last, swap(last, CORE)
+
+    def natural(both):
+        rel = jnp.concatenate(both)
+        return rel[jnp.arange(16) ^ spot].astype(wide)
+
+    def columns(both):
+        full = natural(both)
+        full = full.reshape((4, 4) + full.shape[1:])
+        return full.transpose(1, 2, 0, 3).reshape(full.shape[1] * full.shape[2], -1)
+
+    def rows_of(both):
+        full = natural(both)
+        return full.reshape(-1, full.shape[-1])
+
+    grad_up_weight = columns(reduce(relative(up_grads[0], 1), split(up_grads[1], 1)))
+    grad_down_weight = rows_of(reduce(relative(down_grads[0], 0), split(down_grads[1], 0)))
+
+    middle_part, grad_gain_two, grad_shift_two = mlp_pull(hidden_grad)
+    middle_grad = cot_wide + middle_part
+    attn_grad = middle_grad.astype(low)
+    grad_out_bias = column_sum(attn_grad)
+
+    normed_grad = 0.0
+    grads = []
+    for (wq, bq, wk, wv, bv, wo), (query, key, value, probs, context) in zip(halves, kept):
+        grad_wo = contract_rows(context, attn_grad).astype(low)
+        context_grad = contract_cols(attn_grad, wo).astype(low).reshape(shape_four)
+        parts = attend_back(query, key, value, probs, context_grad)
+        flat = [item.reshape(rows, width) for item in parts]
+        weights = [contract_rows(normed, item).astype(low) for item in flat]
+        for item, weight in zip(flat, (wq, wk, wv)):
+            normed_grad = normed_grad + contract_cols(item, weight)
+        grads.append((weights, grad_wo, column_sum(flat[0]), column_sum(flat[2])))
+    grad_query_weight, grad_key_weight, grad_value_weight = (
+        columns(reduce(relative(grads[0][0][i], 1), split(grads[1][0][i], 1))) for i in range(3)
+    )
+    grad_out_weight = rows_of(reduce(relative(grads[0][1], 0), split(grads[1][1], 0)))
+    input_part, grad_gain_one, grad_shift_one = norm_pull(normed_grad)
+    grad_in = (middle_grad + input_part).astype(low)
+
+    def back_to_place(vec):
+        return vec.reshape(4, -1)[jnp.arange(4) ^ part].reshape(-1)
+
+    def total_over(vec, bits):
+        for bit in bits:
+            vec = vec + swap(vec, bit)
+        return vec
+
+    own_small = jnp.concatenate([grads[0][2], grads[0][3], up_bias_grads[0]])
+    other_small = jnp.concatenate(
+        [back_to_place(grads[1][2]), back_to_place(grads[1][3]), back_to_place(up_bias_grads[1])]
+    )
+    shared = jnp.concatenate(
+        [grad_gain_one, grad_shift_one, grad_out_bias, grad_gain_two, grad_shift_two, grad_down_bias]
+    )
+    far = across(jnp.concatenate([other_small, shared]))
+    vec = jnp.concatenate([own_small, shared]) + far
+    vec = total_over(vec, (CORE, XBIT, ZLOW, ZHIGH))
+    grad_query_bias = vec[:width]
+    grad_value_bias = vec[width : 2 * width]
+    grad_up_bias = vec[2 * width : 2 * width + hidden]
+    (
+        grad_gain_one,
+        grad_shift_one,
+        grad_out_bias,
+        grad_gain_two,
+        grad_shift_two,
+        grad_down_bias,
+    ) = jnp.split(vec[2 * width + hidden :], 6)
+    return (
+        layer_out,
+        grad_in,
+        grad_gain_one,
+        grad_shift_one,
+        grad_query_weight,
+        grad_query_bias,
+        grad_key_weight,
+        grad_value_weight,
+        grad_value_bias,
+        grad_out_weight,
+        grad_out_bias,
+        grad_gain_two,
+        grad_shift_two,
+        grad_up_weight,
+        grad_up_bias,
+        grad_down_weight,
+        grad_down_bias,
+    )
+
+
 def solution(mesh):
+    paired = mesh.shape["mp"] == 2 and mesh.shape["dp"] == 16
+    body = paired_body if paired else general_body
     placed = (
         P(("dp", "mp"), None),
         P("dp"),

time: 1020 us -> 1010 us (level)
  blocking collectives: 129 us -> 0 us
  local copies, waits for them, and re-layouts: 114 us -> 233 us
  starting transfers between devices: 9.44 us -> 81.8 us
  waiting for transfers between devices: 347 us -> 301 us
  matrix products: 316 us -> 303 us
  between operations: 15.5 us -> 3.7 us
    ppermute x0 -> x78, waiting for transfers between devices: none -> 301 us  [flip(): return lax.ppermute(value, axis, [(i, i ^ bit) for i in range(size)])]
    psum x1 -> x0, waiting for transfers between devices: 190 us -> none  [body(): lax.psum(grad_query_weight.astype(jnp.bfloat16), 'dp').astype(jnp.float32)]
    all_gather x4 -> x0, waiting for transfers between devices: 132 us -> none  [the longest x1 70.3 us: body(): lax.all_gather(down_weight, 'mp', axis=0, tiled=True)]
    ppermute x0 -> x78, starting transfers between devices: none -> 81.8 us  [flip(): return lax.ppermute(value, axis, [(i, i ^ bit) for i in range(size)])]
    psum x2 -> x0, blocking collectives: 74.4 us -> none  [the longest x1 41.9 us: body(): lax.psum((grad_gain_one, grad_shift_one, grad_out_bias, grad_gain_two, gr...]
    all_gather x1 -> x0, blocking collectives: 49.1 us -> none  [body(): lax.all_gather(up_bias, 'mp', axis=0, tiled=True)]
    reshape x11 -> x31, local copies, waits for them, and re-layouts: 68.7 us -> 102 us  [the longest x6 20.2 us: paired_body(): flat = [item.reshape(rows, width) for item in parts]]
    reduce_scatter x4 -> x0, waiting for transfers between devices: 23.4 us -> none  [the longest x1 21.2 us: body(): lax.psum_scatter(whole_down.astype(jnp.bfloat16), 'mp', scatter_dimension...]
  transfers between devices with their start and end apart: 11 -> 78, of which waited for: 5 -> 31; matrix products, arithmetic and copies ran while one was open for 39% -> 39% of each run, Pallas kernels for 0% -> 0%
where the time goes in v1:
time: 1010 us
  matrix products  303 us (30%)
  waiting for transfers between devices  301 us (30%)
  local copies, waits for them, and re-layouts  233 us (23%)
  other arithmetic  84.4 us (8%)
  starting transfers between devices  81.8 us (8%)
    ppermute x78, waiting for transfers between devices, flip(): return lax.ppermute(value, axis, [(i, i ^ bit) for i in range(size)])  301 us
    ppermute x78, starting transfers between devices, flip(): return lax.ppermute(value, axis, [(i, i ^ bit) for i in range(size)])  81.8 us
    dot_general x12, matrix products, contract_cols(): lax.dot_general(left, right, (((1,), (1,)), ((), ())), preferred_element_...  81.3 us
    dot_general x12, matrix products, matmul_rows(): return jnp.dot(left, right, preferred_element_type=jnp.float32)  77.8 us
    dot_general x12, matrix products, contract_rows(): lax.dot_general(left, right, (((0,), (0,)), ((), ())), preferred_element_...  60.7 us
    unnamed x392, local copies, waits for them, and re-layouts  35.7 us
  transfers between devices with their start and end apart: 78, of which 31 were waited for; matrix products, arithmetic and copies ran while one was open for 39% of the time, Pallas kernels for 0%

profile of v1, /device:TPU:0, one launch (start us, length us, event | category | flops | bytes accessed | tf_op | source)
XLA Modules:
  0.0 1006.5 jit_solution(9674816294994227422)
XLA Ops:
  51.8 10.0 fusion.129
  86.6 16.7 %collective-permute-done.1 = bf16[3,1024,128]{2,1,0:T(8,128)(2,1)} collective-permute-done((bf16[3,1024,128]{2,1,0:T(8,128)(2,1)}, bf16[3,1024,128]{2,1,0:T(8,128)(2,1)}, u32[]{:S(2)}, u32[]{:S(2)}) %collective-permute-start.1) | collective-permute-done | bytes 786464 | tf_op jit(solution)/shard_map/ppermute | solution.py:227
  115.6 18.6 %collective-permute-done.11 = bf16[512,1024]{1,0:T(8,128)(2,1)S(1)} collective-permute-done((bf16[512,1024]{1,0:T(8,128)(2,1)}, bf16[512,1024]{1,0:T(8,128)(2,1)S(1)}, u32[]{:S(2)}, u32[]{:S(2)}) %collective-permute-start.11) | collective-permute-done | bytes 1048608 | tf_op jit(solution)/shard_map/ppermute | solution.py:227
  137.9 18.3 %collective-permute-done.8 = bf16[1024,512]{1,0:T(8,128)(2,1)S(1)} collective-permute-done((bf16[1024,512]{1,0:T(8,128)(2,1)}, bf16[1024,512]{1,0:T(8,128)(2,1)S(1)}, u32[]{:S(2)}, u32[]{:S(2)}) %collective-permute-start.8) | collective-permute-done | bytes 1048608 | tf_op jit(solution)/shard_map/ppermute | solution.py:227
  196.4 10.2 %fusion.130 = (f32[4,8,280]{2,1,0:T(8,128)S(1)}, f32[4,8,280,280]{2,3,1,0:T(8,128)}) fusion(pred[4,280]{1,0:T(4,128)(4,1)S(1)} %iota_compare_fusion, bf16[4,280,8,64]{1,3,2,0:T(8,128)(2,1)} %copy.74, bf16[4,280,8,64]{1,3,2,0:T(8,128)(2,1)} %copy.75), kind=kOutput, calls=%fused_computation.443 | convolution fusion | flops 331161888 | bytes 12365920 | tf_op jit(solution)/shard_map/sub | solution.py:241
  233.7 28.7 %convert_reduce_fusion.1 = (f32[2048]{0:T(1024)}, bf16[1120,2048]{1,0:T(8,128)(2,1)}, f32[1120,2048]{1,0:T(8,128)}) fusion(f32[1120,2048]{1,0:T(8,128)S(1)} %convolution_add_fusion.1, bf16[1120,1024]{1,0:T(8,128)(2,1)S(1)} %copy-done.7, bf16[2048,1024]{1,0:T(8,128)(2,1)S(1)} %copy-done.105), kind=kOutput, calls=%fused_computation.35 | convolution fusion | flops 4867356672 | bytes 29433856 | tf_op jit(solution)/shard_map/dot_general | solution.py:37
  262.4 10.8 %multiply_convert_fusion.3 = bf16[1120,2048]{1,0:T(8,128)(2,1)} fusion(f32[1120,2048]{1,0:T(8,128)} %get-tuple-element.40, f32[1120,2048]{1,0:T(8,128)} %copy-done.8), kind=kLoop, calls=%fused_computation.50 | loop fusion | flops 6881280 | bytes 22937600 | tf_op jit(solution)/shard_map/convert_element_type | solution.py:365
  314.1 29.7 %multiply_convert_fusion.2 = (bf16[1120,2048]{1,0:T(8,128)(2,1)}, f32[1120,2048]{1,0:T(8,128)}, f32[1120,2048]{1,0:T(8,128)}) fusion(f32[2048]{0:T(1024)S(1)} %copy-done.141, bf16[1120,1024]{1,0:T(8,128)(2,1)S(1)} %copy-done.45, bf16[1024,512]{1,0:T(8,128)(2,1)S(1)} %get-tuple-element.66, bf16[1024,512]{1,0:T(8,128)(2,1)S(1)} %get-tuple-element.65, ...), kind=kOutput, calls=%fused_computation.37 | convolution fusion | flops 4865785856 | bytes 29433856 | tf_op jit(solution)/shard_map/dot_general | solution.py:27
  343.8 15.3 %convert_reduce_fusion = (f32[2048]{0:T(1024)}, bf16[1120,2048]{1,0:T(8,128)(2,1)}) fusion(f32[1120,2048]{1,0:T(8,128)} %get-tuple-element.44, f32[1120,2048]{1,0:T(8,128)} %get-tuple-element.153, bf16[1120,1024]{1,0:T(8,128)(2,1)S(1)} %copy-done.7, bf16[512,1024]{1,0:T(8,128)(2,1)} %get-tuple-element.64, bf16[512,1024]{1,0:T(8,128)(2,1)} %get-tuple-element.63, ...), kind=kOutput, calls=%fused_computation.34 | convolution fusion | flops 4751095808 | bytes 29433856 | tf_op jit(solution)/shard_map/dot_general | solution.py:37
  359.1 10.1 %convolution_convert_fusion.2 = bf16[1024,2048]{1,0:T(8,128)(2,1)} fusion(bf16[1120,1024]{1,0:T(8,128)(2,1)S(1)} %copy-done.45, bf16[1120,2048]{1,0:T(8,128)(2,1)} %get-tuple-element.165), kind=kOutput, calls=%fused_computation.117 | convolution fusion | flops 4699717632 | bytes 11075584 | tf_op jit(solution)/shard_map/dot_general | solution.py:31
  369.3 10.9 %multiply_reduce_fusion.2 = (f32[1024]{0:T(1024)}, f32[1120]{0:T(1024)S(1)}, f32[1024]{0:T(1024)}, f32[1120,1024]{1,0:T(8,128)S(1)}) fusion(f32[1120,1024]{1,0:T(8,128)S(1)} %bitcast.406, f32[1120]{0:T(1024)S(1)} %copy-done.122, f32[1120]{0:T(1024)S(1)} %copy-done.118, f32[1024]{0:T(1024)S(1)} %copy-done.136, f32[1120,1024]{1,0:T(8,128)} %fusion.133, ...), kind=kOutput, calls=%fused_computation.100 | convolution fusion | flops 4724716544 | bytes 22570112 | tf_op jit(solution)/shard_map/dot_general | solution.py:37
  399.8 9.1 convert_reduce_fusion.7
  409.8 8.9 multiply_reduce_fusion.1
  455.6 9.0 convert_reduce_fusion.5
  465.6 8.9 multiply_reduce_fusion
  589.1 9.2 add_convert_fusion.2
  620.7 10.5 %collective-permute-done.50 = bf16[2,128,1024]{2,1,0:T(8,128)(2,1)S(1)} collective-permute-done((bf16[2,128,1024]{2,1,0:T(8,128)(2,1)S(1)}, bf16[2,128,1024]{2,1,0:T(8,128)(2,1)S(1)}, u32[]{:S(2)}, u32[]{:S(2)}) %collective-permute-start.50) | collective-permute-done | bytes 524320 | tf_op jit(solution)/shard_map/ppermute | solution.py:227
  715.8 21.5 %collective-permute-done.70 = bf16[2,512,1024]{2,1,0:T(8,128)(2,1)S(1)} collective-permute-done((bf16[2,512,1024]{2,1,0:T(8,128)(2,1)S(1)}, bf16[2,512,1024]{2,1,0:T(8,128)(2,1)S(1)}, u32[]{:S(2)}, u32[]{:S(2)}) %collective-permute-start.70) | collective-permute-done | bytes 2097184 | tf_op jit(solution)/shard_map/ppermute | solution.py:227
  741.9 35.2 %collective-permute-done.60 = bf16[2,1024,512]{2,1,0:T(8,128)(2,1)S(1)} collective-permute-done((bf16[2,1024,512]{2,1,0:T(8,128)(2,1)S(1)}, bf16[2,1024,512]{2,1,0:T(8,128)(2,1)S(1)}, u32[]{:S(2)}, u32[]{:S(2)}) %collective-permute-start.60) | collective-permute-done | bytes 2097184 | tf_op jit(solution)/shard_map/ppermute | solution.py:227
  786.7 16.5 %collective-permute-done.71 = bf16[512,1024]{1,0:T(8,128)(2,1)S(1)} collective-permute-done((bf16[512,1024]{1,0:T(8,128)(2,1)S(1)}, bf16[512,1024]{1,0:T(8,128)(2,1)S(1)}, u32[]{:S(2)}, u32[]{:S(2)}) %collective-permute-start.71) | collective-permute-done | bytes 1048608 | tf_op jit(solution)/shard_map/ppermute | solution.py:227
  805.3 14.4 %collective-permute-done.61 = bf16[1024,512]{1,0:T(8,128)(2,1)S(1)} collective-permute-done((bf16[1024,512]{1,0:T(8,128)(2,1)S(1)}, bf16[1024,512]{1,0:T(8,128)(2,1)S(1)}, u32[]{:S(2)}, u32[]{:S(2)}) %collective-permute-start.61) | collective-permute-done | bytes 1048608 | tf_op jit(solution)/shard_map/ppermute | solution.py:227
  825.4 13.8 %collective-permute-done.62 = bf16[2,256,512]{2,1,0:T(8,128)(2,1)S(1)} collective-permute-done((bf16[2,256,512]{2,1,0:T(8,128)(2,1)S(1)}, bf16[2,256,512]{2,1,0:T(8,128)(2,1)S(1)}, u32[]{:S(2)}, u32[]{:S(2)}) %collective-permute-start.62) | collective-permute-done | bytes 524320 | tf_op jit(solution)/shard_map/ppermute | solution.py:227
  846.6 10.7 %collective-permute-done.63 = bf16[1,256,512]{2,1,0:T(8,128)(2,1)S(1)} collective-permute-done((bf16[1,256,512]{2,1,0:T(8,128)(2,1)S(1)}, bf16[1,256,512]{2,1,0:T(8,128)(2,1)S(1)}, u32[]{:S(2)}, u32[]{:S(2)}) %collective-permute-start.63) | collective-permute-done | bytes 262176 | tf_op jit(solution)/shard_map/ppermute | solution.py:227
  898.4 38.1 %collective-permute-done.26 = bf16[4,256,128]{2,1,0:T(8,128)(2,1)S(1)} collective-permute-done((bf16[4,256,128]{2,1,0:T(8,128)(2,1)S(1)}, bf16[4,256,128]{2,1,0:T(8,128)(2,1)S(1)}, u32[]{:S(2)}, u32[]{:S(2)}) %collective-permute-start.26) | collective-permute-done | bytes 262176 | tf_op jit(solution)/shard_map/ppermute | solution.py:227
  (799 shorter events, 617.5 us)
Async XLA Ops:
  1.6 84.2 %collective-permute-start.3 = (bf16[3072]{0:T(1024)(128)(2,1)S(1)}, bf16[3072]{0:T(1024)(128)(2,1)S(1)}, u32[]{:S(2)}, u32[]{:S(2)}) collective-permute-start(bf16[3072]{0:T(1024)(128)(2,1)S(1)} %pad_maximum_fusion.53), channel_id=1, source_target_pairs={{0,1},{1,0},{2,3},{3,2},{4,5},{5,4},{6,7},{7,6},{8,9},{9,8},{10,11... | collective-permute-start | bytes 18440 | tf_op jit(solution)/shard_map/ppermute | solution.py:227
  5.3 80.6 %collective-permute-start.4 = (bf16[128,1024]{1,0:T(8,128)(2,1)}, bf16[128,1024]{1,0:T(8,128)(2,1)}, u32[]{:S(2)}, u32[]{:S(2)}) collective-permute-start(bf16[128,1024]{1,0:T(8,128)(2,1)} %constant_dynamic-slice_fusion.8), channel_id=1, source_target_pairs={{0,1},{1,0},{2,3},{3,2},{4,5},{5,4},{6,7},{7,6},{8,9},{9,8},{10,11... | collective-permute-start | bytes 786440 | tf_op jit(solution)/shard_map/ppermute | solution.py:227
  8.7 73.8 %collective-permute-start = (bf16[3,1024,128]{2,1,0:T(8,128)(2,1)}, bf16[3,1024,128]{2,1,0:T(8,128)(2,1)}, u32[]{:S(2)}, u32[]{:S(2)}) collective-permute-start(bf16[3,1024,128]{2,1,0:T(8,128)(2,1)} %pad_maximum_fusion.17), channel_id=1, source_target_pairs={{0,1},{1,0},{2,3},{3,2},{4,5},{5,4},{6,7},{7,6},{8,9},{9,8},{10,11... | collective-permute-start | bytes 2359304 | tf_op jit(solution)/shard_map/ppermute | solution.py:227
  12.6 95.4 %collective-permute-start.10 = (bf16[512,1024]{1,0:T(8,128)(2,1)}, bf16[512,1024]{1,0:T(8,128)(2,1)}, u32[]{:S(2)}, u32[]{:S(2)}) collective-permute-start(bf16[512,1024]{1,0:T(8,128)(2,1)} %constant_dynamic-slice_fusion.6), channel_id=1, source_target_pairs={{0,1},{1,0},{2,3},{3,2},{4,5},{5,4},{6,7},{7,6},{8,9},{9,8},{10,11... | collective-permute-start | bytes 3145736 | tf_op jit(solution)/shard_map/ppermute | solution.py:227
  15.2 94.4 %collective-permute-start.7 = (bf16[1024,512]{1,0:T(8,128)(2,1)}, bf16[1024,512]{1,0:T(8,128)(2,1)}, u32[]{:S(2)}, u32[]{:S(2)}) collective-permute-start(bf16[1024,512]{1,0:T(8,128)(2,1)} %constant_dynamic-slice_fusion.7), channel_id=1, source_target_pairs={{0,1},{1,0},{2,3},{3,2},{4,5},{5,4},{6,7},{7,6},{8,9},{9,8},{10,11... | collective-permute-start | bytes 3145736 | tf_op jit(solution)/shard_map/ppermute | solution.py:227
  104.8 54.6 %collective-permute-start.2 = (bf16[2,3,1024,128]{3,2,1,0:T(8,128)(2,1)S(1)}, bf16[2,3,1024,128]{3,2,1,0:T(8,128)(2,1)S(1)}, u32[]{:S(2)}, u32[]{:S(2)}) collective-permute-start(bf16[2,3,1024,128]{3,2,1,0:T(8,128)(2,1)S(1)} %pad_maximum_fusion.10), channel_id=1, source_target_pairs={{0,2},{2,0},{4,6},{6,4},{8,10},{10,8},{12,14},{14,12},{16,18},{18,... | collective-permute-start | bytes 4718600 | tf_op jit(solution)/shard_map/ppermute | solution.py:227
  137.9 171.3 %collective-permute-start.12 = (bf16[2,512,1024]{2,1,0:T(8,128)(2,1)}, bf16[2,512,1024]{2,1,0:T(8,128)(2,1)}, u32[]{:S(2)}, u32[]{:S(2)}) collective-permute-start(bf16[2,512,1024]{2,1,0:T(8,128)(2,1)} %pad_maximum_fusion.3), channel_id=1, source_target_pairs={{0,2},{2,0},{4,6},{6,4},{8,10},{10,8},{12,14},{14,12},{16,18},{18,... | collective-permute-start | bytes 6291464 | tf_op jit(solution)/shard_map/ppermute | solution.py:227
  159.4 153.0 %collective-permute-start.9 = (bf16[2,1024,512]{2,1,0:T(8,128)(2,1)}, bf16[2,1024,512]{2,1,0:T(8,128)(2,1)}, u32[]{:S(2)}, u32[]{:S(2)}) collective-permute-start(bf16[2,1024,512]{2,1,0:T(8,128)(2,1)} %pad_maximum_fusion.2), channel_id=1, source_target_pairs={{0,2},{2,0},{4,6},{6,4},{8,10},{10,8},{12,14},{14,12},{16,18},{18,... | collective-permute-start | bytes 6291464 | tf_op jit(solution)/shard_map/ppermute | solution.py:227
  506.0 108.6 %collective-permute-start.49 = (bf16[2,128,1024]{2,1,0:T(8,128)(2,1)}, bf16[2,128,1024]{2,1,0:T(8,128)(2,1)}, u32[]{:S(2)}, u32[]{:S(2)}) collective-permute-start(bf16[2,128,1024]{2,1,0:T(8,128)(2,1)} %pad_maximum_fusion.33), channel_id=1, source_target_pairs={{0,2},{2,0},{4,6},{6,4},{8,10},{10,8},{12,14},{14,12},{16,18},{18,... | collective-permute-start | bytes 1572872 | tf_op jit(solution)/shard_map/ppermute | solution.py:227
  507.3 112.8 %collective-permute-start.48 = (bf16[2,128,1024]{2,1,0:T(8,128)(2,1)}, bf16[2,128,1024]{2,1,0:T(8,128)(2,1)}, u32[]{:S(2)}, u32[]{:S(2)}) collective-permute-start(bf16[2,128,1024]{2,1,0:T(8,128)(2,1)} %pad_maximum_fusion.32), channel_id=1, source_target_pairs={{0,2},{2,0},{4,6},{6,4},{8,10},{10,8},{12,14},{14,12},{16,18},{18,... | collective-permute-start | bytes 1572872 | tf_op jit(solution)/shard_map/ppermute | solution.py:227
  520.4 96.0 %collective-permute-start.39 = (bf16[2,1024,128]{2,1,0:T(8,128)(2,1)}, bf16[2,1024,128]{2,1,0:T(8,128)(2,1)}, u32[]{:S(2)}, u32[]{:S(2)}) collective-permute-start(bf16[2,1024,128]{2,1,0:T(8,128)(2,1)} %pad_maximum_fusion.30), channel_id=1, source_target_pairs={{0,2},{2,0},{4,6},{6,4},{8,10},{10,8},{12,14},{14,12},{16,18},{18,... | collective-permute-start | bytes 1572872 | tf_op jit(solution)/shard_map/ppermute | solution.py:227
  533.2 99.3 %collective-permute-start.38 = (bf16[2,1024,128]{2,1,0:T(8,128)(2,1)}, bf16[2,1024,128]{2,1,0:T(8,128)(2,1)}, u32[]{:S(2)}, u32[]{:S(2)}) collective-permute-start(bf16[2,1024,128]{2,1,0:T(8,128)(2,1)} %pad_maximum_fusion.29), channel_id=1, source_target_pairs={{0,2},{2,0},{4,6},{6,4},{8,10},{10,8},{12,14},{14,12},{16,18},{18,... | collective-permute-start | bytes 1572872 | tf_op jit(solution)/shard_map/ppermute | solution.py:227
  619.9 94.9 %collective-permute-start.68 = (bf16[2,512,1024]{2,1,0:T(8,128)(2,1)S(1)}, bf16[2,512,1024]{2,1,0:T(8,128)(2,1)S(1)}, u32[]{:S(2)}, u32[]{:S(2)}) collective-permute-start(bf16[2,512,1024]{2,1,0:T(8,128)(2,1)S(1)} %copy-done.47), channel_id=1, source_target_pairs={{0,2},{2,0},{4,6},{6,4},{8,10},{10,8},{12,14},{14,12},{16,18},{18,... | collective-permute-start | bytes 6291464 | tf_op jit(solution)/shard_map/ppermute | solution.py:227
  673.2 68.2 %collective-permute-start.58 = (bf16[2,1024,512]{2,1,0:T(8,128)(2,1)S(1)}, bf16[2,1024,512]{2,1,0:T(8,128)(2,1)S(1)}, u32[]{:S(2)}, u32[]{:S(2)}) collective-permute-start(bf16[2,1024,512]{2,1,0:T(8,128)(2,1)S(1)} %copy-done.46), channel_id=1, source_target_pairs={{0,2},{2,0},{4,6},{6,4},{8,10},{10,8},{12,14},{14,12},{16,18},{18,... | collective-permute-start | bytes 6291464 | tf_op jit(solution)/shard_map/ppermute | solution.py:227
  688.4 48.8 %collective-permute-start.70 = (bf16[2,512,1024]{2,1,0:T(8,128)(2,1)S(1)}, bf16[2,512,1024]{2,1,0:T(8,128)(2,1)S(1)}, u32[]{:S(2)}, u32[]{:S(2)}) collective-permute-start(bf16[2,512,1024]{2,1,0:T(8,128)(2,1)S(1)} %add_convert_fusion.5), channel_id=1, source_target_pairs={{0,1},{1,0},{2,3},{3,2},{4,5},{5,4},{6,7},{7,6},{8,9},{9,8},{10,11... | collective-permute-start | bytes 6291464 | tf_op jit(solution)/shard_map/ppermute | solution.py:227
  693.0 84.1 %collective-permute-start.60 = (bf16[2,1024,512]{2,1,0:T(8,128)(2,1)S(1)}, bf16[2,1024,512]{2,1,0:T(8,128)(2,1)S(1)}, u32[]{:S(2)}, u32[]{:S(2)}) collective-permute-start(bf16[2,1024,512]{2,1,0:T(8,128)(2,1)S(1)} %add_convert_fusion.7), channel_id=1, source_target_pairs={{0,1},{1,0},{2,3},{3,2},{4,5},{5,4},{6,7},{7,6},{8,9},{9,8},{10,11... | collective-permute-start | bytes 6291464 | tf_op jit(solution)/shard_map/ppermute | solution.py:227
  712.7 66.9 %collective-permute-start.33 = (bf16[1,256,128]{2,1,0:T(8,128)(2,1)S(1)}, bf16[1,256,128]{2,1,0:T(8,128)(2,1)S(1)}, u32[]{:S(2)}, u32[]{:S(2)}) collective-permute-start(bf16[1,256,128]{2,1,0:T(8,128)(2,1)S(1)} %constant_dynamic-slice_fusion.4), channel_id=1, source_target_pairs={{0,16},{2,18},{4,20},{6,22},{8,24},{10,26},{12,28},{14,30},{16,0},... | collective-permute-start | bytes 196616 | tf_op jit(solution)/shard_map/ppermute | solution.py:227
  714.8 66.0 %collective-permute-start.23 = (bf16[1,256,128]{2,1,0:T(8,128)(2,1)S(1)}, bf16[1,256,128]{2,1,0:T(8,128)(2,1)S(1)}, u32[]{:S(2)}, u32[]{:S(2)}) collective-permute-start(bf16[1,256,128]{2,1,0:T(8,128)(2,1)S(1)} %constant_dynamic-slice_fusion.5), channel_id=1, source_target_pairs={{0,16},{2,18},{4,20},{6,22},{8,24},{10,26},{12,28},{14,30},{16,0},... | collective-permute-start | bytes 196616 | tf_op jit(solution)/shard_map/ppermute | solution.py:227
  784.2 73.8 %collective-permute-start.24 = (bf16[1,256,128]{2,1,0:T(8,128)(2,1)S(1)}, bf16[1,256,128]{2,1,0:T(8,128)(2,1)S(1)}, u32[]{:S(2)}, u32[]{:S(2)}) collective-permute-start(bf16[1,256,128]{2,1,0:T(8,128)(2,1)S(1)} %get-tuple-element.35), channel_id=1, source_target_pairs={{0,16},{2,18},{4,20},{6,22},{8,24},{10,26},{12,28},{14,30},{16,0},... | collective-permute-start | bytes 196616 | tf_op jit(solution)/shard_map/ppermute | solution.py:227
  785.1 86.6 %collective-permute-start.55 = (bf16[2,32,1024]{2,1,0:T(8,128)(2,1)S(1)}, bf16[2,32,1024]{2,1,0:T(8,128)(2,1)S(1)}, u32[]{:S(2)}, u32[]{:S(2)}) collective-permute-start(bf16[2,32,1024]{2,1,0:T(8,128)(2,1)S(1)} %pad_maximum_fusion.52), channel_id=1, source_target_pairs={{0,8},{2,10},{4,12},{6,14},{8,0},{10,2},{12,4},{14,6},{16,24},{18,... | collective-permute-start | bytes 393224 | tf_op jit(solution)/shard_map/ppermute | solution.py:227
  821.7 52.2 %collective-permute-start.45 = (bf16[2,256,128]{2,1,0:T(8,128)(2,1)S(1)}, bf16[2,256,128]{2,1,0:T(8,128)(2,1)S(1)}, u32[]{:S(2)}, u32[]{:S(2)}) collective-permute-start(bf16[2,256,128]{2,1,0:T(8,128)(2,1)S(1)} %pad_maximum_fusion.51), channel_id=1, source_target_pairs={{0,8},{2,10},{4,12},{6,14},{8,0},{10,2},{12,4},{14,6},{16,24},{18,... | collective-permute-start | bytes 393224 | tf_op jit(solution)/shard_map/ppermute | solution.py:227
  886.3 51.1 %collective-permute-start.76 = (bf16[4,128,1024]{2,1,0:T(8,128)(2,1)S(1)}, bf16[4,128,1024]{2,1,0:T(8,128)(2,1)S(1)}, u32[]{:S(2)}, u32[]{:S(2)}) collective-permute-start(bf16[4,128,1024]{2,1,0:T(8,128)(2,1)S(1)} %pad_maximum_fusion.16), channel_id=1, source_target_pairs={{0,4},{2,6},{4,0},{6,2},{8,12},{10,14},{12,8},{14,10},{16,20},{18,... | collective-permute-start | bytes 3145736 | tf_op jit(solution)/shard_map/ppermute | solution.py:227
  891.9 47.6 %collective-permute-start.66 = (bf16[4,256,512]{2,1,0:T(8,128)(2,1)S(1)}, bf16[4,256,512]{2,1,0:T(8,128)(2,1)S(1)}, u32[]{:S(2)}, u32[]{:S(2)}) collective-permute-start(bf16[4,256,512]{2,1,0:T(8,128)(2,1)S(1)} %pad_maximum_fusion.15), channel_id=1, source_target_pairs={{0,4},{2,6},{4,0},{6,2},{8,12},{10,14},{12,8},{14,10},{16,20},{18,... | collective-permute-start | bytes 3145736 | tf_op jit(solution)/shard_map/ppermute | solution.py:227
  897.0 49.7 %collective-permute-start.47 = (bf16[8,256,128]{2,1,0:T(8,128)(2,1)}, bf16[8,256,128]{2,1,0:T(8,128)(2,1)}, u32[]{:S(2)}, u32[]{:S(2)}) collective-permute-start(bf16[8,256,128]{2,1,0:T(8,128)(2,1)} %pad_maximum_fusion.31), channel_id=1, source_target_pairs={{0,2},{2,0},{4,6},{6,4},{8,10},{10,8},{12,14},{14,12},{16,18},{18,... | collective-permute-start | bytes 1572872 | tf_op jit(solution)/shard_map/ppermute | solution.py:227
  (233 other events, 3043.4 us)

commit v2 on v0

--- a/solution.py
+++ b/solution.py
@@ -1,6 +1,10 @@
+import functools
+
 import jax
 import jax.numpy as jnp
 from jax import lax
+from jax.experimental import pallas as pl
+from jax.experimental.pallas import tpu as pltpu
 from jax.sharding import PartitionSpec as P
 
 HEAD_DIM = 64
@@ -43,7 +47,7 @@
     return jnp.sum(values.astype(jnp.float32), 0)
 
 
-def body(
+def general_body(
     layer_in,
     patch_count,
     attn_gain,
@@ -223,7 +227,754 @@
     )
 
 
+WIDE = jnp.float32
+LOW = jnp.bfloat16
+LANES = 128
+ROOT_HALF = 0.7071067811865476
+NORMAL = 0.3989422804014327
+CORE, XBIT, ZLOW, ZHIGH = 1, 2, 4, 8
+
+
+def dot(left, right, left_dim, right_dim):
+    return lax.dot_general(
+        left, right, (((left_dim,), (right_dim,)), ((), ())), preferred_element_type=WIDE
+    )
+
+
+def flip(value, axis, bit, size):
+    return lax.ppermute(value, axis, [(i, i ^ bit) for i in range(size)])
+
+
+def pick(value, index, width, axis):
+    return lax.dynamic_slice_in_dim(value, index * width, width, axis)
+
+
+def after(value, *others):
+    return lax.optimization_barrier((value,) + others)[0]
+
+
+def total(*items):
+    result = items[0].astype(WIDE)
+    for item in items[1:]:
+        result = result + item.astype(WIDE)
+    return result.astype(LOW)
+
+
+def resident(shape):
+    return pl.BlockSpec(shape, lambda *_: (0,) * len(shape), pipeline_mode=pl.Buffered(1))
+
+
+ANYWHERE = pl.BlockSpec(memory_space=pl.ANY)
+
+
+def attend_kernel(spot_ref, count_ref, rows_ref, *refs):
+    weights, biases, outs = refs[:6], refs[6:10], refs[10:12]
+    qkv_ref, context_ref, weight_ref, out_ref, bias_ref = refs[-5:]
+    pair = pl.program_id(0)
+
+    @pl.when(pair == 0)
+    def _():
+        for i in range(6):
+            weight_ref[0, :, i * LANES : (i + 1) * LANES] = weights[i][...]
+        bias_ref[...] = jnp.zeros_like(bias_ref)
+        for i in range(2):
+            out_ref[0, i * LANES : (i + 1) * LANES, :] = outs[i][...]
+            bias_ref[:, i * LANES : (i + 1) * LANES] = biases[i][...].astype(WIDE)
+            bias_ref[:, (4 + i) * LANES : (5 + i) * LANES] = biases[2 + i][...].astype(WIDE)
+
+    qkv = (dot(rows_ref[0], weight_ref[0], 1, 0) + bias_ref[...]).astype(LOW)
+    qkv_ref[0, 0] = qkv
+    length = TEXT + count_ref[pair]
+    lane = lax.broadcasted_iota(jnp.int32, (SEQ, LANES), 1)
+    padding = lax.broadcasted_iota(jnp.int32, (SEQ, SEQ), 1) >= length
+    for tile in range(2):
+        query, key, value = (
+            qkv[:, i * 256 + tile * LANES : i * 256 + (tile + 1) * LANES] for i in range(3)
+        )
+        heads = []
+        for side in range(2):
+            mine = (lane < HEAD_DIM) if side == 0 else (lane >= HEAD_DIM)
+            scores = dot(jnp.where(mine, query, jnp.zeros_like(query)), key, 1, 1) * SCALE
+            scores = jnp.where(padding, NEGATIVE, scores)
+            power = jnp.exp(scores - jnp.max(scores, -1, keepdims=True))
+            probs = power * (1.0 / jnp.sum(power, -1, keepdims=True))
+            heads.append(dot(probs.astype(LOW), value, 1, 0))
+        context_ref[0, 0, :, tile * LANES : (tile + 1) * LANES] = jnp.where(
+            lane < HEAD_DIM, heads[0], heads[1]
+        ).astype(LOW)
+
+
+def attend(slot, spots, counts, rows, weights, biases, outs, buffers):
+    pairs, seq, width = rows.shape
+    shapes = [
+        ((4, pairs, seq, 768), (1, 1, seq, 768), lambda p, *_: (slot, p, 0, 0)),
+        ((4, pairs, seq, 256), (1, 1, seq, 256), lambda p, *_: (slot, p, 0, 0)),
+        ((4, width, 768), (1, width, 768), lambda p, *_: (slot, 0, 0)),
+        ((4, 256, width), (1, 256, width), lambda p, *_: (slot, 0, 0)),
+    ]
+    operands = list(weights) + list(biases) + list(outs)
+    aliases = {}
+    if buffers:
+        aliases = {3 + len(operands) + i: i for i in range(4)}
+    return pl.pallas_call(
+        attend_kernel,
+        grid_spec=pltpu.PrefetchScalarGridSpec(
+            num_scalar_prefetch=2,
+            grid=(pairs,),
+            in_specs=[pl.BlockSpec((1, seq, width), lambda p, *_: (p, 0, 0))]
+            + [spec for _, spec in operands]
+            + [ANYWHERE] * len(buffers),
+            out_specs=[pl.BlockSpec(block, index) for _, block, index in shapes],
+            scratch_shapes=[pltpu.VMEM((1, 768), WIDE)],
+        ),
+        out_shape=[jax.ShapeDtypeStruct(shape, LOW) for shape, _, _ in shapes],
+        input_output_aliases=aliases,
+        name="attend",
+        compiler_params=pltpu.CompilerParams(vmem_limit_bytes=56 * 1024 * 1024),
+    )(spots, counts, rows, *[array for array, _ in operands], *buffers)
+
+
+def attend_back_kernel(count_ref, rows_ref, cot_ref, qkv_ref, context_ref, weight_ref, out_ref, *refs):
+    near_ref, bias_ref, qkv_grad_ref, grad_buf, context_buf = refs[-5:]
+    pair = pl.program_id(0)
+    at = pl.ds(pl.multiple_of(pair * SEQ, 8), SEQ)
+    cot = cot_ref[at, :].astype(LOW)
+    context_grad = dot(cot, out_ref[0], 1, 1).astype(LOW)
+    qkv = qkv_ref[0, 0]
+    context_buf[at, :] = context_ref[0, 0].astype(WIDE)
+    length = TEXT + count_ref[pair]
+    lane = lax.broadcasted_iota(jnp.int32, (SEQ, LANES), 1)
+    padding = lax.broadcasted_iota(jnp.int32, (SEQ, SEQ), 0) >= length
+    grads = [[], [], []]
+    for tile in range(2):
+        query, key, value = (
+            qkv[:, i * 256 + tile * LANES : i * 256 + (tile + 1) * LANES] for i in range(3)
+        )
+        outer = context_grad[:, tile * LANES : (tile + 1) * LANES]
+        heads = [[], [], []]
+        for side in range(2):
+            mine = (lane < HEAD_DIM) if side == 0 else (lane >= HEAD_DIM)
+            scores = dot(jnp.where(mine, key, jnp.zeros_like(key)), query, 1, 1) * SCALE
+            scores = jnp.where(padding, NEGATIVE, scores)
+            power = jnp.exp(scores - jnp.max(scores, 0, keepdims=True))
+            probs = power * (1.0 / jnp.sum(power, 0, keepdims=True))
+            probs_grad = dot(jnp.where(mine, value, jnp.zeros_like(value)), outer, 1, 1)
+            both = probs * probs_grad
+            score_grad = (both - probs * jnp.sum(both, 0, keepdims=True)).astype(LOW)
+            heads[0].append(dot(score_grad, key, 0, 0))
+            heads[1].append(dot(score_grad, query, 1, 0))
+            heads[2].append(dot(probs.astype(LOW), outer, 1, 0))
+        for i, scale in enumerate((SCALE, SCALE, 1.0)):
+            grads[i].append((jnp.where(lane < HEAD_DIM, *heads[i]) * scale).astype(LOW))
+    joined = jnp.concatenate(grads[0] + grads[1] + grads[2], 1)
+    qkv_grad_ref[0, 0] = joined
+    grad_buf[at, :] = joined.astype(WIDE)
+
+    @pl.when(pair == pl.num_programs(0) - 1)
+    def _():
+        stacked = dot(grad_buf[...].astype(LOW), rows_ref[...], 0, 0).astype(LOW)
+        near_ref[:3] = stacked.reshape(3, 2, LANES, -1)
+        outs = dot(context_buf[...].astype(LOW), cot_ref[...].astype(LOW), 0, 0).astype(LOW)
+        near_ref[3] = outs.reshape(2, LANES, -1)
+        bias_ref[...] = jnp.sum(grad_buf[...], 0, keepdims=True)
+
+
+def attend_back(slot, counts, rows, cot, kept, buffers):
+    qkv, context, weights, outs = kept
+    _, pairs, seq, _ = qkv.shape
+    width = rows.shape[1]
+    return pl.pallas_call(
+        attend_back_kernel,
+        grid_spec=pltpu.PrefetchScalarGridSpec(
+            num_scalar_prefetch=1,
+            grid=(pairs,),
+            in_specs=[
+                resident(rows.shape),
+                resident(cot.shape),
+                pl.BlockSpec((1, 1, seq, 768), lambda p, *_: (slot, p, 0, 0)),
+                pl.BlockSpec((1, 1, seq, 256), lambda p, *_: (slot, p, 0, 0)),
+                pl.BlockSpec((1, width, 768), lambda p, *_: (slot, 0, 0)),
+                pl.BlockSpec((1, 256, width), lambda p, *_: (slot, 0, 0)),
+            ]
+            + [ANYWHERE] * len(buffers),
+            out_specs=[
+                pl.BlockSpec((4, 2, LANES, width), lambda p, *_: (0, 0, 0, 0)),
+                pl.BlockSpec((1, 768), lambda p, *_: (0, 0)),
+                pl.BlockSpec((1, 1, seq, 768), lambda p, *_: (slot, p, 0, 0)),
+            ],
+            scratch_shapes=[
+                pltpu.VMEM((pairs * seq, 768), WIDE),
+                pltpu.VMEM((pairs * seq, 256), WIDE),
+            ],
+        ),
+        out_shape=[
+            jax.ShapeDtypeStruct((4, 2, LANES, width), LOW),
+            jax.ShapeDtypeStruct((1, 768), WIDE),
+            jax.ShapeDtypeStruct(qkv.shape, LOW),
+        ],
+        input_output_aliases={7: 2} if buffers else {},
+        name="attend_back",
+        compiler_params=pltpu.CompilerParams(vmem_limit_bytes=56 * 1024 * 1024),
+    )(counts, rows, cot, qkv, context, weights, outs, *buffers)
+
+
+def middle_kernel(rows_ref, context_ref, out_ref, bias_ref, gain_ref, shift_ref, middle_ref, hidden_ref):
+    context = jnp.concatenate([context_ref[i, 0] for i in range(4)], 1)
+    attended = dot(context, out_ref[...].reshape(-1, out_ref.shape[2]), 1, 0)
+    middle = rows_ref[0].astype(WIDE) + attended + bias_ref[...].astype(WIDE)
+    middle_ref[0] = middle
+    center = middle - jnp.mean(middle, -1, keepdims=True)
+    spread = jnp.mean(center * center, -1, keepdims=True)
+    hidden = center * lax.rsqrt(spread + EPS) * gain_ref[...].astype(WIDE)
+    hidden_ref[0] = (hidden + shift_ref[...].astype(WIDE)).astype(LOW)
+
+
+def middle_step(rows, context, outs, bias, gain, shift):
+    pairs, seq, width = rows.shape
+    block = lambda: pl.BlockSpec((1, seq, width), lambda p: (p, 0, 0))
+    return pl.pallas_call(
+        middle_kernel,
+        grid=(pairs,),
+        in_specs=[
+            block(),
+            pl.BlockSpec((4, 1, seq, 256), lambda p: (0, p, 0, 0)),
+            resident(outs.shape),
+        ]
+        + [resident((1, width))] * 3,
+        out_specs=[block(), block()],
+        out_shape=[
+            jax.ShapeDtypeStruct(rows.shape, WIDE),
+            jax.ShapeDtypeStruct(rows.shape, LOW),
+        ],
+        name="middle",
+        compiler_params=pltpu.CompilerParams(vmem_limit_bytes=56 * 1024 * 1024),
+    )(rows, context, outs, bias, gain, shift)
+
+
+def mlp_kernel(step, spot_ref, hidden_ref, cot_ref, *refs):
+    ups, downs, biases = refs[:4], refs[4:8], refs[8:12]
+    near_a, far_a, near_b, far_b, bias_out, act_ref, pre_ref, up_ref, down_ref, bias_ref = refs[-10:]
+    rows = hidden_ref.shape[0]
+    for r in range(4):
+        span = slice(r * LANES, (r + 1) * LANES)
+        up_ref[0, :, span] = ups[r][...]
+        down_ref[0, span, :] = downs[r][...]
+        bias_ref[:, span] = biases[r][...].astype(WIDE)
+
+    def one(i, carry):
+        at = pl.ds(pl.multiple_of(i * step, step), step)
+        pre_act = dot(hidden_ref[at, :], up_ref[0], 1, 0) + bias_ref[...]
+        act_grad = dot(cot_ref[at, :], down_ref[0], 1, 1)
+        chance = 0.5 + 0.5 * lax.erf(pre_act * ROOT_HALF)
+        act_ref[0, at, :] = (pre_act * chance).astype(LOW)
+        slope = chance + pre_act * (NORMAL * jnp.exp(-0.5 * pre_act * pre_act))
+        pre_ref[0, at, :] = (act_grad * slope).astype(LOW)
+        return carry
+
+    lax.fori_loop(0, rows // step, one, 0)
+    up_grad = dot(pre_ref[0], hidden_ref[...], 0, 0).astype(LOW).reshape(4, LANES, -1)
+    down_grad = dot(act_ref[0], cot_ref[...], 0, 0).astype(LOW).reshape(4, LANES, -1)
+    bias_out[0] = jnp.sum(pre_ref[0].astype(WIDE), 0, keepdims=True)
+    for j, (near, far) in enumerate(((near_a, far_a), (near_b, far_b))):
+
+        @pl.when(pl.program_id(0) == j)
+        def _(near=near, far=far):
+            near[0] = up_grad[:2]
+            near[1] = down_grad[:2]
+            far[0] = up_grad[2:]
+            far[1] = down_grad[2:]
+
+
+def mlp(first, spots, hidden, cot, ups, downs, biases, buffers):
+    rows, width = hidden.shape
+    operands = list(ups) + list(downs) + list(biases)
+    tile = 4 * LANES
+    grad = jax.ShapeDtypeStruct((2, 2, LANES, width), LOW)
+    return pl.pallas_call(
+        functools.partial(mlp_kernel, rows // 2),
+        grid_spec=pltpu.PrefetchScalarGridSpec(
+            num_scalar_prefetch=1,
+            grid=(2,),
+            in_specs=[resident(hidden.shape), resident(cot.shape)]
+            + [spec for _, spec in operands]
+            + [ANYWHERE] * len(buffers),
+            out_specs=[resident(grad.shape)] * 4
+            + [
+                pl.BlockSpec((1, 1, tile), lambda j, *_: (j, 0, 0)),
+                pl.BlockSpec((1, rows, tile), lambda j, *_: (first + j, 0, 0)),
+                pl.BlockSpec((1, rows, tile), lambda j, *_: (first + j, 0, 0)),
+                pl.BlockSpec((1, width, tile), lambda j, *_: (first + j, 0, 0)),
+                pl.BlockSpec((1, tile, width), lambda j, *_: (first + j, 0, 0)),
+            ],
+            scratch_shapes=[pltpu.VMEM((1, tile), WIDE)],
+        ),
+        out_shape=[grad] * 4
+        + [
+            jax.ShapeDtypeStruct((2, 1, tile), WIDE),
+            jax.ShapeDtypeStruct((8, rows, tile), LOW),
+            jax.ShapeDtypeStruct((8, rows, tile), LOW),
+            jax.ShapeDtypeStruct((8, width, tile), LOW),
+            jax.ShapeDtypeStruct((8, tile, width), LOW),
+        ],
+        input_output_aliases={3 + len(operands) + i: 5 + i for i in range(len(buffers))},
+        name="mlp",
+        compiler_params=pltpu.CompilerParams(vmem_limit_bytes=56 * 1024 * 1024),
+    )(spots, hidden, cot, *[array for array, _ in operands], *buffers)
+
+
+def norm_back(values, gain, grad):
+    center = values - jnp.mean(values, -1, keepdims=True)
+    scale = lax.rsqrt(jnp.mean(center * center, -1, keepdims=True) + EPS)
+    unit = center * scale
+    inner = grad * gain
+    pulled = scale * (
+        inner
+        - jnp.mean(inner, -1, keepdims=True)
+        - unit * jnp.mean(inner * unit, -1, keepdims=True)
+    )
+    return pulled, jnp.sum(grad * unit, 0, keepdims=True), jnp.sum(grad, 0, keepdims=True)
+
+
+def mlp_back_kernel(pre_ref, up_ref, middle_ref, cot_ref, gain_ref, grad_ref, sums_ref, sum_buf):
+    step = pl.program_id(0)
+
+    @pl.when(step == 0)
+    def _():
+        sum_buf[...] = dot(pre_ref[0], up_ref[0], 1, 1)
+
+    @pl.when(step > 0)
+    def _():
+        sum_buf[...] += dot(pre_ref[0], up_ref[0], 1, 1)
+
+    @pl.when(step == pl.num_programs(0) - 1)
+    def _():
+        sums_ref[...] = jnp.zeros_like(sums_ref)
+        chunk = 224
+
+        def one(i, carry):
+            at = pl.ds(pl.multiple_of(i * chunk, chunk), chunk)
+            cot = cot_ref[at, :].astype(WIDE)
+            pulled, gain_grad, shift_grad = norm_back(
+                middle_ref[at, :], gain_ref[...].astype(WIDE), sum_buf[at, :]
+            )
+            grad = cot + pulled
+            grad_ref[at, :] = grad
+            sums_ref[0:1, :] += gain_grad
+            sums_ref[1:2, :] += shift_grad
+            sums_ref[2:3, :] += jnp.sum(grad.astype(LOW).astype(WIDE), 0, keepdims=True)
+            sums_ref[3:4, :] += jnp.sum(cot, 0, keepdims=True)
+            return carry
+
+        lax.fori_loop(0, grad_ref.shape[0] // chunk, one, 0)
+
+
+def mlp_back(pre_grads, ups, middle, cot, gain):
+    tiles, rows, tile = pre_grads.shape
+    width = cot.shape[1]
+    return pl.pallas_call(
+        mlp_back_kernel,
+        grid=(tiles,),
+        in_specs=[
+            pl.BlockSpec((1, rows, tile), lambda j: (j, 0, 0)),
+            pl.BlockSpec((1, width, tile), lambda j: (j, 0, 0)),
+            resident(middle.shape),
+            resident(cot.shape),
+            resident((1, width)),
+        ],
+        out_specs=[resident((rows, width)), resident((8, width))],
+        out_shape=[
+            jax.ShapeDtypeStruct((rows, width), WIDE),
+            jax.ShapeDtypeStruct((8, width), WIDE),
+        ],
+        scratch_shapes=[pltpu.VMEM((rows, width), WIDE)],
+        name="mlp_back",
+        compiler_params=pltpu.CompilerParams(vmem_limit_bytes=56 * 1024 * 1024),
+    )(pre_grads, ups, middle, cot, gain)
+
+
+def mlp_out_kernel(act_ref, down_ref, middle_ref, bias_ref, out_ref, sum_buf):
+    step = pl.program_id(0)
+
+    @pl.when(step == 0)
+    def _():
+        sum_buf[...] = middle_ref[...] + bias_ref[...].astype(WIDE)
+
+    sum_buf[...] += dot(act_ref[0], down_ref[0], 1, 0)
+
+    @pl.when(step == pl.num_programs(0) - 1)
+    def _():
+        out_ref[...] = sum_buf[...].astype(LOW)
+
+
+def mlp_out(acts, downs, middle, bias):
+    tiles, rows, tile = acts.shape
+    width = middle.shape[1]
+    return pl.pallas_call(
+        mlp_out_kernel,
+        grid=(tiles,),
+        in_specs=[
+            pl.BlockSpec((1, rows, tile), lambda j: (j, 0, 0)),
+            pl.BlockSpec((1, tile, width), lambda j: (j, 0, 0)),
+            resident(middle.shape),
+            resident((1, width)),
+        ],
+        out_specs=resident((rows, width)),
+        out_shape=jax.ShapeDtypeStruct((rows, width), LOW),
+        scratch_shapes=[pltpu.VMEM((rows, width), WIDE)],
+        name="mlp_out",
+        compiler_params=pltpu.CompilerParams(vmem_limit_bytes=56 * 1024 * 1024),
+    )(acts, downs, middle, bias)
+
+
+def input_kernel(grad_ref, weight_ref, rows_ref, above_ref, gain_ref, out_ref, sums_ref):
+    pulled_sum = dot(grad_ref[0, 0], weight_ref[0], 1, 1)
+    for i in range(1, 4):
+        pulled_sum = pulled_sum + dot(grad_ref[i, 0], weight_ref[i], 1, 1)
+    pulled, gain_grad, shift_grad = norm_back(
+        rows_ref[0].astype(WIDE), gain_ref[...].astype(WIDE), pulled_sum
+    )
+    out_ref[0] = (above_ref[0] + pulled).astype(LOW)
+
+    @pl.when(pl.program_id(0) == 0)
+    def _():
+        sums_ref[...] = jnp.zeros_like(sums_ref)
+
+    sums_ref[0:1, :] += gain_grad
+    sums_ref[1:2, :] += shift_grad
+
+
+def input_step(grads, weights, rows, above, gain):
+    pairs, seq, width = rows.shape
+    block = lambda: pl.BlockSpec((1, seq, width), lambda p: (p, 0, 0))
+    return pl.pallas_call(
+        input_kernel,
+        grid=(pairs,),
+        in_specs=[
+            pl.BlockSpec((4, 1, seq, 768), lambda p: (0, p, 0, 0)),
+            resident(weights.shape),
+            block(),
+            block(),
+            resident((1, width)),
+        ],
+        out_specs=[block(), resident((8, width))],
+        out_shape=[
+            jax.ShapeDtypeStruct(rows.shape, LOW),
+            jax.ShapeDtypeStruct((8, width), WIDE),
+        ],
+        name="input_grad",
+        compiler_params=pltpu.CompilerParams(vmem_limit_bytes=56 * 1024 * 1024),
+    )(grads, weights, rows, above, gain)
+
+
+def place_kernel(turned, spot_ref, near_ref, far_ref, *refs):
+    outs = refs[-len(turned) :]
+    core = pl.program_id(1) ^ spot_ref[0]
+    for i, turn in enumerate(turned):
+        parts = []
+        for z in range(4):
+            at = z ^ spot_ref[2]
+            parts.append(
+                jnp.where(core == 0, near_ref[at, i].astype(WIDE), far_ref[at, i].astype(WIDE))
+            )
+        block = jnp.concatenate(parts, 0)
+        outs[i][...] = block.T if turn else block
+
+
+def place(turned, chunk, chunks, spots, near, far, shapes, buffers):
+    _, kinds, rows, width = near.shape
+    source = lambda: pl.BlockSpec(
+        (4, kinds, rows, width), lambda x, c, spot: (x ^ spot[1], 0, 0, 0)
+    )
+    specs = [
+        pl.BlockSpec((width, LANES), lambda x, c, spot: (0, (c * 2 + x) * chunks + chunk))
+        if turn
+        else pl.BlockSpec((LANES, width), lambda x, c, spot: ((c * 2 + x) * chunks + chunk, 0))
+        for turn in turned
+    ]
+    return pl.pallas_call(
+        functools.partial(place_kernel, turned),
+        grid_spec=pltpu.PrefetchScalarGridSpec(
+            num_scalar_prefetch=1,
+            grid=(2, 2),
+            in_specs=[source(), source()] + [ANYWHERE] * len(buffers),
+            out_specs=specs,
+        ),
+        out_shape=[jax.ShapeDtypeStruct(shape, WIDE) for shape in shapes],
+        input_output_aliases={3 + i: i for i in range(len(buffers))},
+        name="place",
+        compiler_params=pltpu.CompilerParams(vmem_limit_bytes=56 * 1024 * 1024),
+    )(spots, near, far, *buffers)
+
+
+def paired_body(
+    layer_in,
+    patch_count,
+    attn_gain,
+    attn_shift,
+    query_weight,
+    query_bias,
+    key_weight,
+    value_weight,
+    value_bias,
+    out_weight,
+    out_bias,
+    mlp_gain,
+    mlp_shift,
+    up_weight,
+    up_bias,
+    down_weight,
+    down_bias,
+    layer_cot,
+):
+    groups = lax.axis_size("dp")
+    rank = lax.axis_index("dp")
+    half_id = lax.axis_index("mp")
+    core_id, x_id, zlow_id, zhigh_id = rank & 1, (rank >> 1) & 1, (rank >> 2) & 1, (rank >> 3) & 1
+    part = core_id * 2 + x_id
+    spots = jnp.stack([part, part ^ 1, part ^ 2, part ^ 3]).astype(jnp.int32)
+    sides = jnp.stack([x_id, x_id ^ 1, x_id, x_id ^ 1]).astype(jnp.int32)
+    place_spots = jnp.stack([core_id, x_id, zlow_id * 2 + zhigh_id]).astype(jnp.int32)
+
+    swap = lambda value, bit: flip(value, "dp", bit, groups)
+    across = lambda value: flip(value, "mp", 1, 2)
+
+    rows, width = layer_in.shape
+    heads_width = query_weight.shape[1]
+    hidden_width = up_weight.shape[1]
+    block = hidden_width // 4
+    pairs = rows // SEQ
+    counts = pick(patch_count, half_id, pairs, 0)
+    row_vec = lambda vec: vec.reshape(1, -1)
+
+    near_qkv = across(
+        jnp.stack([pick(w, core_id, heads_width // 2, 1) for w in (query_weight, key_weight, value_weight)])
+    )
+    bias_other = across(jnp.concatenate([query_bias, value_bias, up_bias]))
+    query_bias_other = row_vec(bias_other[:heads_width])
+    value_bias_other = row_vec(bias_other[heads_width : 2 * heads_width])
+    up_bias_other = row_vec(bias_other[2 * heads_width :])
+
+    rows_in = layer_in.astype(WIDE)
+    normed = layer_norm(
+        rows_in, attn_gain.astype(WIDE), attn_shift.astype(WIDE)
+    ).astype(LOW)
+    shape_three = (pairs, SEQ, width)
+    normed_three = normed.reshape(shape_three)
+
+    def own_inputs(group):
+        weights = [
+            (w, pl.BlockSpec((width, LANES), lambda p, spot, count, i=i: (0, spot[2 * group + i])))
+            for w in (query_weight, key_weight, value_weight)
+            for i in range(2)
+        ]
+        biases = [
+            (row_vec(b), pl.BlockSpec((1, LANES), lambda p, spot, count, i=i: (0, spot[2 * group + i])))
+            for b in (query_bias, value_bias)
+            for i in range(2)
+        ]
+        outs = [
+            (out_weight, pl.BlockSpec((LANES, width), lambda p, spot, count, i=i: (spot[2 * group + i], 0)))
+            for i in range(2)
+        ]
+        return weights, biases, outs
+
+    kept = attend(0, spots, counts, normed_three, *own_inputs(0), [])
+    kept = attend(1, spots, counts, normed_three, *own_inputs(1), kept)
+
+    far_qkv = swap(near_qkv, CORE)
+    out_near = across(after(pick(out_weight, part, heads_width // 4, 0), near_qkv))
+    half = block // 2
+    eighth = part * 2 + zlow_id
+    up_near = across(after(pick(up_weight, eighth, half, 1), near_qkv))
+    down_near = across(after(pick(down_weight, eighth, half, 0), near_qkv))
+    out_side = swap(out_near, XBIT)
+    out_pieces = [out_near, out_side, swap(out_near, CORE), swap(out_side, CORE)]
+
+    def other_inputs(group):
+        source = (near_qkv, far_qkv)[group]
+        weights = [
+            (source, pl.BlockSpec((None, width, LANES), lambda p, side, count, k=k, i=i: (k, 0, side[i])))
+            for k in range(3)
+            for i in range(2)
+        ]
+        biases = [
+            (b, pl.BlockSpec((1, LANES), lambda p, side, count, i=i: (0, side[4 + 2 * group + i])))
+            for b in (query_bias_other, value_bias_other)
+            for i in range(2)
+        ]
+        outs = [(out_pieces[2 * group + i], pl.BlockSpec((LANES, width), lambda p, side, count: (0, 0))) for i in range(2)]
+        return weights, biases, outs
+
+    other_spots = jnp.concatenate([sides, spots])
+    kept = attend(2, other_spots, counts, normed_three, *other_inputs(0), kept)
+
+    def pair_up(mine, axis):
+        theirs = swap(mine, ZLOW)
+        low_first = zlow_id == 0
+        return jnp.concatenate(
+            [jnp.where(low_first, mine, theirs), jnp.where(low_first, theirs, mine)], axis
+        )
+
+    up_mine, down_mine = pair_up(up_near, 1), pair_up(down_near, 0)
+    kept = attend(3, other_spots, counts, normed_three, *other_inputs(1), kept)
+    up_side, down_side = swap(up_mine, XBIT), swap(down_mine, XBIT)
+    up_pieces = [up_mine, up_side, swap(up_mine, CORE), swap(up_side, CORE)]
+    down_pieces = [down_mine, down_side, swap(down_mine, CORE), swap(down_side, CORE)]
+
+    middle, hidden = middle_step(
+        layer_in.reshape(shape_three),
+        kept[1],
+        kept[3],
+        row_vec(out_bias),
+        row_vec(mlp_gain),
+        row_vec(mlp_shift),
+    )
+    middle = middle.reshape(rows, width)
+    hidden = hidden.reshape(rows, width)
+    subs = block // LANES
+
+    def own_mlp(first):
+        ups = [
+            (up_weight, pl.BlockSpec((width, LANES), lambda j, spot, r=r: (0, spot[r] * subs + first + j)))
+            for r in range(4)
+        ]
+        downs = [
+            (down_weight, pl.BlockSpec((LANES, width), lambda j, spot, r=r: (spot[r] * subs + first + j, 0)))
+            for r in range(4)
+        ]
+        biases = [
+            (row_vec(up_bias), pl.BlockSpec((1, LANES), lambda j, spot, r=r: (0, spot[r] * subs + first + j)))
+            for r in range(4)
+        ]
+        return ups, downs, biases
+
+    def other_mlp(first):
+        ups = [(piece, pl.BlockSpec((width, LANES), lambda j, spot: (0, first + j))) for piece in up_pieces]
+        downs = [(piece, pl.BlockSpec((LANES, width), lambda j, spot: (first + j, 0))) for piece in down_pieces]
+        biases = [
+            (up_bias_other, pl.BlockSpec((1, LANES), lambda j, spot, r=r: (0, spot[r] * subs + first + j)))
+            for r in range(4)
+        ]
+        return ups, downs, biases
+
+    own_a = mlp(0, spots, hidden, layer_cot, *own_mlp(0), [])
+    other_a = mlp(2, spots, hidden, layer_cot, *other_mlp(0), own_a[5:])
+    own_b = mlp(4, spots, hidden, layer_cot, *own_mlp(2), other_a[5:])
+    other_b = mlp(6, spots, hidden, layer_cot, *other_mlp(2), own_b[5:])
+    acts, pre_grads, ups_all, downs_all = other_b[5:]
+
+    def chain(other_near, other_far, own_near, own_far):
+        outbound = total(other_near, swap(other_far, CORE))
+        parts = (own_near, swap(own_far, CORE), across(outbound))
+
+        def reduce():
+            side = swap(total(*[item[:, 1] for item in parts]), XBIT)
+            kinds, lanes, cols = side.shape
+            cut = lambda item, index: pick(item.reshape(kinds, 2, lanes // 2, cols), index, 1, 1)[:, 0]
+            items = [item[:, 0] for item in parts] + [side]
+            sent = swap(total(*[cut(item, zlow_id ^ 1) for item in items]), ZLOW)
+            two = total(*[cut(item, zlow_id) for item in items], sent)
+            cut_two = lambda index: pick(two.reshape(kinds, 2, lanes // 4, cols), index, 1, 1)[:, 0]
+            one = total(cut_two(zhigh_id), swap(cut_two(zhigh_id ^ 1), ZHIGH))
+            have = one[None]
+            for bit in (ZHIGH, ZLOW, XBIT):
+                have = jnp.concatenate([have, swap(have, bit)])
+            return have, swap(have, CORE)
+
+        return reduce
+
+    chains = [
+        chain(other_a[0], other_a[1], own_a[0], own_a[1]),
+        chain(other_a[2], other_a[3], own_a[2], own_a[3]),
+        chain(other_b[0], other_b[1], own_b[0], own_b[1]),
+        chain(other_b[2], other_b[3], own_b[2], own_b[3]),
+    ]
+    middle_grad, sums_two = mlp_back(pre_grads, ups_all, middle, layer_cot, row_vec(mlp_gain))
+    other_far, bias_other_far, qkv_grads = attend_back(3, counts, normed, middle_grad, kept, [])
+    other_near, bias_other_near, qkv_grads = attend_back(2, counts, normed, middle_grad, kept, [qkv_grads])
+    own_far, bias_own_far, qkv_grads = attend_back(1, counts, normed, middle_grad, kept, [qkv_grads])
+    own_near, bias_own_near, qkv_grads = attend_back(0, counts, normed, middle_grad, kept, [qkv_grads])
+    late = [
+        chain(other_near[i : i + 2], other_far[i : i + 2], own_near[i : i + 2], own_far[i : i + 2])
+        for i in (0, 2)
+    ]
+    layer_out = mlp_out(acts, downs_all, middle, row_vec(down_bias))
+    grad_in, sums_one = input_step(
+        qkv_grads,
+        kept[2],
+        layer_in.reshape(shape_three),
+        middle_grad.reshape(shape_three),
+        row_vec(attn_gain),
+    )
+    up_shape, down_shape = up_weight.shape, down_weight.shape
+    placed = []
+    for i, finish in enumerate(chains):
+        placed = place((True, False), i, subs, place_spots, *finish(), (up_shape, down_shape), placed)
+    grad_up_weight, grad_down_weight = placed
+    grad_query_weight, grad_key_weight = place(
+        (True, True), 0, 1, place_spots, *late[0](), (query_weight.shape,) * 2, []
+    )
+    grad_value_weight, grad_out_weight = place(
+        (True, False), 0, 1, place_spots, *late[1](), (value_weight.shape, out_weight.shape), []
+    )
+
+    def back_to_place(near, far):
+        return jnp.concatenate([near, far]).reshape(4, -1)[jnp.arange(4) ^ part].reshape(-1)
+
+    def up_bias_grad(first, second):
+        sums = jnp.concatenate([first[4], second[4]]).reshape(4, 4, LANES).transpose(1, 0, 2)
+        return sums[jnp.arange(4) ^ part].reshape(-1)
+
+    def small(near, far, first, second):
+        return jnp.concatenate(
+            [
+                back_to_place(near[0, :256], far[0, :256]),
+                back_to_place(near[0, 512:], far[0, 512:]),
+                up_bias_grad(first, second),
+            ]
+        )
+
+    own_small = small(bias_own_near, bias_own_far, own_a, own_b)
+    other_small = small(bias_other_near, bias_other_far, other_a, other_b)
+    shared = jnp.concatenate([sums_one[0], sums_one[1], sums_two[2], sums_two[0], sums_two[1], sums_two[3]])
+    vec = jnp.concatenate([own_small, shared]) + across(jnp.concatenate([other_small, shared]))
+    for bit in (CORE, XBIT, ZLOW, ZHIGH):
+        vec = vec + swap(vec, bit)
+    grad_query_bias = vec[:heads_width]
+    grad_value_bias = vec[heads_width : 2 * heads_width]
+    grad_up_bias = vec[2 * heads_width : 2 * heads_width + hidden_width]
+    (
+        grad_attn_gain,
+        grad_attn_shift,
+        grad_out_bias,
+        grad_mlp_gain,
+        grad_mlp_shift,
+        grad_down_bias,
+    ) = jnp.split(vec[2 * heads_width + hidden_width :], 6)
+    return (
+        layer_out,
+        grad_in.reshape(rows, width),
+        grad_attn_gain,
+        grad_attn_shift,
+        grad_query_weight,
+        grad_query_bias,
+        grad_key_weight,
+        grad_value_weight,
+        grad_value_bias,
+        grad_out_weight,
+        grad_out_bias,
+        grad_mlp_gain,
+        grad_mlp_shift,
+        grad_up_weight,
+        grad_up_bias,
+        grad_down_weight,
+        grad_down_bias,
+    )
+
+
 def solution(mesh):
+    paired = mesh.shape["mp"] == 2 and mesh.shape["dp"] == 16
+    body = paired_body if paired else general_body
     placed = (
         P(("dp", "mp"), None),
         P("dp"),

time: 1020 us -> 792 us (0.78)
  matrix products: 316 us -> 0 us
  Pallas kernels: 0 us -> 308 us
  blocking collectives: 129 us -> 0 us
  local copies, waits for them, and re-layouts: 114 us -> 38.3 us
  starting transfers between devices: 9.44 us -> 71.8 us
  other arithmetic: 80.3 us -> 27.1 us
  between operations: 15.5 us -> 2.17 us
    ppermute x0 -> x82, waiting for transfers between devices: none -> 339 us  [flip(): return lax.ppermute(value, axis, [(i, i ^ bit) for i in range(size)])]
    pallas_call x0 -> x22, Pallas kernels: none -> 308 us  [the longest x4 81.6 us: attend_back(): pl.pallas_call(attend_back_kernel, grid_spec=pltpu.PrefetchScalarGridSpec...]
    dot_general x23 -> x0, matrix products: 281 us -> none  [the longest x6 98.7 us: contract_cols(): lax.dot_general(left, right, (((1,), (1,)), ((), ())), preferred_element_...]
    psum x1 -> x0, waiting for transfers between devices: 190 us -> none  [body(): lax.psum(grad_query_weight.astype(jnp.bfloat16), 'dp').astype(jnp.float32)]
    all_gather x4 -> x0, waiting for transfers between devices: 132 us -> none  [the longest x1 70.3 us: body(): lax.all_gather(down_weight, 'mp', axis=0, tiled=True)]
    psum x2 -> x0, blocking collectives: 74.4 us -> none  [the longest x1 41.9 us: body(): lax.psum((grad_gain_one, grad_shift_one, grad_out_bias, grad_gain_two, gr...]
    ppermute x0 -> x82, starting transfers between devices: none -> 71.8 us  [flip(): return lax.ppermute(value, axis, [(i, i ^ bit) for i in range(size)])]
    reshape x11 -> x13, local copies, waits for them, and re-layouts: 68.7 us -> 6.52 us  [the longest x11 6.51 us: paired_body(): row_vec = lambda vec: vec.reshape(1, -1)]
  transfers between devices with their start and end apart: 11 -> 82, of which waited for: 5 -> 31; matrix products, arithmetic and copies ran while one was open for 39% -> 7% of each run, Pallas kernels for 0% -> 39%
where the time goes in v2:
time: 792 us; the launch traced here: 786 us
  waiting for transfers between devices  339 us (43%)
  Pallas kernels  308 us (39%)
  starting transfers between devices  71.8 us (9%)
  local copies, waits for them, and re-layouts  38.3 us (5%)
  other arithmetic  27.1 us (3%)
    ppermute x82, waiting for transfers between devices, flip(): return lax.ppermute(value, axis, [(i, i ^ bit) for i in range(size)])  339 us
    pallas_call x4, Pallas kernels, attend_back(): pl.pallas_call(attend_back_kernel, grid_spec=pltpu.PrefetchScalarGridSpec...  81.6 us
    pallas_call x4, Pallas kernels, mlp(): pl.pallas_call(functools.partial(mlp_kernel, rows // 2), grid_spec=pltpu....  79.5 us
    ppermute x82, starting transfers between devices, flip(): return lax.ppermute(value, axis, [(i, i ^ bit) for i in range(size)])  71.8 us
    pallas_call x4, Pallas kernels, attend(): pl.pallas_call(attend_kernel, grid_spec=pltpu.PrefetchScalarGridSpec(num_...  53.6 us
    pallas_call x6, Pallas kernels, place(): pl.pallas_call(functools.partial(place_kernel, turned), grid_spec=pltpu.P...  32.7 us
    pallas_call x1, Pallas kernels, mlp_back(): pl.pallas_call(mlp_back_kernel, grid=(tiles,), in_specs=[pl.BlockSpec((1,...  21.7 us
    pallas_call x1, Pallas kernels, mlp_out(): pl.pallas_call(mlp_out_kernel, grid=(tiles,), in_specs=[pl.BlockSpec((1,...  16.5 us
  transfers between devices with their start and end apart: 82, of which 31 were waited for; matrix products, arithmetic and copies ran while one was open for 7% of the time, Pallas kernels for 39%

profile of v2, /device:TPU:0, one launch (start us, length us, event | category | flops | bytes accessed | tf_op | source)
XLA Modules:
  0.0 786.4 jit_solution(13262471378034766709)
XLA Ops:
  7.4 33.4 %collective-permute-done.refs_0_.refs_1_.refs_2_.refs_3_.refs_4_.refs_5_ = bf16[3,1024,256]{2,1,0:T(8,128)(2,1)} collective-permute-done((bf16[3,1024,256]{2,1,0:T(8,128)(2,1)S(1)}, bf16[3,1024,256]{2,1,0:T(8,128)(2,1)}, u32[]{:S(2)}, u32[]{:S(2)}) %collective-permute-start) | collective-permute-done | bytes 1572896 | tf_op jit(solution)/shard_map/ppermute | solution.py:245
  43.9 11.7 %collective-permute-done.12 = bf16[256,1024]{1,0:T(8,128)(2,1)S(1)} collective-permute-done((bf16[256,1024]{1,0:T(8,128)(2,1)S(1)}, bf16[256,1024]{1,0:T(8,128)(2,1)S(1)}, u32[]{:S(2)}, u32[]{:S(2)}) %collective-permute-start.12) | collective-permute-done | bytes 524320 | tf_op jit(solution)/shard_map/ppermute | solution.py:245
  83.4 36.8 %collective-permute-done.5.refs_11_ = bf16[128,1024]{1,0:T(8,128)(2,1)} collective-permute-done((bf16[128,1024]{1,0:T(8,128)(2,1)}, bf16[128,1024]{1,0:T(8,128)(2,1)}, u32[]{:S(2)}, u32[]{:S(2)}) %collective-permute-start.5) | collective-permute-done | bytes 262176 | tf_op jit(solution)/shard_map/ppermute | solution.py:245
  129.8 13.8 %attend.4 = (bf16[4,4,280,768]{3,2,1,0:T(8,128)(2,1)}, bf16[4,4,280,256]{3,2,1,0:T(8,128)(2,1)}, bf16[4,1024,768]{2,1,0:T(8,128)(2,1)}, bf16[4,256,1024]{2,1,0:T(8,128)(2,1)}) custom-call(s32[4]{0:T(128)} %pad_add_fusion.spot_ref, s32[4]{0:T(128)} %dynamic_slice.201.count_ref, bf16[4,280,1024]{2,1,0:T(8,128)(2,1)} %bitcast.282, bf16[1024,512]{1,0:T(8,128)(2,1)} %refs_1_.5, ...), custom_call_target="tpu_custom_call" | custom-call | tf_op jit(solution)/shard_map/attend/pallas_call | solution.py:319
  143.6 13.3 %attend.5 = (bf16[4,4,280,768]{3,2,1,0:T(8,128)(2,1)}, bf16[4,4,280,256]{3,2,1,0:T(8,128)(2,1)}, bf16[4,1024,768]{2,1,0:T(8,128)(2,1)}, bf16[4,256,1024]{2,1,0:T(8,128)(2,1)}) custom-call(s32[4]{0:T(128)} %pad_add_fusion.spot_ref, s32[4]{0:T(128)} %dynamic_slice.201.count_ref, ...), custom_call_target="tpu_custom_call", output_to_operand_aliasing={{0}: (15, {}), {1}: (16, {}), {2}: (17, {}), {3}: (18, {})} | custom-call | tf_op jit(solution)/shard_map/attend/pallas_call | solution.py:319
  158.7 13.2 %attend.6 = (bf16[4,4,280,768]{3,2,1,0:T(8,128)(2,1)}, bf16[4,4,280,256]{3,2,1,0:T(8,128)(2,1)}, bf16[4,1024,768]{2,1,0:T(8,128)(2,1)}, bf16[4,256,1024]{2,1,0:T(8,128)(2,1)}) custom-call(s32[8]{0:T(128)} %concatenate.126.spot_ref, s32[4]{0:T(128)} %dynamic_slice.201.count_ref, ...), custom_call_target="tpu_custom_call", output_to_operand_aliasing={{0}: (15, {}), {1}: (16, {}), {2}: (17, {}), {3}: (18, {})} | custom-call | tf_op jit(solution)/shard_map/attend/pallas_call | solution.py:319
  171.9 13.2 %attend.7 = (bf16[4,4,280,768]{3,2,1,0:T(8,128)(2,1)}, bf16[4,4,280,256]{3,2,1,0:T(8,128)(2,1)}, bf16[4,1024,768]{2,1,0:T(8,128)(2,1)}, bf16[4,256,1024]{2,1,0:T(8,128)(2,1)}) custom-call(s32[8]{0:T(128)} %concatenate.126.spot_ref, s32[4]{0:T(128)} %dynamic_slice.201.count_ref, ...), custom_call_target="tpu_custom_call", output_to_operand_aliasing={{0}: (15, {}), {1}: (16, {}), {2}: (17, {}), {3}: (18, {})} | custom-call | tf_op jit(solution)/shard_map/attend/pallas_call | solution.py:319
  193.0 19.9 %mlp.4 = (bf16[2,2,128,1024]{3,2,1,0:T(8,128)(2,1)}, bf16[2,2,128,1024]{3,2,1,0:T(8,128)(2,1)}, bf16[2,2,128,1024]{3,2,1,0:T(8,128)(2,1)}, bf16[2,2,128,1024]{3,...) custom-call(s32[4]{0:T(128)} %pad_add_fusion.spot_ref, ...), custom_call_target="tpu_custom_call" | custom-call | tf_op jit(solution)/shard_map/mlp/pallas_call | solution.py:493
  215.4 19.9 %mlp.5 = (bf16[2,2,128,1024]{3,2,1,0:T(8,128)(2,1)}, bf16[2,2,128,1024]{3,2,1,0:T(8,128)(2,1)}, bf16[2,2,128,1024]{3,2,1,0:T(8,128)(2,1)}, bf16[2,2,128,1024]{3,...) custom-call(s32[4]{0:T(128)} %pad_add_fusion.spot_ref, ...), custom_call_target="tpu_custom_call", output_to_operand_aliasing={{5}: (15, {}), {6}: (16, {}), {7}: (17, {}), {8}: (18, {})} | custom-call | tf_op jit(solution)/shard_map/mlp/pallas_call | solution.py:493
  235.9 20.0 %mlp.6 = (bf16[2,2,128,1024]{3,2,1,0:T(8,128)(2,1)}, bf16[2,2,128,1024]{3,2,1,0:T(8,128)(2,1)}, bf16[2,2,128,1024]{3,2,1,0:T(8,128)(2,1)}, bf16[2,2,128,1024]{3,...) custom-call(s32[4]{0:T(128)} %pad_add_fusion.spot_ref, ...), custom_call_target="tpu_custom_call", output_to_operand_aliasing={{5}: (15, {}), {6}: (16, {}), {7}: (17, {}), {8}: (18, {})} | custom-call | tf_op jit(solution)/shard_map/mlp/pallas_call | solution.py:493
  256.0 19.6 %mlp.7 = (bf16[2,2,128,1024]{3,2,1,0:T(8,128)(2,1)}, bf16[2,2,128,1024]{3,2,1,0:T(8,128)(2,1)}, bf16[2,2,128,1024]{3,2,1,0:T(8,128)(2,1)}, bf16[2,2,128,1024]{3,...) custom-call(s32[4]{0:T(128)} %pad_add_fusion.spot_ref, ...), custom_call_target="tpu_custom_call", output_to_operand_aliasing={{5}: (15, {}), {6}: (16, {}), {7}: (17, {}), {8}: (18, {})} | custom-call | tf_op jit(solution)/shard_map/mlp/pallas_call | solution.py:493
  277.5 21.7 %mlp_back.1 = (f32[1120,1024]{1,0:T(8,128)}, f32[8,1024]{1,0:T(8,128)}) custom-call(bf16[8,1120,512]{2,1,0:T(8,128)(2,1)} %get-tuple-element.135.pre_ref, bf16[8,1024,512]{2,1,0:T(8,128)(2,1)} %get-tuple-element.136.up_ref, f32[1120,1024]{1,0:T(8,128)} %bitcast.293, bf16[1120,1024]{1,0:T(8,128)(2,1)} %cot_ref.9, bf16[1,1024]{1,0:T(2,128)(2,1)} %reshape.367.gain_ref), custom_call_target="tpu_custom_call" | custom-call | tf_op jit(solution)/shard_map/mlp_back/pallas_call | solution.py:574
  299.2 20.6 %attend_back.4 = (bf16[4,2,128,1024]{3,2,1,0:T(8,128)(2,1)}, f32[1,768]{1,0:T(1,128)}, bf16[4,4,280,768]{3,2,1,0:T(8,128)(2,1)}) custom-call(s32[4]{0:T(128)} %dynamic_slice.201.count_ref, bf16[1120,1024]{1,0:T(8,128)(2,1)} %fusion.5.rows_ref, f32[1120,1024]{1,0:T(8,128)} %get-tuple-element.137.cot_ref, bf16[4,4,280,768]{3,2,1,0:T(8,128)(2,1)} %get-tuple-element.138.qkv_ref, ...), custom_call_target="tpu_custom_call" | custom-call | tf_op jit(solution)/shard_map/attend_back/pallas_call | solution.py:386
  320.6 20.2 %attend_back.5 = (bf16[4,2,128,1024]{3,2,1,0:T(8,128)(2,1)}, f32[1,768]{1,0:T(1,128)}, bf16[4,4,280,768]{3,2,1,0:T(8,128)(2,1)}) custom-call(s32[4]{0:T(128)} %dynamic_slice.201.count_ref, bf16[1120,1024]{1,0:T(8,128)(2,1)} %fusion.5.rows_ref, f32[1120,1024]{1,0:T(8,128)} %get-tuple-element.137.cot_ref, ...), custom_call_target="tpu_custom_call", output_to_operand_aliasing={{2}: (7, {})} | custom-call | tf_op jit(solution)/shard_map/attend_back/pallas_call | solution.py:386
  342.6 20.4 %attend_back.6 = (bf16[4,2,128,1024]{3,2,1,0:T(8,128)(2,1)}, f32[1,768]{1,0:T(1,128)}, bf16[4,4,280,768]{3,2,1,0:T(8,128)(2,1)}) custom-call(s32[4]{0:T(128)} %dynamic_slice.201.count_ref, bf16[1120,1024]{1,0:T(8,128)(2,1)} %fusion.5.rows_ref, f32[1120,1024]{1,0:T(8,128)} %get-tuple-element.137.cot_ref, ...), custom_call_target="tpu_custom_call", output_to_operand_aliasing={{2}: (7, {})} | custom-call | tf_op jit(solution)/shard_map/attend_back/pallas_call | solution.py:386
  363.0 20.4 %attend_back.7 = (bf16[4,2,128,1024]{3,2,1,0:T(8,128)(2,1)}, f32[1,768]{1,0:T(1,128)}, bf16[4,4,280,768]{3,2,1,0:T(8,128)(2,1)}) custom-call(s32[4]{0:T(128)} %dynamic_slice.201.count_ref, bf16[1120,1024]{1,0:T(8,128)(2,1)} %fusion.5.rows_ref, f32[1120,1024]{1,0:T(8,128)} %get-tuple-element.137.cot_ref, ...), custom_call_target="tpu_custom_call", output_to_operand_aliasing={{2}: (7, {})} | custom-call | tf_op jit(solution)/shard_map/attend_back/pallas_call | solution.py:386
  385.3 14.8 %input_grad.1 = (bf16[4,280,1024]{2,1,0:T(8,128)(2,1)}, f32[8,1024]{1,0:T(8,128)}) custom-call(bf16[4,4,280,768]{3,2,1,0:T(8,128)(2,1)} %get-tuple-element.143.grad_ref, bf16[4,1024,768]{2,1,0:T(8,128)(2,1)} %get-tuple-element.139.weight_ref, bf16[4,280,1024]{2,1,0:T(8,128)(2,1)} %bitcast.288, f32[4,280,1024]{2,1,0:T(8,128)} %bitcast.286, ...), custom_call_target="tpu_custom_call" | custom-call | tf_op jit(solution)/shard_map/input_grad/pallas_call | solution.py:649
  440.7 22.5 %collective-permute-done.74 = bf16[2,2,128,1024]{3,2,1,0:T(8,128)(2,1)} collective-permute-done((bf16[2,2,128,1024]{3,2,1,0:T(8,128)(2,1)}, bf16[2,2,128,1024]{3,2,1,0:T(8,128)(2,1)}, u32[]{:S(2)}, u32[]{:S(2)}) %collective-permute-start.74) | collective-permute-done | bytes 1048608 | tf_op jit(solution)/shard_map/ppermute | solution.py:245
  463.7 22.0 %collective-permute-done.44 = bf16[2,2,128,1024]{3,2,1,0:T(8,128)(2,1)} collective-permute-done((bf16[2,2,128,1024]{3,2,1,0:T(8,128)(2,1)}, bf16[2,2,128,1024]{3,2,1,0:T(8,128)(2,1)}, u32[]{:S(2)}, u32[]{:S(2)}) %collective-permute-start.44) | collective-permute-done | bytes 1048608 | tf_op jit(solution)/shard_map/ppermute | solution.py:245
  490.6 17.5 %collective-permute-done.54 = bf16[2,2,128,1024]{3,2,1,0:T(8,128)(2,1)S(1)} collective-permute-done((bf16[2,2,128,1024]{3,2,1,0:T(8,128)(2,1)S(1)}, bf16[2,2,128,1024]{3,2,1,0:T(8,128)(2,1)S(1)}, u32[]{:S(2)}, u32[]{:S(2)}) %collective-permute-start.54) | collective-permute-done | bytes 1048608 | tf_op jit(solution)/shard_map/ppermute | solution.py:245
  511.9 18.6 %collective-permute-done.34 = bf16[2,2,128,1024]{3,2,1,0:T(8,128)(2,1)S(1)} collective-permute-done((bf16[2,2,128,1024]{3,2,1,0:T(8,128)(2,1)S(1)}, bf16[2,2,128,1024]{3,2,1,0:T(8,128)(2,1)S(1)}, u32[]{:S(2)}, u32[]{:S(2)}) %collective-permute-start.34) | collective-permute-done | bytes 1048608 | tf_op jit(solution)/shard_map/ppermute | solution.py:245
  532.0 20.1 %collective-permute-done.24 = bf16[2,2,128,1024]{3,2,1,0:T(8,128)(2,1)S(1)} collective-permute-done((bf16[2,2,128,1024]{3,2,1,0:T(8,128)(2,1)S(1)}, bf16[2,2,128,1024]{3,2,1,0:T(8,128)(2,1)S(1)}, u32[]{:S(2)}, u32[]{:S(2)}) %collective-permute-start.24) | collective-permute-done | bytes 1048608 | tf_op jit(solution)/shard_map/ppermute | solution.py:245
  637.2 13.2 %collective-permute-done.38 = bf16[1,2,32,1024]{3,2,1,0:T(8,128)(2,1)S(1)} collective-permute-done((bf16[1,2,32,1024]{3,2,1,0:T(8,128)(2,1)S(1)}, bf16[1,2,32,1024]{3,2,1,0:T(8,128)(2,1)S(1)}, u32[]{:S(2)}, u32[]{:S(2)}) %collective-permute-start.38) | collective-permute-done | bytes 131104 | tf_op jit(solution)/shard_map/ppermute | solution.py:245
  734.1 16.5 %mlp_out.1 = bf16[1120,1024]{1,0:T(8,128)(2,1)} custom-call(bf16[8,1120,512]{2,1,0:T(8,128)(2,1)} %get-tuple-element.132.act_ref, bf16[8,512,1024]{2,1,0:T(8,128)(2,1)} %get-tuple-element.133.down_ref, f32[1120,1024]{1,0:T(8,128)} %bitcast.294, bf16[1,1024]{1,0:T(2,128)(2,1)} %reshape.373.bias_ref), custom_call_target="tpu_custom_call" | custom-call | tf_op jit(solution)/shard_map/mlp_out/pallas_call | solution.py:612
  (404 shorter events, 320.8 us)
Async XLA Ops:
  69.5 57.5 %collective-permute-start.14 = (bf16[512,1024]{1,0:T(8,128)(2,1)S(1)}, bf16[512,1024]{1,0:T(8,128)(2,1)}, u32[]{:S(2)}, u32[]{:S(2)}) collective-permute-start(bf16[512,1024]{1,0:T(8,128)(2,1)S(1)} %pad_maximum_fusion.2.refs_4_), channel_id=1, source_target_pairs={{0,4},{2,6},{4,0},{6,2},{8,12},{10,14},{12,8},{14,10},{16,20},{18,... | collective-permute-start | bytes 3145736 | tf_op jit(solution)/shard_map/ppermute | solution.py:245
  79.8 47.6 %collective-permute-start.9 = (bf16[1024,512]{1,0:T(8,128)(2,1)}, bf16[1024,512]{1,0:T(8,128)(2,1)}, u32[]{:S(2)}, u32[]{:S(2)}) collective-permute-start(bf16[1024,512]{1,0:T(8,128)(2,1)} %pad_maximum_fusion.1.refs_0_), channel_id=1, source_target_pairs={{0,4},{2,6},{4,0},{6,2},{8,12},{10,14},{12,8},{14,10},{16,20},{18,... | collective-permute-start | bytes 3145736 | tf_op jit(solution)/shard_map/ppermute | solution.py:245
  81.4 90.6 %collective-permute-start.1 = (bf16[3,1024,256]{2,1,0:T(8,128)(2,1)}, bf16[3,1024,256]{2,1,0:T(8,128)(2,1)}, u32[]{:S(2)}, u32[]{:S(2)}) collective-permute-start(bf16[3,1024,256]{2,1,0:T(8,128)(2,1)} %collective-permute-done.refs_0_.refs_1_.refs_2_.refs_3_.refs_4_.refs_5_), channel_id=1, source_target_pairs={{0,2},{2,0},{4,6},{6,4},{8,10},{10,8},{12,14},{14,12},{16,18},{18,... | collective-permute-start | bytes 4718600 | tf_op jit(solution)/shard_map/ppermute | solution.py:245
  126.3 87.1 %collective-permute-start.15 = (bf16[512,1024]{1,0:T(8,128)(2,1)S(1)}, bf16[512,1024]{1,0:T(8,128)(2,1)S(1)}, u32[]{:S(2)}, u32[]{:S(2)}) collective-permute-start(bf16[512,1024]{1,0:T(8,128)(2,1)S(1)} %pad_maximum_fusion.2.refs_4_), channel_id=1, source_target_pairs={{0,2},{2,0},{4,6},{6,4},{8,10},{10,8},{12,14},{14,12},{16,18},{18,... | collective-permute-start | bytes 3145736 | tf_op jit(solution)/shard_map/ppermute | solution.py:245
  126.9 86.6 %collective-permute-start.10 = (bf16[1024,512]{1,0:T(8,128)(2,1)}, bf16[1024,512]{1,0:T(8,128)(2,1)S(1)}, u32[]{:S(2)}, u32[]{:S(2)}) collective-permute-start(bf16[1024,512]{1,0:T(8,128)(2,1)} %pad_maximum_fusion.1.refs_0_), channel_id=1, source_target_pairs={{0,2},{2,0},{4,6},{6,4},{8,10},{10,8},{12,14},{14,12},{16,18},{18,... | collective-permute-start | bytes 3145736 | tf_op jit(solution)/shard_map/ppermute | solution.py:245
  127.0 86.5 %collective-permute-start.16 = (bf16[512,1024]{1,0:T(8,128)(2,1)}, bf16[512,1024]{1,0:T(8,128)(2,1)S(1)}, u32[]{:S(2)}, u32[]{:S(2)}) collective-permute-start(bf16[512,1024]{1,0:T(8,128)(2,1)} %collective-permute-done.14.refs_5_), channel_id=1, source_target_pairs={{0,2},{2,0},{4,6},{6,4},{8,10},{10,8},{12,14},{14,12},{16,18},{18,... | collective-permute-start | bytes 3145736 | tf_op jit(solution)/shard_map/ppermute | solution.py:245
  127.4 86.1 %collective-permute-start.11 = (bf16[1024,512]{1,0:T(8,128)(2,1)}, bf16[1024,512]{1,0:T(8,128)(2,1)S(1)}, u32[]{:S(2)}, u32[]{:S(2)}) collective-permute-start(bf16[1024,512]{1,0:T(8,128)(2,1)} %collective-permute-done.9.refs_1_), channel_id=1, source_target_pairs={{0,2},{2,0},{4,6},{6,4},{8,10},{10,8},{12,14},{14,12},{16,18},{18,... | collective-permute-start | bytes 3145736 | tf_op jit(solution)/shard_map/ppermute | solution.py:245
  212.9 194.9 %collective-permute-start.62 = (bf16[2,2,128,1024]{3,2,1,0:T(8,128)(2,1)}, bf16[2,2,128,1024]{3,2,1,0:T(8,128)(2,1)S(1)}, u32[]{:S(2)}, u32[]{:S(2)}) collective-permute-start(bf16[2,2,128,1024]{3,2,1,0:T(8,128)(2,1)} %get-tuple-element.172), channel_id=1, source_target_pairs={{0,2},{2,0},{4,6},{6,4},{8,10},{10,8},{12,14},{14,12},{16,18},{18,... | collective-permute-start | bytes 3145736 | tf_op jit(solution)/shard_map/ppermute | solution.py:245
  213.4 194.5 %collective-permute-start.72 = (bf16[2,2,128,1024]{3,2,1,0:T(8,128)(2,1)}, bf16[2,2,128,1024]{3,2,1,0:T(8,128)(2,1)}, u32[]{:S(2)}, u32[]{:S(2)}) collective-permute-start(bf16[2,2,128,1024]{3,2,1,0:T(8,128)(2,1)} %get-tuple-element.176), channel_id=1, source_target_pairs={{0,2},{2,0},{4,6},{6,4},{8,10},{10,8},{12,14},{14,12},{16,18},{18,... | collective-permute-start | bytes 3145736 | tf_op jit(solution)/shard_map/ppermute | solution.py:245
  235.4 176.1 %collective-permute-start.63 = (bf16[2,2,128,1024]{3,2,1,0:T(8,128)(2,1)}, bf16[2,2,128,1024]{3,2,1,0:T(8,128)(2,1)S(1)}, u32[]{:S(2)}, u32[]{:S(2)}) collective-permute-start(bf16[2,2,128,1024]{3,2,1,0:T(8,128)(2,1)} %get-tuple-element.174), channel_id=1, source_target_pairs={{0,2},{2,0},{4,6},{6,4},{8,10},{10,8},{12,14},{14,12},{16,18},{18,... | collective-permute-start | bytes 3145736 | tf_op jit(solution)/shard_map/ppermute | solution.py:245
  235.6 176.8 %collective-permute-start.73 = (bf16[2,2,128,1024]{3,2,1,0:T(8,128)(2,1)}, bf16[2,2,128,1024]{3,2,1,0:T(8,128)(2,1)S(1)}, u32[]{:S(2)}, u32[]{:S(2)}) collective-permute-start(bf16[2,2,128,1024]{3,2,1,0:T(8,128)(2,1)} %get-tuple-element.178), channel_id=1, source_target_pairs={{0,2},{2,0},{4,6},{6,4},{8,10},{10,8},{12,14},{14,12},{16,18},{18,... | collective-permute-start | bytes 3145736 | tf_op jit(solution)/shard_map/ppermute | solution.py:245
  415.1 48.1 %collective-permute-start.74 = (bf16[2,2,128,1024]{3,2,1,0:T(8,128)(2,1)}, bf16[2,2,128,1024]{3,2,1,0:T(8,128)(2,1)}, u32[]{:S(2)}, u32[]{:S(2)}) collective-permute-start(bf16[2,2,128,1024]{3,2,1,0:T(8,128)(2,1)} %add_convert_fusion), channel_id=1, source_target_pairs={{0,1},{1,0},{2,3},{3,2},{4,5},{5,4},{6,7},{7,6},{8,9},{9,8},{10,11... | collective-permute-start | bytes 3145736 | tf_op jit(solution)/shard_map/ppermute | solution.py:245
  419.0 66.7 %collective-permute-start.44 = (bf16[2,2,128,1024]{3,2,1,0:T(8,128)(2,1)}, bf16[2,2,128,1024]{3,2,1,0:T(8,128)(2,1)}, u32[]{:S(2)}, u32[]{:S(2)}) collective-permute-start(bf16[2,2,128,1024]{3,2,1,0:T(8,128)(2,1)} %add_convert_fusion.3), channel_id=1, source_target_pairs={{0,1},{1,0},{2,3},{3,2},{4,5},{5,4},{6,7},{7,6},{8,9},{9,8},{10,11... | collective-permute-start | bytes 3145736 | tf_op jit(solution)/shard_map/ppermute | solution.py:245
  425.8 82.2 %collective-permute-start.54 = (bf16[2,2,128,1024]{3,2,1,0:T(8,128)(2,1)S(1)}, bf16[2,2,128,1024]{3,2,1,0:T(8,128)(2,1)S(1)}, u32[]{:S(2)}, u32[]{:S(2)}) collective-permute-start(bf16[2,2,128,1024]{3,2,1,0:T(8,128)(2,1)S(1)} %add_convert_fusion.2), channel_id=1, source_target_pairs={{0,1},{1,0},{2,3},{3,2},{4,5},{5,4},{6,7},{7,6},{8,9},{9,8},{10,11... | collective-permute-start | bytes 3145736 | tf_op jit(solution)/shard_map/ppermute | solution.py:245
  429.8 79.9 %collective-permute-start.32 = (bf16[2,2,128,1024]{3,2,1,0:T(8,128)(2,1)S(1)}, bf16[2,2,128,1024]{3,2,1,0:T(8,128)(2,1)S(1)}, u32[]{:S(2)}, u32[]{:S(2)}) collective-permute-start(bf16[2,2,128,1024]{3,2,1,0:T(8,128)(2,1)S(1)} %get-tuple-element.191), channel_id=1, source_target_pairs={{0,2},{2,0},{4,6},{6,4},{8,10},{10,8},{12,14},{14,12},{16,18},{18,... | collective-permute-start | bytes 3145736 | tf_op jit(solution)/shard_map/ppermute | solution.py:245
  440.7 70.7 %collective-permute-start.22 = (bf16[2,2,128,1024]{3,2,1,0:T(8,128)(2,1)S(1)}, bf16[2,2,128,1024]{3,2,1,0:T(8,128)(2,1)S(1)}, u32[]{:S(2)}, u32[]{:S(2)}) collective-permute-start(bf16[2,2,128,1024]{3,2,1,0:T(8,128)(2,1)S(1)} %get-tuple-element.192), channel_id=1, source_target_pairs={{0,2},{2,0},{4,6},{6,4},{8,10},{10,8},{12,14},{14,12},{16,18},{18,... | collective-permute-start | bytes 3145736 | tf_op jit(solution)/shard_map/ppermute | solution.py:245
  463.2 67.3 %collective-permute-start.34 = (bf16[2,2,128,1024]{3,2,1,0:T(8,128)(2,1)S(1)}, bf16[2,2,128,1024]{3,2,1,0:T(8,128)(2,1)S(1)}, u32[]{:S(2)}, u32[]{:S(2)}) collective-permute-start(bf16[2,2,128,1024]{3,2,1,0:T(8,128)(2,1)S(1)} %get-tuple-element.193), channel_id=1, source_target_pairs={{0,1},{1,0},{2,3},{3,2},{4,5},{5,4},{6,7},{7,6},{8,9},{9,8},{10,11... | collective-permute-start | bytes 3145736 | tf_op jit(solution)/shard_map/ppermute | solution.py:245
  485.6 66.4 %collective-permute-start.24 = (bf16[2,2,128,1024]{3,2,1,0:T(8,128)(2,1)S(1)}, bf16[2,2,128,1024]{3,2,1,0:T(8,128)(2,1)S(1)}, u32[]{:S(2)}, u32[]{:S(2)}) collective-permute-start(bf16[2,2,128,1024]{3,2,1,0:T(8,128)(2,1)S(1)} %get-tuple-element.194), channel_id=1, source_target_pairs={{0,1},{1,0},{2,3},{3,2},{4,5},{5,4},{6,7},{7,6},{8,9},{9,8},{10,11... | collective-permute-start | bytes 3145736 | tf_op jit(solution)/shard_map/ppermute | solution.py:245
  508.0 46.2 %collective-permute-start.20 = (f32[9216]{0:T(1024)S(1)}, f32[9216]{0:T(1024)S(1)}, u32[]{:S(2)}, u32[]{:S(2)}) collective-permute-start(f32[9216]{0:T(1024)S(1)} %add.424), channel_id=1, source_target_pairs={{0,8},{2,10},{4,12},{6,14},{8,0},{10,2},{12,4},{14,6},{16,24},{18,... | collective-permute-start | bytes 110600 | tf_op jit(solution)/shard_map/ppermute | solution.py:245
  509.8 49.8 %collective-permute-start.65 = (bf16[2,128,1024]{2,1,0:T(8,128)(2,1)S(1)}, bf16[2,128,1024]{2,1,0:T(8,128)(2,1)S(1)}, u32[]{:S(2)}, u32[]{:S(2)}) collective-permute-start(bf16[2,128,1024]{2,1,0:T(8,128)(2,1)S(1)} %fusion.10), channel_id=1, source_target_pairs={{0,4},{2,6},{4,0},{6,2},{8,12},{10,14},{12,8},{14,10},{16,20},{18,... | collective-permute-start | bytes 1572872 | tf_op jit(solution)/shard_map/ppermute | solution.py:245
  511.4 50.0 %collective-permute-start.75 = (bf16[2,128,1024]{2,1,0:T(8,128)(2,1)S(1)}, bf16[2,128,1024]{2,1,0:T(8,128)(2,1)S(1)}, u32[]{:S(2)}, u32[]{:S(2)}) collective-permute-start(bf16[2,128,1024]{2,1,0:T(8,128)(2,1)S(1)} %fusion.11), channel_id=1, source_target_pairs={{0,4},{2,6},{4,0},{6,2},{8,12},{10,14},{12,8},{14,10},{16,20},{18,... | collective-permute-start | bytes 1572872 | tf_op jit(solution)/shard_map/ppermute | solution.py:245
  711.6 57.2 %collective-permute-start.71 = (bf16[8,2,32,1024]{3,2,1,0:T(8,128)(2,1)}, bf16[8,2,32,1024]{3,2,1,0:T(8,128)(2,1)S(1)}, u32[]{:S(2)}, u32[]{:S(2)}) collective-permute-start(bf16[8,2,32,1024]{3,2,1,0:T(8,128)(2,1)} %pad_maximum_fusion.7.near_ref), channel_id=1, source_target_pairs={{0,2},{2,0},{4,6},{6,4},{8,10},{10,8},{12,14},{14,12},{16,18},{18,... | collective-permute-start | bytes 3145736 | tf_op jit(solution)/shard_map/ppermute | solution.py:245
  723.0 52.2 %collective-permute-start.61 = (bf16[8,2,32,1024]{3,2,1,0:T(8,128)(2,1)}, bf16[8,2,32,1024]{3,2,1,0:T(8,128)(2,1)}, u32[]{:S(2)}, u32[]{:S(2)}) collective-permute-start(bf16[8,2,32,1024]{3,2,1,0:T(8,128)(2,1)} %pad_maximum_fusion.6.near_ref), channel_id=1, source_target_pairs={{0,2},{2,0},{4,6},{6,4},{8,10},{10,8},{12,14},{14,12},{16,18},{18,... | collective-permute-start | bytes 3145736 | tf_op jit(solution)/shard_map/ppermute | solution.py:245
  732.4 48.3 %collective-permute-start.51 = (bf16[8,2,32,1024]{3,2,1,0:T(8,128)(2,1)}, bf16[8,2,32,1024]{3,2,1,0:T(8,128)(2,1)}, u32[]{:S(2)}, u32[]{:S(2)}) collective-permute-start(bf16[8,2,32,1024]{3,2,1,0:T(8,128)(2,1)} %pad_maximum_fusion.5.near_ref), channel_id=1, source_target_pairs={{0,2},{2,0},{4,6},{6,4},{8,10},{10,8},{12,14},{14,12},{16,18},{18,... | collective-permute-start | bytes 3145736 | tf_op jit(solution)/shard_map/ppermute | solution.py:245
  (104 other events, 2388.0 us)

commit v3 on v2

--- a/solution.py
+++ b/solution.py
@@ -268,9 +268,9 @@
 
 
 def attend_kernel(spot_ref, count_ref, rows_ref, *refs):
-    weights, biases, outs = refs[:6], refs[6:10], refs[10:12]
-    qkv_ref, context_ref, weight_ref, out_ref, bias_ref = refs[-5:]
-    pair = pl.program_id(0)
+    weights, biases = refs[:6], refs[6:10]
+    qkv_ref, context_ref, weight_ref, bias_ref = refs[-4:]
+    pair = pl.program_id(1)
 
     @pl.when(pair == 0)
     def _():
@@ -278,7 +278,6 @@
             weight_ref[0, :, i * LANES : (i + 1) * LANES] = weights[i][...]
         bias_ref[...] = jnp.zeros_like(bias_ref)
         for i in range(2):
-            out_ref[0, i * LANES : (i + 1) * LANES, :] = outs[i][...]
             bias_ref[:, i * LANES : (i + 1) * LANES] = biases[i][...].astype(WIDE)
             bias_ref[:, (4 + i) * LANES : (5 + i) * LANES] = biases[2 + i][...].astype(WIDE)
 
@@ -304,24 +303,21 @@
         ).astype(LOW)
 
 
-def attend(slot, spots, counts, rows, weights, biases, outs, buffers):
+def attend(slot, groups, spots, counts, rows, weights, biases, buffers):
     pairs, seq, width = rows.shape
     shapes = [
-        ((4, pairs, seq, 768), (1, 1, seq, 768), lambda p, *_: (slot, p, 0, 0)),
-        ((4, pairs, seq, 256), (1, 1, seq, 256), lambda p, *_: (slot, p, 0, 0)),
-        ((4, width, 768), (1, width, 768), lambda p, *_: (slot, 0, 0)),
-        ((4, 256, width), (1, 256, width), lambda p, *_: (slot, 0, 0)),
+        ((4, pairs, seq, 768), (1, 1, seq, 768), lambda g, p, *_: (slot + g, p, 0, 0)),
+        ((4, pairs, seq, 256), (1, 1, seq, 256), lambda g, p, *_: (slot + g, p, 0, 0)),
+        ((4, width, 768), (1, width, 768), lambda g, p, *_: (slot + g, 0, 0)),
     ]
-    operands = list(weights) + list(biases) + list(outs)
-    aliases = {}
-    if buffers:
-        aliases = {3 + len(operands) + i: i for i in range(4)}
+    operands = list(weights) + list(biases)
+    aliases = {3 + len(operands) + i: i for i in range(len(buffers))}
     return pl.pallas_call(
         attend_kernel,
         grid_spec=pltpu.PrefetchScalarGridSpec(
             num_scalar_prefetch=2,
-            grid=(pairs,),
-            in_specs=[pl.BlockSpec((1, seq, width), lambda p, *_: (p, 0, 0))]
+            grid=(groups, pairs),
+            in_specs=[pl.BlockSpec((1, seq, width), lambda g, p, *_: (p, 0, 0))]
             + [spec for _, spec in operands]
             + [ANYWHERE] * len(buffers),
             out_specs=[pl.BlockSpec(block, index) for _, block, index in shapes],
@@ -373,14 +369,16 @@
     @pl.when(pair == pl.num_programs(0) - 1)
     def _():
         stacked = dot(grad_buf[...].astype(LOW), rows_ref[...], 0, 0).astype(LOW)
-        near_ref[:3] = stacked.reshape(3, 2, LANES, -1)
+        for i in range(2):
+            near_ref[i, :3] = stacked.reshape(3, 2, LANES, -1)[:, i]
         outs = dot(context_buf[...].astype(LOW), cot_ref[...].astype(LOW), 0, 0).astype(LOW)
-        near_ref[3] = outs.reshape(2, LANES, -1)
+        for i in range(2):
+            near_ref[i, 3] = outs[i * LANES : (i + 1) * LANES]
         bias_ref[...] = jnp.sum(grad_buf[...], 0, keepdims=True)
 
 
-def attend_back(slot, counts, rows, cot, kept, buffers):
-    qkv, context, weights, outs = kept
+def attend_back(slot, counts, rows, cot, kept, outs, buffers):
+    qkv, context, weights = kept
     _, pairs, seq, _ = qkv.shape
     width = rows.shape[1]
     return pl.pallas_call(
@@ -398,7 +396,7 @@
             ]
             + [ANYWHERE] * len(buffers),
             out_specs=[
-                pl.BlockSpec((4, 2, LANES, width), lambda p, *_: (0, 0, 0, 0)),
+                pl.BlockSpec((2, 4, LANES, width), lambda p, *_: (0, 0, 0, 0)),
                 pl.BlockSpec((1, 768), lambda p, *_: (0, 0)),
                 pl.BlockSpec((1, 1, seq, 768), lambda p, *_: (slot, p, 0, 0)),
             ],
@@ -408,7 +406,7 @@
             ],
         ),
         out_shape=[
-            jax.ShapeDtypeStruct((4, 2, LANES, width), LOW),
+            jax.ShapeDtypeStruct((2, 4, LANES, width), LOW),
             jax.ShapeDtypeStruct((1, 768), WIDE),
             jax.ShapeDtypeStruct(qkv.shape, LOW),
         ],
@@ -418,7 +416,18 @@
     )(counts, rows, cot, qkv, context, weights, outs, *buffers)
 
 
-def middle_kernel(rows_ref, context_ref, out_ref, bias_ref, gain_ref, shift_ref, middle_ref, hidden_ref):
+def middle_kernel(
+    spot_ref, rows_ref, context_ref, own_ref, near_ref, far_ref, bias_ref, gain_ref, shift_ref, *refs
+):
+    middle_ref, hidden_ref, out_ref = refs
+
+    @pl.when(pl.program_id(0) == 0)
+    def _():
+        for i in range(8):
+            source = own_ref if i < 4 else (near_ref if i < 6 else far_ref)
+            start = pl.multiple_of(spot_ref[i] * LANES, LANES)
+            out_ref[i // 2, (i % 2) * LANES : (i % 2 + 1) * LANES, :] = source[pl.ds(start, LANES), :]
+
     context = jnp.concatenate([context_ref[i, 0] for i in range(4)], 1)
     attended = dot(context, out_ref[...].reshape(-1, out_ref.shape[2]), 1, 0)
     middle = rows_ref[0].astype(WIDE) + attended + bias_ref[...].astype(WIDE)
@@ -429,36 +438,46 @@
     hidden_ref[0] = (hidden + shift_ref[...].astype(WIDE)).astype(LOW)
 
 
-def middle_step(rows, context, outs, bias, gain, shift):
+def middle_step(spots, rows, context, own, near, far, bias, gain, shift):
     pairs, seq, width = rows.shape
-    block = lambda: pl.BlockSpec((1, seq, width), lambda p: (p, 0, 0))
+    block = lambda: pl.BlockSpec((1, seq, width), lambda p, *_: (p, 0, 0))
     return pl.pallas_call(
         middle_kernel,
-        grid=(pairs,),
-        in_specs=[
-            block(),
-            pl.BlockSpec((4, 1, seq, 256), lambda p: (0, p, 0, 0)),
-            resident(outs.shape),
-        ]
-        + [resident((1, width))] * 3,
-        out_specs=[block(), block()],
+        grid_spec=pltpu.PrefetchScalarGridSpec(
+            num_scalar_prefetch=1,
+            grid=(pairs,),
+            in_specs=[
+                block(),
+                pl.BlockSpec((4, 1, seq, 256), lambda p, *_: (0, p, 0, 0)),
+                resident(own.shape),
+                resident(near.shape),
+                resident(far.shape),
+            ]
+            + [resident((1, width))] * 3,
+            out_specs=[block(), block(), resident((4, 256, width))],
+        ),
         out_shape=[
             jax.ShapeDtypeStruct(rows.shape, WIDE),
             jax.ShapeDtypeStruct(rows.shape, LOW),
+            jax.ShapeDtypeStruct((4, 256, width), LOW),
         ],
         name="middle",
         compiler_params=pltpu.CompilerParams(vmem_limit_bytes=56 * 1024 * 1024),
-    )(rows, context, outs, bias, gain, shift)
-
-
-def mlp_kernel(step, spot_ref, hidden_ref, cot_ref, *refs):
+    )(spots, rows, context, own, near, far, bias, gain, shift)
+
+
+def mlp_kernel(step, turned, spot_ref, hidden_ref, cot_ref, *refs):
     ups, downs, biases = refs[:4], refs[4:8], refs[8:12]
-    near_a, far_a, near_b, far_b, bias_out, act_ref, pre_ref, up_ref, down_ref, bias_ref = refs[-10:]
+    near_ref, far_ref, bias_out, act_ref, pre_ref, up_ref, down_ref, bias_ref = refs[-8:]
     rows = hidden_ref.shape[0]
     for r in range(4):
         span = slice(r * LANES, (r + 1) * LANES)
-        up_ref[0, :, span] = ups[r][...]
-        down_ref[0, span, :] = downs[r][...]
+        if turned:
+            up_ref[0, :, span] = ups[r][:, 0].reshape(LANES, -1).T
+            down_ref[0, span, :] = downs[r][:, 0].reshape(LANES, -1)
+        else:
+            up_ref[0, :, span] = ups[r][...]
+            down_ref[0, span, :] = downs[r][...]
         bias_ref[:, span] = biases[r][...].astype(WIDE)
 
     def one(i, carry):
@@ -475,30 +494,28 @@
     up_grad = dot(pre_ref[0], hidden_ref[...], 0, 0).astype(LOW).reshape(4, LANES, -1)
     down_grad = dot(act_ref[0], cot_ref[...], 0, 0).astype(LOW).reshape(4, LANES, -1)
     bias_out[0] = jnp.sum(pre_ref[0].astype(WIDE), 0, keepdims=True)
-    for j, (near, far) in enumerate(((near_a, far_a), (near_b, far_b))):
-
-        @pl.when(pl.program_id(0) == j)
-        def _(near=near, far=far):
-            near[0] = up_grad[:2]
-            near[1] = down_grad[:2]
-            far[0] = up_grad[2:]
-            far[1] = down_grad[2:]
-
-
-def mlp(first, spots, hidden, cot, ups, downs, biases, buffers):
+    for i in range(2):
+        near_ref[i, 0] = up_grad[i]
+        near_ref[i, 1] = down_grad[i]
+        far_ref[i, 0] = up_grad[2 + i]
+        far_ref[i, 1] = down_grad[2 + i]
+
+
+def mlp(first, turned, spots, hidden, cot, ups, downs, biases, buffers):
     rows, width = hidden.shape
     operands = list(ups) + list(downs) + list(biases)
     tile = 4 * LANES
-    grad = jax.ShapeDtypeStruct((2, 2, LANES, width), LOW)
+    grad = jax.ShapeDtypeStruct((2, 4, LANES, width), LOW)
+    grad_block = pl.BlockSpec((2, 2, LANES, width), lambda j, *_: (0, j, 0, 0))
     return pl.pallas_call(
-        functools.partial(mlp_kernel, rows // 2),
+        functools.partial(mlp_kernel, rows // 2, turned),
         grid_spec=pltpu.PrefetchScalarGridSpec(
             num_scalar_prefetch=1,
             grid=(2,),
             in_specs=[resident(hidden.shape), resident(cot.shape)]
             + [spec for _, spec in operands]
             + [ANYWHERE] * len(buffers),
-            out_specs=[resident(grad.shape)] * 4
+            out_specs=[grad_block] * 2
             + [
                 pl.BlockSpec((1, 1, tile), lambda j, *_: (j, 0, 0)),
                 pl.BlockSpec((1, rows, tile), lambda j, *_: (first + j, 0, 0)),
@@ -508,7 +525,7 @@
             ],
             scratch_shapes=[pltpu.VMEM((1, tile), WIDE)],
         ),
-        out_shape=[grad] * 4
+        out_shape=[grad] * 2
         + [
             jax.ShapeDtypeStruct((2, 1, tile), WIDE),
             jax.ShapeDtypeStruct((8, rows, tile), LOW),
@@ -516,7 +533,7 @@
             jax.ShapeDtypeStruct((8, width, tile), LOW),
             jax.ShapeDtypeStruct((8, tile, width), LOW),
         ],
-        input_output_aliases={3 + len(operands) + i: 5 + i for i in range(len(buffers))},
+        input_output_aliases={3 + len(operands) + i: 3 + i for i in range(len(buffers))},
         name="mlp",
         compiler_params=pltpu.CompilerParams(vmem_limit_bytes=56 * 1024 * 1024),
     )(spots, hidden, cot, *[array for array, _ in operands], *buffers)
@@ -674,10 +691,10 @@
         for z in range(4):
             at = z ^ spot_ref[2]
             parts.append(
-                jnp.where(core == 0, near_ref[at, i].astype(WIDE), far_ref[at, i].astype(WIDE))
+                jnp.where(core == 0, near_ref[at, i], far_ref[at, i])
             )
         block = jnp.concatenate(parts, 0)
-        outs[i][...] = block.T if turn else block
+        outs[i][...] = (block.T if turn else block).astype(WIDE)
 
 
 def place(turned, chunk, chunks, spots, near, far, shapes, buffers):
@@ -704,6 +721,41 @@
         name="place",
         compiler_params=pltpu.CompilerParams(vmem_limit_bytes=56 * 1024 * 1024),
     )(spots, near, far, *buffers)
+
+
+def gathered_kernel(source_ref, *refs):
+    up_ref, down_ref = refs[-2:]
+    rows = [[source_ref[high, low, 0, 0] for high in range(2)] for low in range(2)]
+    for kind, out_ref in enumerate((up_ref, down_ref)):
+        parts = []
+        for sub in range(2):
+            for low in range(2):
+                for high in range(2):
+                    parts.append(rows[low][high][2 * sub + kind])
+        block = jnp.concatenate(parts, 0)
+        out_ref[...] = (block.T if kind == 0 else block).astype(WIDE)
+
+
+def gathered(chunk, chunks, source, shapes, buffers):
+    kinds, rows, width = source.shape[1:]
+    source = source.reshape((2, 2, 2, 2, kinds, rows, width))
+    span = 2 * LANES
+    return pl.pallas_call(
+        gathered_kernel,
+        grid=(2, 2),
+        in_specs=[
+            pl.BlockSpec((2, 2, 1, 1, kinds, rows, width), lambda c, x: (0, 0, x, c, 0, 0, 0))
+        ]
+        + [ANYWHERE] * len(buffers),
+        out_specs=[
+            pl.BlockSpec((width, span), lambda c, x: (0, (c * 2 + x) * chunks + chunk)),
+            pl.BlockSpec((span, width), lambda c, x: ((c * 2 + x) * chunks + chunk, 0)),
+        ],
+        out_shape=[jax.ShapeDtypeStruct(shape, WIDE) for shape in shapes],
+        input_output_aliases={1 + i: i for i in range(len(buffers))},
+        name="gathered",
+        compiler_params=pltpu.CompilerParams(vmem_limit_bytes=56 * 1024 * 1024),
+    )(source, *buffers)
 
 
 def paired_body(
@@ -746,92 +798,95 @@
     counts = pick(patch_count, half_id, pairs, 0)
     row_vec = lambda vec: vec.reshape(1, -1)
 
-    near_qkv = across(
-        jnp.stack([pick(w, core_id, heads_width // 2, 1) for w in (query_weight, key_weight, value_weight)])
-    )
-    bias_other = across(jnp.concatenate([query_bias, value_bias, up_bias]))
-    query_bias_other = row_vec(bias_other[:heads_width])
-    value_bias_other = row_vec(bias_other[heads_width : 2 * heads_width])
-    up_bias_other = row_vec(bias_other[2 * heads_width :])
-
+    gate = lambda value, *waits: after(value, *waits) if waits else value
+    shape_three = (pairs, SEQ, width)
+    subs = block // LANES
+
+    slice_rows = LANES // 2
+    slice_at = (rank // 4) * 2 * subs + rank % 4
+    slices = jnp.stack(
+        [
+            jnp.stack(
+                [
+                    pick(up_weight, slice_at + 4 * i, slice_rows, 1).T,
+                    pick(down_weight, slice_at + 4 * i, slice_rows, 0),
+                ]
+            )
+            for i in range(2)
+        ]
+    )
+    slices = across(slices)
+    sent_qkv = jnp.stack(
+        [pick(w, core_id, heads_width // 2, 1) for w in (query_weight, key_weight, value_weight)]
+    )
+    sent_bias = jnp.concatenate([query_bias, value_bias, up_bias])
+    near_qkv = across(sent_qkv)
+    bias_other = across(sent_bias)
     rows_in = layer_in.astype(WIDE)
     normed = layer_norm(
         rows_in, attn_gain.astype(WIDE), attn_shift.astype(WIDE)
     ).astype(LOW)
-    shape_three = (pairs, SEQ, width)
     normed_three = normed.reshape(shape_three)
 
-    def own_inputs(group):
+    def own_inputs():
         weights = [
-            (w, pl.BlockSpec((width, LANES), lambda p, spot, count, i=i: (0, spot[2 * group + i])))
+            (w, pl.BlockSpec((width, LANES), lambda g, p, spot, count, i=i: (0, spot[2 * g + i])))
             for w in (query_weight, key_weight, value_weight)
             for i in range(2)
         ]
         biases = [
-            (row_vec(b), pl.BlockSpec((1, LANES), lambda p, spot, count, i=i: (0, spot[2 * group + i])))
+            (row_vec(b), pl.BlockSpec((1, LANES), lambda g, p, spot, count, i=i: (0, spot[2 * g + i])))
             for b in (query_bias, value_bias)
             for i in range(2)
         ]
-        outs = [
-            (out_weight, pl.BlockSpec((LANES, width), lambda p, spot, count, i=i: (spot[2 * group + i], 0)))
-            for i in range(2)
-        ]
-        return weights, biases, outs
-
-    kept = attend(0, spots, counts, normed_three, *own_inputs(0), [])
-    kept = attend(1, spots, counts, normed_three, *own_inputs(1), kept)
-
-    far_qkv = swap(near_qkv, CORE)
-    out_near = across(after(pick(out_weight, part, heads_width // 4, 0), near_qkv))
-    half = block // 2
-    eighth = part * 2 + zlow_id
-    up_near = across(after(pick(up_weight, eighth, half, 1), near_qkv))
-    down_near = across(after(pick(down_weight, eighth, half, 0), near_qkv))
-    out_side = swap(out_near, XBIT)
-    out_pieces = [out_near, out_side, swap(out_near, CORE), swap(out_side, CORE)]
-
-    def other_inputs(group):
-        source = (near_qkv, far_qkv)[group]
+        return weights, biases
+
+    def other_inputs(group, qkv):
         weights = [
-            (source, pl.BlockSpec((None, width, LANES), lambda p, side, count, k=k, i=i: (k, 0, side[i])))
+            (qkv, pl.BlockSpec((None, width, LANES), lambda g, p, side, count, k=k, i=i: (k, 0, side[i])))
             for k in range(3)
             for i in range(2)
         ]
         biases = [
-            (b, pl.BlockSpec((1, LANES), lambda p, side, count, i=i: (0, side[4 + 2 * group + i])))
+            (b, pl.BlockSpec((1, LANES), lambda g, p, side, count, i=i: (0, side[4 + 2 * group + i])))
             for b in (query_bias_other, value_bias_other)
             for i in range(2)
         ]
-        outs = [(out_pieces[2 * group + i], pl.BlockSpec((LANES, width), lambda p, side, count: (0, 0))) for i in range(2)]
-        return weights, biases, outs
+        return weights, biases
 
     other_spots = jnp.concatenate([sides, spots])
-    kept = attend(2, other_spots, counts, normed_three, *other_inputs(0), kept)
-
-    def pair_up(mine, axis):
-        theirs = swap(mine, ZLOW)
-        low_first = zlow_id == 0
-        return jnp.concatenate(
-            [jnp.where(low_first, mine, theirs), jnp.where(low_first, theirs, mine)], axis
-        )
-
-    up_mine, down_mine = pair_up(up_near, 1), pair_up(down_near, 0)
-    kept = attend(3, other_spots, counts, normed_three, *other_inputs(1), kept)
-    up_side, down_side = swap(up_mine, XBIT), swap(down_mine, XBIT)
-    up_pieces = [up_mine, up_side, swap(up_mine, CORE), swap(up_side, CORE)]
-    down_pieces = [down_mine, down_side, swap(down_mine, CORE), swap(down_side, CORE)]
-
-    middle, hidden = middle_step(
+    gathered_weights = [lax.all_gather(slices[0], "dp"), lax.all_gather(slices[1], "dp")]
+    kept = attend(
+        0, 2, gate(spots, sent_qkv, sent_bias, slices), counts, normed_three, *own_inputs(), []
+    )
+    near_qkv, bias_other, _ = lax.optimization_barrier((near_qkv, bias_other, kept[1]))
+    query_bias_other = row_vec(bias_other[:heads_width])
+    value_bias_other = row_vec(bias_other[heads_width : 2 * heads_width])
+    up_bias_other = row_vec(bias_other[2 * heads_width :])
+    sent_out = after(pick(out_weight, core_id, heads_width // 2, 0), near_qkv)
+    near_out = across(sent_out)
+    far_qkv = swap(near_qkv, CORE)
+    kept = attend(
+        2, 1, gate(other_spots, sent_out), counts, normed_three, *other_inputs(0, near_qkv), kept
+    )
+    near_out = after(near_out, kept[1])
+    far_out = swap(near_out, CORE)
+    kept = attend(
+        3, 1, gate(other_spots, near_out), counts, normed_three, *other_inputs(1, far_qkv), kept
+    )
+    middle, hidden, outs_all = middle_step(
+        jnp.concatenate([spots, sides]),
         layer_in.reshape(shape_three),
         kept[1],
-        kept[3],
+        out_weight,
+        near_out,
+        far_out,
         row_vec(out_bias),
         row_vec(mlp_gain),
         row_vec(mlp_shift),
     )
     middle = middle.reshape(rows, width)
     hidden = hidden.reshape(rows, width)
-    subs = block // LANES
 
     def own_mlp(first):
         ups = [
@@ -849,80 +904,154 @@
         return ups, downs, biases
 
     def other_mlp(first):
-        ups = [(piece, pl.BlockSpec((width, LANES), lambda j, spot: (0, first + j))) for piece in up_pieces]
-        downs = [(piece, pl.BlockSpec((LANES, width), lambda j, spot: (first + j, 0))) for piece in down_pieces]
+        source = gathered_weights[first // 2]
+        ups, downs = (
+            [
+                (source, pl.BlockSpec((2, 1, slice_rows, width), lambda j, spot, r=r, k=k: (spot[r] * 2 + j, k, 0, 0)))
+                for r in range(4)
+            ]
+            for k in range(2)
+        )
         biases = [
             (up_bias_other, pl.BlockSpec((1, LANES), lambda j, spot, r=r: (0, spot[r] * subs + first + j)))
             for r in range(4)
         ]
         return ups, downs, biases
 
-    own_a = mlp(0, spots, hidden, layer_cot, *own_mlp(0), [])
-    other_a = mlp(2, spots, hidden, layer_cot, *other_mlp(0), own_a[5:])
-    own_b = mlp(4, spots, hidden, layer_cot, *own_mlp(2), other_a[5:])
-    other_b = mlp(6, spots, hidden, layer_cot, *other_mlp(2), own_b[5:])
-    acts, pre_grads, ups_all, downs_all = other_b[5:]
-
-    def chain(other_near, other_far, own_near, own_far):
-        outbound = total(other_near, swap(other_far, CORE))
-        parts = (own_near, swap(own_far, CORE), across(outbound))
-
-        def reduce():
-            side = swap(total(*[item[:, 1] for item in parts]), XBIT)
-            kinds, lanes, cols = side.shape
-            cut = lambda item, index: pick(item.reshape(kinds, 2, lanes // 2, cols), index, 1, 1)[:, 0]
-            items = [item[:, 0] for item in parts] + [side]
-            sent = swap(total(*[cut(item, zlow_id ^ 1) for item in items]), ZLOW)
-            two = total(*[cut(item, zlow_id) for item in items], sent)
-            cut_two = lambda index: pick(two.reshape(kinds, 2, lanes // 4, cols), index, 1, 1)[:, 0]
-            one = total(cut_two(zhigh_id), swap(cut_two(zhigh_id ^ 1), ZHIGH))
-            have = one[None]
-            for bit in (ZHIGH, ZLOW, XBIT):
-                have = jnp.concatenate([have, swap(have, bit)])
-            return have, swap(have, CORE)
-
-        return reduce
-
-    chains = [
-        chain(other_a[0], other_a[1], own_a[0], own_a[1]),
-        chain(other_a[2], other_a[3], own_a[2], own_a[3]),
-        chain(other_b[0], other_b[1], own_b[0], own_b[1]),
-        chain(other_b[2], other_b[3], own_b[2], own_b[3]),
-    ]
-    middle_grad, sums_two = mlp_back(pre_grads, ups_all, middle, layer_cot, row_vec(mlp_gain))
-    other_far, bias_other_far, qkv_grads = attend_back(3, counts, normed, middle_grad, kept, [])
-    other_near, bias_other_near, qkv_grads = attend_back(2, counts, normed, middle_grad, kept, [qkv_grads])
-    own_far, bias_own_far, qkv_grads = attend_back(1, counts, normed, middle_grad, kept, [qkv_grads])
-    own_near, bias_own_near, qkv_grads = attend_back(0, counts, normed, middle_grad, kept, [qkv_grads])
-    late = [
-        chain(other_near[i : i + 2], other_far[i : i + 2], own_near[i : i + 2], own_far[i : i + 2])
-        for i in (0, 2)
-    ]
-    layer_out = mlp_out(acts, downs_all, middle, row_vec(down_bias))
+    def cut(item, index):
+        count, lanes, cols = item.shape
+        return pick(item.reshape(count, 2, lanes // 2, cols), index, 1, 1)[:, 0]
+
+    def outbound(near, far, first, last):
+        return total(near[:, first:last], far[:, first:last])
+
+    def sideways(near, far, beyond, first, last):
+        return total(near[1, first:last], far[1, first:last], beyond[1])
+
+    def collected(near, far, beyond, side, first, last):
+        return total(near[0, first:last], far[0, first:last], beyond[0], side)
+
+    def halves(item):
+        return cut(item, zlow_id ^ 1), cut(item, zlow_id)
+
+    def quarters(item):
+        return cut(item, zhigh_id ^ 1), cut(item, zhigh_id)
+
+    back = lambda slot, wait, qkv_grads: attend_back(
+        slot, gate(counts, *wait), normed, middle_grad, kept, outs_all, qkv_grads
+    )
+
+    other_a = mlp(2, True, spots, hidden, layer_cot, *other_mlp(0), [])
+    far_other_a = swap(other_a[1], CORE)
+    own_a = mlp(0, False, spots, hidden, layer_cot, *own_mlp(0), other_a[3:])
+    far_own_a = swap(own_a[1], CORE)
+    far_other_a = after(far_other_a, own_a[2])
+    out_a = [outbound(other_a[0], far_other_a, *span) for span in ((0, 1), (1, 2), (2, 4))]
+    own_b = mlp(6, False, gate(spots, *out_a), hidden, layer_cot, *own_mlp(2), own_a[3:])
+    beyond_a0 = across(out_a[0])
+    far_own_b = swap(own_b[1], CORE)
+    far_own_a = after(far_own_a, own_b[2])
+    other_b = mlp(
+        4, True, gate(spots, beyond_a0, far_own_a), hidden, layer_cot, *other_mlp(2), own_b[3:]
+    )
+    beyond_a1 = across(after(out_a[1], beyond_a0))
+    far_other_b = swap(other_b[1], CORE)
+    acts, pre_grads, ups_all, downs_all = other_b[3:]
+    beyond_a1 = after(beyond_a1, other_b[2])
+    beyond_a01 = jnp.concatenate([beyond_a0, beyond_a1], 1)
+    side_a01 = sideways(own_a[0], far_own_a, beyond_a01, 0, 2)
+    middle_grad, sums_two = mlp_back(
+        pre_grads, ups_all, middle, layer_cot, gate(row_vec(mlp_gain), side_a01, beyond_a01, far_own_b)
+    )
+    beyond_a23 = after(across(after(out_a[2], beyond_a1)), sums_two)
+    arrived_a01 = after(swap(side_a01, XBIT), sums_two)
+    far_other_b = after(far_other_b, sums_two)
+    side_a23 = sideways(own_a[0], far_own_a, beyond_a23, 2, 4)
+    out_b = [outbound(other_b[0], far_other_b, *span) for span in ((0, 2), (2, 4))]
+    other_far, bias_other_far, qkv_grads = back(3, (side_a23, arrived_a01, *out_b), [])
+    beyond_b01 = after(across(out_b[0]), bias_other_far)
+    arrived_a23 = after(swap(side_a23, XBIT), bias_other_far)
+    late_other_far = swap(other_far, CORE)
+    sum_a = jnp.concatenate(
+        [
+            collected(own_a[0], far_own_a, beyond_a01, arrived_a01, 0, 2),
+            collected(own_a[0], far_own_a, beyond_a23, arrived_a23, 2, 4),
+        ]
+    )
+    low_a, keep_a = halves(sum_a)
+    side_b01 = sideways(own_b[0], far_own_b, beyond_b01, 0, 2)
+    other_near, bias_other_near, qkv_grads = back(2, (low_a, sum_a, side_b01), [qkv_grads])
+    beyond_b23 = after(across(after(out_b[1], beyond_b01)), bias_other_near)
+    arrived_b01 = after(swap(side_b01, XBIT), bias_other_near)
+    low_a = after(swap(low_a, ZLOW), bias_other_near)
+    late_other_far = after(late_other_far, bias_other_near)
+    high_a, keep_a = quarters(total(keep_a, low_a))
+    side_b23 = sideways(own_b[0], far_own_b, beyond_b23, 2, 4)
+    late_out = [outbound(other_near, late_other_far, *span) for span in ((0, 2), (2, 4))]
+    own_far, bias_own_far, qkv_grads = back(1, (high_a, side_b23, arrived_b01, *late_out), [qkv_grads])
+    late_own_far = swap(own_far, CORE)
+    late_beyond0 = after(across(late_out[0]), bias_own_far)
+    arrived_b23 = after(swap(side_b23, XBIT), bias_own_far)
+    high_a = after(swap(high_a, ZHIGH), bias_own_far)
+    one_a = total(keep_a, high_a)
+    sum_b = jnp.concatenate(
+        [
+            collected(own_b[0], far_own_b, beyond_b01, arrived_b01, 0, 2),
+            collected(own_b[0], far_own_b, beyond_b23, arrived_b23, 2, 4),
+        ]
+    )
+    low_b, keep_b = halves(sum_b)
+    gathered_a = lax.all_gather(one_a, "dp")
+    own_near, bias_own_near, qkv_grads = back(0, (one_a, low_b, sum_b, late_beyond0), [qkv_grads])
+    late_beyond1 = after(across(after(late_out[1], late_beyond0)), bias_own_near)
+    late_own_far = after(late_own_far, bias_own_near)
+    low_b = after(swap(low_b, ZLOW), bias_own_near)
+    high_b, keep_b = quarters(total(keep_b, low_b))
+    late_side0 = sideways(own_near, late_own_far, late_beyond0, 0, 2)
     grad_in, sums_one = input_step(
         qkv_grads,
         kept[2],
         layer_in.reshape(shape_three),
         middle_grad.reshape(shape_three),
-        row_vec(attn_gain),
-    )
+        gate(row_vec(attn_gain), high_b, late_side0, late_beyond1),
+    )
+    high_b = after(swap(high_b, ZHIGH), sums_one)
+    one_b = total(keep_b, high_b)
+    gathered_b = lax.all_gather(one_b, "dp")
+    late_arrived0 = after(swap(late_side0, XBIT), sums_one)
+    late_side1 = sideways(own_near, late_own_far, after(late_beyond1, sums_one), 2, 4)
+    late_low0, late_keep0 = halves(
+        collected(own_near, late_own_far, late_beyond0, late_arrived0, 0, 2)
+    )
+    layer_out = mlp_out(
+        acts, downs_all, middle, gate(row_vec(down_bias), one_b, late_side1, late_low0)
+    )
+    late_arrived1 = after(swap(late_side1, XBIT), layer_out)
+    late_low1, late_keep1 = halves(
+        collected(own_near, late_own_far, late_beyond1, late_arrived1, 2, 4)
+    )
+    late_all = []
+    for low, keep in ((after(swap(late_low0, ZLOW), layer_out), late_keep0), (swap(late_low1, ZLOW), late_keep1)):
+        high, keep = quarters(total(keep, low))
+        have = total(keep, swap(high, ZHIGH))[None]
+        for bit in (ZHIGH, ZLOW, XBIT):
+            have = jnp.concatenate([have, swap(have, bit)])
+        late_all.append((have, swap(have, CORE)))
     up_shape, down_shape = up_weight.shape, down_weight.shape
-    placed = []
-    for i, finish in enumerate(chains):
-        placed = place((True, False), i, subs, place_spots, *finish(), (up_shape, down_shape), placed)
-    grad_up_weight, grad_down_weight = placed
+    placed = gathered(0, 2, gathered_a, (up_shape, down_shape), [])
+    grad_up_weight, grad_down_weight = gathered(1, 2, gathered_b, (up_shape, down_shape), placed)
     grad_query_weight, grad_key_weight = place(
-        (True, True), 0, 1, place_spots, *late[0](), (query_weight.shape,) * 2, []
+        (True, True), 0, 1, place_spots, *late_all[0], (query_weight.shape,) * 2, []
     )
     grad_value_weight, grad_out_weight = place(
-        (True, False), 0, 1, place_spots, *late[1](), (value_weight.shape, out_weight.shape), []
+        (True, False), 0, 1, place_spots, *late_all[1], (value_weight.shape, out_weight.shape), []
     )
 
     def back_to_place(near, far):
         return jnp.concatenate([near, far]).reshape(4, -1)[jnp.arange(4) ^ part].reshape(-1)
 
     def up_bias_grad(first, second):
-        sums = jnp.concatenate([first[4], second[4]]).reshape(4, 4, LANES).transpose(1, 0, 2)
+        sums = jnp.concatenate([first[2], second[2]]).reshape(4, 4, LANES).transpose(1, 0, 2)
         return sums[jnp.arange(4) ^ part].reshape(-1)
 
     def small(near, far, first, second):

time: 792 us -> 566 us (0.71)
  waiting for transfers between devices: 339 us -> 139 us
  starting transfers between devices: 71.8 us -> 43.6 us
  local copies, waits for them, and re-layouts: 38.3 us -> 23.7 us
  between operations: 2.17 us -> 15.3 us
  Pallas kernels: 308 us -> 296 us
  other arithmetic: 27.1 us -> 38.7 us
    ppermute x82 -> x46, waiting for transfers between devices: 339 us -> 138 us  [flip(): return lax.ppermute(value, axis, [(i, i ^ bit) for i in range(size)])]
    ppermute x82 -> x46, starting transfers between devices: 71.8 us -> 43.5 us  [flip(): return lax.ppermute(value, axis, [(i, i ^ bit) for i in range(size)])]
    pallas_call x6 -> x2, Pallas kernels: 32.7 us -> 10.9 us  [place(): pl.pallas_call(functools.partial(place_kernel, turned), grid_spec=pltpu.P...]
    convert_element_type x16 -> x20, other arithmetic: 13.5 us -> 31.9 us  [total(): return result.astype(LOW)]
    pallas_call x5 -> x7, Pallas kernels: 87.3 us -> 98.1 us  [the longest x4 76.4 us: mlp(): pl.pallas_call(functools.partial(mlp_kernel, rows // 2, turned), grid_spe...]
    slice x19 -> x1, local copies, waits for them, and re-layouts: 10.4 us -> 0.82 us  [paired_body(): slices[1]]
    pallas_call x4 -> x3, Pallas kernels: 53.6 us -> 51.3 us  [attend(): pl.pallas_call(attend_kernel, grid_spec=pltpu.PrefetchScalarGridSpec(num_...]
  transfers between devices with their start and end apart: 82 -> 50, of which waited for: 31 -> 24; matrix products, arithmetic and copies ran while one was open for 7% -> 9% of each run, Pallas kernels for 39% -> 48%
where the time goes in v3:
time: 566 us; the launch traced here: 556 us
  Pallas kernels  296 us (52%)
  waiting for transfers between devices  139 us (25%)
  starting transfers between devices  43.6 us (8%)
  other arithmetic  38.7 us (7%)
  local copies, waits for them, and re-layouts  23.7 us (4%)
  between operations  15.3 us (3%)
    ppermute x46, waiting for transfers between devices, flip(): return lax.ppermute(value, axis, [(i, i ^ bit) for i in range(size)])  138 us
    pallas_call x4, Pallas kernels, attend_back(): pl.pallas_call(attend_back_kernel, grid_spec=pltpu.PrefetchScalarGridSpec...  81.7 us
    pallas_call x4, Pallas kernels, mlp(): pl.pallas_call(functools.partial(mlp_kernel, rows // 2, turned), grid_spe...  76.4 us
    pallas_call x3, Pallas kernels, attend(): pl.pallas_call(attend_kernel, grid_spec=pltpu.PrefetchScalarGridSpec(num_...  51.3 us
    ppermute x46, starting transfers between devices, flip(): return lax.ppermute(value, axis, [(i, i ^ bit) for i in range(size)])  43.5 us
    convert_element_type x20, other arithmetic, total(): return result.astype(LOW)  31.9 us
    pallas_call x1, Pallas kernels, mlp_back(): pl.pallas_call(mlp_back_kernel, grid=(tiles,), in_specs=[pl.BlockSpec((1,...  22.5 us
    pallas_call x1, Pallas kernels, mlp_out(): pl.pallas_call(mlp_out_kernel, grid=(tiles,), in_specs=[pl.BlockSpec((1,...  17 us
  transfers between devices with their start and end apart: 50, of which 24 were waited for; matrix products, arithmetic and copies ran while one was open for 9% of the time, Pallas kernels for 48%

profile of v3, /device:TPU:0, one launch (start us, length us, event | category | flops | bytes accessed | tf_op | source)
XLA Modules:
  0.0 556.2 jit_solution(25641092992162586)
XLA Ops:
  13.1 11.9 %collective-permute-done.2 = bf16[2,2,64,1024]{3,2,1,0:T(8,128)(2,1)S(1)} collective-permute-done((bf16[2,2,64,1024]{3,2,1,0:T(8,128)(2,1)S(1)}, bf16[2,2,64,1024]{3,2,1,0:T(8,128)(2,1)S(1)}, u32[]{:S(2)}, u32[]{:S(2)}) %collective-permute-start.2) | collective-permute-done | bytes 524320 | tf_op jit(solution)/shard_map/ppermute | solution.py:245
  36.6 25.0 %attend.3 = (bf16[4,4,280,768]{3,2,1,0:T(8,128)(2,1)}, bf16[4,4,280,256]{3,2,1,0:T(8,128)(2,1)}, bf16[4,1024,768]{2,1,0:T(8,128)(2,1)}) custom-call(s32[4]{0:T(128)} %pad_add_fusion.spot_ref, s32[4]{0:T(128)} %dynamic_slice.83.count_ref, bf16[4,280,1024]{2,1,0:T(8,128)(2,1)} %bitcast.170, bf16[1024,512]{1,0:T(8,128)(2,1)} %refs_1_.3, ...), custom_call_target="tpu_custom_call" | custom-call | tf_op jit(solution)/shard_map/attend/pallas_call | solution.py:315
  67.5 13.2 %attend.4 = (bf16[4,4,280,768]{3,2,1,0:T(8,128)(2,1)}, bf16[4,4,280,256]{3,2,1,0:T(8,128)(2,1)}, bf16[4,1024,768]{2,1,0:T(8,128)(2,1)}) custom-call(s32[8]{0:T(128)} %concatenate.90.spot_ref, s32[4]{0:T(128)} %dynamic_slice.83.count_ref, bf16[4,280,1024]{2,1,0:T(8,128)(2,1)} %bitcast.171, ...), custom_call_target="tpu_custom_call", output_to_operand_aliasing={{0}: (13, {}), {1}: (14, {}), {2}: (15, {})} | custom-call | tf_op jit(solution)/shard_map/attend/pallas_call | solution.py:315
  85.1 13.1 %attend.5 = (bf16[4,4,280,768]{3,2,1,0:T(8,128)(2,1)}, bf16[4,4,280,256]{3,2,1,0:T(8,128)(2,1)}, bf16[4,1024,768]{2,1,0:T(8,128)(2,1)}) custom-call(s32[8]{0:T(128)} %concatenate.90.spot_ref, s32[4]{0:T(128)} %dynamic_slice.83.count_ref, bf16[4,280,1024]{2,1,0:T(8,128)(2,1)} %bitcast.172, ...), custom_call_target="tpu_custom_call", output_to_operand_aliasing={{0}: (13, {}), {1}: (14, {}), {2}: (15, {})} | custom-call | tf_op jit(solution)/shard_map/attend/pallas_call | solution.py:315
  99.0 9.3 %middle.1 = (f32[4,280,1024]{2,1,0:T(8,128)}, bf16[4,280,1024]{2,1,0:T(8,128)(2,1)}, bf16[4,256,1024]{2,1,0:T(8,128)(2,1)}) custom-call(s32[8]{0:T(128)} %concatenate.89.spot_ref, bf16[4,280,1024]{2,1,0:T(8,128)(2,1)} %bitcast.174, bf16[4,4,280,256]{3,2,1,0:T(8,128)(2,1)} %get-tuple-element.137.context_ref, bf16[512,1024]{1,0:T(8,128)(2,1)} %own_ref.1, ...), custom_call_target="tpu_custom_call" | custom-call | tf_op jit(solution)/shard_map/middle/pallas_call | solution.py:444
  108.2 19.2 %mlp.4 = (bf16[2,4,128,1024]{3,2,1,0:T(8,128)(2,1)}, bf16[2,4,128,1024]{3,2,1,0:T(8,128)(2,1)}, f32[2,1,512]{2,1,0:T(1,128)}, bf16[8,1120,512]{2,1,0:T(8,128)(2,...) custom-call(s32[4]{0:T(128)} %pad_add_fusion.spot_ref, ...), custom_call_target="tpu_custom_call" | custom-call | tf_op jit(solution)/shard_map/mlp/pallas_call | solution.py:510
  128.5 19.0 %mlp.5 = (bf16[2,4,128,1024]{3,2,1,0:T(8,128)(2,1)}, bf16[2,4,128,1024]{3,2,1,0:T(8,128)(2,1)}, f32[2,1,512]{2,1,0:T(1,128)}, bf16[8,1120,512]{2,1,0:T(8,128)(2,...) custom-call(s32[4]{0:T(128)} %pad_add_fusion.spot_ref, ...), custom_call_target="tpu_custom_call", output_to_operand_aliasing={{3}: (15, {}), {4}: (16, {}), {5}: (17, {}), {6}: (18, {})} | custom-call | tf_op jit(solution)/shard_map/mlp/pallas_call | solution.py:510
  150.4 18.8 %mlp.6 = (bf16[2,4,128,1024]{3,2,1,0:T(8,128)(2,1)}, bf16[2,4,128,1024]{3,2,1,0:T(8,128)(2,1)}, f32[2,1,512]{2,1,0:T(1,128)}, bf16[8,1120,512]{2,1,0:T(8,128)(2,...) custom-call(s32[4]{0:T(128)} %pad_add_fusion.spot_ref, ...), custom_call_target="tpu_custom_call", output_to_operand_aliasing={{3}: (15, {}), {4}: (16, {}), {5}: (17, {}), {6}: (18, {})} | custom-call | tf_op jit(solution)/shard_map/mlp/pallas_call | solution.py:510
  169.3 19.4 %mlp.7 = (bf16[2,4,128,1024]{3,2,1,0:T(8,128)(2,1)}, bf16[2,4,128,1024]{3,2,1,0:T(8,128)(2,1)}, f32[2,1,512]{2,1,0:T(1,128)}, bf16[8,1120,512]{2,1,0:T(8,128)(2,...) custom-call(s32[4]{0:T(128)} %pad_add_fusion.spot_ref, ...), custom_call_target="tpu_custom_call", output_to_operand_aliasing={{3}: (15, {}), {4}: (16, {}), {5}: (17, {}), {6}: (18, {})} | custom-call | tf_op jit(solution)/shard_map/mlp/pallas_call | solution.py:510
  190.5 12.7 %collective-permute-done.11 = bf16[2,1,128,1024]{3,2,1,0:T(8,128)(2,1)S(1)} collective-permute-done((bf16[2,1,128,1024]{3,2,1,0:T(8,128)(2,1)S(1)}, bf16[2,1,128,1024]{3,2,1,0:T(8,128)(2,1)S(1)}, u32[]{:S(2)}, u32[]{:S(2)}) %collective-permute-start.11) | collective-permute-done | bytes 524320 | tf_op jit(solution)/shard_map/ppermute | solution.py:245
  209.3 22.5 %mlp_back.1 = (f32[1120,1024]{1,0:T(8,128)}, f32[8,1024]{1,0:T(8,128)}) custom-call(bf16[8,1120,512]{2,1,0:T(8,128)(2,1)} %get-tuple-element.167.pre_ref, bf16[8,1024,512]{2,1,0:T(8,128)(2,1)} %get-tuple-element.168.up_ref, f32[1120,1024]{1,0:T(8,128)} %bitcast.180, bf16[1120,1024]{1,0:T(8,128)(2,1)} %cot_ref.9, bf16[1,1024]{1,0:T(2,128)(2,1)} %reshape.297.gain_ref), custom_call_target="tpu_custom_call" | custom-call | tf_op jit(solution)/shard_map/mlp_back/pallas_call | solution.py:591
  236.8 20.4 %attend_back.4 = (bf16[2,4,128,1024]{3,2,1,0:T(8,128)(2,1)}, f32[1,768]{1,0:T(1,128)}, bf16[4,4,280,768]{3,2,1,0:T(8,128)(2,1)}) custom-call(s32[4]{0:T(128)} %dynamic_slice.83.count_ref, bf16[1120,1024]{1,0:T(8,128)(2,1)} %fusion.5.rows_ref, f32[1120,1024]{1,0:T(8,128)} %get-tuple-element.180.cot_ref, bf16[4,4,280,768]{3,2,1,0:T(8,128)(2,1)} %get-tuple-element.181.qkv_ref, ...), custom_call_target="tpu_custom_call" | custom-call | tf_op jit(solution)/shard_map/attend_back/pallas_call | solution.py:384
  258.7 13.3 %collective-permute-done.16 = bf16[2,128,1024]{2,1,0:T(8,128)(2,1)} collective-permute-done((bf16[2,128,1024]{2,1,0:T(8,128)(2,1)}, bf16[2,128,1024]{2,1,0:T(8,128)(2,1)}, u32[]{:S(2)}, u32[]{:S(2)}) %collective-permute-start.16) | collective-permute-done | bytes 524320 | tf_op jit(solution)/shard_map/ppermute | solution.py:245
  287.8 20.4 %attend_back.5 = (bf16[2,4,128,1024]{3,2,1,0:T(8,128)(2,1)}, f32[1,768]{1,0:T(1,128)}, bf16[4,4,280,768]{3,2,1,0:T(8,128)(2,1)}) custom-call(s32[4]{0:T(128)} %dynamic_slice.83.count_ref, bf16[1120,1024]{1,0:T(8,128)(2,1)} %fusion.5.rows_ref, f32[1120,1024]{1,0:T(8,128)} %get-tuple-element.180.cot_ref, ...), custom_call_target="tpu_custom_call", output_to_operand_aliasing={{2}: (7, {})} | custom-call | tf_op jit(solution)/shard_map/attend_back/pallas_call | solution.py:384
  317.1 20.4 %attend_back.6 = (bf16[2,4,128,1024]{3,2,1,0:T(8,128)(2,1)}, f32[1,768]{1,0:T(1,128)}, bf16[4,4,280,768]{3,2,1,0:T(8,128)(2,1)}) custom-call(s32[4]{0:T(128)} %dynamic_slice.83.count_ref, bf16[1120,1024]{1,0:T(8,128)(2,1)} %fusion.5.rows_ref, f32[1120,1024]{1,0:T(8,128)} %get-tuple-element.180.cot_ref, ...), custom_call_target="tpu_custom_call", output_to_operand_aliasing={{2}: (7, {})} | custom-call | tf_op jit(solution)/shard_map/attend_back/pallas_call | solution.py:384
  340.5 16.8 %collective-permute-done.18 = bf16[2,128,1024]{2,1,0:T(8,128)(2,1)S(1)} collective-permute-done((bf16[2,128,1024]{2,1,0:T(8,128)(2,1)}, bf16[2,128,1024]{2,1,0:T(8,128)(2,1)S(1)}, u32[]{:S(2)}, u32[]{:S(2)}) %collective-permute-start.18) | collective-permute-done | bytes 524320 | tf_op jit(solution)/shard_map/ppermute | solution.py:245
  366.1 20.5 %attend_back.7 = (bf16[2,4,128,1024]{3,2,1,0:T(8,128)(2,1)}, f32[1,768]{1,0:T(1,128)}, bf16[4,4,280,768]{3,2,1,0:T(8,128)(2,1)}) custom-call(s32[4]{0:T(128)} %dynamic_slice.83.count_ref, bf16[1120,1024]{1,0:T(8,128)(2,1)} %fusion.5.rows_ref, f32[1120,1024]{1,0:T(8,128)} %get-tuple-element.180.cot_ref, ...), custom_call_target="tpu_custom_call", output_to_operand_aliasing={{2}: (7, {})} | custom-call | tf_op jit(solution)/shard_map/attend_back/pallas_call | solution.py:384
  386.5 6.1 %collective-permute-done.21 = bf16[4,64,1024]{2,1,0:T(8,128)(2,1)S(1)} collective-permute-done((bf16[4,64,1024]{2,1,0:T(8,128)(2,1)S(1)}, bf16[4,64,1024]{2,1,0:T(8,128)(2,1)S(1)}, u32[]{:S(2)}, u32[]{:S(2)}) %collective-permute-start.21) | collective-permute-done | bytes 524320 | tf_op jit(solution)/shard_map/ppermute | solution.py:245
  395.6 14.5 %input_grad.1 = (bf16[4,280,1024]{2,1,0:T(8,128)(2,1)}, f32[8,1024]{1,0:T(8,128)}) custom-call(bf16[4,4,280,768]{3,2,1,0:T(8,128)(2,1)} %get-tuple-element.207.grad_ref, bf16[4,1024,768]{2,1,0:T(8,128)(2,1)} %get-tuple-element.182.weight_ref, bf16[4,280,1024]{2,1,0:T(8,128)(2,1)} %bitcast.175, f32[4,280,1024]{2,1,0:T(8,128)} %bitcast.173, ...), custom_call_target="tpu_custom_call" | custom-call | tf_op jit(solution)/shard_map/input_grad/pallas_call | solution.py:666
  417.7 10.6 %collective-permute-done.27 = bf16[2,128,1024]{2,1,0:T(8,128)(2,1)S(1)} collective-permute-done((bf16[2,128,1024]{2,1,0:T(8,128)(2,1)}, bf16[2,128,1024]{2,1,0:T(8,128)(2,1)S(1)}, u32[]{:S(2)}, u32[]{:S(2)}) %collective-permute-start.27) | collective-permute-done | bytes 524320 | tf_op jit(solution)/shard_map/ppermute | solution.py:245
  429.9 17.0 %mlp_out.1 = bf16[1120,1024]{1,0:T(8,128)(2,1)} custom-call(bf16[8,1120,512]{2,1,0:T(8,128)(2,1)} %get-tuple-element.160.act_ref, bf16[8,512,1024]{2,1,0:T(8,128)(2,1)} %get-tuple-element.161.down_ref, f32[1120,1024]{1,0:T(8,128)} %bitcast.181, bf16[1,1024]{1,0:T(2,128)(2,1)} %reshape.303.bias_ref), custom_call_target="tpu_custom_call" | custom-call | tf_op jit(solution)/shard_map/mlp_out/pallas_call | solution.py:629
  451.1 14.2 %collective-permute-done.40 = bf16[2,64,1024]{2,1,0:T(8,128)(2,1)S(1)} collective-permute-done((bf16[2,64,1024]{2,1,0:T(8,128)(2,1)S(1)}, bf16[2,64,1024]{2,1,0:T(8,128)(2,1)S(1)}, u32[]{:S(2)}, u32[]{:S(2)}) %collective-permute-start.40) | collective-permute-done | bytes 262176 | tf_op jit(solution)/shard_map/ppermute | solution.py:245
  536.8 6.2 %gathered.2 = (f32[1024,2048]{1,0:T(8,128)}, f32[2048,1024]{1,0:T(8,128)}) custom-call(bf16[2,2,2,2,4,32,1024]{6,5,4,3,2,1,0:T(8,128)(2,1)} %bitcast.183), custom_call_target="tpu_custom_call" | custom-call | tf_op jit(solution)/shard_map/gathered/pallas_call | solution.py:743
  543.0 6.2 %gathered.3 = (f32[1024,2048]{1,0:T(8,128)}, f32[2048,1024]{1,0:T(8,128)}) custom-call(bf16[2,2,2,2,4,32,1024]{6,5,4,3,2,1,0:T(8,128)(2,1)} %bitcast.182, f32[1024,2048]{1,0:T(8,128)} %get-tuple-element.227.refs_0_, f32[2048,1024]{1,0:T(8,128)} %get-tuple-element.228.refs_1_), custom_call_target="tpu_custom_call", output_to_operand_aliasing={{0}: (1, {}), {1}: (2, {})} | custom-call | tf_op jit(solution)/shard_map/gathered/pallas_call | solution.py:743
  (305 shorter events, 170.4 us)
Async XLA Ops:
  7.2 101.0 %all-gather.7.cloned.1.call-start = ((), (), s32[]{:S(2)}) async-start(), calls=%async_computation | async-start | bytes 4456448 | tf_op jit(solution)/shard_map/all_gather | solution.py:858
  25.8 143.5 %all-gather.9.cloned.1.call-start = ((), (), s32[]{:S(2)}) async-start(), calls=%async_computation.1 | async-start | bytes 4456448 | tf_op jit(solution)/shard_map/all_gather | solution.py:858
  26.6 510.2 %all-gather.13.cloned.1.call-start = ((), (), s32[]{:S(2)}) async-start(), calls=%async_computation.3 | async-start | bytes 4456448 | tf_op jit(solution)/shard_map/all_gather | solution.py:1004
  28.2 36.0 %collective-permute-start = (bf16[3,1024,256]{2,1,0:T(8,128)(2,1)}, bf16[3,1024,256]{2,1,0:T(8,128)(2,1)}, u32[]{:S(2)}, u32[]{:S(2)}) collective-permute-start(bf16[3,1024,256]{2,1,0:T(8,128)(2,1)} %pad_maximum_fusion), channel_id=1, source_target_pairs={{0,1},{1,0},{2,3},{3,2},{4,5},{5,4},{6,7},{7,6},{8,9},{9,8},{10,11... | collective-permute-start | bytes 4718600 | tf_op jit(solution)/shard_map/ppermute | solution.py:245
  30.3 33.8 %collective-permute-start.1 = (bf16[3072]{0:T(1024)(128)(2,1)S(1)}, bf16[3072]{0:T(1024)(128)(2,1)S(1)}, u32[]{:S(2)}, u32[]{:S(2)}) collective-permute-start(bf16[3072]{0:T(1024)(128)(2,1)S(1)} %constant_dynamic-update-slice_fusion), channel_id=1, source_target_pairs={{0,1},{1,0},{2,3},{3,2},{4,5},{5,4},{6,7},{7,6},{8,9},{9,8},{10,11... | collective-permute-start | bytes 18440 | tf_op jit(solution)/shard_map/ppermute | solution.py:245
  147.4 21.8 %collective-permute-start.8 = (bf16[2,4,128,1024]{3,2,1,0:T(8,128)(2,1)}, bf16[2,4,128,1024]{3,2,1,0:T(8,128)(2,1)}, u32[]{:S(2)}, u32[]{:S(2)}) collective-permute-start(bf16[2,4,128,1024]{3,2,1,0:T(8,128)(2,1)} %get-tuple-element.147), channel_id=1, source_target_pairs={{0,2},{2,0},{4,6},{6,4},{8,10},{10,8},{12,14},{14,12},{16,18},{18,... | collective-permute-start | bytes 6291464 | tf_op jit(solution)/shard_map/ppermute | solution.py:245
  169.2 40.1 %collective-permute-start.9 = (bf16[2,4,128,1024]{3,2,1,0:T(8,128)(2,1)}, bf16[2,4,128,1024]{3,2,1,0:T(8,128)(2,1)S(1)}, u32[]{:S(2)}, u32[]{:S(2)}) collective-permute-start(bf16[2,4,128,1024]{3,2,1,0:T(8,128)(2,1)} %get-tuple-element.164), channel_id=1, source_target_pairs={{0,2},{2,0},{4,6},{6,4},{8,10},{10,8},{12,14},{14,12},{16,18},{18,... | collective-permute-start | bytes 6291464 | tf_op jit(solution)/shard_map/ppermute | solution.py:245
  188.8 45.7 %collective-permute-start.10 = (bf16[2,4,128,1024]{3,2,1,0:T(8,128)(2,1)}, bf16[2,4,128,1024]{3,2,1,0:T(8,128)(2,1)S(1)}, u32[]{:S(2)}, u32[]{:S(2)}) collective-permute-start(bf16[2,4,128,1024]{3,2,1,0:T(8,128)(2,1)} %get-tuple-element.166), channel_id=1, source_target_pairs={{0,2},{2,0},{4,6},{6,4},{8,10},{10,8},{12,14},{14,12},{16,18},{18,... | collective-permute-start | bytes 6291464 | tf_op jit(solution)/shard_map/ppermute | solution.py:245
  203.2 28.6 %collective-permute-start.13 = (bf16[2,2,128,1024]{3,2,1,0:T(8,128)(2,1)}, bf16[2,2,128,1024]{3,2,1,0:T(8,128)(2,1)}, u32[]{:S(2)}, u32[]{:S(2)}) collective-permute-start(bf16[2,2,128,1024]{3,2,1,0:T(8,128)(2,1)} %add_convert_fusion.4), channel_id=1, source_target_pairs={{0,1},{1,0},{2,3},{3,2},{4,5},{5,4},{6,7},{7,6},{8,9},{9,8},{10,11... | collective-permute-start | bytes 3145736 | tf_op jit(solution)/shard_map/ppermute | solution.py:245
  207.8 24.0 %collective-permute-start.14 = (bf16[2,128,1024]{2,1,0:T(8,128)(2,1)}, bf16[2,128,1024]{2,1,0:T(8,128)(2,1)S(1)}, u32[]{:S(2)}, u32[]{:S(2)}) collective-permute-start(bf16[2,128,1024]{2,1,0:T(8,128)(2,1)} %fusion.14), channel_id=1, source_target_pairs={{0,4},{2,6},{4,0},{6,2},{8,12},{10,14},{12,8},{14,10},{16,20},{18,... | collective-permute-start | bytes 1572872 | tf_op jit(solution)/shard_map/ppermute | solution.py:245
  257.3 55.1 %collective-permute-start.20 = (bf16[2,4,128,1024]{3,2,1,0:T(8,128)(2,1)}, bf16[2,4,128,1024]{3,2,1,0:T(8,128)(2,1)S(1)}, u32[]{:S(2)}, u32[]{:S(2)}) collective-permute-start(bf16[2,4,128,1024]{3,2,1,0:T(8,128)(2,1)} %get-tuple-element.195), channel_id=1, source_target_pairs={{0,2},{2,0},{4,6},{6,4},{8,10},{10,8},{12,14},{14,12},{16,18},{18,... | collective-permute-start | bytes 6291464 | tf_op jit(solution)/shard_map/ppermute | solution.py:245
  257.8 25.5 %collective-permute-start.12 = (bf16[2,2,128,1024]{3,2,1,0:T(8,128)(2,1)}, bf16[2,2,128,1024]{3,2,1,0:T(8,128)(2,1)}, u32[]{:S(2)}, u32[]{:S(2)}) collective-permute-start(bf16[2,2,128,1024]{3,2,1,0:T(8,128)(2,1)} %get-tuple-element.237), channel_id=1, source_target_pairs={{0,1},{1,0},{2,3},{3,2},{4,5},{5,4},{6,7},{7,6},{8,9},{9,8},{10,11... | collective-permute-start | bytes 3145736 | tf_op jit(solution)/shard_map/ppermute | solution.py:245
  275.7 32.5 %collective-permute-start.19 = (bf16[4,64,1024]{2,1,0:T(8,128)(2,1)}, bf16[4,64,1024]{2,1,0:T(8,128)(2,1)}, u32[]{:S(2)}, u32[]{:S(2)}) collective-permute-start(bf16[4,64,1024]{2,1,0:T(8,128)(2,1)} %dynamic-slice_bitcast_fusion.1), channel_id=1, source_target_pairs={{0,8},{2,10},{4,12},{6,14},{8,0},{10,2},{12,4},{14,6},{16,24},{18,... | collective-permute-start | bytes 1572872 | tf_op jit(solution)/shard_map/ppermute | solution.py:245
  283.4 31.3 %collective-permute-start.17 = (bf16[2,2,128,1024]{3,2,1,0:T(8,128)(2,1)}, bf16[2,2,128,1024]{3,2,1,0:T(8,128)(2,1)}, u32[]{:S(2)}, u32[]{:S(2)}) collective-permute-start(bf16[2,2,128,1024]{3,2,1,0:T(8,128)(2,1)} %get-tuple-element.191), channel_id=1, source_target_pairs={{0,1},{1,0},{2,3},{3,2},{4,5},{5,4},{6,7},{7,6},{8,9},{9,8},{10,11... | collective-permute-start | bytes 3145736 | tf_op jit(solution)/shard_map/ppermute | solution.py:245
  286.6 25.7 %collective-permute-start.15 = (bf16[2,128,1024]{2,1,0:T(8,128)(2,1)}, bf16[2,128,1024]{2,1,0:T(8,128)(2,1)}, u32[]{:S(2)}, u32[]{:S(2)}) collective-permute-start(bf16[2,128,1024]{2,1,0:T(8,128)(2,1)} %fusion.16), channel_id=1, source_target_pairs={{0,4},{2,6},{4,0},{6,2},{8,12},{10,14},{12,8},{14,10},{16,20},{18,... | collective-permute-start | bytes 1572872 | tf_op jit(solution)/shard_map/ppermute | solution.py:245
  309.7 27.7 %collective-permute-start.22 = (bf16[4,32,1024]{2,1,0:T(8,128)(2,1)S(1)}, bf16[4,32,1024]{2,1,0:T(8,128)(2,1)S(1)}, u32[]{:S(2)}, u32[]{:S(2)}) collective-permute-start(bf16[4,32,1024]{2,1,0:T(8,128)(2,1)S(1)} %dynamic-slice_bitcast_fusion.8), channel_id=1, source_target_pairs={{0,16},{2,18},{4,20},{6,22},{8,24},{10,26},{12,28},{14,30},{16,0},... | collective-permute-start | bytes 786440 | tf_op jit(solution)/shard_map/ppermute | solution.py:245
  338.3 204.8 %all-gather.11.cloned.1.call-start = ((), (), s32[]{:S(2)}) async-start(), calls=%async_computation.2 | async-start | bytes 4456448 | tf_op jit(solution)/shard_map/all_gather | solution.py:1020
  338.3 23.8 %collective-permute-start.23 = (bf16[2,2,128,1024]{3,2,1,0:T(8,128)(2,1)}, bf16[2,2,128,1024]{3,2,1,0:T(8,128)(2,1)S(1)}, u32[]{:S(2)}, u32[]{:S(2)}) collective-permute-start(bf16[2,2,128,1024]{3,2,1,0:T(8,128)(2,1)} %get-tuple-element.234), channel_id=1, source_target_pairs={{0,1},{1,0},{2,3},{3,2},{4,5},{5,4},{6,7},{7,6},{8,9},{9,8},{10,11... | collective-permute-start | bytes 3145736 | tf_op jit(solution)/shard_map/ppermute | solution.py:245
  340.0 53.0 %collective-permute-start.25 = (bf16[2,4,128,1024]{3,2,1,0:T(8,128)(2,1)}, bf16[2,4,128,1024]{3,2,1,0:T(8,128)(2,1)S(1)}, u32[]{:S(2)}, u32[]{:S(2)}) collective-permute-start(bf16[2,4,128,1024]{3,2,1,0:T(8,128)(2,1)} %get-tuple-element.209), channel_id=1, source_target_pairs={{0,2},{2,0},{4,6},{6,4},{8,10},{10,8},{12,14},{14,12},{16,18},{18,... | collective-permute-start | bytes 6291464 | tf_op jit(solution)/shard_map/ppermute | solution.py:245
  362.1 30.8 %collective-permute-start.26 = (bf16[2,2,128,1024]{3,2,1,0:T(8,128)(2,1)}, bf16[2,2,128,1024]{3,2,1,0:T(8,128)(2,1)S(1)}, u32[]{:S(2)}, u32[]{:S(2)}) collective-permute-start(bf16[2,2,128,1024]{3,2,1,0:T(8,128)(2,1)} %get-tuple-element.211), channel_id=1, source_target_pairs={{0,1},{1,0},{2,3},{3,2},{4,5},{5,4},{6,7},{7,6},{8,9},{9,8},{10,11... | collective-permute-start | bytes 3145736 | tf_op jit(solution)/shard_map/ppermute | solution.py:245
  363.9 28.7 %collective-permute-start.21 = (bf16[4,64,1024]{2,1,0:T(8,128)(2,1)S(1)}, bf16[4,64,1024]{2,1,0:T(8,128)(2,1)S(1)}, u32[]{:S(2)}, u32[]{:S(2)}) collective-permute-start(bf16[4,64,1024]{2,1,0:T(8,128)(2,1)S(1)} %dynamic-slice_bitcast_fusion), channel_id=1, source_target_pairs={{0,8},{2,10},{4,12},{6,14},{8,0},{10,2},{12,4},{14,6},{16,24},{18,... | collective-permute-start | bytes 1572872 | tf_op jit(solution)/shard_map/ppermute | solution.py:245
  416.1 30.8 %collective-permute-start.39 = (bf16[2,128,1024]{2,1,0:T(8,128)(2,1)S(1)}, bf16[2,128,1024]{2,1,0:T(8,128)(2,1)S(1)}, u32[]{:S(2)}, u32[]{:S(2)}) collective-permute-start(bf16[2,128,1024]{2,1,0:T(8,128)(2,1)S(1)} %fusion.19), channel_id=1, source_target_pairs={{0,4},{2,6},{4,0},{6,2},{8,12},{10,14},{12,8},{14,10},{16,20},{18,... | collective-permute-start | bytes 1572872 | tf_op jit(solution)/shard_map/ppermute | solution.py:245
  499.0 26.0 %collective-permute-start.45 = (bf16[8,2,32,1024]{3,2,1,0:T(8,128)(2,1)S(1)}, bf16[8,2,32,1024]{3,2,1,0:T(8,128)(2,1)S(1)}, u32[]{:S(2)}, u32[]{:S(2)}) collective-permute-start(bf16[8,2,32,1024]{3,2,1,0:T(8,128)(2,1)S(1)} %pad_maximum_fusion.4.near_ref), channel_id=1, source_target_pairs={{0,2},{2,0},{4,6},{6,4},{8,10},{10,8},{12,14},{14,12},{16,18},{18,... | collective-permute-start | bytes 3145736 | tf_op jit(solution)/shard_map/ppermute | solution.py:245
  504.6 26.8 %collective-permute-start.38 = (bf16[8,2,32,1024]{3,2,1,0:T(8,128)(2,1)S(1)}, bf16[8,2,32,1024]{3,2,1,0:T(8,128)(2,1)}, u32[]{:S(2)}, u32[]{:S(2)}) collective-permute-start(bf16[8,2,32,1024]{3,2,1,0:T(8,128)(2,1)S(1)} %pad_maximum_fusion.3.near_ref), channel_id=1, source_target_pairs={{0,2},{2,0},{4,6},{6,4},{8,10},{10,8},{12,14},{14,12},{16,18},{18,... | collective-permute-start | bytes 3145736 | tf_op jit(solution)/shard_map/ppermute | solution.py:245
  (67 other events, 891.5 us)
Sparse Core Ops, SparseCore 0:
  25.9 52.1 all-gather.6
  80.3 51.7 all-gather.8
  338.4 55.6 all-gather.12
  411.1 54.8 all-gather.10

commit v4 on v3

--- a/solution.py
+++ b/solution.py
@@ -286,20 +286,25 @@
     length = TEXT + count_ref[pair]
     lane = lax.broadcasted_iota(jnp.int32, (SEQ, LANES), 1)
     padding = lax.broadcasted_iota(jnp.int32, (SEQ, SEQ), 1) >= length
+    lane_low = lane < HEAD_DIM
+    everything = []
     for tile in range(2):
         query, key, value = (
             qkv[:, i * 256 + tile * LANES : i * 256 + (tile + 1) * LANES] for i in range(3)
         )
-        heads = []
+        query = query * SCALE
         for side in range(2):
-            mine = (lane < HEAD_DIM) if side == 0 else (lane >= HEAD_DIM)
-            scores = dot(jnp.where(mine, query, jnp.zeros_like(query)), key, 1, 1) * SCALE
-            scores = jnp.where(padding, NEGATIVE, scores)
-            power = jnp.exp(scores - jnp.max(scores, -1, keepdims=True))
-            probs = power * (1.0 / jnp.sum(power, -1, keepdims=True))
-            heads.append(dot(probs.astype(LOW), value, 1, 0))
+            mine = lane_low if side == 0 else jnp.logical_not(lane_low)
+            everything.append((dot(jnp.where(mine, query, jnp.zeros_like(query)), key, 1, 1), value))
+    heads = []
+    for scores, value in everything:
+        scores = jnp.where(padding, NEGATIVE, scores)
+        power = jnp.exp(scores - jnp.max(scores, -1, keepdims=True))
+        inverse = 1.0 / jnp.sum(power, -1, keepdims=True)
+        heads.append(dot(power.astype(LOW), value, 1, 0) * inverse)
+    for tile in range(2):
         context_ref[0, 0, :, tile * LANES : (tile + 1) * LANES] = jnp.where(
-            lane < HEAD_DIM, heads[0], heads[1]
+            lane_low, heads[2 * tile], heads[2 * tile + 1]
         ).astype(LOW)
 
 
@@ -330,55 +335,72 @@
     )(spots, counts, rows, *[array for array, _ in operands], *buffers)
 
 
-def attend_back_kernel(count_ref, rows_ref, cot_ref, qkv_ref, context_ref, weight_ref, out_ref, *refs):
-    near_ref, bias_ref, qkv_grad_ref, grad_buf, context_buf = refs[-5:]
+def attend_back_kernel(count_ref, rows_hbm, cots_hbm, cot_ref, qkv_ref, context_ref, out_ref, *refs):
+    near_ref, bias_ref, qkv_grad_ref, grad_buf, context_buf, rows_buf, cots_buf, sems = refs[-8:]
     pair = pl.program_id(0)
+    copies = [
+        pltpu.make_async_copy(rows_hbm, rows_buf, sems.at[0]),
+        pltpu.make_async_copy(cots_hbm, cots_buf, sems.at[1]),
+    ]
+
+    @pl.when(pair == 0)
+    def _():
+        for copy in copies:
+            copy.start()
+
     at = pl.ds(pl.multiple_of(pair * SEQ, 8), SEQ)
-    cot = cot_ref[at, :].astype(LOW)
-    context_grad = dot(cot, out_ref[0], 1, 1).astype(LOW)
+    context_grad = dot(cot_ref[0], out_ref[0], 1, 1).astype(LOW)
     qkv = qkv_ref[0, 0]
     context_buf[at, :] = context_ref[0, 0].astype(WIDE)
     length = TEXT + count_ref[pair]
     lane = lax.broadcasted_iota(jnp.int32, (SEQ, LANES), 1)
     padding = lax.broadcasted_iota(jnp.int32, (SEQ, SEQ), 0) >= length
     grads = [[], [], []]
+    lane_low = lane < HEAD_DIM
+    work = []
     for tile in range(2):
         query, key, value = (
             qkv[:, i * 256 + tile * LANES : i * 256 + (tile + 1) * LANES] for i in range(3)
         )
+        query = query * SCALE
         outer = context_grad[:, tile * LANES : (tile + 1) * LANES]
-        heads = [[], [], []]
         for side in range(2):
-            mine = (lane < HEAD_DIM) if side == 0 else (lane >= HEAD_DIM)
-            scores = dot(jnp.where(mine, key, jnp.zeros_like(key)), query, 1, 1) * SCALE
-            scores = jnp.where(padding, NEGATIVE, scores)
-            power = jnp.exp(scores - jnp.max(scores, 0, keepdims=True))
-            probs = power * (1.0 / jnp.sum(power, 0, keepdims=True))
+            mine = lane_low if side == 0 else jnp.logical_not(lane_low)
+            scores = dot(jnp.where(mine, key, jnp.zeros_like(key)), query, 1, 1)
             probs_grad = dot(jnp.where(mine, value, jnp.zeros_like(value)), outer, 1, 1)
-            both = probs * probs_grad
-            score_grad = (both - probs * jnp.sum(both, 0, keepdims=True)).astype(LOW)
-            heads[0].append(dot(score_grad, key, 0, 0))
-            heads[1].append(dot(score_grad, query, 1, 0))
-            heads[2].append(dot(probs.astype(LOW), outer, 1, 0))
-        for i, scale in enumerate((SCALE, SCALE, 1.0)):
-            grads[i].append((jnp.where(lane < HEAD_DIM, *heads[i]) * scale).astype(LOW))
+            work.append((scores, probs_grad, query, key, outer))
+    heads = []
+    for scores, probs_grad, query, key, outer in work:
+        scores = jnp.where(padding, NEGATIVE, scores)
+        power = jnp.exp(scores - jnp.max(scores, 0, keepdims=True))
+        probs = power * (1.0 / jnp.sum(power, 0, keepdims=True))
+        both = probs * probs_grad
+        score_grad = (both - probs * jnp.sum(both, 0, keepdims=True)).astype(LOW)
+        heads.append(
+            (dot(score_grad, key, 0, 0), dot(score_grad, query, 1, 0), dot(probs.astype(LOW), outer, 1, 0))
+        )
+    for tile in range(2):
+        for i, scale in enumerate((SCALE, 1.0, 1.0)):
+            pair_of = [heads[2 * tile + side][i] for side in range(2)]
+            grads[i].append((jnp.where(lane_low, *pair_of) * scale).astype(LOW))
     joined = jnp.concatenate(grads[0] + grads[1] + grads[2], 1)
     qkv_grad_ref[0, 0] = joined
     grad_buf[at, :] = joined.astype(WIDE)
 
     @pl.when(pair == pl.num_programs(0) - 1)
     def _():
-        stacked = dot(grad_buf[...].astype(LOW), rows_ref[...], 0, 0).astype(LOW)
+        for copy in copies:
+            copy.wait()
+        stacked = dot(grad_buf[...].astype(LOW), rows_buf[...], 0, 0).astype(LOW)
+        outs = dot(context_buf[...].astype(LOW), cots_buf[...], 0, 0).astype(LOW)
         for i in range(2):
             near_ref[i, :3] = stacked.reshape(3, 2, LANES, -1)[:, i]
-        outs = dot(context_buf[...].astype(LOW), cot_ref[...].astype(LOW), 0, 0).astype(LOW)
-        for i in range(2):
             near_ref[i, 3] = outs[i * LANES : (i + 1) * LANES]
         bias_ref[...] = jnp.sum(grad_buf[...], 0, keepdims=True)
 
 
 def attend_back(slot, counts, rows, cot, kept, outs, buffers):
-    qkv, context, weights = kept
+    qkv, context, _ = kept
     _, pairs, seq, _ = qkv.shape
     width = rows.shape[1]
     return pl.pallas_call(
@@ -387,11 +409,11 @@
             num_scalar_prefetch=1,
             grid=(pairs,),
             in_specs=[
-                resident(rows.shape),
-                resident(cot.shape),
+                ANYWHERE,
+                ANYWHERE,
+                pl.BlockSpec((1, seq, width), lambda p, *_: (p, 0, 0)),
                 pl.BlockSpec((1, 1, seq, 768), lambda p, *_: (slot, p, 0, 0)),
                 pl.BlockSpec((1, 1, seq, 256), lambda p, *_: (slot, p, 0, 0)),
-                pl.BlockSpec((1, width, 768), lambda p, *_: (slot, 0, 0)),
                 pl.BlockSpec((1, 256, width), lambda p, *_: (slot, 0, 0)),
             ]
             + [ANYWHERE] * len(buffers),
@@ -403,6 +425,9 @@
             scratch_shapes=[
                 pltpu.VMEM((pairs * seq, 768), WIDE),
                 pltpu.VMEM((pairs * seq, 256), WIDE),
+                pltpu.VMEM(rows.shape, LOW),
+                pltpu.VMEM(cot.shape, LOW),
+                pltpu.SemaphoreType.DMA((2,)),
             ],
         ),
         out_shape=[
@@ -413,7 +438,7 @@
         input_output_aliases={7: 2} if buffers else {},
         name="attend_back",
         compiler_params=pltpu.CompilerParams(vmem_limit_bytes=56 * 1024 * 1024),
-    )(counts, rows, cot, qkv, context, weights, outs, *buffers)
+    )(counts, rows, cot, cot.reshape(pairs, seq, width), qkv, context, outs, *buffers)
 
 
 def middle_kernel(
@@ -518,20 +543,20 @@
             out_specs=[grad_block] * 2
             + [
                 pl.BlockSpec((1, 1, tile), lambda j, *_: (j, 0, 0)),
-                pl.BlockSpec((1, rows, tile), lambda j, *_: (first + j, 0, 0)),
-                pl.BlockSpec((1, rows, tile), lambda j, *_: (first + j, 0, 0)),
-                pl.BlockSpec((1, width, tile), lambda j, *_: (first + j, 0, 0)),
-                pl.BlockSpec((1, tile, width), lambda j, *_: (first + j, 0, 0)),
+                pl.BlockSpec((1, rows, tile), lambda j, *_: (first // 2, 0, j)),
+                pl.BlockSpec((1, rows, tile), lambda j, *_: (first // 2, 0, j)),
+                pl.BlockSpec((1, width, tile), lambda j, *_: (first // 2, 0, j)),
+                pl.BlockSpec((1, tile, width), lambda j, *_: (first // 2, j, 0)),
             ],
             scratch_shapes=[pltpu.VMEM((1, tile), WIDE)],
         ),
         out_shape=[grad] * 2
         + [
             jax.ShapeDtypeStruct((2, 1, tile), WIDE),
-            jax.ShapeDtypeStruct((8, rows, tile), LOW),
-            jax.ShapeDtypeStruct((8, rows, tile), LOW),
-            jax.ShapeDtypeStruct((8, width, tile), LOW),
-            jax.ShapeDtypeStruct((8, tile, width), LOW),
+            jax.ShapeDtypeStruct((4, rows, 2 * tile), LOW),
+            jax.ShapeDtypeStruct((4, rows, 2 * tile), LOW),
+            jax.ShapeDtypeStruct((4, width, 2 * tile), LOW),
+            jax.ShapeDtypeStruct((4, 2 * tile, width), LOW),
         ],
         input_output_aliases={3 + len(operands) + i: 3 + i for i in range(len(buffers))},
         name="mlp",
@@ -552,33 +577,45 @@
     return pulled, jnp.sum(grad * unit, 0, keepdims=True), jnp.sum(grad, 0, keepdims=True)
 
 
-def mlp_back_kernel(pre_ref, up_ref, middle_ref, cot_ref, gain_ref, grad_ref, sums_ref, sum_buf):
+def mlp_back_kernel(pre_ref, up_ref, middle_hbm, cot_hbm, gain_ref, grad_ref, low_ref, sums_ref, *refs):
+    sum_buf, middle_buf, cot_buf, sems = refs
     step = pl.program_id(0)
+    copies = [
+        pltpu.make_async_copy(middle_hbm, middle_buf, sems.at[0]),
+        pltpu.make_async_copy(cot_hbm, cot_buf, sems.at[1]),
+    ]
+    part = dot(pre_ref[0], up_ref[0], 1, 1)
 
     @pl.when(step == 0)
     def _():
-        sum_buf[...] = dot(pre_ref[0], up_ref[0], 1, 1)
+        for copy in copies:
+            copy.start()
+        sum_buf[...] = part
 
     @pl.when(step > 0)
     def _():
-        sum_buf[...] += dot(pre_ref[0], up_ref[0], 1, 1)
+        sum_buf[...] += part
 
     @pl.when(step == pl.num_programs(0) - 1)
     def _():
+        for copy in copies:
+            copy.wait()
         sums_ref[...] = jnp.zeros_like(sums_ref)
         chunk = 224
 
         def one(i, carry):
             at = pl.ds(pl.multiple_of(i * chunk, chunk), chunk)
-            cot = cot_ref[at, :].astype(WIDE)
+            cot = cot_buf[at, :].astype(WIDE)
             pulled, gain_grad, shift_grad = norm_back(
-                middle_ref[at, :], gain_ref[...].astype(WIDE), sum_buf[at, :]
+                middle_buf[at, :], gain_ref[...].astype(WIDE), sum_buf[at, :]
             )
             grad = cot + pulled
+            low = grad.astype(LOW)
             grad_ref[at, :] = grad
+            low_ref[at, :] = low
             sums_ref[0:1, :] += gain_grad
             sums_ref[1:2, :] += shift_grad
-            sums_ref[2:3, :] += jnp.sum(grad.astype(LOW).astype(WIDE), 0, keepdims=True)
+            sums_ref[2:3, :] += jnp.sum(low.astype(WIDE), 0, keepdims=True)
             sums_ref[3:4, :] += jnp.sum(cot, 0, keepdims=True)
             return carry
 
@@ -594,53 +631,111 @@
         in_specs=[
             pl.BlockSpec((1, rows, tile), lambda j: (j, 0, 0)),
             pl.BlockSpec((1, width, tile), lambda j: (j, 0, 0)),
-            resident(middle.shape),
-            resident(cot.shape),
+            ANYWHERE,
+            ANYWHERE,
             resident((1, width)),
         ],
-        out_specs=[resident((rows, width)), resident((8, width))],
+        out_specs=[resident((rows, width)), resident((rows, width)), resident((8, width))],
         out_shape=[
             jax.ShapeDtypeStruct((rows, width), WIDE),
+            jax.ShapeDtypeStruct((rows, width), LOW),
             jax.ShapeDtypeStruct((8, width), WIDE),
         ],
-        scratch_shapes=[pltpu.VMEM((rows, width), WIDE)],
+        scratch_shapes=[
+            pltpu.VMEM((rows, width), WIDE),
+            pltpu.VMEM((rows, width), WIDE),
+            pltpu.VMEM((rows, width), LOW),
+            pltpu.SemaphoreType.DMA((2,)),
+        ],
         name="mlp_back",
         compiler_params=pltpu.CompilerParams(vmem_limit_bytes=56 * 1024 * 1024),
     )(pre_grads, ups, middle, cot, gain)
 
 
-def mlp_out_kernel(act_ref, down_ref, middle_ref, bias_ref, out_ref, sum_buf):
+def mlp_out_kernel(half, act_ref, down_ref, middle_hbm, bias_ref, *refs):
+    out_ref, sum_buf, middle_buf, sem = refs[-4:]
     step = pl.program_id(0)
+    rows = out_ref.shape[0]
+    copy = pltpu.make_async_copy(middle_hbm.at[pl.ds(half * rows, rows), :], middle_buf, sem)
+    part = dot(act_ref[0], down_ref[0], 1, 0)
 
     @pl.when(step == 0)
     def _():
-        sum_buf[...] = middle_ref[...] + bias_ref[...].astype(WIDE)
-
-    sum_buf[...] += dot(act_ref[0], down_ref[0], 1, 0)
+        copy.start()
+        sum_buf[...] = part
+
+    @pl.when(step > 0)
+    def _():
+        sum_buf[...] += part
 
     @pl.when(step == pl.num_programs(0) - 1)
     def _():
-        out_ref[...] = sum_buf[...].astype(LOW)
-
-
-def mlp_out(acts, downs, middle, bias):
+        copy.wait()
+        out_ref[...] = (sum_buf[...] + middle_buf[...] + bias_ref[...].astype(WIDE)).astype(LOW)
+
+
+def mlp_out(half, acts, downs, middle, bias, buffers):
     tiles, rows, tile = acts.shape
     width = middle.shape[1]
+    count = rows // 2
     return pl.pallas_call(
-        mlp_out_kernel,
+        functools.partial(mlp_out_kernel, half),
         grid=(tiles,),
         in_specs=[
-            pl.BlockSpec((1, rows, tile), lambda j: (j, 0, 0)),
+            pl.BlockSpec((1, count, tile), lambda j: (j, half, 0)),
             pl.BlockSpec((1, tile, width), lambda j: (j, 0, 0)),
-            resident(middle.shape),
+            ANYWHERE,
             resident((1, width)),
+        ]
+        + [ANYWHERE] * len(buffers),
+        out_specs=pl.BlockSpec((count, width), lambda j: (half, 0)),
+        out_shape=jax.ShapeDtypeStruct((rows, width), LOW),
+        scratch_shapes=[
+            pltpu.VMEM((count, width), WIDE),
+            pltpu.VMEM((count, width), WIDE),
+            pltpu.SemaphoreType.DMA(()),
         ],
-        out_specs=resident((rows, width)),
-        out_shape=jax.ShapeDtypeStruct((rows, width), LOW),
-        scratch_shapes=[pltpu.VMEM((rows, width), WIDE)],
+        input_output_aliases={4: 0} if buffers else {},
         name="mlp_out",
         compiler_params=pltpu.CompilerParams(vmem_limit_bytes=56 * 1024 * 1024),
-    )(acts, downs, middle, bias)
+    )(acts, downs, middle, bias, *buffers)
+
+
+def pack_kernel(spot_ref, *refs):
+    out_refs = refs[-2:]
+    shared_one, shared_two = refs[8:10]
+    for side in range(2):
+        near, far, first, second = refs[4 * side : 4 * side + 4]
+        out = out_refs[side]
+        for r in range(4):
+            at = spot_ref[r]
+            source = near if r < 2 else far
+            lanes = (r % 2) * LANES
+            out[pl.ds(at, 1), :] = source[:, lanes : lanes + LANES]
+            out[pl.ds(4 + at, 1), :] = source[:, 512 + lanes : 512 + lanes + LANES]
+            for j in range(4):
+                sums = first if j < 2 else second
+                out[pl.ds(8 + at * 4 + j, 1), :] = sums[j % 2, :, r * LANES : (r + 1) * LANES]
+        rows = [(shared_one, 0), (shared_one, 1), (shared_two, 2), (shared_two, 0), (shared_two, 1), (shared_two, 3)]
+        for k, (source, row) in enumerate(rows):
+            for i in range(8):
+                at = 24 + 8 * k + i
+                out[at : at + 1, :] = source[row : row + 1, i * LANES : (i + 1) * LANES]
+
+
+def pack(spots, own, other, sums_one, sums_two):
+    return pl.pallas_call(
+        pack_kernel,
+        grid_spec=pltpu.PrefetchScalarGridSpec(
+            num_scalar_prefetch=1,
+            grid=(1,),
+            in_specs=[resident(item.shape) for item in (*own, *other, sums_one, sums_two)],
+            out_specs=[resident((72, LANES))] * 2,
+        ),
+        out_shape=[jax.ShapeDtypeStruct((72, LANES), WIDE)] * 2,
+        name="pack",
+        compiler_params=pltpu.CompilerParams(vmem_limit_bytes=56 * 1024 * 1024),
+    )(spots, *own, *other, sums_one, sums_two)
 
 
 def input_kernel(grad_ref, weight_ref, rows_ref, above_ref, gain_ref, out_ref, sums_ref):
@@ -855,6 +950,7 @@
         return weights, biases
 
     other_spots = jnp.concatenate([sides, spots])
+    slices = after(slices, normed)
     gathered_weights = [lax.all_gather(slices[0], "dp"), lax.all_gather(slices[1], "dp")]
     kept = attend(
         0, 2, gate(spots, sent_qkv, sent_bias, slices), counts, normed_three, *own_inputs(), []
@@ -869,7 +965,7 @@
     kept = attend(
         2, 1, gate(other_spots, sent_out), counts, normed_three, *other_inputs(0, near_qkv), kept
     )
-    near_out = after(near_out, kept[1])
+    near_out, far_qkv, _ = lax.optimization_barrier((near_out, far_qkv, kept[1]))
     far_out = swap(near_out, CORE)
     kept = attend(
         3, 1, gate(other_spots, near_out), counts, normed_three, *other_inputs(1, far_qkv), kept
@@ -938,40 +1034,42 @@
         return cut(item, zhigh_id ^ 1), cut(item, zhigh_id)
 
     back = lambda slot, wait, qkv_grads: attend_back(
-        slot, gate(counts, *wait), normed, middle_grad, kept, outs_all, qkv_grads
-    )
-
+        slot, gate(counts, *wait), normed, attn_grad, kept, outs_all, qkv_grads
+    )
+
+    together = lambda *items: lax.optimization_barrier(items)
     other_a = mlp(2, True, spots, hidden, layer_cot, *other_mlp(0), [])
     far_other_a = swap(other_a[1], CORE)
     own_a = mlp(0, False, spots, hidden, layer_cot, *own_mlp(0), other_a[3:])
-    far_own_a = swap(own_a[1], CORE)
-    far_other_a = after(far_other_a, own_a[2])
+    far_other_a, far, _ = together(far_other_a, own_a[1], own_a[2])
+    far_own_a = swap(far, CORE)
     out_a = [outbound(other_a[0], far_other_a, *span) for span in ((0, 1), (1, 2), (2, 4))]
     own_b = mlp(6, False, gate(spots, *out_a), hidden, layer_cot, *own_mlp(2), own_a[3:])
-    beyond_a0 = across(out_a[0])
-    far_own_b = swap(own_b[1], CORE)
-    far_own_a = after(far_own_a, own_b[2])
+    beyond_a0, far_own_a, far, _ = together(across(out_a[0]), far_own_a, own_b[1], own_b[2])
+    far_own_b = swap(far, CORE)
     other_b = mlp(
         4, True, gate(spots, beyond_a0, far_own_a), hidden, layer_cot, *other_mlp(2), own_b[3:]
     )
-    beyond_a1 = across(after(out_a[1], beyond_a0))
-    far_other_b = swap(other_b[1], CORE)
     acts, pre_grads, ups_all, downs_all = other_b[3:]
-    beyond_a1 = after(beyond_a1, other_b[2])
+    beyond_a1, far_own_b, far, _ = together(
+        across(after(out_a[1], beyond_a0)), far_own_b, other_b[1], other_b[2]
+    )
+    far_other_b = swap(far, CORE)
     beyond_a01 = jnp.concatenate([beyond_a0, beyond_a1], 1)
     side_a01 = sideways(own_a[0], far_own_a, beyond_a01, 0, 2)
-    middle_grad, sums_two = mlp_back(
+    middle_grad, attn_grad, sums_two = mlp_back(
         pre_grads, ups_all, middle, layer_cot, gate(row_vec(mlp_gain), side_a01, beyond_a01, far_own_b)
     )
-    beyond_a23 = after(across(after(out_a[2], beyond_a1)), sums_two)
-    arrived_a01 = after(swap(side_a01, XBIT), sums_two)
-    far_other_b = after(far_other_b, sums_two)
+    beyond_a23, arrived_a01, far_other_b, _ = together(
+        across(after(out_a[2], beyond_a1)), swap(side_a01, XBIT), far_other_b, sums_two
+    )
     side_a23 = sideways(own_a[0], far_own_a, beyond_a23, 2, 4)
     out_b = [outbound(other_b[0], far_other_b, *span) for span in ((0, 2), (2, 4))]
     other_far, bias_other_far, qkv_grads = back(3, (side_a23, arrived_a01, *out_b), [])
-    beyond_b01 = after(across(out_b[0]), bias_other_far)
-    arrived_a23 = after(swap(side_a23, XBIT), bias_other_far)
-    late_other_far = swap(other_far, CORE)
+    beyond_b01, arrived_a23, far, _ = together(
+        across(out_b[0]), swap(side_a23, XBIT), other_far, bias_other_far
+    )
+    late_other_far = swap(far, CORE)
     sum_a = jnp.concatenate(
         [
             collected(own_a[0], far_own_a, beyond_a01, arrived_a01, 0, 2),
@@ -981,18 +1079,17 @@
     low_a, keep_a = halves(sum_a)
     side_b01 = sideways(own_b[0], far_own_b, beyond_b01, 0, 2)
     other_near, bias_other_near, qkv_grads = back(2, (low_a, sum_a, side_b01), [qkv_grads])
-    beyond_b23 = after(across(after(out_b[1], beyond_b01)), bias_other_near)
-    arrived_b01 = after(swap(side_b01, XBIT), bias_other_near)
-    low_a = after(swap(low_a, ZLOW), bias_other_near)
-    late_other_far = after(late_other_far, bias_other_near)
+    beyond_b23, arrived_b01, low_a, late_other_far, _ = together(
+        across(after(out_b[1], beyond_b01)), swap(side_b01, XBIT), swap(low_a, ZLOW), late_other_far, bias_other_near
+    )
     high_a, keep_a = quarters(total(keep_a, low_a))
     side_b23 = sideways(own_b[0], far_own_b, beyond_b23, 2, 4)
     late_out = [outbound(other_near, late_other_far, *span) for span in ((0, 2), (2, 4))]
     own_far, bias_own_far, qkv_grads = back(1, (high_a, side_b23, arrived_b01, *late_out), [qkv_grads])
-    late_own_far = swap(own_far, CORE)
-    late_beyond0 = after(across(late_out[0]), bias_own_far)
-    arrived_b23 = after(swap(side_b23, XBIT), bias_own_far)
-    high_a = after(swap(high_a, ZHIGH), bias_own_far)
+    late_beyond0, arrived_b23, high_a, far, _ = together(
+        across(late_out[0]), swap(side_b23, XBIT), swap(high_a, ZHIGH), own_far, bias_own_far
+    )
+    late_own_far = swap(far, CORE)
     one_a = total(keep_a, high_a)
     sum_b = jnp.concatenate(
         [
@@ -1003,72 +1100,86 @@
     low_b, keep_b = halves(sum_b)
     gathered_a = lax.all_gather(one_a, "dp")
     own_near, bias_own_near, qkv_grads = back(0, (one_a, low_b, sum_b, late_beyond0), [qkv_grads])
-    late_beyond1 = after(across(after(late_out[1], late_beyond0)), bias_own_near)
-    late_own_far = after(late_own_far, bias_own_near)
-    low_b = after(swap(low_b, ZLOW), bias_own_near)
+    late_beyond1, late_own_far, low_b, _ = together(
+        across(after(late_out[1], late_beyond0)), late_own_far, swap(low_b, ZLOW), bias_own_near
+    )
     high_b, keep_b = quarters(total(keep_b, low_b))
     late_side0 = sideways(own_near, late_own_far, late_beyond0, 0, 2)
+    late_side1 = sideways(own_near, late_own_far, late_beyond1, 2, 4)
     grad_in, sums_one = input_step(
         qkv_grads,
         kept[2],
         layer_in.reshape(shape_three),
         middle_grad.reshape(shape_three),
-        gate(row_vec(attn_gain), high_b, late_side0, late_beyond1),
-    )
-    high_b = after(swap(high_b, ZHIGH), sums_one)
+        gate(row_vec(attn_gain), high_b, late_side0, late_side1),
+    )
+    high_b, late_arrived0, sums_one = together(swap(high_b, ZHIGH), swap(late_side0, XBIT), sums_one)
     one_b = total(keep_b, high_b)
     gathered_b = lax.all_gather(one_b, "dp")
-    late_arrived0 = after(swap(late_side0, XBIT), sums_one)
-    late_side1 = sideways(own_near, late_own_far, after(late_beyond1, sums_one), 2, 4)
-    late_low0, late_keep0 = halves(
-        collected(own_near, late_own_far, late_beyond0, late_arrived0, 0, 2)
+    quarter_id = zlow_id * 2 + zhigh_id
+    z_bits = [None, ZHIGH, ZLOW, ZLOW | ZHIGH]
+
+    def four(item):
+        count, lanes, cols = item.shape
+        item = item.reshape(count, 4, lanes // 4, cols)
+        return [pick(item, quarter_id ^ r, 1, 1)[:, 0] for r in range(4)]
+
+    def send_four(items):
+        return [swap(items[r], z_bits[r]) for r in range(1, 4)]
+
+    late_four0 = four(collected(own_near, late_own_far, late_beyond0, late_arrived0, 0, 2))
+    own_vec, other_vec = pack(
+        spots,
+        (bias_own_near, bias_own_far, own_a[2], own_b[2]),
+        (bias_other_near, bias_other_far, other_a[2], other_b[2]),
+        sums_one,
+        sums_two,
     )
     layer_out = mlp_out(
-        acts, downs_all, middle, gate(row_vec(down_bias), one_b, late_side1, late_low0)
-    )
-    late_arrived1 = after(swap(late_side1, XBIT), layer_out)
-    late_low1, late_keep1 = halves(
-        collected(own_near, late_own_far, late_beyond1, late_arrived1, 2, 4)
-    )
-    late_all = []
-    for low, keep in ((after(swap(late_low0, ZLOW), layer_out), late_keep0), (swap(late_low1, ZLOW), late_keep1)):
-        high, keep = quarters(total(keep, low))
-        have = total(keep, swap(high, ZHIGH))[None]
-        for bit in (ZHIGH, ZLOW, XBIT):
-            have = jnp.concatenate([have, swap(have, bit)])
-        late_all.append((have, swap(have, CORE)))
+        0, acts, downs_all, middle, gate(row_vec(down_bias), one_b, other_vec, *late_four0), []
+    )
+    late_arrived1, late_got0, vec_got, mark = together(
+        swap(after(late_side1, late_arrived0), XBIT), send_four(late_four0), across(other_vec), layer_out
+    )
+    late_one0 = total(late_four0[0], *late_got0)
+    late_four1 = four(collected(own_near, late_own_far, late_beyond1, late_arrived1, 2, 4))
+    vec = own_vec + vec_got
+    layer_out = mlp_out(
+        1, acts, downs_all, middle, gate(row_vec(down_bias), late_one0, vec, *late_four1), [mark]
+    )
+    late_got1, late_have0, vec_got, layer_out = together(
+        send_four(late_four1), send_four([late_one0] * 4), swap(vec, CORE), layer_out
+    )
+    late_one1 = total(late_four1[0], *late_got1)
+    late_have0 = jnp.stack([late_one0, *late_have0])
+    vec = vec + vec_got
     up_shape, down_shape = up_weight.shape, down_weight.shape
-    placed = gathered(0, 2, gathered_a, (up_shape, down_shape), [])
-    grad_up_weight, grad_down_weight = gathered(1, 2, gathered_b, (up_shape, down_shape), placed)
+    placed = gathered(
+        0, 2, gate(gathered_a, late_one1, late_have0, vec), (up_shape, down_shape), []
+    )
+    late_have1, late_side0, vec_got, *placed = together(
+        send_four([late_one1] * 4), swap(late_have0, XBIT), swap(vec, XBIT), *placed
+    )
+    late_have1 = jnp.stack([late_one1, *late_have1])
+    late_have0 = jnp.concatenate([late_have0, late_side0])
+    vec = vec + vec_got
+    placed = gathered(
+        1, 2, gate(gathered_b, late_have1, late_have0, vec), (up_shape, down_shape), placed
+    )
+    late_side1, late_far0, vec_got, grad_up_weight, grad_down_weight = together(
+        swap(late_have1, XBIT), swap(late_have0, CORE), send_four([vec] * 4), *placed
+    )
+    late_have1 = jnp.concatenate([late_have1, late_side1])
+    vec = ((vec + vec_got[0]) + (vec_got[1] + vec_got[2])).reshape(-1)
     grad_query_weight, grad_key_weight = place(
-        (True, True), 0, 1, place_spots, *late_all[0], (query_weight.shape,) * 2, []
+        (True, True), 0, 1, gate(place_spots, late_have1), late_have0, late_far0, (query_weight.shape,) * 2, []
+    )
+    late_far1, grad_query_weight, grad_key_weight = together(
+        swap(late_have1, CORE), grad_query_weight, grad_key_weight
     )
     grad_value_weight, grad_out_weight = place(
-        (True, False), 0, 1, place_spots, *late_all[1], (value_weight.shape, out_weight.shape), []
-    )
-
-    def back_to_place(near, far):
-        return jnp.concatenate([near, far]).reshape(4, -1)[jnp.arange(4) ^ part].reshape(-1)
-
-    def up_bias_grad(first, second):
-        sums = jnp.concatenate([first[2], second[2]]).reshape(4, 4, LANES).transpose(1, 0, 2)
-        return sums[jnp.arange(4) ^ part].reshape(-1)
-
-    def small(near, far, first, second):
-        return jnp.concatenate(
-            [
-                back_to_place(near[0, :256], far[0, :256]),
-                back_to_place(near[0, 512:], far[0, 512:]),
-                up_bias_grad(first, second),
-            ]
-        )
-
-    own_small = small(bias_own_near, bias_own_far, own_a, own_b)
-    other_small = small(bias_other_near, bias_other_far, other_a, other_b)
-    shared = jnp.concatenate([sums_one[0], sums_one[1], sums_two[2], sums_two[0], sums_two[1], sums_two[3]])
-    vec = jnp.concatenate([own_small, shared]) + across(jnp.concatenate([other_small, shared]))
-    for bit in (CORE, XBIT, ZLOW, ZHIGH):
-        vec = vec + swap(vec, bit)
+        (True, False), 0, 1, place_spots, late_have1, late_far1, (value_weight.shape, out_weight.shape), []
+    )
     grad_query_bias = vec[:heads_width]
     grad_value_bias = vec[heads_width : 2 * heads_width]
     grad_up_bias = vec[2 * heads_width : 2 * heads_width + hidden_width]

time: 566 us -> 488 us (0.86)
  waiting for transfers between devices: 139 us -> 70.8 us
  Pallas kernels: 296 us -> 264 us
  starting transfers between devices: 43.6 us -> 65.5 us
    ppermute x46 -> x51, waiting for transfers between devices: 138 us -> 70.7 us  [flip(): return lax.ppermute(value, axis, [(i, i ^ bit) for i in range(size)])]
    ppermute x46 -> x51, starting transfers between devices: 43.5 us -> 65.3 us  [flip(): return lax.ppermute(value, axis, [(i, i ^ bit) for i in range(size)])]
    pallas_call x4, Pallas kernels: 81.7 us -> 62.8 us  [attend_back(): pl.pallas_call(attend_back_kernel, grid_spec=pltpu.PrefetchScalarGridSpec...]
    pallas_call x3, Pallas kernels: 51.3 us -> 34.3 us  [attend(): pl.pallas_call(attend_kernel, grid_spec=pltpu.PrefetchScalarGridSpec(num_...]
    pallas_call x1 -> x3, Pallas kernels: 17 us -> 22.4 us  [the longest x2 20.2 us: mlp_out(): pl.pallas_call(functools.partial(mlp_out_kernel, half), grid=(tiles,), in...]
    convert_element_type x20 -> x17, other arithmetic: 31.9 us -> 30.1 us  [total(): return result.astype(LOW)]
  transfers between devices with their start and end apart: 50 -> 55, of which waited for: 24 -> 12; matrix products, arithmetic and copies ran while one was open for 9% -> 10% of each run, Pallas kernels for 48% -> 54%
where the time goes in v4:
time: 488 us; the launch traced here: 482 us
  Pallas kernels  264 us (54%)
  waiting for transfers between devices  70.8 us (15%)
  starting transfers between devices  65.5 us (13%)
  other arithmetic  41 us (8%)
  local copies, waits for them, and re-layouts  24.8 us (5%)
  between operations  14.9 us (3%)
    pallas_call x4, Pallas kernels, mlp(): pl.pallas_call(functools.partial(mlp_kernel, rows // 2, turned), grid_spe...  76.2 us
    ppermute x51, waiting for transfers between devices, flip(): return lax.ppermute(value, axis, [(i, i ^ bit) for i in range(size)])  70.7 us
    ppermute x51, starting transfers between devices, flip(): return lax.ppermute(value, axis, [(i, i ^ bit) for i in range(size)])  65.3 us
    pallas_call x4, Pallas kernels, attend_back(): pl.pallas_call(attend_back_kernel, grid_spec=pltpu.PrefetchScalarGridSpec...  62.8 us
    pallas_call x3, Pallas kernels, attend(): pl.pallas_call(attend_kernel, grid_spec=pltpu.PrefetchScalarGridSpec(num_...  34.3 us
    convert_element_type x17, other arithmetic, total(): return result.astype(LOW)  30.1 us
    pallas_call x1, Pallas kernels, mlp_back(): pl.pallas_call(mlp_back_kernel, grid=(tiles,), in_specs=[pl.BlockSpec((1,...  21.6 us
    pallas_call x2, Pallas kernels, mlp_out(): pl.pallas_call(functools.partial(mlp_out_kernel, half), grid=(tiles,), in...  20.2 us
  transfers between devices with their start and end apart: 55, of which 12 were waited for; matrix products, arithmetic and copies ran while one was open for 10% of the time, Pallas kernels for 54%

profile of v4, /device:TPU:0, one launch (start us, length us, event | category | flops | bytes accessed | tf_op | source)
XLA Modules:
  0.0 481.6 jit_solution(4250740170903053062)
XLA Ops:
  16.6 8.4 %collective-permute-done.2 = bf16[2,2,64,1024]{3,2,1,0:T(8,128)(2,1)S(1)} collective-permute-done((bf16[2,2,64,1024]{3,2,1,0:T(8,128)(2,1)S(1)}, bf16[2,2,64,1024]{3,2,1,0:T(8,128)(2,1)S(1)}, u32[]{:S(2)}, u32[]{:S(2)}) %collective-permute-start.2) | collective-permute-done | bytes 524320 | tf_op jit(solution)/shard_map/ppermute | solution.py:245
  31.4 16.3 %attend.3 = (bf16[4,4,280,768]{3,2,1,0:T(8,128)(2,1)}, bf16[4,4,280,256]{3,2,1,0:T(8,128)(2,1)}, bf16[4,1024,768]{2,1,0:T(8,128)(2,1)}) custom-call(s32[4]{0:T(128)} %pad_add_fusion.spot_ref, s32[4]{0:T(128)} %dynamic_slice.75.count_ref, bf16[4,280,1024]{2,1,0:T(8,128)(2,1)} %bitcast.171, bf16[1024,512]{1,0:T(8,128)(2,1)} %refs_1_.3, ...), custom_call_target="tpu_custom_call" | custom-call | tf_op jit(solution)/shard_map/attend/pallas_call | solution.py:320
  47.7 14.4 %collective-permute-done.1 = bf16[3072]{0:T(1024)(128)(2,1)S(1)} collective-permute-done((bf16[3072]{0:T(1024)(128)(2,1)S(1)}, bf16[3072]{0:T(1024)(128)(2,1)S(1)}, u32[]{:S(2)}, u32[]{:S(2)}) %collective-permute-start.1) | collective-permute-done | bytes 6176 | tf_op jit(solution)/shard_map/ppermute | solution.py:245
  67.7 9.2 %attend.4 = (bf16[4,4,280,768]{3,2,1,0:T(8,128)(2,1)}, bf16[4,4,280,256]{3,2,1,0:T(8,128)(2,1)}, bf16[4,1024,768]{2,1,0:T(8,128)(2,1)}) custom-call(s32[8]{0:T(128)} %concatenate.29.spot_ref, s32[4]{0:T(128)} %dynamic_slice.75.count_ref, bf16[4,280,1024]{2,1,0:T(8,128)(2,1)} %bitcast.172, ...), custom_call_target="tpu_custom_call", output_to_operand_aliasing={{0}: (13, {}), {1}: (14, {}), {2}: (15, {})} | custom-call | tf_op jit(solution)/shard_map/attend/pallas_call | solution.py:320
  81.9 8.8 %attend.5 = (bf16[4,4,280,768]{3,2,1,0:T(8,128)(2,1)}, bf16[4,4,280,256]{3,2,1,0:T(8,128)(2,1)}, bf16[4,1024,768]{2,1,0:T(8,128)(2,1)}) custom-call(s32[8]{0:T(128)} %concatenate.29.spot_ref, s32[4]{0:T(128)} %dynamic_slice.75.count_ref, bf16[4,280,1024]{2,1,0:T(8,128)(2,1)} %bitcast.173, ...), custom_call_target="tpu_custom_call", output_to_operand_aliasing={{0}: (13, {}), {1}: (14, {}), {2}: (15, {})} | custom-call | tf_op jit(solution)/shard_map/attend/pallas_call | solution.py:320
  91.4 9.3 %middle.1 = (f32[4,280,1024]{2,1,0:T(8,128)}, bf16[4,280,1024]{2,1,0:T(8,128)(2,1)}, bf16[4,256,1024]{2,1,0:T(8,128)(2,1)}) custom-call(s32[8]{0:T(128)} %concatenate.28.spot_ref, bf16[4,280,1024]{2,1,0:T(8,128)(2,1)} %bitcast.178, bf16[4,4,280,256]{3,2,1,0:T(8,128)(2,1)} %get-tuple-element.185.context_ref, bf16[512,1024]{1,0:T(8,128)(2,1)} %own_ref.1, ...), custom_call_target="tpu_custom_call" | custom-call | tf_op jit(solution)/shard_map/middle/pallas_call | solution.py:469
  100.7 19.0 %mlp.4 = (bf16[2,4,128,1024]{3,2,1,0:T(8,128)(2,1)}, bf16[2,4,128,1024]{3,2,1,0:T(8,128)(2,1)}, f32[2,1,512]{2,1,0:T(1,128)}, bf16[4,1120,1024]{2,1,0:T(8,128)(2...) custom-call(s32[4]{0:T(128)} %pad_add_fusion.spot_ref, ...), custom_call_target="tpu_custom_call" | custom-call | tf_op jit(solution)/shard_map/mlp/pallas_call | solution.py:535
  120.7 19.4 %mlp.5 = (bf16[2,4,128,1024]{3,2,1,0:T(8,128)(2,1)}, bf16[2,4,128,1024]{3,2,1,0:T(8,128)(2,1)}, f32[2,1,512]{2,1,0:T(1,128)}, bf16[4,1120,1024]{2,1,0:T(8,128)(2...) custom-call(s32[4]{0:T(128)} %pad_add_fusion.spot_ref, ...), custom_call_target="tpu_custom_call", output_to_operand_aliasing={{3}: (15, {}), {4}: (16, {}), {5}: (17, {}), {6}: (18, {})} | custom-call | tf_op jit(solution)/shard_map/mlp/pallas_call | solution.py:535
  143.6 18.8 %mlp.6 = (bf16[2,4,128,1024]{3,2,1,0:T(8,128)(2,1)}, bf16[2,4,128,1024]{3,2,1,0:T(8,128)(2,1)}, f32[2,1,512]{2,1,0:T(1,128)}, bf16[4,1120,1024]{2,1,0:T(8,128)(2...) custom-call(s32[4]{0:T(128)} %pad_add_fusion.spot_ref, ...), custom_call_target="tpu_custom_call", output_to_operand_aliasing={{3}: (15, {}), {4}: (16, {}), {5}: (17, {}), {6}: (18, {})} | custom-call | tf_op jit(solution)/shard_map/mlp/pallas_call | solution.py:535
  164.5 19.1 %mlp.7 = (bf16[2,4,128,1024]{3,2,1,0:T(8,128)(2,1)}, bf16[2,4,128,1024]{3,2,1,0:T(8,128)(2,1)}, f32[2,1,512]{2,1,0:T(1,128)}, bf16[4,1120,1024]{2,1,0:T(8,128)(2...) custom-call(s32[4]{0:T(128)} %pad_add_fusion.spot_ref, ...), custom_call_target="tpu_custom_call", output_to_operand_aliasing={{3}: (15, {}), {4}: (16, {}), {5}: (17, {}), {6}: (18, {})} | custom-call | tf_op jit(solution)/shard_map/mlp/pallas_call | solution.py:535
  190.6 21.6 %mlp_back.1 = (f32[1120,1024]{1,0:T(8,128)}, bf16[1120,1024]{1,0:T(8,128)(2,1)}, f32[8,1024]{1,0:T(8,128)}) custom-call(bf16[4,1120,1024]{2,1,0:T(8,128)(2,1)} %get-tuple-element.219.pre_ref, bf16[4,1024,1024]{2,1,0:T(8,128)(2,1)} %get-tuple-element.220.up_ref, f32[1120,1024]{1,0:T(8,128)} %bitcast.180, bf16[1120,1024]{1,0:T(8,128)(2,1)} %cot_hbm.1, ...), custom_call_target="tpu_custom_call" | custom-call | tf_op jit(solution)/shard_map/mlp_back/pallas_call | solution.py:628
  217.1 15.5 %attend_back.4 = (bf16[2,4,128,1024]{3,2,1,0:T(8,128)(2,1)}, f32[1,768]{1,0:T(1,128)}, bf16[4,4,280,768]{3,2,1,0:T(8,128)(2,1)}) custom-call(s32[4]{0:T(128)} %dynamic_slice.75.count_ref, bf16[1120,1024]{1,0:T(8,128)(2,1)} %fusion.5.rows_hbm, bf16[1120,1024]{1,0:T(8,128)(2,1)} %get-tuple-element.230.cots_hbm, bf16[4,280,1024]{2,1,0:T(8,128)(2,1)} %bitcast.174, ...), custom_call_target="tpu_custom_call" | custom-call | tf_op jit(solution)/shard_map/attend_back/pallas_call | solution.py:406
  232.6 6.4 %collective-permute-done.14 = bf16[2,2,128,1024]{3,2,1,0:T(8,128)(2,1)S(1)} collective-permute-done((bf16[2,2,128,1024]{3,2,1,0:T(8,128)(2,1)S(1)}, bf16[2,2,128,1024]{3,2,1,0:T(8,128)(2,1)S(1)}, u32[]{:S(2)}, u32[]{:S(2)}) %collective-permute-start.14) | collective-permute-done | bytes 1048608 | tf_op jit(solution)/shard_map/ppermute | solution.py:245
  247.1 15.7 %attend_back.5 = (bf16[2,4,128,1024]{3,2,1,0:T(8,128)(2,1)}, f32[1,768]{1,0:T(1,128)}, bf16[4,4,280,768]{3,2,1,0:T(8,128)(2,1)}) custom-call(s32[4]{0:T(128)} %dynamic_slice.75.count_ref, bf16[1120,1024]{1,0:T(8,128)(2,1)} %fusion.5.rows_hbm, bf16[1120,1024]{1,0:T(8,128)(2,1)} %get-tuple-element.230.cots_hbm, ...), custom_call_target="tpu_custom_call", output_to_operand_aliasing={{2}: (7, {})} | custom-call | tf_op jit(solution)/shard_map/attend_back/pallas_call | solution.py:406
  276.3 15.6 %attend_back.6 = (bf16[2,4,128,1024]{3,2,1,0:T(8,128)(2,1)}, f32[1,768]{1,0:T(1,128)}, bf16[4,4,280,768]{3,2,1,0:T(8,128)(2,1)}) custom-call(s32[4]{0:T(128)} %dynamic_slice.75.count_ref, bf16[1120,1024]{1,0:T(8,128)(2,1)} %fusion.5.rows_hbm, bf16[1120,1024]{1,0:T(8,128)(2,1)} %get-tuple-element.230.cots_hbm, ...), custom_call_target="tpu_custom_call", output_to_operand_aliasing={{2}: (7, {})} | custom-call | tf_op jit(solution)/shard_map/attend_back/pallas_call | solution.py:406
  302.0 16.0 %attend_back.7 = (bf16[2,4,128,1024]{3,2,1,0:T(8,128)(2,1)}, f32[1,768]{1,0:T(1,128)}, bf16[4,4,280,768]{3,2,1,0:T(8,128)(2,1)}) custom-call(s32[4]{0:T(128)} %dynamic_slice.75.count_ref, bf16[1120,1024]{1,0:T(8,128)(2,1)} %fusion.5.rows_hbm, bf16[1120,1024]{1,0:T(8,128)(2,1)} %get-tuple-element.230.cots_hbm, ...), custom_call_target="tpu_custom_call", output_to_operand_aliasing={{2}: (7, {})} | custom-call | tf_op jit(solution)/shard_map/attend_back/pallas_call | solution.py:406
  330.2 14.6 %input_grad.1 = (bf16[4,280,1024]{2,1,0:T(8,128)(2,1)}, f32[8,1024]{1,0:T(8,128)}) custom-call(bf16[4,4,280,768]{3,2,1,0:T(8,128)(2,1)} %get-tuple-element.264.grad_ref, bf16[4,1024,768]{2,1,0:T(8,128)(2,1)} %get-tuple-element.265.weight_ref, bf16[4,280,1024]{2,1,0:T(8,128)(2,1)} %bitcast.179, f32[4,280,1024]{2,1,0:T(8,128)} %bitcast.187, ...), custom_call_target="tpu_custom_call" | custom-call | tf_op jit(solution)/shard_map/input_grad/pallas_call | solution.py:761
  344.9 6.8 %collective-permute-done.26 = bf16[4,32,1024]{2,1,0:T(8,128)(2,1)S(1)} collective-permute-done((bf16[4,32,1024]{2,1,0:T(8,128)(2,1)S(1)}, bf16[4,32,1024]{2,1,0:T(8,128)(2,1)S(1)}, u32[]{:S(2)}, u32[]{:S(2)}) %collective-permute-start.26) | collective-permute-done | bytes 262176 | tf_op jit(solution)/shard_map/ppermute | solution.py:245
  368.1 10.0 %mlp_out.2.refs_0_ = bf16[1120,1024]{1,0:T(8,128)(2,1)} custom-call(bf16[4,1120,1024]{2,1,0:T(8,128)(2,1)} %get-tuple-element.274.act_ref, bf16[4,1024,1024]{2,1,0:T(8,128)(2,1)} %get-tuple-element.275.down_ref, f32[1120,1024]{1,0:T(8,128)} %bitcast.181, bf16[1,1024]{1,0:T(2,128)(2,1)} %reshape.251.bias_ref), custom_call_target="tpu_custom_call" | custom-call | tf_op jit(solution)/shard_map/mlp_out/pallas_call | solution.py:681
  388.7 8.2 %collective-permute-done.33 = bf16[2,32,1024]{2,1,0:T(8,128)(2,1)S(1)} collective-permute-done((bf16[2,32,1024]{2,1,0:T(8,128)(2,1)S(1)}, bf16[2,32,1024]{2,1,0:T(8,128)(2,1)S(1)}, u32[]{:S(2)}, u32[]{:S(2)}) %collective-permute-start.33) | collective-permute-done | bytes 131104 | tf_op jit(solution)/shard_map/ppermute | solution.py:245
  399.0 10.2 %mlp_out.3 = bf16[1120,1024]{1,0:T(8,128)(2,1)} custom-call(bf16[4,1120,1024]{2,1,0:T(8,128)(2,1)} %get-tuple-element.274.act_ref, bf16[4,1024,1024]{2,1,0:T(8,128)(2,1)} %get-tuple-element.275.down_ref, f32[1120,1024]{1,0:T(8,128)} %bitcast.182, bf16[1,1024]{1,0:T(2,128)(2,1)} %reshape.251.bias_ref, ...), custom_call_target="tpu_custom_call", output_to_operand_aliasing={{}: (4, {})} | custom-call | tf_op jit(solution)/shard_map/mlp_out/pallas_call | solution.py:681
  414.4 8.2 %collective-permute-start.40 = (bf16[2,32,1024]{2,1,0:T(8,128)(2,1)}, bf16[2,32,1024]{2,1,0:T(8,128)(2,1)S(1)}, u32[]{:S(2)}, u32[]{:S(2)}) collective-permute-start(bf16[2,32,1024]{2,1,0:T(8,128)(2,1)} %get-tuple-element.324), channel_id=1, source_target_pairs={{0,16},{2,18},{4,20},{6,22},{8,24},{10,26},{12,28},{14,30},{16,0},... | collective-permute-start | bytes 393224 | tf_op jit(solution)/shard_map/ppermute | solution.py:245
  444.7 6.2 %gathered.3 = (f32[1024,2048]{1,0:T(8,128)}, f32[2048,1024]{1,0:T(8,128)}) custom-call(bf16[2,2,2,2,4,32,1024]{6,5,4,3,2,1,0:T(8,128)(2,1)} %bitcast.188, f32[1024,2048]{1,0:T(8,128)} %get-tuple-element.304.refs_0_, f32[2048,1024]{1,0:T(8,128)} %get-tuple-element.305.refs_1_), custom_call_target="tpu_custom_call", output_to_operand_aliasing={{0}: (1, {}), {1}: (2, {})} | custom-call | tf_op jit(solution)/shard_map/gathered/pallas_call | solution.py:838
  451.0 7.1 %collective-permute-done.45 = bf16[4,2,32,1024]{3,2,1,0:T(8,128)(2,1)} collective-permute-done((bf16[4,2,32,1024]{3,2,1,0:T(8,128)(2,1)}, bf16[4,2,32,1024]{3,2,1,0:T(8,128)(2,1)}, u32[]{:S(2)}, u32[]{:S(2)}) %collective-permute-start.45) | collective-permute-done | bytes 524320 | tf_op jit(solution)/shard_map/ppermute | solution.py:245
  (277 shorter events, 161.9 us)
Async XLA Ops:
  7.2 93.5 %all-gather.7.cloned.1.call-start = ((), (), s32[]{:S(2)}) async-start(), calls=%async_computation | async-start | bytes 4456448 | tf_op jit(solution)/shard_map/all_gather | solution.py:954
  25.9 138.6 %all-gather.9.cloned.1.call-start = ((), (), s32[]{:S(2)}) async-start(), calls=%async_computation.1 | async-start | bytes 4456448 | tf_op jit(solution)/shard_map/all_gather | solution.py:954
  26.3 35.8 %collective-permute-start = (bf16[3,1024,256]{2,1,0:T(8,128)(2,1)S(1)}, bf16[3,1024,256]{2,1,0:T(8,128)(2,1)S(1)}, u32[]{:S(2)}, u32[]{:S(2)}) collective-permute-start(bf16[3,1024,256]{2,1,0:T(8,128)(2,1)S(1)} %pad_maximum_fusion), channel_id=1, source_target_pairs={{0,1},{1,0},{2,3},{3,2},{4,5},{5,4},{6,7},{7,6},{8,9},{9,8},{10,11... | collective-permute-start | bytes 4718600 | tf_op jit(solution)/shard_map/ppermute | solution.py:245
  28.6 33.6 %collective-permute-start.1 = (bf16[3072]{0:T(1024)(128)(2,1)S(1)}, bf16[3072]{0:T(1024)(128)(2,1)S(1)}, u32[]{:S(2)}, u32[]{:S(2)}) collective-permute-start(bf16[3072]{0:T(1024)(128)(2,1)S(1)} %constant_dynamic-update-slice_fusion.12), channel_id=1, source_target_pairs={{0,1},{1,0},{2,3},{3,2},{4,5},{5,4},{6,7},{7,6},{8,9},{9,8},{10,11... | collective-permute-start | bytes 18440 | tf_op jit(solution)/shard_map/ppermute | solution.py:245
  62.2 365.8 %all-gather.11.cloned.1.call-start = ((), (), s32[]{:S(2)}) async-start(), calls=%async_computation.2 | async-start | bytes 4456448 | tf_op jit(solution)/shard_map/all_gather | solution.py:1101
  140.1 22.3 %collective-permute-start.8 = (bf16[2,4,128,1024]{3,2,1,0:T(8,128)(2,1)}, bf16[2,4,128,1024]{3,2,1,0:T(8,128)(2,1)S(1)}, u32[]{:S(2)}, u32[]{:S(2)}) collective-permute-start(bf16[2,4,128,1024]{3,2,1,0:T(8,128)(2,1)} %get-tuple-element.197), channel_id=1, source_target_pairs={{0,2},{2,0},{4,6},{6,4},{8,10},{10,8},{12,14},{14,12},{16,18},{18,... | collective-permute-start | bytes 6291464 | tf_op jit(solution)/shard_map/ppermute | solution.py:245
  183.6 28.6 %collective-permute-start.13 = (bf16[2,4,128,1024]{3,2,1,0:T(8,128)(2,1)}, bf16[2,4,128,1024]{3,2,1,0:T(8,128)(2,1)S(1)}, u32[]{:S(2)}, u32[]{:S(2)}) collective-permute-start(bf16[2,4,128,1024]{3,2,1,0:T(8,128)(2,1)} %get-tuple-element.218), channel_id=1, source_target_pairs={{0,2},{2,0},{4,6},{6,4},{8,10},{10,8},{12,14},{14,12},{16,18},{18,... | collective-permute-start | bytes 6291464 | tf_op jit(solution)/shard_map/ppermute | solution.py:245
  185.0 27.2 %collective-permute-start.11 = (bf16[2,2,128,1024]{3,2,1,0:T(8,128)(2,1)S(1)}, bf16[2,2,128,1024]{3,2,1,0:T(8,128)(2,1)}, u32[]{:S(2)}, u32[]{:S(2)}) collective-permute-start(bf16[2,2,128,1024]{3,2,1,0:T(8,128)(2,1)S(1)} %add_convert_fusion.4), channel_id=1, source_target_pairs={{0,1},{1,0},{2,3},{3,2},{4,5},{5,4},{6,7},{7,6},{8,9},{9,8},{10,11... | collective-permute-start | bytes 3145736 | tf_op jit(solution)/shard_map/ppermute | solution.py:245
  189.0 23.2 %collective-permute-start.12 = (bf16[2,128,1024]{2,1,0:T(8,128)(2,1)S(1)}, bf16[2,128,1024]{2,1,0:T(8,128)(2,1)S(1)}, u32[]{:S(2)}, u32[]{:S(2)}) collective-permute-start(bf16[2,128,1024]{2,1,0:T(8,128)(2,1)S(1)} %fusion.14), channel_id=1, source_target_pairs={{0,4},{2,6},{4,0},{6,2},{8,12},{10,14},{12,8},{14,10},{16,20},{18,... | collective-permute-start | bytes 1572872 | tf_op jit(solution)/shard_map/ppermute | solution.py:245
  214.2 24.7 %collective-permute-start.14 = (bf16[2,2,128,1024]{3,2,1,0:T(8,128)(2,1)S(1)}, bf16[2,2,128,1024]{3,2,1,0:T(8,128)(2,1)S(1)}, u32[]{:S(2)}, u32[]{:S(2)}) collective-permute-start(bf16[2,2,128,1024]{3,2,1,0:T(8,128)(2,1)S(1)} %get-tuple-element.335), channel_id=1, source_target_pairs={{0,1},{1,0},{2,3},{3,2},{4,5},{5,4},{6,7},{7,6},{8,9},{9,8},{10,11... | collective-permute-start | bytes 3145736 | tf_op jit(solution)/shard_map/ppermute | solution.py:245
  240.0 25.8 %collective-permute-start.19 = (bf16[2,4,128,1024]{3,2,1,0:T(8,128)(2,1)}, bf16[2,4,128,1024]{3,2,1,0:T(8,128)(2,1)S(1)}, u32[]{:S(2)}, u32[]{:S(2)}) collective-permute-start(bf16[2,4,128,1024]{3,2,1,0:T(8,128)(2,1)} %get-tuple-element.239), channel_id=1, source_target_pairs={{0,2},{2,0},{4,6},{6,4},{8,10},{10,8},{12,14},{14,12},{16,18},{18,... | collective-permute-start | bytes 6291464 | tf_op jit(solution)/shard_map/ppermute | solution.py:245
  240.0 25.8 %collective-permute-start.16 = (bf16[2,2,128,1024]{3,2,1,0:T(8,128)(2,1)}, bf16[2,2,128,1024]{3,2,1,0:T(8,128)(2,1)S(1)}, u32[]{:S(2)}, u32[]{:S(2)}) collective-permute-start(bf16[2,2,128,1024]{3,2,1,0:T(8,128)(2,1)} %get-tuple-element.237), channel_id=1, source_target_pairs={{0,1},{1,0},{2,3},{3,2},{4,5},{5,4},{6,7},{7,6},{8,9},{9,8},{10,11... | collective-permute-start | bytes 3145736 | tf_op jit(solution)/shard_map/ppermute | solution.py:245
  270.0 25.1 %collective-permute-start.20 = (bf16[2,2,128,1024]{3,2,1,0:T(8,128)(2,1)}, bf16[2,2,128,1024]{3,2,1,0:T(8,128)(2,1)}, u32[]{:S(2)}, u32[]{:S(2)}) collective-permute-start(bf16[2,2,128,1024]{3,2,1,0:T(8,128)(2,1)} %get-tuple-element.331), channel_id=1, source_target_pairs={{0,1},{1,0},{2,3},{3,2},{4,5},{5,4},{6,7},{7,6},{8,9},{9,8},{10,11... | collective-permute-start | bytes 3145736 | tf_op jit(solution)/shard_map/ppermute | solution.py:245
  296.8 147.9 %all-gather.13.cloned.1.call-start = ((), (), s32[]{:S(2)}) async-start(), calls=%async_computation.3 | async-start | bytes 4456448 | tf_op jit(solution)/shard_map/all_gather | solution.py:1118
  296.9 25.9 %collective-permute-start.24 = (bf16[2,4,128,1024]{3,2,1,0:T(8,128)(2,1)}, bf16[2,4,128,1024]{3,2,1,0:T(8,128)(2,1)S(1)}, u32[]{:S(2)}, u32[]{:S(2)}) collective-permute-start(bf16[2,4,128,1024]{3,2,1,0:T(8,128)(2,1)} %get-tuple-element.259), channel_id=1, source_target_pairs={{0,2},{2,0},{4,6},{6,4},{8,10},{10,8},{12,14},{14,12},{16,18},{18,... | collective-permute-start | bytes 6291464 | tf_op jit(solution)/shard_map/ppermute | solution.py:245
  296.9 25.8 %collective-permute-start.23 = (bf16[2,2,128,1024]{3,2,1,0:T(8,128)(2,1)}, bf16[2,2,128,1024]{3,2,1,0:T(8,128)(2,1)S(1)}, u32[]{:S(2)}, u32[]{:S(2)}) collective-permute-start(bf16[2,2,128,1024]{3,2,1,0:T(8,128)(2,1)} %get-tuple-element.258), channel_id=1, source_target_pairs={{0,1},{1,0},{2,3},{3,2},{4,5},{5,4},{6,7},{7,6},{8,9},{9,8},{10,11... | collective-permute-start | bytes 3145736 | tf_op jit(solution)/shard_map/ppermute | solution.py:245
  300.4 22.4 %collective-permute-start.25 = (bf16[4,64,1024]{2,1,0:T(8,128)(2,1)S(1)}, bf16[4,64,1024]{2,1,0:T(8,128)(2,1)S(1)}, u32[]{:S(2)}, u32[]{:S(2)}) collective-permute-start(bf16[4,64,1024]{2,1,0:T(8,128)(2,1)S(1)} %dynamic-slice_bitcast_fusion), channel_id=1, source_target_pairs={{0,8},{2,10},{4,12},{6,14},{8,0},{10,2},{12,4},{14,6},{16,24},{18,... | collective-permute-start | bytes 1572872 | tf_op jit(solution)/shard_map/ppermute | solution.py:245
  326.3 25.4 %collective-permute-start.27 = (bf16[2,128,1024]{2,1,0:T(8,128)(2,1)S(1)}, bf16[2,128,1024]{2,1,0:T(8,128)(2,1)}, u32[]{:S(2)}, u32[]{:S(2)}) collective-permute-start(bf16[2,128,1024]{2,1,0:T(8,128)(2,1)S(1)} %get-tuple-element.327), channel_id=1, source_target_pairs={{0,4},{2,6},{4,0},{6,2},{8,12},{10,14},{12,8},{14,10},{16,20},{18,... | collective-permute-start | bytes 1572872 | tf_op jit(solution)/shard_map/ppermute | solution.py:245
  327.0 24.7 %collective-permute-start.26 = (bf16[4,32,1024]{2,1,0:T(8,128)(2,1)S(1)}, bf16[4,32,1024]{2,1,0:T(8,128)(2,1)S(1)}, u32[]{:S(2)}, u32[]{:S(2)}) collective-permute-start(bf16[4,32,1024]{2,1,0:T(8,128)(2,1)S(1)} %dynamic-slice_bitcast_fusion.5), channel_id=1, source_target_pairs={{0,16},{2,18},{4,20},{6,22},{8,24},{10,26},{12,28},{14,30},{16,0},... | collective-permute-start | bytes 786440 | tf_op jit(solution)/shard_map/ppermute | solution.py:245
  352.5 25.6 %collective-permute-start.28 = (bf16[2,128,1024]{2,1,0:T(8,128)(2,1)}, bf16[2,128,1024]{2,1,0:T(8,128)(2,1)S(1)}, u32[]{:S(2)}, u32[]{:S(2)}) collective-permute-start(bf16[2,128,1024]{2,1,0:T(8,128)(2,1)} %get-tuple-element.270), channel_id=1, source_target_pairs={{0,4},{2,6},{4,0},{6,2},{8,12},{10,14},{12,8},{14,10},{16,20},{18,... | collective-permute-start | bytes 1572872 | tf_op jit(solution)/shard_map/ppermute | solution.py:245
  381.2 28.0 %collective-permute-start.34 = (bf16[2,32,1024]{2,1,0:T(8,128)(2,1)S(1)}, bf16[2,32,1024]{2,1,0:T(8,128)(2,1)S(1)}, u32[]{:S(2)}, u32[]{:S(2)}) collective-permute-start(bf16[2,32,1024]{2,1,0:T(8,128)(2,1)S(1)} %get-tuple-element.345), channel_id=1, source_target_pairs={{0,8},{2,10},{4,12},{6,14},{8,0},{10,2},{12,4},{14,6},{16,24},{18,... | collective-permute-start | bytes 393224 | tf_op jit(solution)/shard_map/ppermute | solution.py:245
  384.1 25.1 %collective-permute-start.35 = (bf16[2,32,1024]{2,1,0:T(8,128)(2,1)S(1)}, bf16[2,32,1024]{2,1,0:T(8,128)(2,1)S(1)}, u32[]{:S(2)}, u32[]{:S(2)}) collective-permute-start(bf16[2,32,1024]{2,1,0:T(8,128)(2,1)S(1)} %get-tuple-element.344), channel_id=1, source_target_pairs={{0,24},{2,26},{4,28},{6,30},{8,16},{10,18},{12,20},{14,22},{16,8},... | collective-permute-start | bytes 393224 | tf_op jit(solution)/shard_map/ppermute | solution.py:245
  384.3 29.4 %collective-permute-start.36 = (bf16[2,32,1024]{2,1,0:T(8,128)(2,1)S(1)}, bf16[2,32,1024]{2,1,0:T(8,128)(2,1)S(1)}, u32[]{:S(2)}, u32[]{:S(2)}) collective-permute-start(bf16[2,32,1024]{2,1,0:T(8,128)(2,1)S(1)} %get-tuple-element.326), channel_id=1, source_target_pairs={{0,16},{2,18},{4,20},{6,22},{8,24},{10,26},{12,28},{14,30},{16,0},... | collective-permute-start | bytes 393224 | tf_op jit(solution)/shard_map/ppermute | solution.py:245
  385.8 27.8 %collective-permute-start.37 = (bf16[2,32,1024]{2,1,0:T(8,128)(2,1)S(1)}, bf16[2,32,1024]{2,1,0:T(8,128)(2,1)S(1)}, u32[]{:S(2)}, u32[]{:S(2)}) collective-permute-start(bf16[2,32,1024]{2,1,0:T(8,128)(2,1)S(1)} %get-tuple-element.326), channel_id=1, source_target_pairs={{0,8},{2,10},{4,12},{6,14},{8,0},{10,2},{12,4},{14,6},{16,24},{18,... | collective-permute-start | bytes 393224 | tf_op jit(solution)/shard_map/ppermute | solution.py:245
  (71 other events, 796.9 us)
Sparse Core Ops, SparseCore 0:
  26.0 52.1 all-gather.6
  80.4 49.2 all-gather.8
  296.9 69.9 all-gather.10
  369.5 63.8 all-gather.12

commit v5 on v4

--- a/solution.py
+++ b/solution.py
@@ -384,7 +384,7 @@
             pair_of = [heads[2 * tile + side][i] for side in range(2)]
             grads[i].append((jnp.where(lane_low, *pair_of) * scale).astype(LOW))
     joined = jnp.concatenate(grads[0] + grads[1] + grads[2], 1)
-    qkv_grad_ref[0, 0] = joined
+    qkv_grad_ref[0] = joined
     grad_buf[at, :] = joined.astype(WIDE)
 
     @pl.when(pair == pl.num_programs(0) - 1)
@@ -399,7 +399,7 @@
         bias_ref[...] = jnp.sum(grad_buf[...], 0, keepdims=True)
 
 
-def attend_back(slot, counts, rows, cot, kept, outs, buffers):
+def attend_back(slot, counts, rows, cot, kept, outs):
     qkv, context, _ = kept
     _, pairs, seq, _ = qkv.shape
     width = rows.shape[1]
@@ -415,12 +415,11 @@
                 pl.BlockSpec((1, 1, seq, 768), lambda p, *_: (slot, p, 0, 0)),
                 pl.BlockSpec((1, 1, seq, 256), lambda p, *_: (slot, p, 0, 0)),
                 pl.BlockSpec((1, 256, width), lambda p, *_: (slot, 0, 0)),
-            ]
-            + [ANYWHERE] * len(buffers),
+            ],
             out_specs=[
                 pl.BlockSpec((2, 4, LANES, width), lambda p, *_: (0, 0, 0, 0)),
                 pl.BlockSpec((1, 768), lambda p, *_: (0, 0)),
-                pl.BlockSpec((1, 1, seq, 768), lambda p, *_: (slot, p, 0, 0)),
+                pl.BlockSpec((1, seq, 768), lambda p, *_: (p, 0, 0)),
             ],
             scratch_shapes=[
                 pltpu.VMEM((pairs * seq, 768), WIDE),
@@ -433,12 +432,11 @@
         out_shape=[
             jax.ShapeDtypeStruct((2, 4, LANES, width), LOW),
             jax.ShapeDtypeStruct((1, 768), WIDE),
-            jax.ShapeDtypeStruct(qkv.shape, LOW),
+            jax.ShapeDtypeStruct(qkv.shape[1:], LOW),
         ],
-        input_output_aliases={7: 2} if buffers else {},
         name="attend_back",
         compiler_params=pltpu.CompilerParams(vmem_limit_bytes=56 * 1024 * 1024),
-    )(counts, rows, cot, cot.reshape(pairs, seq, width), qkv, context, outs, *buffers)
+    )(counts, rows, cot, cot.reshape(pairs, seq, width), qkv, context, outs)
 
 
 def middle_kernel(
@@ -537,7 +535,7 @@
         grid_spec=pltpu.PrefetchScalarGridSpec(
             num_scalar_prefetch=1,
             grid=(2,),
-            in_specs=[resident(hidden.shape), resident(cot.shape)]
+            in_specs=[pl.BlockSpec(memory_space=pltpu.VMEM)] * 2
             + [spec for _, spec in operands]
             + [ANYWHERE] * len(buffers),
             out_specs=[grad_block] * 2
@@ -560,7 +558,7 @@
         ],
         input_output_aliases={3 + len(operands) + i: 3 + i for i in range(len(buffers))},
         name="mlp",
-        compiler_params=pltpu.CompilerParams(vmem_limit_bytes=56 * 1024 * 1024),
+        compiler_params=pltpu.CompilerParams(vmem_limit_bytes=36 * 1024 * 1024),
     )(spots, hidden, cot, *[array for array, _ in operands], *buffers)
 
 
@@ -648,7 +646,7 @@
             pltpu.SemaphoreType.DMA((2,)),
         ],
         name="mlp_back",
-        compiler_params=pltpu.CompilerParams(vmem_limit_bytes=56 * 1024 * 1024),
+        compiler_params=pltpu.CompilerParams(vmem_limit_bytes=44 * 1024 * 1024),
     )(pre_grads, ups, middle, cot, gain)
 
 
@@ -734,14 +732,14 @@
         ),
         out_shape=[jax.ShapeDtypeStruct((72, LANES), WIDE)] * 2,
         name="pack",
-        compiler_params=pltpu.CompilerParams(vmem_limit_bytes=56 * 1024 * 1024),
+        compiler_params=pltpu.CompilerParams(vmem_limit_bytes=8 * 1024 * 1024),
     )(spots, *own, *other, sums_one, sums_two)
 
 
-def input_kernel(grad_ref, weight_ref, rows_ref, above_ref, gain_ref, out_ref, sums_ref):
-    pulled_sum = dot(grad_ref[0, 0], weight_ref[0], 1, 1)
-    for i in range(1, 4):
-        pulled_sum = pulled_sum + dot(grad_ref[i, 0], weight_ref[i], 1, 1)
+def input_kernel(zero_ref, one_ref, two_ref, three_ref, weight_ref, rows_ref, above_ref, gain_ref, out_ref, sums_ref):
+    pulled_sum = dot(zero_ref[0], weight_ref[0], 1, 1)
+    for i, grad_ref in enumerate((one_ref, two_ref, three_ref)):
+        pulled_sum = pulled_sum + dot(grad_ref[0], weight_ref[i + 1], 1, 1)
     pulled, gain_grad, shift_grad = norm_back(
         rows_ref[0].astype(WIDE), gain_ref[...].astype(WIDE), pulled_sum
     )
@@ -762,7 +760,10 @@
         input_kernel,
         grid=(pairs,),
         in_specs=[
-            pl.BlockSpec((4, 1, seq, 768), lambda p: (0, p, 0, 0)),
+            pl.BlockSpec((1, seq, 768), lambda p: (p, 0, 0)),
+            pl.BlockSpec((1, seq, 768), lambda p: (p, 0, 0)),
+            pl.BlockSpec((1, seq, 768), lambda p: (p, 0, 0)),
+            pl.BlockSpec((1, seq, 768), lambda p: (p, 0, 0)),
             resident(weights.shape),
             block(),
             block(),
@@ -774,8 +775,8 @@
             jax.ShapeDtypeStruct((8, width), WIDE),
         ],
         name="input_grad",
-        compiler_params=pltpu.CompilerParams(vmem_limit_bytes=56 * 1024 * 1024),
-    )(grads, weights, rows, above, gain)
+        compiler_params=pltpu.CompilerParams(vmem_limit_bytes=28 * 1024 * 1024),
+    )(*grads, weights, rows, above, gain)
 
 
 def place_kernel(turned, spot_ref, near_ref, far_ref, *refs):
@@ -814,7 +815,7 @@
         out_shape=[jax.ShapeDtypeStruct(shape, WIDE) for shape in shapes],
         input_output_aliases={3 + i: i for i in range(len(buffers))},
         name="place",
-        compiler_params=pltpu.CompilerParams(vmem_limit_bytes=56 * 1024 * 1024),
+        compiler_params=pltpu.CompilerParams(vmem_limit_bytes=20 * 1024 * 1024),
     )(spots, near, far, *buffers)
 
 
@@ -849,7 +850,7 @@
         out_shape=[jax.ShapeDtypeStruct(shape, WIDE) for shape in shapes],
         input_output_aliases={1 + i: i for i in range(len(buffers))},
         name="gathered",
-        compiler_params=pltpu.CompilerParams(vmem_limit_bytes=56 * 1024 * 1024),
+        compiler_params=pltpu.CompilerParams(vmem_limit_bytes=24 * 1024 * 1024),
     )(source, *buffers)
 
 
@@ -911,12 +912,10 @@
         ]
     )
     slices = across(slices)
-    sent_qkv = jnp.stack(
-        [pick(w, core_id, heads_width // 2, 1) for w in (query_weight, key_weight, value_weight)]
-    )
-    sent_bias = jnp.concatenate([query_bias, value_bias, up_bias])
-    near_qkv = across(sent_qkv)
-    bias_other = across(sent_bias)
+    sent_qk = jnp.stack([pick(w, core_id, heads_width // 2, 1) for w in (query_weight, key_weight)])
+    value_near = across(pick(value_weight, part, LANES, 1))
+    sent_bias = row_vec(jnp.concatenate([query_bias, value_bias, up_bias]))
+    raw_out = pick(out_weight, core_id, heads_width // 2, 0)
     rows_in = layer_in.astype(WIDE)
     normed = layer_norm(
         rows_in, attn_gain.astype(WIDE), attn_shift.astype(WIDE)
@@ -936,39 +935,43 @@
         ]
         return weights, biases
 
-    def other_inputs(group, qkv):
+    def other_inputs(group, qk, values):
         weights = [
-            (qkv, pl.BlockSpec((None, width, LANES), lambda g, p, side, count, k=k, i=i: (k, 0, side[i])))
-            for k in range(3)
+            (qk, pl.BlockSpec((None, width, LANES), lambda g, p, side, count, k=k, i=i: (k, 0, side[i])))
+            for k in range(2)
             for i in range(2)
         ]
+        weights += [(item, pl.BlockSpec((width, LANES), lambda g, p, *_: (0, 0))) for item in values]
         biases = [
-            (b, pl.BlockSpec((1, LANES), lambda g, p, side, count, i=i: (0, side[4 + 2 * group + i])))
-            for b in (query_bias_other, value_bias_other)
+            (bias_other, pl.BlockSpec((1, LANES), lambda g, p, side, count, k=k, i=i: (0, 4 * k + side[4 + 2 * group + i])))
+            for k in range(2)
             for i in range(2)
         ]
         return weights, biases
 
     other_spots = jnp.concatenate([sides, spots])
-    slices = after(slices, normed)
+    slices, value_near, sent_qk, raw_out, sent_bias, normed, spots, other_spots, counts = lax.optimization_barrier(
+        (slices, value_near, sent_qk, raw_out, sent_bias, normed, spots, other_spots, counts)
+    )
+    normed_three = normed.reshape(shape_three)
+    near_qk = across(sent_qk)
+    bias_other = across(sent_bias)
+    value_side = swap(value_near, XBIT)
     gathered_weights = [lax.all_gather(slices[0], "dp"), lax.all_gather(slices[1], "dp")]
     kept = attend(
-        0, 2, gate(spots, sent_qkv, sent_bias, slices), counts, normed_three, *own_inputs(), []
-    )
-    near_qkv, bias_other, _ = lax.optimization_barrier((near_qkv, bias_other, kept[1]))
-    query_bias_other = row_vec(bias_other[:heads_width])
-    value_bias_other = row_vec(bias_other[heads_width : 2 * heads_width])
-    up_bias_other = row_vec(bias_other[2 * heads_width :])
-    sent_out = after(pick(out_weight, core_id, heads_width // 2, 0), near_qkv)
+        0, 2, spots, counts, normed_three, *own_inputs(), []
+    )
+    near_qk, bias_other, value_side, _ = lax.optimization_barrier((near_qk, bias_other, value_side, kept[1]))
+    sent_out = after(raw_out, near_qk)
     near_out = across(sent_out)
-    far_qkv = swap(near_qkv, CORE)
+    far_qk, far_values = swap(near_qk, CORE), [swap(value_near, CORE), swap(value_side, CORE)]
     kept = attend(
-        2, 1, gate(other_spots, sent_out), counts, normed_three, *other_inputs(0, near_qkv), kept
-    )
-    near_out, far_qkv, _ = lax.optimization_barrier((near_out, far_qkv, kept[1]))
+        2, 1, gate(other_spots, sent_out), counts, normed_three, *other_inputs(0, near_qk, (value_near, value_side)), kept
+    )
+    near_out, far_qk, far_values, _ = lax.optimization_barrier((near_out, far_qk, far_values, kept[1]))
     far_out = swap(near_out, CORE)
     kept = attend(
-        3, 1, gate(other_spots, near_out), counts, normed_three, *other_inputs(1, far_qkv), kept
+        3, 1, gate(other_spots, near_out), counts, normed_three, *other_inputs(1, far_qk, far_values), kept
     )
     middle, hidden, outs_all = middle_step(
         jnp.concatenate([spots, sides]),
@@ -1009,7 +1012,7 @@
             for k in range(2)
         )
         biases = [
-            (up_bias_other, pl.BlockSpec((1, LANES), lambda j, spot, r=r: (0, spot[r] * subs + first + j)))
+            (bias_other, pl.BlockSpec((1, LANES), lambda j, spot, r=r: (0, 8 + spot[r] * subs + first + j)))
             for r in range(4)
         ]
         return ups, downs, biases
@@ -1033,8 +1036,8 @@
     def quarters(item):
         return cut(item, zhigh_id ^ 1), cut(item, zhigh_id)
 
-    back = lambda slot, wait, qkv_grads: attend_back(
-        slot, gate(counts, *wait), normed, attn_grad, kept, outs_all, qkv_grads
+    back = lambda slot, *wait: attend_back(
+        slot, gate(counts, *wait), normed, attn_grad, kept, outs_all
     )
 
     together = lambda *items: lax.optimization_barrier(items)
@@ -1065,7 +1068,7 @@
     )
     side_a23 = sideways(own_a[0], far_own_a, beyond_a23, 2, 4)
     out_b = [outbound(other_b[0], far_other_b, *span) for span in ((0, 2), (2, 4))]
-    other_far, bias_other_far, qkv_grads = back(3, (side_a23, arrived_a01, *out_b), [])
+    other_far, bias_other_far, grads_three = back(3, side_a23, arrived_a01, *out_b)
     beyond_b01, arrived_a23, far, _ = together(
         across(out_b[0]), swap(side_a23, XBIT), other_far, bias_other_far
     )
@@ -1078,14 +1081,14 @@
     )
     low_a, keep_a = halves(sum_a)
     side_b01 = sideways(own_b[0], far_own_b, beyond_b01, 0, 2)
-    other_near, bias_other_near, qkv_grads = back(2, (low_a, sum_a, side_b01), [qkv_grads])
+    other_near, bias_other_near, grads_two = back(2, low_a, sum_a, side_b01, grads_three)
     beyond_b23, arrived_b01, low_a, late_other_far, _ = together(
         across(after(out_b[1], beyond_b01)), swap(side_b01, XBIT), swap(low_a, ZLOW), late_other_far, bias_other_near
     )
     high_a, keep_a = quarters(total(keep_a, low_a))
     side_b23 = sideways(own_b[0], far_own_b, beyond_b23, 2, 4)
     late_out = [outbound(other_near, late_other_far, *span) for span in ((0, 2), (2, 4))]
-    own_far, bias_own_far, qkv_grads = back(1, (high_a, side_b23, arrived_b01, *late_out), [qkv_grads])
+    own_far, bias_own_far, grads_one = back(1, high_a, side_b23, arrived_b01, *late_out, grads_two)
     late_beyond0, arrived_b23, high_a, far, _ = together(
         across(late_out[0]), swap(side_b23, XBIT), swap(high_a, ZHIGH), own_far, bias_own_far
     )
@@ -1099,7 +1102,7 @@
     )
     low_b, keep_b = halves(sum_b)
     gathered_a = lax.all_gather(one_a, "dp")
-    own_near, bias_own_near, qkv_grads = back(0, (one_a, low_b, sum_b, late_beyond0), [qkv_grads])
+    own_near, bias_own_near, grads_zero = back(0, one_a, low_b, sum_b, late_beyond0, grads_one)
     late_beyond1, late_own_far, low_b, _ = together(
         across(after(late_out[1], late_beyond0)), late_own_far, swap(low_b, ZLOW), bias_own_near
     )
@@ -1107,7 +1110,7 @@
     late_side0 = sideways(own_near, late_own_far, late_beyond0, 0, 2)
     late_side1 = sideways(own_near, late_own_far, late_beyond1, 2, 4)
     grad_in, sums_one = input_step(
-        qkv_grads,
+        (grads_zero, grads_one, grads_two, grads_three),
         kept[2],
         layer_in.reshape(shape_three),
         middle_grad.reshape(shape_three),

time: 488 us -> 467 us (0.957)
  Pallas kernels: 264 us -> 234 us
  local copies, waits for them, and re-layouts: 24.8 us -> 42.9 us
  waiting for transfers between devices: 70.8 us -> 58.1 us
    unnamed x91 -> x141, local copies, waits for them, and re-layouts: 6.17 us -> 24.2 us
    pallas_call x4, Pallas kernels: 76.2 us -> 62.8 us  [mlp(): pl.pallas_call(functools.partial(mlp_kernel, rows // 2, turned), grid_spe...]
    ppermute x51 -> x55, waiting for transfers between devices: 70.7 us -> 58 us  [flip(): return lax.ppermute(value, axis, [(i, i ^ bit) for i in range(size)])]
    ppermute x51 -> x55, starting transfers between devices: 65.3 us -> 67.3 us  [flip(): return lax.ppermute(value, axis, [(i, i ^ bit) for i in range(size)])]
  transfers between devices with their start and end apart: 55 -> 59, of which waited for: 12 -> 13; matrix products, arithmetic and copies ran while one was open for 10% -> 10% of each run, Pallas kernels for 54% -> 50%
where the time goes in v5:
time: 467 us; the launch traced here: 461 us
  Pallas kernels  234 us (50%)
  starting transfers between devices  67.7 us (14%)
  waiting for transfers between devices  58.1 us (12%)
  other arithmetic  43.1 us (9%)
  local copies, waits for them, and re-layouts  42.9 us (9%)
  between operations  15.4 us (3%)
    ppermute x55, starting transfers between devices, flip(): return lax.ppermute(value, axis, [(i, i ^ bit) for i in range(size)])  67.3 us
    pallas_call x4, Pallas kernels, attend_back(): pl.pallas_call(attend_back_kernel, grid_spec=pltpu.PrefetchScalarGridSpec...  63.8 us
    pallas_call x4, Pallas kernels, mlp(): pl.pallas_call(functools.partial(mlp_kernel, rows // 2, turned), grid_spe...  62.8 us
    ppermute x55, waiting for transfers between devices, flip(): return lax.ppermute(value, axis, [(i, i ^ bit) for i in range(size)])  58 us
    pallas_call x3, Pallas kernels, attend(): pl.pallas_call(attend_kernel, grid_spec=pltpu.PrefetchScalarGridSpec(num_...  34 us
    convert_element_type x17, other arithmetic, total(): return result.astype(LOW)  32.4 us
    unnamed x141, local copies, waits for them, and re-layouts  24.2 us
    pallas_call x2, Pallas kernels, mlp_out(): pl.pallas_call(functools.partial(mlp_out_kernel, half), grid=(tiles,), in...  20.2 us
  transfers between devices with their start and end apart: 59, of which 13 were waited for; matrix products, arithmetic and copies ran while one was open for 10% of the time, Pallas kernels for 50%

profile of v5, /device:TPU:0, one launch (start us, length us, event | category | flops | bytes accessed | tf_op | source)
XLA Modules:
  0.0 461.5 jit_solution(1334888867411401705)
XLA Ops:
  23.1 8.6 %collective-permute-done.1.refs_4_ = bf16[1024,128]{1,0:T(8,128)(2,1)} collective-permute-done((bf16[1024,128]{1,0:T(8,128)(2,1)}, bf16[1024,128]{1,0:T(8,128)(2,1)}, u32[]{:S(2)}, u32[]{:S(2)}) %collective-permute-start.1) | collective-permute-done | bytes 262176 | tf_op jit(solution)/shard_map/ppermute | solution.py:245
  38.6 16.3 %attend.3 = (bf16[4,4,280,768]{3,2,1,0:T(8,128)(2,1)}, bf16[4,4,280,256]{3,2,1,0:T(8,128)(2,1)}, bf16[4,1024,768]{2,1,0:T(8,128)(2,1)}) custom-call(s32[4]{0:T(128)} %pad_add_fusion.spot_ref, s32[4]{0:T(128)} %dynamic_slice.83.count_ref, bf16[4,280,1024]{2,1,0:T(8,128)(2,1)} %bitcast.184, bf16[1024,512]{1,0:T(8,128)(2,1)} %refs_1_.3, ...), custom_call_target="tpu_custom_call" | custom-call | tf_op jit(solution)/shard_map/attend/pallas_call | solution.py:320
  61.3 8.9 %attend.4 = (bf16[4,4,280,768]{3,2,1,0:T(8,128)(2,1)}, bf16[4,4,280,256]{3,2,1,0:T(8,128)(2,1)}, bf16[4,1024,768]{2,1,0:T(8,128)(2,1)}) custom-call(s32[8]{0:T(128)} %concatenate.29.spot_ref, s32[4]{0:T(128)} %dynamic_slice.83.count_ref, bf16[4,280,1024]{2,1,0:T(8,128)(2,1)} %bitcast.185, ...), custom_call_target="tpu_custom_call", output_to_operand_aliasing={{0}: (13, {}), {1}: (14, {}), {2}: (15, {})} | custom-call | tf_op jit(solution)/shard_map/attend/pallas_call | solution.py:320
  76.6 8.7 %attend.5 = (bf16[4,4,280,768]{3,2,1,0:T(8,128)(2,1)}, bf16[4,4,280,256]{3,2,1,0:T(8,128)(2,1)}, bf16[4,1024,768]{2,1,0:T(8,128)(2,1)}) custom-call(s32[8]{0:T(128)} %concatenate.29.spot_ref, s32[4]{0:T(128)} %dynamic_slice.83.count_ref, bf16[4,280,1024]{2,1,0:T(8,128)(2,1)} %bitcast.186, ...), custom_call_target="tpu_custom_call", output_to_operand_aliasing={{0}: (13, {}), {1}: (14, {}), {2}: (15, {})} | custom-call | tf_op jit(solution)/shard_map/attend/pallas_call | solution.py:320
  86.1 9.4 %middle.1 = (f32[4,280,1024]{2,1,0:T(8,128)}, bf16[4,280,1024]{2,1,0:T(8,128)(2,1)}, bf16[4,256,1024]{2,1,0:T(8,128)(2,1)}) custom-call(s32[8]{0:T(128)} %concatenate.30.spot_ref, bf16[4,280,1024]{2,1,0:T(8,128)(2,1)} %bitcast.173, bf16[4,4,280,256]{3,2,1,0:T(8,128)(2,1)} %get-tuple-element.204.context_ref, bf16[512,1024]{1,0:T(8,128)(2,1)} %own_ref.1, ...), custom_call_target="tpu_custom_call" | custom-call | tf_op jit(solution)/shard_map/middle/pallas_call | solution.py:467
  99.4 15.5 %mlp.4 = (bf16[2,4,128,1024]{3,2,1,0:T(8,128)(2,1)S(1)}, bf16[2,4,128,1024]{3,2,1,0:T(8,128)(2,1)S(1)}, f32[2,1,512]{2,1,0:T(1,128)S(1)}, bf16[4,1120,1024]{2,1,...) custom-call(s32[4]{0:T(128)S(1)} %copy-done.26, ...), custom_call_target="tpu_custom_call" | custom-call | tf_op jit(solution)/shard_map/mlp/pallas_call | solution.py:533
  115.2 15.7 %mlp.5 = (bf16[2,4,128,1024]{3,2,1,0:T(8,128)(2,1)S(1)}, bf16[2,4,128,1024]{3,2,1,0:T(8,128)(2,1)S(1)}, f32[2,1,512]{2,1,0:T(1,128)S(1)}, bf16[4,1120,1024]{2,1,...) custom-call(s32[4]{0:T(128)S(1)} %copy-done.26, ...), custom_call_target="tpu_custom_call", output_to_operand_aliasing={{3}: (15, {}), {4}: (16, {}), {5}: (17, {}), {6}: (18, {})} | custom-call | tf_op jit(solution)/shard_map/mlp/pallas_call | solution.py:533
  135.2 15.7 %mlp.6 = (bf16[2,4,128,1024]{3,2,1,0:T(8,128)(2,1)S(1)}, bf16[2,4,128,1024]{3,2,1,0:T(8,128)(2,1)}, f32[2,1,512]{2,1,0:T(1,128)S(1)}, bf16[4,1120,1024]{2,1,0:T(...) custom-call(s32[4]{0:T(128)S(1)} %copy-done.26, ...), custom_call_target="tpu_custom_call", output_to_operand_aliasing={{3}: (15, {}), {4}: (16, {}), {5}: (17, {}), {6}: (18, {})} | custom-call | tf_op jit(solution)/shard_map/mlp/pallas_call | solution.py:533
  158.0 15.9 %mlp.7 = (bf16[2,4,128,1024]{3,2,1,0:T(8,128)(2,1)S(1)}, bf16[2,4,128,1024]{3,2,1,0:T(8,128)(2,1)S(1)}, f32[2,1,512]{2,1,0:T(1,128)S(1)}, bf16[4,1120,1024]{2,1,...) custom-call(s32[4]{0:T(128)S(1)} %copy-done.26, ...), custom_call_target="tpu_custom_call", output_to_operand_aliasing={{3}: (15, {}), {4}: (16, {}), {5}: (17, {}), {6}: (18, {})} | custom-call | tf_op jit(solution)/shard_map/mlp/pallas_call | solution.py:533
  180.0 18.9 %mlp_back.1 = (f32[1120,1024]{1,0:T(8,128)S(1)}, bf16[1120,1024]{1,0:T(8,128)(2,1)S(1)}, f32[8,1024]{1,0:T(8,128)S(1)}) custom-call(bf16[4,1120,1024]{2,1,0:T(8,128)(2,1)} %get-tuple-element.239.pre_ref, bf16[4,1024,1024]{2,1,0:T(8,128)(2,1)} %get-tuple-element.240.up_ref, f32[1120,1024]{1,0:T(8,128)} %bitcast.187, bf16[1120,1024]{1,0:T(8,128)(2,1)S(1)} %copy-done.7, ...), custom_call_target="tpu_custom_call" | custom-call | tf_op jit(solution)/shard_map/mlp_back/pallas_call | solution.py:626
  206.1 15.8 %attend_back.4 = (bf16[2,4,128,1024]{3,2,1,0:T(8,128)(2,1)}, f32[1,768]{1,0:T(1,128)}, bf16[4,280,768]{2,1,0:T(8,128)(2,1)}) custom-call(s32[4]{0:T(128)} %dynamic_slice.83.count_ref, bf16[1120,1024]{1,0:T(8,128)(2,1)} %fusion.5.rows_hbm, bf16[1120,1024]{1,0:T(8,128)(2,1)} %copy-done.4, bf16[4,280,1024]{2,1,0:T(8,128)(2,1)} %bitcast.169, ...), custom_call_target="tpu_custom_call" | custom-call | tf_op jit(solution)/shard_map/attend_back/pallas_call | solution.py:406
  221.9 6.1 %collective-permute-done.18 = bf16[2,2,128,1024]{3,2,1,0:T(8,128)(2,1)} collective-permute-done((bf16[2,2,128,1024]{3,2,1,0:T(8,128)(2,1)S(1)}, bf16[2,2,128,1024]{3,2,1,0:T(8,128)(2,1)}, u32[]{:S(2)}, u32[]{:S(2)}) %collective-permute-start.18) | collective-permute-done | bytes 1048608 | tf_op jit(solution)/shard_map/ppermute | solution.py:245
  235.2 15.7 %attend_back.5 = (bf16[2,4,128,1024]{3,2,1,0:T(8,128)(2,1)}, f32[1,768]{1,0:T(1,128)}, bf16[4,280,768]{2,1,0:T(8,128)(2,1)}) custom-call(s32[4]{0:T(128)} %dynamic_slice.83.count_ref, bf16[1120,1024]{1,0:T(8,128)(2,1)} %fusion.5.rows_hbm, bf16[1120,1024]{1,0:T(8,128)(2,1)} %copy-done.4, bf16[4,280,1024]{2,1,0:T(8,128)(2,1)} %bitcast.170, ...), custom_call_target="tpu_custom_call" | custom-call | tf_op jit(solution)/shard_map/attend_back/pallas_call | solution.py:406
  253.8 4.9 %add_convert_fusion.1 = (bf16[2,2,128,1024]{3,2,1,0:T(8,128)(2,1)}, bf16[2,2,128,1024]{3,2,1,0:T(8,128)(2,1)}) fusion(bf16[2,4,128,1024]{3,2,1,0:T(8,128)(2,1)} %collective-permute-done.23, bf16[2,4,128,1024]{3,2,1,0:T(8,128)(2,1)} %get-tuple-element.264), kind=kLoop, calls=%fused_computation.9 | loop fusion | flops 4194304 | bytes 6291456 | tf_op jit(solution)/shard_map/convert_element_type | solution.py:260
  266.2 15.6 %attend_back.6 = (bf16[2,4,128,1024]{3,2,1,0:T(8,128)(2,1)}, f32[1,768]{1,0:T(1,128)}, bf16[4,280,768]{2,1,0:T(8,128)(2,1)}) custom-call(s32[4]{0:T(128)} %dynamic_slice.83.count_ref, bf16[1120,1024]{1,0:T(8,128)(2,1)} %fusion.5.rows_hbm, bf16[1120,1024]{1,0:T(8,128)(2,1)} %copy-done.4, bf16[4,280,1024]{2,1,0:T(8,128)(2,1)} %bitcast.171, ...), custom_call_target="tpu_custom_call" | custom-call | tf_op jit(solution)/shard_map/attend_back/pallas_call | solution.py:406
  290.7 16.6 %attend_back.7 = (bf16[2,4,128,1024]{3,2,1,0:T(8,128)(2,1)}, f32[1,768]{1,0:T(1,128)}, bf16[4,280,768]{2,1,0:T(8,128)(2,1)}) custom-call(s32[4]{0:T(128)} %dynamic_slice.83.count_ref, bf16[1120,1024]{1,0:T(8,128)(2,1)} %fusion.5.rows_hbm, bf16[1120,1024]{1,0:T(8,128)(2,1)} %copy-done.4, bf16[4,280,1024]{2,1,0:T(8,128)(2,1)} %bitcast.172, ...), custom_call_target="tpu_custom_call" | custom-call | tf_op jit(solution)/shard_map/attend_back/pallas_call | solution.py:406
  324.1 10.7 %input_grad.1 = (bf16[4,280,1024]{2,1,0:T(8,128)(2,1)}, f32[8,1024]{1,0:T(8,128)S(1)}) custom-call(bf16[4,280,768]{2,1,0:T(8,128)(2,1)S(1)} %copy-done.24, bf16[4,280,768]{2,1,0:T(8,128)(2,1)S(1)} %copy-done.23, bf16[4,280,768]{2,1,0:T(8,128)(2,1)S(1)} %copy-done.22, bf16[4,280,768]{2,1,0:T(8,128)(2,1)S(1)} %copy-done.21, ...), custom_call_target="tpu_custom_call" | custom-call | tf_op jit(solution)/shard_map/input_grad/pallas_call | solution.py:759
  334.8 7.4 %collective-permute-done.30 = bf16[4,32,1024]{2,1,0:T(8,128)(2,1)S(1)} collective-permute-done((bf16[4,32,1024]{2,1,0:T(8,128)(2,1)S(1)}, bf16[4,32,1024]{2,1,0:T(8,128)(2,1)S(1)}, u32[]{:S(2)}, u32[]{:S(2)}) %collective-permute-start.30) | collective-permute-done | bytes 262176 | tf_op jit(solution)/shard_map/ppermute | solution.py:245
  355.2 10.0 %mlp_out.2.refs_0_ = bf16[1120,1024]{1,0:T(8,128)(2,1)} custom-call(bf16[4,1120,1024]{2,1,0:T(8,128)(2,1)} %get-tuple-element.294.act_ref, bf16[4,1024,1024]{2,1,0:T(8,128)(2,1)} %get-tuple-element.295.down_ref, f32[1120,1024]{1,0:T(8,128)} %bitcast.188, bf16[1,1024]{1,0:T(2,128)(2,1)} %reshape.243.bias_ref), custom_call_target="tpu_custom_call" | custom-call | tf_op jit(solution)/shard_map/mlp_out/pallas_call | solution.py:679
  373.0 7.3 %collective-permute-done.37 = bf16[2,32,1024]{2,1,0:T(8,128)(2,1)S(1)} collective-permute-done((bf16[2,32,1024]{2,1,0:T(8,128)(2,1)S(1)}, bf16[2,32,1024]{2,1,0:T(8,128)(2,1)S(1)}, u32[]{:S(2)}, u32[]{:S(2)}) %collective-permute-start.37) | collective-permute-done | bytes 131104 | tf_op jit(solution)/shard_map/ppermute | solution.py:245
  380.3 5.1 %collective-permute-start.42 = (bf16[2,32,1024]{2,1,0:T(8,128)(2,1)S(1)}, bf16[2,32,1024]{2,1,0:T(8,128)(2,1)S(1)}, u32[]{:S(2)}, u32[]{:S(2)}) collective-permute-start(bf16[2,32,1024]{2,1,0:T(8,128)(2,1)S(1)} %get-tuple-element.346), channel_id=1, source_target_pairs={{0,24},{2,26},{4,28},{6,30},{8,16},{10,18},{12,20},{14,22},{16,8},... | collective-permute-start | bytes 393224 | tf_op jit(solution)/shard_map/ppermute | solution.py:245
  385.4 10.2 %mlp_out.3 = bf16[1120,1024]{1,0:T(8,128)(2,1)} custom-call(bf16[4,1120,1024]{2,1,0:T(8,128)(2,1)} %get-tuple-element.294.act_ref, bf16[4,1024,1024]{2,1,0:T(8,128)(2,1)} %get-tuple-element.295.down_ref, f32[1120,1024]{1,0:T(8,128)} %bitcast.189, bf16[1,1024]{1,0:T(2,128)(2,1)} %reshape.243.bias_ref, ...), custom_call_target="tpu_custom_call", output_to_operand_aliasing={{}: (4, {})} | custom-call | tf_op jit(solution)/shard_map/mlp_out/pallas_call | solution.py:679
  396.7 9.6 %collective-permute-start.44 = (bf16[2,32,1024]{2,1,0:T(8,128)(2,1)}, bf16[2,32,1024]{2,1,0:T(8,128)(2,1)S(1)}, u32[]{:S(2)}, u32[]{:S(2)}) collective-permute-start(bf16[2,32,1024]{2,1,0:T(8,128)(2,1)} %get-tuple-element.344), channel_id=1, source_target_pairs={{0,16},{2,18},{4,20},{6,22},{8,24},{10,26},{12,28},{14,30},{16,0},... | collective-permute-start | bytes 393224 | tf_op jit(solution)/shard_map/ppermute | solution.py:245
  437.7 6.7 %collective-permute-done.49 = bf16[4,2,32,1024]{3,2,1,0:T(8,128)(2,1)} collective-permute-done((bf16[4,2,32,1024]{3,2,1,0:T(8,128)(2,1)}, bf16[4,2,32,1024]{3,2,1,0:T(8,128)(2,1)}, u32[]{:S(2)}, u32[]{:S(2)}) %collective-permute-start.49) | collective-permute-done | bytes 524320 | tf_op jit(solution)/shard_map/ppermute | solution.py:245
  (331 shorter events, 170.6 us)
Async XLA Ops:
  7.2 88.3 %all-gather.7.cloned.1.call-start = ((), (), s32[]{:S(2)}) async-start(), calls=%async_computation | async-start | bytes 4456448 | tf_op jit(solution)/shard_map/all_gather | solution.py:960
  33.6 120.6 %all-gather.9.cloned.1.call-start = ((), (), s32[]{:S(2)}) async-start(), calls=%async_computation.1 | async-start | bytes 4456448 | tf_op jit(solution)/shard_map/all_gather | solution.py:960
  33.6 24.7 %collective-permute-start.2 = (bf16[2,1024,256]{2,1,0:T(8,128)(2,1)S(1)}, bf16[2,1024,256]{2,1,0:T(8,128)(2,1)S(1)}, u32[]{:S(2)}, u32[]{:S(2)}) collective-permute-start(bf16[2,1024,256]{2,1,0:T(8,128)(2,1)S(1)} %pad_maximum_fusion), channel_id=1, source_target_pairs={{0,1},{1,0},{2,3},{3,2},{4,5},{5,4},{6,7},{7,6},{8,9},{9,8},{10,11... | collective-permute-start | bytes 3145736 | tf_op jit(solution)/shard_map/ppermute | solution.py:245
  35.4 22.9 %collective-permute-start.4 = (bf16[1024,128]{1,0:T(8,128)(2,1)}, bf16[1024,128]{1,0:T(8,128)(2,1)S(1)}, u32[]{:S(2)}, u32[]{:S(2)}) collective-permute-start(bf16[1024,128]{1,0:T(8,128)(2,1)} %collective-permute-done.1.refs_4_), channel_id=1, source_target_pairs={{0,4},{2,6},{4,0},{6,2},{8,12},{10,14},{12,8},{14,10},{16,20},{18,... | collective-permute-start | bytes 786440 | tf_op jit(solution)/shard_map/ppermute | solution.py:245
  59.0 352.6 %all-gather.11.cloned.1.call-start = ((), (), s32[]{:S(2)}) async-start(), calls=%async_computation.2 | async-start | bytes 4456448 | tf_op jit(solution)/shard_map/all_gather | solution.py:1104
  173.9 27.2 %collective-permute-start.17 = (bf16[2,4,128,1024]{3,2,1,0:T(8,128)(2,1)S(1)}, bf16[2,4,128,1024]{3,2,1,0:T(8,128)(2,1)S(1)}, u32[]{:S(2)}, u32[]{:S(2)}) collective-permute-start(bf16[2,4,128,1024]{3,2,1,0:T(8,128)(2,1)S(1)} %get-tuple-element.238), channel_id=1, source_target_pairs={{0,2},{2,0},{4,6},{6,4},{8,10},{10,8},{12,14},{14,12},{16,18},{18,... | collective-permute-start | bytes 6291464 | tf_op jit(solution)/shard_map/ppermute | solution.py:245
  174.2 26.9 %collective-permute-start.15 = (bf16[2,2,128,1024]{3,2,1,0:T(8,128)(2,1)S(1)}, bf16[2,2,128,1024]{3,2,1,0:T(8,128)(2,1)}, u32[]{:S(2)}, u32[]{:S(2)}) collective-permute-start(bf16[2,2,128,1024]{3,2,1,0:T(8,128)(2,1)S(1)} %copy-done.41), channel_id=1, source_target_pairs={{0,1},{1,0},{2,3},{3,2},{4,5},{5,4},{6,7},{7,6},{8,9},{9,8},{10,11... | collective-permute-start | bytes 3145736 | tf_op jit(solution)/shard_map/ppermute | solution.py:245
  178.5 22.6 %collective-permute-start.16 = (bf16[2,128,1024]{2,1,0:T(8,128)(2,1)S(1)}, bf16[2,128,1024]{2,1,0:T(8,128)(2,1)S(1)}, u32[]{:S(2)}, u32[]{:S(2)}) collective-permute-start(bf16[2,128,1024]{2,1,0:T(8,128)(2,1)S(1)} %fusion.14), channel_id=1, source_target_pairs={{0,4},{2,6},{4,0},{6,2},{8,12},{10,14},{12,8},{14,10},{16,20},{18,... | collective-permute-start | bytes 1572872 | tf_op jit(solution)/shard_map/ppermute | solution.py:245
  203.1 24.9 %collective-permute-start.18 = (bf16[2,2,128,1024]{3,2,1,0:T(8,128)(2,1)S(1)}, bf16[2,2,128,1024]{3,2,1,0:T(8,128)(2,1)}, u32[]{:S(2)}, u32[]{:S(2)}) collective-permute-start(bf16[2,2,128,1024]{3,2,1,0:T(8,128)(2,1)S(1)} %get-tuple-element.355), channel_id=1, source_target_pairs={{0,1},{1,0},{2,3},{3,2},{4,5},{5,4},{6,7},{7,6},{8,9},{9,8},{10,11... | collective-permute-start | bytes 3145736 | tf_op jit(solution)/shard_map/ppermute | solution.py:245
  228.0 25.8 %collective-permute-start.23 = (bf16[2,4,128,1024]{3,2,1,0:T(8,128)(2,1)}, bf16[2,4,128,1024]{3,2,1,0:T(8,128)(2,1)}, u32[]{:S(2)}, u32[]{:S(2)}) collective-permute-start(bf16[2,4,128,1024]{3,2,1,0:T(8,128)(2,1)} %get-tuple-element.259), channel_id=1, source_target_pairs={{0,2},{2,0},{4,6},{6,4},{8,10},{10,8},{12,14},{14,12},{16,18},{18,... | collective-permute-start | bytes 6291464 | tf_op jit(solution)/shard_map/ppermute | solution.py:245
  228.0 25.8 %collective-permute-start.20 = (bf16[2,2,128,1024]{3,2,1,0:T(8,128)(2,1)}, bf16[2,2,128,1024]{3,2,1,0:T(8,128)(2,1)S(1)}, u32[]{:S(2)}, u32[]{:S(2)}) collective-permute-start(bf16[2,2,128,1024]{3,2,1,0:T(8,128)(2,1)} %get-tuple-element.257), channel_id=1, source_target_pairs={{0,1},{1,0},{2,3},{3,2},{4,5},{5,4},{6,7},{7,6},{8,9},{9,8},{10,11... | collective-permute-start | bytes 3145736 | tf_op jit(solution)/shard_map/ppermute | solution.py:245
  258.7 25.1 %collective-permute-start.24 = (bf16[2,2,128,1024]{3,2,1,0:T(8,128)(2,1)}, bf16[2,2,128,1024]{3,2,1,0:T(8,128)(2,1)}, u32[]{:S(2)}, u32[]{:S(2)}) collective-permute-start(bf16[2,2,128,1024]{3,2,1,0:T(8,128)(2,1)} %get-tuple-element.351), channel_id=1, source_target_pairs={{0,1},{1,0},{2,3},{3,2},{4,5},{5,4},{6,7},{7,6},{8,9},{9,8},{10,11... | collective-permute-start | bytes 3145736 | tf_op jit(solution)/shard_map/ppermute | solution.py:245
  284.6 146.9 %all-gather.13.cloned.1.call-start = ((), (), s32[]{:S(2)}) async-start(), calls=%async_computation.3 | async-start | bytes 4456448 | tf_op jit(solution)/shard_map/all_gather | solution.py:1121
  284.7 27.1 %collective-permute-start.28 = (bf16[2,4,128,1024]{3,2,1,0:T(8,128)(2,1)}, bf16[2,4,128,1024]{3,2,1,0:T(8,128)(2,1)}, u32[]{:S(2)}, u32[]{:S(2)}) collective-permute-start(bf16[2,4,128,1024]{3,2,1,0:T(8,128)(2,1)} %get-tuple-element.279), channel_id=1, source_target_pairs={{0,2},{2,0},{4,6},{6,4},{8,10},{10,8},{12,14},{14,12},{16,18},{18,... | collective-permute-start | bytes 6291464 | tf_op jit(solution)/shard_map/ppermute | solution.py:245
  284.8 27.1 %collective-permute-start.27 = (bf16[2,2,128,1024]{3,2,1,0:T(8,128)(2,1)}, bf16[2,2,128,1024]{3,2,1,0:T(8,128)(2,1)}, u32[]{:S(2)}, u32[]{:S(2)}) collective-permute-start(bf16[2,2,128,1024]{3,2,1,0:T(8,128)(2,1)} %get-tuple-element.278), channel_id=1, source_target_pairs={{0,1},{1,0},{2,3},{3,2},{4,5},{5,4},{6,7},{7,6},{8,9},{9,8},{10,11... | collective-permute-start | bytes 3145736 | tf_op jit(solution)/shard_map/ppermute | solution.py:245
  289.1 22.7 %collective-permute-start.29 = (bf16[4,64,1024]{2,1,0:T(8,128)(2,1)}, bf16[4,64,1024]{2,1,0:T(8,128)(2,1)}, u32[]{:S(2)}, u32[]{:S(2)}) collective-permute-start(bf16[4,64,1024]{2,1,0:T(8,128)(2,1)} %dynamic-slice_bitcast_fusion), channel_id=1, source_target_pairs={{0,8},{2,10},{4,12},{6,14},{8,0},{10,2},{12,4},{14,6},{16,24},{18,... | collective-permute-start | bytes 1572872 | tf_op jit(solution)/shard_map/ppermute | solution.py:245
  315.3 27.0 %collective-permute-start.31 = (bf16[2,128,1024]{2,1,0:T(8,128)(2,1)S(1)}, bf16[2,128,1024]{2,1,0:T(8,128)(2,1)S(1)}, u32[]{:S(2)}, u32[]{:S(2)}) collective-permute-start(bf16[2,128,1024]{2,1,0:T(8,128)(2,1)S(1)} %get-tuple-element.347), channel_id=1, source_target_pairs={{0,4},{2,6},{4,0},{6,2},{8,12},{10,14},{12,8},{14,10},{16,20},{18,... | collective-permute-start | bytes 1572872 | tf_op jit(solution)/shard_map/ppermute | solution.py:245
  317.8 24.5 %collective-permute-start.30 = (bf16[4,32,1024]{2,1,0:T(8,128)(2,1)S(1)}, bf16[4,32,1024]{2,1,0:T(8,128)(2,1)S(1)}, u32[]{:S(2)}, u32[]{:S(2)}) collective-permute-start(bf16[4,32,1024]{2,1,0:T(8,128)(2,1)S(1)} %dynamic-slice_bitcast_fusion.4), channel_id=1, source_target_pairs={{0,16},{2,18},{4,20},{6,22},{8,24},{10,26},{12,28},{14,30},{16,0},... | collective-permute-start | bytes 786440 | tf_op jit(solution)/shard_map/ppermute | solution.py:245
  367.1 28.6 %collective-permute-start.38 = (bf16[2,32,1024]{2,1,0:T(8,128)(2,1)S(1)}, bf16[2,32,1024]{2,1,0:T(8,128)(2,1)S(1)}, u32[]{:S(2)}, u32[]{:S(2)}) collective-permute-start(bf16[2,32,1024]{2,1,0:T(8,128)(2,1)S(1)} %get-tuple-element.365), channel_id=1, source_target_pairs={{0,8},{2,10},{4,12},{6,14},{8,0},{10,2},{12,4},{14,6},{16,24},{18,... | collective-permute-start | bytes 393224 | tf_op jit(solution)/shard_map/ppermute | solution.py:245
  368.4 27.2 %collective-permute-start.39 = (bf16[2,32,1024]{2,1,0:T(8,128)(2,1)S(1)}, bf16[2,32,1024]{2,1,0:T(8,128)(2,1)S(1)}, u32[]{:S(2)}, u32[]{:S(2)}) collective-permute-start(bf16[2,32,1024]{2,1,0:T(8,128)(2,1)S(1)} %get-tuple-element.364), channel_id=1, source_target_pairs={{0,24},{2,26},{4,28},{6,30},{8,16},{10,18},{12,20},{14,22},{16,8},... | collective-permute-start | bytes 393224 | tf_op jit(solution)/shard_map/ppermute | solution.py:245
  371.6 24.4 %collective-permute-start.40 = (bf16[2,32,1024]{2,1,0:T(8,128)(2,1)S(1)}, bf16[2,32,1024]{2,1,0:T(8,128)(2,1)S(1)}, u32[]{:S(2)}, u32[]{:S(2)}) collective-permute-start(bf16[2,32,1024]{2,1,0:T(8,128)(2,1)S(1)} %get-tuple-element.346), channel_id=1, source_target_pairs={{0,16},{2,18},{4,20},{6,22},{8,24},{10,26},{12,28},{14,30},{16,0},... | collective-permute-start | bytes 393224 | tf_op jit(solution)/shard_map/ppermute | solution.py:245
  372.7 23.2 %collective-permute-start.41 = (bf16[2,32,1024]{2,1,0:T(8,128)(2,1)S(1)}, bf16[2,32,1024]{2,1,0:T(8,128)(2,1)S(1)}, u32[]{:S(2)}, u32[]{:S(2)}) collective-permute-start(bf16[2,32,1024]{2,1,0:T(8,128)(2,1)S(1)} %get-tuple-element.346), channel_id=1, source_target_pairs={{0,8},{2,10},{4,12},{6,14},{8,0},{10,2},{12,4},{14,6},{16,24},{18,... | collective-permute-start | bytes 393224 | tf_op jit(solution)/shard_map/ppermute | solution.py:245
  396.7 25.2 %collective-permute-start.44 = (bf16[2,32,1024]{2,1,0:T(8,128)(2,1)}, bf16[2,32,1024]{2,1,0:T(8,128)(2,1)S(1)}, u32[]{:S(2)}, u32[]{:S(2)}) collective-permute-start(bf16[2,32,1024]{2,1,0:T(8,128)(2,1)} %get-tuple-element.344), channel_id=1, source_target_pairs={{0,16},{2,18},{4,20},{6,22},{8,24},{10,26},{12,28},{14,30},{16,0},... | collective-permute-start | bytes 393224 | tf_op jit(solution)/shard_map/ppermute | solution.py:245
  422.0 22.5 %collective-permute-start.50 = (bf16[8,2,32,1024]{3,2,1,0:T(8,128)(2,1)S(1)}, bf16[8,2,32,1024]{3,2,1,0:T(8,128)(2,1)S(1)}, u32[]{:S(2)}, u32[]{:S(2)}) collective-permute-start(bf16[8,2,32,1024]{3,2,1,0:T(8,128)(2,1)S(1)} %constant_dynamic-update-slice_fusion.2.near_ref), channel_id=1, source_target_pairs={{0,2},{2,0},{4,6},{6,4},{8,10},{10,8},{12,14},{14,12},{16,18},{18,... | collective-permute-start | bytes 3145736 | tf_op jit(solution)/shard_map/ppermute | solution.py:245
  (101 other events, 1026.0 us)
Sparse Core Ops, SparseCore 0:
  33.7 52.1 all-gather.6
  88.1 49.0 all-gather.8
  284.8 65.2 all-gather.10
  352.6 71.5 all-gather.12

commit v6 on v5

--- a/solution.py
+++ b/solution.py
@@ -335,8 +335,10 @@
     )(spots, counts, rows, *[array for array, _ in operands], *buffers)
 
 
-def attend_back_kernel(count_ref, rows_hbm, cots_hbm, cot_ref, qkv_ref, context_ref, out_ref, *refs):
-    near_ref, bias_ref, qkv_grad_ref, grad_buf, context_buf, rows_buf, cots_buf, sems = refs[-8:]
+def attend_back_kernel(
+    count_ref, place_ref, rows_hbm, cots_hbm, cot_ref, qkv_ref, context_ref, upper_ref, lower_ref, *refs
+):
+    near_ref, bias_ref, qkv_grad_ref, grad_buf, context_buf, rows_buf, cots_buf, out_buf, sems = refs[-9:]
     pair = pl.program_id(0)
     copies = [
         pltpu.make_async_copy(rows_hbm, rows_buf, sems.at[0]),
@@ -347,9 +349,11 @@
     def _():
         for copy in copies:
             copy.start()
+        out_buf[:LANES, :] = upper_ref[...]
+        out_buf[LANES:, :] = lower_ref[...]
 
     at = pl.ds(pl.multiple_of(pair * SEQ, 8), SEQ)
-    context_grad = dot(cot_ref[0], out_ref[0], 1, 1).astype(LOW)
+    context_grad = dot(cot_ref[0], out_buf[...], 1, 1).astype(LOW)
     qkv = qkv_ref[0, 0]
     context_buf[at, :] = context_ref[0, 0].astype(WIDE)
     length = TEXT + count_ref[pair]
@@ -399,14 +403,14 @@
         bias_ref[...] = jnp.sum(grad_buf[...], 0, keepdims=True)
 
 
-def attend_back(slot, counts, rows, cot, kept, outs):
+def attend_back(slot, first, counts, places, rows, cot, kept, out):
     qkv, context, _ = kept
     _, pairs, seq, _ = qkv.shape
     width = rows.shape[1]
     return pl.pallas_call(
         attend_back_kernel,
         grid_spec=pltpu.PrefetchScalarGridSpec(
-            num_scalar_prefetch=1,
+            num_scalar_prefetch=2,
             grid=(pairs,),
             in_specs=[
                 ANYWHERE,
@@ -414,7 +418,8 @@
                 pl.BlockSpec((1, seq, width), lambda p, *_: (p, 0, 0)),
                 pl.BlockSpec((1, 1, seq, 768), lambda p, *_: (slot, p, 0, 0)),
                 pl.BlockSpec((1, 1, seq, 256), lambda p, *_: (slot, p, 0, 0)),
-                pl.BlockSpec((1, 256, width), lambda p, *_: (slot, 0, 0)),
+                pl.BlockSpec((LANES, width), lambda p, count, at: (at[first], 0)),
+                pl.BlockSpec((LANES, width), lambda p, count, at: (at[first + 1], 0)),
             ],
             out_specs=[
                 pl.BlockSpec((2, 4, LANES, width), lambda p, *_: (0, 0, 0, 0)),
@@ -426,6 +431,7 @@
                 pltpu.VMEM((pairs * seq, 256), WIDE),
                 pltpu.VMEM(rows.shape, LOW),
                 pltpu.VMEM(cot.shape, LOW),
+                pltpu.VMEM((2 * LANES, width), LOW),
                 pltpu.SemaphoreType.DMA((2,)),
             ],
         ),
@@ -436,7 +442,7 @@
         ],
         name="attend_back",
         compiler_params=pltpu.CompilerParams(vmem_limit_bytes=56 * 1024 * 1024),
-    )(counts, rows, cot, cot.reshape(pairs, seq, width), qkv, context, outs)
+    )(counts, places, rows, cot, cot.reshape(pairs, seq, width), qkv, context, out, out)
 
 
 def middle_kernel(
@@ -449,10 +455,10 @@
         for i in range(8):
             source = own_ref if i < 4 else (near_ref if i < 6 else far_ref)
             start = pl.multiple_of(spot_ref[i] * LANES, LANES)
-            out_ref[i // 2, (i % 2) * LANES : (i % 2 + 1) * LANES, :] = source[pl.ds(start, LANES), :]
+            out_ref[i * LANES : (i + 1) * LANES, :] = source[pl.ds(start, LANES), :]
 
     context = jnp.concatenate([context_ref[i, 0] for i in range(4)], 1)
-    attended = dot(context, out_ref[...].reshape(-1, out_ref.shape[2]), 1, 0)
+    attended = dot(context, out_ref[...], 1, 0)
     middle = rows_ref[0].astype(WIDE) + attended + bias_ref[...].astype(WIDE)
     middle_ref[0] = middle
     center = middle - jnp.mean(middle, -1, keepdims=True)
@@ -477,12 +483,12 @@
                 resident(far.shape),
             ]
             + [resident((1, width))] * 3,
-            out_specs=[block(), block(), resident((4, 256, width))],
+            out_specs=[block(), block()],
+            scratch_shapes=[pltpu.VMEM((8 * LANES, width), LOW)],
         ),
         out_shape=[
             jax.ShapeDtypeStruct(rows.shape, WIDE),
             jax.ShapeDtypeStruct(rows.shape, LOW),
-            jax.ShapeDtypeStruct((4, 256, width), LOW),
         ],
         name="middle",
         compiler_params=pltpu.CompilerParams(vmem_limit_bytes=56 * 1024 * 1024),
@@ -504,7 +510,7 @@
         bias_ref[:, span] = biases[r][...].astype(WIDE)
 
     def one(i, carry):
-        at = pl.ds(pl.multiple_of(i * step, step), step)
+        at = pl.ds(i * step, step)
         pre_act = dot(hidden_ref[at, :], up_ref[0], 1, 0) + bias_ref[...]
         act_grad = dot(cot_ref[at, :], down_ref[0], 1, 1)
         chance = 0.5 + 0.5 * lax.erf(pre_act * ROOT_HALF)
@@ -513,7 +519,8 @@
         pre_ref[0, at, :] = (act_grad * slope).astype(LOW)
         return carry
 
-    lax.fori_loop(0, rows // step, one, 0)
+    for i in range(rows // step):
+        one(i, 0)
     up_grad = dot(pre_ref[0], hidden_ref[...], 0, 0).astype(LOW).reshape(4, LANES, -1)
     down_grad = dot(act_ref[0], cot_ref[...], 0, 0).astype(LOW).reshape(4, LANES, -1)
     bias_out[0] = jnp.sum(pre_ref[0].astype(WIDE), 0, keepdims=True)
@@ -973,8 +980,9 @@
     kept = attend(
         3, 1, gate(other_spots, near_out), counts, normed_three, *other_inputs(1, far_qk, far_values), kept
     )
-    middle, hidden, outs_all = middle_step(
-        jnp.concatenate([spots, sides]),
+    places = jnp.concatenate([spots, sides])
+    middle, hidden = middle_step(
+        places,
         layer_in.reshape(shape_three),
         kept[1],
         out_weight,
@@ -1037,7 +1045,14 @@
         return cut(item, zhigh_id ^ 1), cut(item, zhigh_id)
 
     back = lambda slot, *wait: attend_back(
-        slot, gate(counts, *wait), normed, attn_grad, kept, outs_all
+        slot,
+        2 * slot,
+        gate(counts, *wait),
+        places,
+        normed,
+        attn_grad,
+        kept,
+        (out_weight, out_weight, near_out, far_out)[slot],
     )
 
     together = lambda *items: lax.optimization_barrier(items)
@@ -1150,18 +1165,17 @@
     layer_out = mlp_out(
         1, acts, downs_all, middle, gate(row_vec(down_bias), late_one0, vec, *late_four1), [mark]
     )
-    late_got1, late_have0, vec_got, layer_out = together(
-        send_four(late_four1), send_four([late_one0] * 4), swap(vec, CORE), layer_out
+    late_got1, late_have0, layer_out = together(
+        send_four(late_four1), send_four([late_one0] * 4), layer_out
     )
     late_one1 = total(late_four1[0], *late_got1)
     late_have0 = jnp.stack([late_one0, *late_have0])
-    vec = vec + vec_got
     up_shape, down_shape = up_weight.shape, down_weight.shape
     placed = gathered(
-        0, 2, gate(gathered_a, late_one1, late_have0, vec), (up_shape, down_shape), []
+        0, 2, gate(gathered_a, late_one1, late_have0), (up_shape, down_shape), []
     )
     late_have1, late_side0, vec_got, *placed = together(
-        send_four([late_one1] * 4), swap(late_have0, XBIT), swap(vec, XBIT), *placed
+        send_four([late_one1] * 4), swap(late_have0, XBIT), swap(vec, CORE), *placed
     )
     late_have1 = jnp.stack([late_one1, *late_have1])
     late_have0 = jnp.concatenate([late_have0, late_side0])
@@ -1170,16 +1184,17 @@
         1, 2, gate(gathered_b, late_have1, late_have0, vec), (up_shape, down_shape), placed
     )
     late_side1, late_far0, vec_got, grad_up_weight, grad_down_weight = together(
-        swap(late_have1, XBIT), swap(late_have0, CORE), send_four([vec] * 4), *placed
+        swap(late_have1, XBIT), swap(late_have0, CORE), swap(vec, XBIT), *placed
     )
     late_have1 = jnp.concatenate([late_have1, late_side1])
+    vec = vec + vec_got
+    grad_query_weight, grad_key_weight = place(
+        (True, True), 0, 1, gate(place_spots, late_have1, vec), late_have0, late_far0, (query_weight.shape,) * 2, []
+    )
+    late_far1, vec_got, grad_query_weight, grad_key_weight = together(
+        swap(late_have1, CORE), send_four([vec] * 4), grad_query_weight, grad_key_weight
+    )
     vec = ((vec + vec_got[0]) + (vec_got[1] + vec_got[2])).reshape(-1)
-    grad_query_weight, grad_key_weight = place(
-        (True, True), 0, 1, gate(place_spots, late_have1), late_have0, late_far0, (query_weight.shape,) * 2, []
-    )
-    late_far1, grad_query_weight, grad_key_weight = together(
-        swap(late_have1, CORE), grad_query_weight, grad_key_weight
-    )
     grad_value_weight, grad_out_weight = place(
         (True, False), 0, 1, place_spots, late_have1, late_far1, (value_weight.shape, out_weight.shape), []
     )

time: 467 us -> 465 us (level)
  no operation moved by 1% of the time
where the time goes in v6:
time: 465 us; the launch traced here: 459 us
  Pallas kernels  233 us (50%)
  starting transfers between devices  68.8 us (15%)
  waiting for transfers between devices  57.6 us (12%)
  local copies, waits for them, and re-layouts  42.8 us (9%)
  other arithmetic  41.7 us (9%)
  between operations  15.3 us (3%)
    ppermute x55, starting transfers between devices, flip(): return lax.ppermute(value, axis, [(i, i ^ bit) for i in range(size)])  68.5 us
    pallas_call x4, Pallas kernels, attend_back(): pl.pallas_call(attend_back_kernel, grid_spec=pltpu.PrefetchScalarGridSpec...  64.1 us
    pallas_call x4, Pallas kernels, mlp(): pl.pallas_call(functools.partial(mlp_kernel, rows // 2, turned), grid_spe...  61.4 us
    ppermute x55, waiting for transfers between devices, flip(): return lax.ppermute(value, axis, [(i, i ^ bit) for i in range(size)])  57.5 us
    pallas_call x3, Pallas kernels, attend(): pl.pallas_call(attend_kernel, grid_spec=pltpu.PrefetchScalarGridSpec(num_...  34 us
    convert_element_type x17, other arithmetic, total(): return result.astype(LOW)  32.3 us
    unnamed x141, local copies, waits for them, and re-layouts  24.3 us
    pallas_call x2, Pallas kernels, mlp_out(): pl.pallas_call(functools.partial(mlp_out_kernel, half), grid=(tiles,), in...  20.3 us
  transfers between devices with their start and end apart: 59, of which 13 were waited for; matrix products, arithmetic and copies ran while one was open for 10% of the time, Pallas kernels for 50%

profile of v6, /device:TPU:0, one launch (start us, length us, event | category | flops | bytes accessed | tf_op | source)
XLA Modules:
  0.0 458.9 jit_solution(7374926016096047437)
XLA Ops:
  23.0 8.7 %collective-permute-done.1.refs_4_ = bf16[1024,128]{1,0:T(8,128)(2,1)} collective-permute-done((bf16[1024,128]{1,0:T(8,128)(2,1)}, bf16[1024,128]{1,0:T(8,128)(2,1)}, u32[]{:S(2)}, u32[]{:S(2)}) %collective-permute-start.1) | collective-permute-done | bytes 262176 | tf_op jit(solution)/shard_map/ppermute | solution.py:245
  38.6 16.3 %attend.3 = (bf16[4,4,280,768]{3,2,1,0:T(8,128)(2,1)}, bf16[4,4,280,256]{3,2,1,0:T(8,128)(2,1)}, bf16[4,1024,768]{2,1,0:T(8,128)(2,1)}) custom-call(s32[4]{0:T(128)} %pad_add_fusion.spot_ref, s32[4]{0:T(128)} %dynamic_slice.83.count_ref, bf16[4,280,1024]{2,1,0:T(8,128)(2,1)} %bitcast.184, bf16[1024,512]{1,0:T(8,128)(2,1)} %refs_1_.3, ...), custom_call_target="tpu_custom_call" | custom-call | tf_op jit(solution)/shard_map/attend/pallas_call | solution.py:320
  61.3 8.9 %attend.4 = (bf16[4,4,280,768]{3,2,1,0:T(8,128)(2,1)}, bf16[4,4,280,256]{3,2,1,0:T(8,128)(2,1)}, bf16[4,1024,768]{2,1,0:T(8,128)(2,1)}) custom-call(s32[8]{0:T(128)} %concatenate.29.spot_ref, s32[4]{0:T(128)} %dynamic_slice.83.count_ref, bf16[4,280,1024]{2,1,0:T(8,128)(2,1)} %bitcast.185, ...), custom_call_target="tpu_custom_call", output_to_operand_aliasing={{0}: (13, {}), {1}: (14, {}), {2}: (15, {})} | custom-call | tf_op jit(solution)/shard_map/attend/pallas_call | solution.py:320
  76.5 8.8 %attend.5 = (bf16[4,4,280,768]{3,2,1,0:T(8,128)(2,1)}, bf16[4,4,280,256]{3,2,1,0:T(8,128)(2,1)}, bf16[4,1024,768]{2,1,0:T(8,128)(2,1)}) custom-call(s32[8]{0:T(128)} %concatenate.29.spot_ref, s32[4]{0:T(128)} %dynamic_slice.83.count_ref, bf16[4,280,1024]{2,1,0:T(8,128)(2,1)} %bitcast.186, ...), custom_call_target="tpu_custom_call", output_to_operand_aliasing={{0}: (13, {}), {1}: (14, {}), {2}: (15, {})} | custom-call | tf_op jit(solution)/shard_map/attend/pallas_call | solution.py:320
  86.1 8.8 %middle.1 = (f32[4,280,1024]{2,1,0:T(8,128)}, bf16[4,280,1024]{2,1,0:T(8,128)(2,1)}) custom-call(s32[8]{0:T(128)} %concatenate.30.spot_ref.place_ref, bf16[4,280,1024]{2,1,0:T(8,128)(2,1)} %bitcast.173, bf16[4,4,280,256]{3,2,1,0:T(8,128)(2,1)} %get-tuple-element.203.context_ref, bf16[512,1024]{1,0:T(8,128)(2,1)} %lower_ref.3, bf16[256,1024]{1,0:T(8,128)(2,1)} %copy-done.35, ...), custom_call_target="tpu_custom_call" | custom-call | tf_op jit(solution)/shard_map/middle/pallas_call | solution.py:473
  98.7 15.1 %mlp.4 = (bf16[2,4,128,1024]{3,2,1,0:T(8,128)(2,1)S(1)}, bf16[2,4,128,1024]{3,2,1,0:T(8,128)(2,1)S(1)}, f32[2,1,512]{2,1,0:T(1,128)S(1)}, bf16[4,1120,1024]{2,1,...) custom-call(s32[4]{0:T(128)S(1)} %copy-done.26, ...), custom_call_target="tpu_custom_call" | custom-call | tf_op jit(solution)/shard_map/mlp/pallas_call | solution.py:540
  114.2 15.4 %mlp.5 = (bf16[2,4,128,1024]{3,2,1,0:T(8,128)(2,1)S(1)}, bf16[2,4,128,1024]{3,2,1,0:T(8,128)(2,1)S(1)}, f32[2,1,512]{2,1,0:T(1,128)S(1)}, bf16[4,1120,1024]{2,1,...) custom-call(s32[4]{0:T(128)S(1)} %copy-done.26, ...), custom_call_target="tpu_custom_call", output_to_operand_aliasing={{3}: (15, {}), {4}: (16, {}), {5}: (17, {}), {6}: (18, {})} | custom-call | tf_op jit(solution)/shard_map/mlp/pallas_call | solution.py:540
  134.0 15.4 %mlp.6 = (bf16[2,4,128,1024]{3,2,1,0:T(8,128)(2,1)S(1)}, bf16[2,4,128,1024]{3,2,1,0:T(8,128)(2,1)}, f32[2,1,512]{2,1,0:T(1,128)S(1)}, bf16[4,1120,1024]{2,1,0:T(...) custom-call(s32[4]{0:T(128)S(1)} %copy-done.26, ...), custom_call_target="tpu_custom_call", output_to_operand_aliasing={{3}: (15, {}), {4}: (16, {}), {5}: (17, {}), {6}: (18, {})} | custom-call | tf_op jit(solution)/shard_map/mlp/pallas_call | solution.py:540
  156.5 15.4 %mlp.7 = (bf16[2,4,128,1024]{3,2,1,0:T(8,128)(2,1)S(1)}, bf16[2,4,128,1024]{3,2,1,0:T(8,128)(2,1)S(1)}, f32[2,1,512]{2,1,0:T(1,128)S(1)}, bf16[4,1120,1024]{2,1,...) custom-call(s32[4]{0:T(128)S(1)} %copy-done.26, ...), custom_call_target="tpu_custom_call", output_to_operand_aliasing={{3}: (15, {}), {4}: (16, {}), {5}: (17, {}), {6}: (18, {})} | custom-call | tf_op jit(solution)/shard_map/mlp/pallas_call | solution.py:540
  178.0 18.9 %mlp_back.1 = (f32[1120,1024]{1,0:T(8,128)S(1)}, bf16[1120,1024]{1,0:T(8,128)(2,1)S(1)}, f32[8,1024]{1,0:T(8,128)S(1)}) custom-call(bf16[4,1120,1024]{2,1,0:T(8,128)(2,1)} %get-tuple-element.238.pre_ref, bf16[4,1024,1024]{2,1,0:T(8,128)(2,1)} %get-tuple-element.239.up_ref, f32[1120,1024]{1,0:T(8,128)} %bitcast.187, bf16[1120,1024]{1,0:T(8,128)(2,1)S(1)} %copy-done.7, ...), custom_call_target="tpu_custom_call" | custom-call | tf_op jit(solution)/shard_map/mlp_back/pallas_call | solution.py:633
  204.1 15.9 %attend_back.4 = (bf16[2,4,128,1024]{3,2,1,0:T(8,128)(2,1)}, f32[1,768]{1,0:T(1,128)}, bf16[4,280,768]{2,1,0:T(8,128)(2,1)}) custom-call(s32[4]{0:T(128)} %dynamic_slice.83.count_ref, s32[8]{0:T(128)} %concatenate.30.spot_ref.place_ref, bf16[1120,1024]{1,0:T(8,128)(2,1)} %fusion.5.rows_hbm, bf16[1120,1024]{1,0:T(8,128)(2,1)} %copy-done.4, ...), custom_call_target="tpu_custom_call" | custom-call | tf_op jit(solution)/shard_map/attend_back/pallas_call | solution.py:410
  220.1 5.9 %collective-permute-done.18 = bf16[2,2,128,1024]{3,2,1,0:T(8,128)(2,1)} collective-permute-done((bf16[2,2,128,1024]{3,2,1,0:T(8,128)(2,1)S(1)}, bf16[2,2,128,1024]{3,2,1,0:T(8,128)(2,1)}, u32[]{:S(2)}, u32[]{:S(2)}) %collective-permute-start.18) | collective-permute-done | bytes 1048608 | tf_op jit(solution)/shard_map/ppermute | solution.py:245
  233.3 15.8 %attend_back.5 = (bf16[2,4,128,1024]{3,2,1,0:T(8,128)(2,1)}, f32[1,768]{1,0:T(1,128)}, bf16[4,280,768]{2,1,0:T(8,128)(2,1)}) custom-call(s32[4]{0:T(128)} %dynamic_slice.83.count_ref, s32[8]{0:T(128)} %concatenate.30.spot_ref.place_ref, bf16[1120,1024]{1,0:T(8,128)(2,1)} %fusion.5.rows_hbm, bf16[1120,1024]{1,0:T(8,128)(2,1)} %copy-done.4, ...), custom_call_target="tpu_custom_call" | custom-call | tf_op jit(solution)/shard_map/attend_back/pallas_call | solution.py:410
  264.2 15.7 %attend_back.6 = (bf16[2,4,128,1024]{3,2,1,0:T(8,128)(2,1)}, f32[1,768]{1,0:T(1,128)}, bf16[4,280,768]{2,1,0:T(8,128)(2,1)}) custom-call(s32[4]{0:T(128)} %dynamic_slice.83.count_ref, s32[8]{0:T(128)} %concatenate.30.spot_ref.place_ref, bf16[1120,1024]{1,0:T(8,128)(2,1)} %fusion.5.rows_hbm, bf16[1120,1024]{1,0:T(8,128)(2,1)} %copy-done.4, ...), custom_call_target="tpu_custom_call" | custom-call | tf_op jit(solution)/shard_map/attend_back/pallas_call | solution.py:410
  288.7 16.7 %attend_back.7 = (bf16[2,4,128,1024]{3,2,1,0:T(8,128)(2,1)}, f32[1,768]{1,0:T(1,128)}, bf16[4,280,768]{2,1,0:T(8,128)(2,1)}) custom-call(s32[4]{0:T(128)} %dynamic_slice.83.count_ref, s32[8]{0:T(128)} %concatenate.30.spot_ref.place_ref, bf16[1120,1024]{1,0:T(8,128)(2,1)} %fusion.5.rows_hbm, bf16[1120,1024]{1,0:T(8,128)(2,1)} %copy-done.4, ...), custom_call_target="tpu_custom_call" | custom-call | tf_op jit(solution)/shard_map/attend_back/pallas_call | solution.py:410
  322.1 10.7 %input_grad.1 = (bf16[4,280,1024]{2,1,0:T(8,128)(2,1)}, f32[8,1024]{1,0:T(8,128)S(1)}) custom-call(bf16[4,280,768]{2,1,0:T(8,128)(2,1)S(1)} %copy-done.24, bf16[4,280,768]{2,1,0:T(8,128)(2,1)S(1)} %copy-done.23, bf16[4,280,768]{2,1,0:T(8,128)(2,1)S(1)} %copy-done.22, bf16[4,280,768]{2,1,0:T(8,128)(2,1)S(1)} %copy-done.21, ...), custom_call_target="tpu_custom_call" | custom-call | tf_op jit(solution)/shard_map/input_grad/pallas_call | solution.py:766
  332.8 7.4 %collective-permute-done.30 = bf16[4,32,1024]{2,1,0:T(8,128)(2,1)S(1)} collective-permute-done((bf16[4,32,1024]{2,1,0:T(8,128)(2,1)S(1)}, bf16[4,32,1024]{2,1,0:T(8,128)(2,1)S(1)}, u32[]{:S(2)}, u32[]{:S(2)}) %collective-permute-start.30) | collective-permute-done | bytes 262176 | tf_op jit(solution)/shard_map/ppermute | solution.py:245
  353.2 10.0 %mlp_out.2.refs_0_ = bf16[1120,1024]{1,0:T(8,128)(2,1)} custom-call(bf16[4,1120,1024]{2,1,0:T(8,128)(2,1)} %get-tuple-element.292.act_ref, bf16[4,1024,1024]{2,1,0:T(8,128)(2,1)} %get-tuple-element.293.down_ref, f32[1120,1024]{1,0:T(8,128)} %bitcast.188, bf16[1,1024]{1,0:T(2,128)(2,1)} %reshape.243.bias_ref), custom_call_target="tpu_custom_call" | custom-call | tf_op jit(solution)/shard_map/mlp_out/pallas_call | solution.py:686
  371.0 7.2 %collective-permute-done.37 = bf16[2,32,1024]{2,1,0:T(8,128)(2,1)S(1)} collective-permute-done((bf16[2,32,1024]{2,1,0:T(8,128)(2,1)S(1)}, bf16[2,32,1024]{2,1,0:T(8,128)(2,1)S(1)}, u32[]{:S(2)}, u32[]{:S(2)}) %collective-permute-start.37) | collective-permute-done | bytes 131104 | tf_op jit(solution)/shard_map/ppermute | solution.py:245
  378.2 5.4 %collective-permute-start.42 = (bf16[2,32,1024]{2,1,0:T(8,128)(2,1)S(1)}, bf16[2,32,1024]{2,1,0:T(8,128)(2,1)S(1)}, u32[]{:S(2)}, u32[]{:S(2)}) collective-permute-start(bf16[2,32,1024]{2,1,0:T(8,128)(2,1)S(1)} %get-tuple-element.342), channel_id=1, source_target_pairs={{0,24},{2,26},{4,28},{6,30},{8,16},{10,18},{12,20},{14,22},{16,8},... | collective-permute-start | bytes 393224 | tf_op jit(solution)/shard_map/ppermute | solution.py:245
  384.2 10.2 %mlp_out.3 = bf16[1120,1024]{1,0:T(8,128)(2,1)} custom-call(bf16[4,1120,1024]{2,1,0:T(8,128)(2,1)} %get-tuple-element.292.act_ref, bf16[4,1024,1024]{2,1,0:T(8,128)(2,1)} %get-tuple-element.293.down_ref, f32[1120,1024]{1,0:T(8,128)} %bitcast.189, bf16[1,1024]{1,0:T(2,128)(2,1)} %reshape.243.bias_ref, ...), custom_call_target="tpu_custom_call", output_to_operand_aliasing={{}: (4, {})} | custom-call | tf_op jit(solution)/shard_map/mlp_out/pallas_call | solution.py:686
  395.5 9.6 %collective-permute-start.43 = (bf16[2,32,1024]{2,1,0:T(8,128)(2,1)}, bf16[2,32,1024]{2,1,0:T(8,128)(2,1)S(1)}, u32[]{:S(2)}, u32[]{:S(2)}) collective-permute-start(bf16[2,32,1024]{2,1,0:T(8,128)(2,1)} %get-tuple-element.344), channel_id=1, source_target_pairs={{0,16},{2,18},{4,20},{6,22},{8,24},{10,26},{12,28},{14,30},{16,0},... | collective-permute-start | bytes 393224 | tf_op jit(solution)/shard_map/ppermute | solution.py:245
  414.4 5.1 %collective-permute-done.43 = bf16[2,32,1024]{2,1,0:T(8,128)(2,1)S(1)} collective-permute-done((bf16[2,32,1024]{2,1,0:T(8,128)(2,1)}, bf16[2,32,1024]{2,1,0:T(8,128)(2,1)S(1)}, u32[]{:S(2)}, u32[]{:S(2)}) %collective-permute-start.43) | collective-permute-done | bytes 131104 | tf_op jit(solution)/shard_map/ppermute | solution.py:245
  430.5 6.3 %collective-permute-done.50 = f32[72,128]{1,0:T(8,128)S(1)} collective-permute-done((f32[72,128]{1,0:T(8,128)S(1)}, f32[72,128]{1,0:T(8,128)S(1)}, u32[]{:S(2)}, u32[]{:S(2)}) %collective-permute-start.50) | collective-permute-done | bytes 36896 | tf_op jit(solution)/shard_map/ppermute | solution.py:245
  (331 shorter events, 169.8 us)
Async XLA Ops:
  7.2 87.7 %all-gather.7.cloned.1.call-start = ((), (), s32[]{:S(2)}) async-start(), calls=%async_computation | async-start | bytes 4456448 | tf_op jit(solution)/shard_map/all_gather | solution.py:967
  33.6 119.0 %all-gather.9.cloned.1.call-start = ((), (), s32[]{:S(2)}) async-start(), calls=%async_computation.1 | async-start | bytes 4456448 | tf_op jit(solution)/shard_map/all_gather | solution.py:967
  33.6 24.7 %collective-permute-start.2 = (bf16[2,1024,256]{2,1,0:T(8,128)(2,1)S(1)}, bf16[2,1024,256]{2,1,0:T(8,128)(2,1)S(1)}, u32[]{:S(2)}, u32[]{:S(2)}) collective-permute-start(bf16[2,1024,256]{2,1,0:T(8,128)(2,1)S(1)} %pad_maximum_fusion), channel_id=1, source_target_pairs={{0,1},{1,0},{2,3},{3,2},{4,5},{5,4},{6,7},{7,6},{8,9},{9,8},{10,11... | collective-permute-start | bytes 3145736 | tf_op jit(solution)/shard_map/ppermute | solution.py:245
  35.4 22.9 %collective-permute-start.4 = (bf16[1024,128]{1,0:T(8,128)(2,1)}, bf16[1024,128]{1,0:T(8,128)(2,1)S(1)}, u32[]{:S(2)}, u32[]{:S(2)}) collective-permute-start(bf16[1024,128]{1,0:T(8,128)(2,1)} %collective-permute-done.1.refs_4_), channel_id=1, source_target_pairs={{0,4},{2,6},{4,0},{6,2},{8,12},{10,14},{12,8},{14,10},{16,20},{18,... | collective-permute-start | bytes 786440 | tf_op jit(solution)/shard_map/ppermute | solution.py:245
  36.9 21.4 %collective-permute-start.3 = (bf16[1,3072]{1,0:T(2,128)(2,1)S(1)}, bf16[1,3072]{1,0:T(2,128)(2,1)S(1)}, u32[]{:S(2)}, u32[]{:S(2)}) collective-permute-start(bf16[1,3072]{1,0:T(2,128)(2,1)S(1)} %reshape.224), channel_id=1, source_target_pairs={{0,1},{1,0},{2,3},{3,2},{4,5},{5,4},{6,7},{7,6},{8,9},{9,8},{10,11... | collective-permute-start | bytes 18440 | tf_op jit(solution)/shard_map/ppermute | solution.py:245
  59.0 349.2 %all-gather.11.cloned.1.call-start = ((), (), s32[]{:S(2)}) async-start(), calls=%async_computation.2 | async-start | bytes 4456448 | tf_op jit(solution)/shard_map/all_gather | solution.py:1119
  171.9 27.2 %collective-permute-start.17 = (bf16[2,4,128,1024]{3,2,1,0:T(8,128)(2,1)S(1)}, bf16[2,4,128,1024]{3,2,1,0:T(8,128)(2,1)S(1)}, u32[]{:S(2)}, u32[]{:S(2)}) collective-permute-start(bf16[2,4,128,1024]{3,2,1,0:T(8,128)(2,1)S(1)} %get-tuple-element.237), channel_id=1, source_target_pairs={{0,2},{2,0},{4,6},{6,4},{8,10},{10,8},{12,14},{14,12},{16,18},{18,... | collective-permute-start | bytes 6291464 | tf_op jit(solution)/shard_map/ppermute | solution.py:245
  172.2 26.9 %collective-permute-start.15 = (bf16[2,2,128,1024]{3,2,1,0:T(8,128)(2,1)S(1)}, bf16[2,2,128,1024]{3,2,1,0:T(8,128)(2,1)}, u32[]{:S(2)}, u32[]{:S(2)}) collective-permute-start(bf16[2,2,128,1024]{3,2,1,0:T(8,128)(2,1)S(1)} %copy-done.43), channel_id=1, source_target_pairs={{0,1},{1,0},{2,3},{3,2},{4,5},{5,4},{6,7},{7,6},{8,9},{9,8},{10,11... | collective-permute-start | bytes 3145736 | tf_op jit(solution)/shard_map/ppermute | solution.py:245
  176.5 22.6 %collective-permute-start.16 = (bf16[2,128,1024]{2,1,0:T(8,128)(2,1)S(1)}, bf16[2,128,1024]{2,1,0:T(8,128)(2,1)S(1)}, u32[]{:S(2)}, u32[]{:S(2)}) collective-permute-start(bf16[2,128,1024]{2,1,0:T(8,128)(2,1)S(1)} %fusion.14), channel_id=1, source_target_pairs={{0,4},{2,6},{4,0},{6,2},{8,12},{10,14},{12,8},{14,10},{16,20},{18,... | collective-permute-start | bytes 1572872 | tf_op jit(solution)/shard_map/ppermute | solution.py:245
  201.1 24.9 %collective-permute-start.18 = (bf16[2,2,128,1024]{3,2,1,0:T(8,128)(2,1)S(1)}, bf16[2,2,128,1024]{3,2,1,0:T(8,128)(2,1)}, u32[]{:S(2)}, u32[]{:S(2)}) collective-permute-start(bf16[2,2,128,1024]{3,2,1,0:T(8,128)(2,1)S(1)} %get-tuple-element.353), channel_id=1, source_target_pairs={{0,1},{1,0},{2,3},{3,2},{4,5},{5,4},{6,7},{7,6},{8,9},{9,8},{10,11... | collective-permute-start | bytes 3145736 | tf_op jit(solution)/shard_map/ppermute | solution.py:245
  226.0 25.8 %collective-permute-start.23 = (bf16[2,4,128,1024]{3,2,1,0:T(8,128)(2,1)}, bf16[2,4,128,1024]{3,2,1,0:T(8,128)(2,1)}, u32[]{:S(2)}, u32[]{:S(2)}) collective-permute-start(bf16[2,4,128,1024]{3,2,1,0:T(8,128)(2,1)} %get-tuple-element.257), channel_id=1, source_target_pairs={{0,2},{2,0},{4,6},{6,4},{8,10},{10,8},{12,14},{14,12},{16,18},{18,... | collective-permute-start | bytes 6291464 | tf_op jit(solution)/shard_map/ppermute | solution.py:245
  226.0 25.8 %collective-permute-start.20 = (bf16[2,2,128,1024]{3,2,1,0:T(8,128)(2,1)}, bf16[2,2,128,1024]{3,2,1,0:T(8,128)(2,1)S(1)}, u32[]{:S(2)}, u32[]{:S(2)}) collective-permute-start(bf16[2,2,128,1024]{3,2,1,0:T(8,128)(2,1)} %get-tuple-element.255), channel_id=1, source_target_pairs={{0,1},{1,0},{2,3},{3,2},{4,5},{5,4},{6,7},{7,6},{8,9},{9,8},{10,11... | collective-permute-start | bytes 3145736 | tf_op jit(solution)/shard_map/ppermute | solution.py:245
  256.8 25.1 %collective-permute-start.24 = (bf16[2,2,128,1024]{3,2,1,0:T(8,128)(2,1)}, bf16[2,2,128,1024]{3,2,1,0:T(8,128)(2,1)}, u32[]{:S(2)}, u32[]{:S(2)}) collective-permute-start(bf16[2,2,128,1024]{3,2,1,0:T(8,128)(2,1)} %get-tuple-element.349), channel_id=1, source_target_pairs={{0,1},{1,0},{2,3},{3,2},{4,5},{5,4},{6,7},{7,6},{8,9},{9,8},{10,11... | collective-permute-start | bytes 3145736 | tf_op jit(solution)/shard_map/ppermute | solution.py:245
  282.7 141.7 %all-gather.13.cloned.1.call-start = ((), (), s32[]{:S(2)}) async-start(), calls=%async_computation.3 | async-start | bytes 4456448 | tf_op jit(solution)/shard_map/all_gather | solution.py:1136
  282.7 27.1 %collective-permute-start.28 = (bf16[2,4,128,1024]{3,2,1,0:T(8,128)(2,1)}, bf16[2,4,128,1024]{3,2,1,0:T(8,128)(2,1)}, u32[]{:S(2)}, u32[]{:S(2)}) collective-permute-start(bf16[2,4,128,1024]{3,2,1,0:T(8,128)(2,1)} %get-tuple-element.277), channel_id=1, source_target_pairs={{0,2},{2,0},{4,6},{6,4},{8,10},{10,8},{12,14},{14,12},{16,18},{18,... | collective-permute-start | bytes 6291464 | tf_op jit(solution)/shard_map/ppermute | solution.py:245
  282.8 27.1 %collective-permute-start.27 = (bf16[2,2,128,1024]{3,2,1,0:T(8,128)(2,1)}, bf16[2,2,128,1024]{3,2,1,0:T(8,128)(2,1)}, u32[]{:S(2)}, u32[]{:S(2)}) collective-permute-start(bf16[2,2,128,1024]{3,2,1,0:T(8,128)(2,1)} %get-tuple-element.276), channel_id=1, source_target_pairs={{0,1},{1,0},{2,3},{3,2},{4,5},{5,4},{6,7},{7,6},{8,9},{9,8},{10,11... | collective-permute-start | bytes 3145736 | tf_op jit(solution)/shard_map/ppermute | solution.py:245
  287.1 22.7 %collective-permute-start.29 = (bf16[4,64,1024]{2,1,0:T(8,128)(2,1)}, bf16[4,64,1024]{2,1,0:T(8,128)(2,1)}, u32[]{:S(2)}, u32[]{:S(2)}) collective-permute-start(bf16[4,64,1024]{2,1,0:T(8,128)(2,1)} %dynamic-slice_bitcast_fusion), channel_id=1, source_target_pairs={{0,8},{2,10},{4,12},{6,14},{8,0},{10,2},{12,4},{14,6},{16,24},{18,... | collective-permute-start | bytes 1572872 | tf_op jit(solution)/shard_map/ppermute | solution.py:245
  313.3 27.0 %collective-permute-start.31 = (bf16[2,128,1024]{2,1,0:T(8,128)(2,1)S(1)}, bf16[2,128,1024]{2,1,0:T(8,128)(2,1)S(1)}, u32[]{:S(2)}, u32[]{:S(2)}) collective-permute-start(bf16[2,128,1024]{2,1,0:T(8,128)(2,1)S(1)} %get-tuple-element.345), channel_id=1, source_target_pairs={{0,4},{2,6},{4,0},{6,2},{8,12},{10,14},{12,8},{14,10},{16,20},{18,... | collective-permute-start | bytes 1572872 | tf_op jit(solution)/shard_map/ppermute | solution.py:245
  315.8 24.5 %collective-permute-start.30 = (bf16[4,32,1024]{2,1,0:T(8,128)(2,1)S(1)}, bf16[4,32,1024]{2,1,0:T(8,128)(2,1)S(1)}, u32[]{:S(2)}, u32[]{:S(2)}) collective-permute-start(bf16[4,32,1024]{2,1,0:T(8,128)(2,1)S(1)} %dynamic-slice_bitcast_fusion.4), channel_id=1, source_target_pairs={{0,16},{2,18},{4,20},{6,22},{8,24},{10,26},{12,28},{14,30},{16,0},... | collective-permute-start | bytes 786440 | tf_op jit(solution)/shard_map/ppermute | solution.py:245
  365.1 29.3 %collective-permute-start.38 = (bf16[2,32,1024]{2,1,0:T(8,128)(2,1)S(1)}, bf16[2,32,1024]{2,1,0:T(8,128)(2,1)S(1)}, u32[]{:S(2)}, u32[]{:S(2)}) collective-permute-start(bf16[2,32,1024]{2,1,0:T(8,128)(2,1)S(1)} %get-tuple-element.363), channel_id=1, source_target_pairs={{0,8},{2,10},{4,12},{6,14},{8,0},{10,2},{12,4},{14,6},{16,24},{18,... | collective-permute-start | bytes 393224 | tf_op jit(solution)/shard_map/ppermute | solution.py:245
  366.5 28.1 %collective-permute-start.39 = (bf16[2,32,1024]{2,1,0:T(8,128)(2,1)S(1)}, bf16[2,32,1024]{2,1,0:T(8,128)(2,1)S(1)}, u32[]{:S(2)}, u32[]{:S(2)}) collective-permute-start(bf16[2,32,1024]{2,1,0:T(8,128)(2,1)S(1)} %get-tuple-element.362), channel_id=1, source_target_pairs={{0,24},{2,26},{4,28},{6,30},{8,16},{10,18},{12,20},{14,22},{16,8},... | collective-permute-start | bytes 393224 | tf_op jit(solution)/shard_map/ppermute | solution.py:245
  369.6 25.2 %collective-permute-start.40 = (bf16[2,32,1024]{2,1,0:T(8,128)(2,1)S(1)}, bf16[2,32,1024]{2,1,0:T(8,128)(2,1)S(1)}, u32[]{:S(2)}, u32[]{:S(2)}) collective-permute-start(bf16[2,32,1024]{2,1,0:T(8,128)(2,1)S(1)} %get-tuple-element.342), channel_id=1, source_target_pairs={{0,16},{2,18},{4,20},{6,22},{8,24},{10,26},{12,28},{14,30},{16,0},... | collective-permute-start | bytes 393224 | tf_op jit(solution)/shard_map/ppermute | solution.py:245
  369.6 25.2 %collective-permute-start.41 = (bf16[2,32,1024]{2,1,0:T(8,128)(2,1)S(1)}, bf16[2,32,1024]{2,1,0:T(8,128)(2,1)S(1)}, u32[]{:S(2)}, u32[]{:S(2)}) collective-permute-start(bf16[2,32,1024]{2,1,0:T(8,128)(2,1)S(1)} %get-tuple-element.342), channel_id=1, source_target_pairs={{0,8},{2,10},{4,12},{6,14},{8,0},{10,2},{12,4},{14,6},{16,24},{18,... | collective-permute-start | bytes 393224 | tf_op jit(solution)/shard_map/ppermute | solution.py:245
  395.5 24.0 %collective-permute-start.43 = (bf16[2,32,1024]{2,1,0:T(8,128)(2,1)}, bf16[2,32,1024]{2,1,0:T(8,128)(2,1)S(1)}, u32[]{:S(2)}, u32[]{:S(2)}) collective-permute-start(bf16[2,32,1024]{2,1,0:T(8,128)(2,1)} %get-tuple-element.344), channel_id=1, source_target_pairs={{0,16},{2,18},{4,20},{6,22},{8,24},{10,26},{12,28},{14,30},{16,0},... | collective-permute-start | bytes 393224 | tf_op jit(solution)/shard_map/ppermute | solution.py:245
  (101 other events, 1023.6 us)
Sparse Core Ops, SparseCore 0:
  33.7 52.1 all-gather.6
  88.1 49.0 all-gather.8
  282.8 65.2 all-gather.10
  350.6 71.5 all-gather.12

commit v7 on v6

--- a/solution.py
+++ b/solution.py
@@ -609,7 +609,7 @@
         chunk = 224
 
         def one(i, carry):
-            at = pl.ds(pl.multiple_of(i * chunk, chunk), chunk)
+            at = pl.ds(i * chunk, chunk)
             cot = cot_buf[at, :].astype(WIDE)
             pulled, gain_grad, shift_grad = norm_back(
                 middle_buf[at, :], gain_ref[...].astype(WIDE), sum_buf[at, :]
@@ -624,7 +624,8 @@
             sums_ref[3:4, :] += jnp.sum(cot, 0, keepdims=True)
             return carry
 
-        lax.fori_loop(0, grad_ref.shape[0] // chunk, one, 0)
+        for i in range(grad_ref.shape[0] // chunk):
+            one(i, 0)
 
 
 def mlp_back(pre_grads, ups, middle, cot, gain):

time: 465 us -> 464 us (level)
  transfers between devices with their start and end apart: 59 -> 59, of which waited for: 13 -> 12; matrix products, arithmetic and copies ran while one was open for 10% -> 10% of each run, Pallas kernels for 50% -> 50%
where the time goes in v7:
time: 464 us; the launch traced here: 458 us
  Pallas kernels  233 us (50%)
  starting transfers between devices  69.2 us (15%)
  waiting for transfers between devices  57.1 us (12%)
  local copies, waits for them, and re-layouts  42.8 us (9%)
  other arithmetic  41.7 us (9%)
  between operations  15.1 us (3%)
    ppermute x55, starting transfers between devices, flip(): return lax.ppermute(value, axis, [(i, i ^ bit) for i in range(size)])  68.8 us
    pallas_call x4, Pallas kernels, attend_back(): pl.pallas_call(attend_back_kernel, grid_spec=pltpu.PrefetchScalarGridSpec...  64.3 us
    pallas_call x4, Pallas kernels, mlp(): pl.pallas_call(functools.partial(mlp_kernel, rows // 2, turned), grid_spe...  61.3 us
    ppermute x55, waiting for transfers between devices, flip(): return lax.ppermute(value, axis, [(i, i ^ bit) for i in range(size)])  57 us
    pallas_call x3, Pallas kernels, attend(): pl.pallas_call(attend_kernel, grid_spec=pltpu.PrefetchScalarGridSpec(num_...  34 us
    convert_element_type x17, other arithmetic, total(): return result.astype(LOW)  32.3 us
    unnamed x141, local copies, waits for them, and re-layouts  24.3 us
    pallas_call x2, Pallas kernels, mlp_out(): pl.pallas_call(functools.partial(mlp_out_kernel, half), grid=(tiles,), in...  20.2 us
  transfers between devices with their start and end apart: 59, of which 12 were waited for; matrix products, arithmetic and copies ran while one was open for 10% of the time, Pallas kernels for 50%

profile of v7, /device:TPU:0, one launch (start us, length us, event | category | flops | bytes accessed | tf_op | source)
XLA Modules:
  0.0 458.4 jit_solution(13411873031885839093)
XLA Ops:
  23.0 8.7 %collective-permute-done.1.refs_4_ = bf16[1024,128]{1,0:T(8,128)(2,1)} collective-permute-done((bf16[1024,128]{1,0:T(8,128)(2,1)}, bf16[1024,128]{1,0:T(8,128)(2,1)}, u32[]{:S(2)}, u32[]{:S(2)}) %collective-permute-start.1) | collective-permute-done | bytes 262176 | tf_op jit(solution)/shard_map/ppermute | solution.py:245
  38.6 16.3 %attend.3 = (bf16[4,4,280,768]{3,2,1,0:T(8,128)(2,1)}, bf16[4,4,280,256]{3,2,1,0:T(8,128)(2,1)}, bf16[4,1024,768]{2,1,0:T(8,128)(2,1)}) custom-call(s32[4]{0:T(128)} %pad_add_fusion.spot_ref, s32[4]{0:T(128)} %dynamic_slice.83.count_ref, bf16[4,280,1024]{2,1,0:T(8,128)(2,1)} %bitcast.184, bf16[1024,512]{1,0:T(8,128)(2,1)} %refs_1_.3, ...), custom_call_target="tpu_custom_call" | custom-call | tf_op jit(solution)/shard_map/attend/pallas_call | solution.py:320
  61.3 8.9 %attend.4 = (bf16[4,4,280,768]{3,2,1,0:T(8,128)(2,1)}, bf16[4,4,280,256]{3,2,1,0:T(8,128)(2,1)}, bf16[4,1024,768]{2,1,0:T(8,128)(2,1)}) custom-call(s32[8]{0:T(128)} %concatenate.29.spot_ref, s32[4]{0:T(128)} %dynamic_slice.83.count_ref, bf16[4,280,1024]{2,1,0:T(8,128)(2,1)} %bitcast.185, ...), custom_call_target="tpu_custom_call", output_to_operand_aliasing={{0}: (13, {}), {1}: (14, {}), {2}: (15, {})} | custom-call | tf_op jit(solution)/shard_map/attend/pallas_call | solution.py:320
  76.6 8.7 %attend.5 = (bf16[4,4,280,768]{3,2,1,0:T(8,128)(2,1)}, bf16[4,4,280,256]{3,2,1,0:T(8,128)(2,1)}, bf16[4,1024,768]{2,1,0:T(8,128)(2,1)}) custom-call(s32[8]{0:T(128)} %concatenate.29.spot_ref, s32[4]{0:T(128)} %dynamic_slice.83.count_ref, bf16[4,280,1024]{2,1,0:T(8,128)(2,1)} %bitcast.186, ...), custom_call_target="tpu_custom_call", output_to_operand_aliasing={{0}: (13, {}), {1}: (14, {}), {2}: (15, {})} | custom-call | tf_op jit(solution)/shard_map/attend/pallas_call | solution.py:320
  86.1 8.8 %middle.1 = (f32[4,280,1024]{2,1,0:T(8,128)}, bf16[4,280,1024]{2,1,0:T(8,128)(2,1)}) custom-call(s32[8]{0:T(128)} %concatenate.30.spot_ref.place_ref, bf16[4,280,1024]{2,1,0:T(8,128)(2,1)} %bitcast.173, bf16[4,4,280,256]{3,2,1,0:T(8,128)(2,1)} %get-tuple-element.203.context_ref, bf16[512,1024]{1,0:T(8,128)(2,1)} %lower_ref.3, bf16[256,1024]{1,0:T(8,128)(2,1)} %copy-done.35, ...), custom_call_target="tpu_custom_call" | custom-call | tf_op jit(solution)/shard_map/middle/pallas_call | solution.py:473
  98.8 15.1 %mlp.4 = (bf16[2,4,128,1024]{3,2,1,0:T(8,128)(2,1)S(1)}, bf16[2,4,128,1024]{3,2,1,0:T(8,128)(2,1)S(1)}, f32[2,1,512]{2,1,0:T(1,128)S(1)}, bf16[4,1120,1024]{2,1,...) custom-call(s32[4]{0:T(128)S(1)} %copy-done.26, ...), custom_call_target="tpu_custom_call" | custom-call | tf_op jit(solution)/shard_map/mlp/pallas_call | solution.py:540
  114.2 15.6 %mlp.5 = (bf16[2,4,128,1024]{3,2,1,0:T(8,128)(2,1)S(1)}, bf16[2,4,128,1024]{3,2,1,0:T(8,128)(2,1)S(1)}, f32[2,1,512]{2,1,0:T(1,128)S(1)}, bf16[4,1120,1024]{2,1,...) custom-call(s32[4]{0:T(128)S(1)} %copy-done.26, ...), custom_call_target="tpu_custom_call", output_to_operand_aliasing={{3}: (15, {}), {4}: (16, {}), {5}: (17, {}), {6}: (18, {})} | custom-call | tf_op jit(solution)/shard_map/mlp/pallas_call | solution.py:540
  134.2 15.4 %mlp.6 = (bf16[2,4,128,1024]{3,2,1,0:T(8,128)(2,1)S(1)}, bf16[2,4,128,1024]{3,2,1,0:T(8,128)(2,1)}, f32[2,1,512]{2,1,0:T(1,128)S(1)}, bf16[4,1120,1024]{2,1,0:T(...) custom-call(s32[4]{0:T(128)S(1)} %copy-done.26, ...), custom_call_target="tpu_custom_call", output_to_operand_aliasing={{3}: (15, {}), {4}: (16, {}), {5}: (17, {}), {6}: (18, {})} | custom-call | tf_op jit(solution)/shard_map/mlp/pallas_call | solution.py:540
  156.7 15.2 %mlp.7 = (bf16[2,4,128,1024]{3,2,1,0:T(8,128)(2,1)S(1)}, bf16[2,4,128,1024]{3,2,1,0:T(8,128)(2,1)S(1)}, f32[2,1,512]{2,1,0:T(1,128)S(1)}, bf16[4,1120,1024]{2,1,...) custom-call(s32[4]{0:T(128)S(1)} %copy-done.26, ...), custom_call_target="tpu_custom_call", output_to_operand_aliasing={{3}: (15, {}), {4}: (16, {}), {5}: (17, {}), {6}: (18, {})} | custom-call | tf_op jit(solution)/shard_map/mlp/pallas_call | solution.py:540
  178.1 18.7 %mlp_back.1 = (f32[1120,1024]{1,0:T(8,128)S(1)}, bf16[1120,1024]{1,0:T(8,128)(2,1)S(1)}, f32[8,1024]{1,0:T(8,128)S(1)}) custom-call(bf16[4,1120,1024]{2,1,0:T(8,128)(2,1)} %get-tuple-element.238.pre_ref, bf16[4,1024,1024]{2,1,0:T(8,128)(2,1)} %get-tuple-element.239.up_ref, f32[1120,1024]{1,0:T(8,128)} %bitcast.187, bf16[1120,1024]{1,0:T(8,128)(2,1)S(1)} %copy-done.7, ...), custom_call_target="tpu_custom_call" | custom-call | tf_op jit(solution)/shard_map/mlp_back/pallas_call | solution.py:634
  204.1 15.9 %attend_back.4 = (bf16[2,4,128,1024]{3,2,1,0:T(8,128)(2,1)}, f32[1,768]{1,0:T(1,128)}, bf16[4,280,768]{2,1,0:T(8,128)(2,1)}) custom-call(s32[4]{0:T(128)} %dynamic_slice.83.count_ref, s32[8]{0:T(128)} %concatenate.30.spot_ref.place_ref, bf16[1120,1024]{1,0:T(8,128)(2,1)} %fusion.5.rows_hbm, bf16[1120,1024]{1,0:T(8,128)(2,1)} %copy-done.4, ...), custom_call_target="tpu_custom_call" | custom-call | tf_op jit(solution)/shard_map/attend_back/pallas_call | solution.py:410
  220.1 5.7 %collective-permute-done.18 = bf16[2,2,128,1024]{3,2,1,0:T(8,128)(2,1)} collective-permute-done((bf16[2,2,128,1024]{3,2,1,0:T(8,128)(2,1)S(1)}, bf16[2,2,128,1024]{3,2,1,0:T(8,128)(2,1)}, u32[]{:S(2)}, u32[]{:S(2)}) %collective-permute-start.18) | collective-permute-done | bytes 1048608 | tf_op jit(solution)/shard_map/ppermute | solution.py:245
  233.2 16.0 %attend_back.5 = (bf16[2,4,128,1024]{3,2,1,0:T(8,128)(2,1)}, f32[1,768]{1,0:T(1,128)}, bf16[4,280,768]{2,1,0:T(8,128)(2,1)}) custom-call(s32[4]{0:T(128)} %dynamic_slice.83.count_ref, s32[8]{0:T(128)} %concatenate.30.spot_ref.place_ref, bf16[1120,1024]{1,0:T(8,128)(2,1)} %fusion.5.rows_hbm, bf16[1120,1024]{1,0:T(8,128)(2,1)} %copy-done.4, ...), custom_call_target="tpu_custom_call" | custom-call | tf_op jit(solution)/shard_map/attend_back/pallas_call | solution.py:410
  264.1 15.7 %attend_back.6 = (bf16[2,4,128,1024]{3,2,1,0:T(8,128)(2,1)}, f32[1,768]{1,0:T(1,128)}, bf16[4,280,768]{2,1,0:T(8,128)(2,1)}) custom-call(s32[4]{0:T(128)} %dynamic_slice.83.count_ref, s32[8]{0:T(128)} %concatenate.30.spot_ref.place_ref, bf16[1120,1024]{1,0:T(8,128)(2,1)} %fusion.5.rows_hbm, bf16[1120,1024]{1,0:T(8,128)(2,1)} %copy-done.4, ...), custom_call_target="tpu_custom_call" | custom-call | tf_op jit(solution)/shard_map/attend_back/pallas_call | solution.py:410
  288.5 16.6 %attend_back.7 = (bf16[2,4,128,1024]{3,2,1,0:T(8,128)(2,1)}, f32[1,768]{1,0:T(1,128)}, bf16[4,280,768]{2,1,0:T(8,128)(2,1)}) custom-call(s32[4]{0:T(128)} %dynamic_slice.83.count_ref, s32[8]{0:T(128)} %concatenate.30.spot_ref.place_ref, bf16[1120,1024]{1,0:T(8,128)(2,1)} %fusion.5.rows_hbm, bf16[1120,1024]{1,0:T(8,128)(2,1)} %copy-done.4, ...), custom_call_target="tpu_custom_call" | custom-call | tf_op jit(solution)/shard_map/attend_back/pallas_call | solution.py:410
  322.1 10.7 %input_grad.1 = (bf16[4,280,1024]{2,1,0:T(8,128)(2,1)}, f32[8,1024]{1,0:T(8,128)S(1)}) custom-call(bf16[4,280,768]{2,1,0:T(8,128)(2,1)S(1)} %copy-done.24, bf16[4,280,768]{2,1,0:T(8,128)(2,1)S(1)} %copy-done.23, bf16[4,280,768]{2,1,0:T(8,128)(2,1)S(1)} %copy-done.22, bf16[4,280,768]{2,1,0:T(8,128)(2,1)S(1)} %copy-done.21, ...), custom_call_target="tpu_custom_call" | custom-call | tf_op jit(solution)/shard_map/input_grad/pallas_call | solution.py:767
  332.8 7.2 %collective-permute-done.30 = bf16[4,32,1024]{2,1,0:T(8,128)(2,1)S(1)} collective-permute-done((bf16[4,32,1024]{2,1,0:T(8,128)(2,1)S(1)}, bf16[4,32,1024]{2,1,0:T(8,128)(2,1)S(1)}, u32[]{:S(2)}, u32[]{:S(2)}) %collective-permute-start.30) | collective-permute-done | bytes 262176 | tf_op jit(solution)/shard_map/ppermute | solution.py:245
  352.9 10.0 %mlp_out.2.refs_0_ = bf16[1120,1024]{1,0:T(8,128)(2,1)} custom-call(bf16[4,1120,1024]{2,1,0:T(8,128)(2,1)} %get-tuple-element.292.act_ref, bf16[4,1024,1024]{2,1,0:T(8,128)(2,1)} %get-tuple-element.293.down_ref, f32[1120,1024]{1,0:T(8,128)} %bitcast.188, bf16[1,1024]{1,0:T(2,128)(2,1)} %reshape.243.bias_ref), custom_call_target="tpu_custom_call" | custom-call | tf_op jit(solution)/shard_map/mlp_out/pallas_call | solution.py:687
  370.7 7.3 %collective-permute-done.37 = bf16[2,32,1024]{2,1,0:T(8,128)(2,1)S(1)} collective-permute-done((bf16[2,32,1024]{2,1,0:T(8,128)(2,1)S(1)}, bf16[2,32,1024]{2,1,0:T(8,128)(2,1)S(1)}, u32[]{:S(2)}, u32[]{:S(2)}) %collective-permute-start.37) | collective-permute-done | bytes 131104 | tf_op jit(solution)/shard_map/ppermute | solution.py:245
  378.0 5.2 %collective-permute-start.42 = (bf16[2,32,1024]{2,1,0:T(8,128)(2,1)S(1)}, bf16[2,32,1024]{2,1,0:T(8,128)(2,1)S(1)}, u32[]{:S(2)}, u32[]{:S(2)}) collective-permute-start(bf16[2,32,1024]{2,1,0:T(8,128)(2,1)S(1)} %get-tuple-element.342), channel_id=1, source_target_pairs={{0,24},{2,26},{4,28},{6,30},{8,16},{10,18},{12,20},{14,22},{16,8},... | collective-permute-start | bytes 393224 | tf_op jit(solution)/shard_map/ppermute | solution.py:245
  383.9 10.1 %mlp_out.3 = bf16[1120,1024]{1,0:T(8,128)(2,1)} custom-call(bf16[4,1120,1024]{2,1,0:T(8,128)(2,1)} %get-tuple-element.292.act_ref, bf16[4,1024,1024]{2,1,0:T(8,128)(2,1)} %get-tuple-element.293.down_ref, f32[1120,1024]{1,0:T(8,128)} %bitcast.189, bf16[1,1024]{1,0:T(2,128)(2,1)} %reshape.243.bias_ref, ...), custom_call_target="tpu_custom_call", output_to_operand_aliasing={{}: (4, {})} | custom-call | tf_op jit(solution)/shard_map/mlp_out/pallas_call | solution.py:687
  394.9 9.8 %collective-permute-start.43 = (bf16[2,32,1024]{2,1,0:T(8,128)(2,1)}, bf16[2,32,1024]{2,1,0:T(8,128)(2,1)S(1)}, u32[]{:S(2)}, u32[]{:S(2)}) collective-permute-start(bf16[2,32,1024]{2,1,0:T(8,128)(2,1)} %get-tuple-element.344), channel_id=1, source_target_pairs={{0,16},{2,18},{4,20},{6,22},{8,24},{10,26},{12,28},{14,30},{16,0},... | collective-permute-start | bytes 393224 | tf_op jit(solution)/shard_map/ppermute | solution.py:245
  413.6 5.7 %collective-permute-done.43 = bf16[2,32,1024]{2,1,0:T(8,128)(2,1)S(1)} collective-permute-done((bf16[2,32,1024]{2,1,0:T(8,128)(2,1)}, bf16[2,32,1024]{2,1,0:T(8,128)(2,1)S(1)}, u32[]{:S(2)}, u32[]{:S(2)}) %collective-permute-start.43) | collective-permute-done | bytes 131104 | tf_op jit(solution)/shard_map/ppermute | solution.py:245
  430.2 6.3 %collective-permute-done.50 = f32[72,128]{1,0:T(8,128)S(1)} collective-permute-done((f32[72,128]{1,0:T(8,128)S(1)}, f32[72,128]{1,0:T(8,128)S(1)}, u32[]{:S(2)}, u32[]{:S(2)}) %collective-permute-start.50) | collective-permute-done | bytes 36896 | tf_op jit(solution)/shard_map/ppermute | solution.py:245
  (331 shorter events, 169.5 us)
Async XLA Ops:
  7.2 87.7 %all-gather.7.cloned.1.call-start = ((), (), s32[]{:S(2)}) async-start(), calls=%async_computation | async-start | bytes 4456448 | tf_op jit(solution)/shard_map/all_gather | solution.py:968
  33.6 119.3 %all-gather.9.cloned.1.call-start = ((), (), s32[]{:S(2)}) async-start(), calls=%async_computation.1 | async-start | bytes 4456448 | tf_op jit(solution)/shard_map/all_gather | solution.py:968
  33.6 24.7 %collective-permute-start.2 = (bf16[2,1024,256]{2,1,0:T(8,128)(2,1)S(1)}, bf16[2,1024,256]{2,1,0:T(8,128)(2,1)S(1)}, u32[]{:S(2)}, u32[]{:S(2)}) collective-permute-start(bf16[2,1024,256]{2,1,0:T(8,128)(2,1)S(1)} %pad_maximum_fusion), channel_id=1, source_target_pairs={{0,1},{1,0},{2,3},{3,2},{4,5},{5,4},{6,7},{7,6},{8,9},{9,8},{10,11... | collective-permute-start | bytes 3145736 | tf_op jit(solution)/shard_map/ppermute | solution.py:245
  35.4 22.9 %collective-permute-start.4 = (bf16[1024,128]{1,0:T(8,128)(2,1)}, bf16[1024,128]{1,0:T(8,128)(2,1)S(1)}, u32[]{:S(2)}, u32[]{:S(2)}) collective-permute-start(bf16[1024,128]{1,0:T(8,128)(2,1)} %collective-permute-done.1.refs_4_), channel_id=1, source_target_pairs={{0,4},{2,6},{4,0},{6,2},{8,12},{10,14},{12,8},{14,10},{16,20},{18,... | collective-permute-start | bytes 786440 | tf_op jit(solution)/shard_map/ppermute | solution.py:245
  36.9 21.4 %collective-permute-start.3 = (bf16[1,3072]{1,0:T(2,128)(2,1)S(1)}, bf16[1,3072]{1,0:T(2,128)(2,1)S(1)}, u32[]{:S(2)}, u32[]{:S(2)}) collective-permute-start(bf16[1,3072]{1,0:T(2,128)(2,1)S(1)} %reshape.224), channel_id=1, source_target_pairs={{0,1},{1,0},{2,3},{3,2},{4,5},{5,4},{6,7},{7,6},{8,9},{9,8},{10,11... | collective-permute-start | bytes 18440 | tf_op jit(solution)/shard_map/ppermute | solution.py:245
  59.0 348.4 %all-gather.11.cloned.1.call-start = ((), (), s32[]{:S(2)}) async-start(), calls=%async_computation.2 | async-start | bytes 4456448 | tf_op jit(solution)/shard_map/all_gather | solution.py:1120
  171.9 27.0 %collective-permute-start.17 = (bf16[2,4,128,1024]{3,2,1,0:T(8,128)(2,1)S(1)}, bf16[2,4,128,1024]{3,2,1,0:T(8,128)(2,1)S(1)}, u32[]{:S(2)}, u32[]{:S(2)}) collective-permute-start(bf16[2,4,128,1024]{3,2,1,0:T(8,128)(2,1)S(1)} %get-tuple-element.237), channel_id=1, source_target_pairs={{0,2},{2,0},{4,6},{6,4},{8,10},{10,8},{12,14},{14,12},{16,18},{18,... | collective-permute-start | bytes 6291464 | tf_op jit(solution)/shard_map/ppermute | solution.py:245
  172.2 26.8 %collective-permute-start.15 = (bf16[2,2,128,1024]{3,2,1,0:T(8,128)(2,1)S(1)}, bf16[2,2,128,1024]{3,2,1,0:T(8,128)(2,1)}, u32[]{:S(2)}, u32[]{:S(2)}) collective-permute-start(bf16[2,2,128,1024]{3,2,1,0:T(8,128)(2,1)S(1)} %copy-done.43), channel_id=1, source_target_pairs={{0,1},{1,0},{2,3},{3,2},{4,5},{5,4},{6,7},{7,6},{8,9},{9,8},{10,11... | collective-permute-start | bytes 3145736 | tf_op jit(solution)/shard_map/ppermute | solution.py:245
  176.5 22.4 %collective-permute-start.16 = (bf16[2,128,1024]{2,1,0:T(8,128)(2,1)S(1)}, bf16[2,128,1024]{2,1,0:T(8,128)(2,1)S(1)}, u32[]{:S(2)}, u32[]{:S(2)}) collective-permute-start(bf16[2,128,1024]{2,1,0:T(8,128)(2,1)S(1)} %fusion.14), channel_id=1, source_target_pairs={{0,4},{2,6},{4,0},{6,2},{8,12},{10,14},{12,8},{14,10},{16,20},{18,... | collective-permute-start | bytes 1572872 | tf_op jit(solution)/shard_map/ppermute | solution.py:245
  200.9 24.9 %collective-permute-start.18 = (bf16[2,2,128,1024]{3,2,1,0:T(8,128)(2,1)S(1)}, bf16[2,2,128,1024]{3,2,1,0:T(8,128)(2,1)}, u32[]{:S(2)}, u32[]{:S(2)}) collective-permute-start(bf16[2,2,128,1024]{3,2,1,0:T(8,128)(2,1)S(1)} %get-tuple-element.353), channel_id=1, source_target_pairs={{0,1},{1,0},{2,3},{3,2},{4,5},{5,4},{6,7},{7,6},{8,9},{9,8},{10,11... | collective-permute-start | bytes 3145736 | tf_op jit(solution)/shard_map/ppermute | solution.py:245
  225.8 25.8 %collective-permute-start.23 = (bf16[2,4,128,1024]{3,2,1,0:T(8,128)(2,1)}, bf16[2,4,128,1024]{3,2,1,0:T(8,128)(2,1)}, u32[]{:S(2)}, u32[]{:S(2)}) collective-permute-start(bf16[2,4,128,1024]{3,2,1,0:T(8,128)(2,1)} %get-tuple-element.257), channel_id=1, source_target_pairs={{0,2},{2,0},{4,6},{6,4},{8,10},{10,8},{12,14},{14,12},{16,18},{18,... | collective-permute-start | bytes 6291464 | tf_op jit(solution)/shard_map/ppermute | solution.py:245
  225.8 25.8 %collective-permute-start.20 = (bf16[2,2,128,1024]{3,2,1,0:T(8,128)(2,1)}, bf16[2,2,128,1024]{3,2,1,0:T(8,128)(2,1)S(1)}, u32[]{:S(2)}, u32[]{:S(2)}) collective-permute-start(bf16[2,2,128,1024]{3,2,1,0:T(8,128)(2,1)} %get-tuple-element.255), channel_id=1, source_target_pairs={{0,1},{1,0},{2,3},{3,2},{4,5},{5,4},{6,7},{7,6},{8,9},{9,8},{10,11... | collective-permute-start | bytes 3145736 | tf_op jit(solution)/shard_map/ppermute | solution.py:245
  256.6 25.1 %collective-permute-start.24 = (bf16[2,2,128,1024]{3,2,1,0:T(8,128)(2,1)}, bf16[2,2,128,1024]{3,2,1,0:T(8,128)(2,1)}, u32[]{:S(2)}, u32[]{:S(2)}) collective-permute-start(bf16[2,2,128,1024]{3,2,1,0:T(8,128)(2,1)} %get-tuple-element.349), channel_id=1, source_target_pairs={{0,1},{1,0},{2,3},{3,2},{4,5},{5,4},{6,7},{7,6},{8,9},{9,8},{10,11... | collective-permute-start | bytes 3145736 | tf_op jit(solution)/shard_map/ppermute | solution.py:245
  282.5 141.6 %all-gather.13.cloned.1.call-start = ((), (), s32[]{:S(2)}) async-start(), calls=%async_computation.3 | async-start | bytes 4456448 | tf_op jit(solution)/shard_map/all_gather | solution.py:1137
  282.5 27.1 %collective-permute-start.28 = (bf16[2,4,128,1024]{3,2,1,0:T(8,128)(2,1)}, bf16[2,4,128,1024]{3,2,1,0:T(8,128)(2,1)}, u32[]{:S(2)}, u32[]{:S(2)}) collective-permute-start(bf16[2,4,128,1024]{3,2,1,0:T(8,128)(2,1)} %get-tuple-element.277), channel_id=1, source_target_pairs={{0,2},{2,0},{4,6},{6,4},{8,10},{10,8},{12,14},{14,12},{16,18},{18,... | collective-permute-start | bytes 6291464 | tf_op jit(solution)/shard_map/ppermute | solution.py:245
  282.6 27.0 %collective-permute-start.27 = (bf16[2,2,128,1024]{3,2,1,0:T(8,128)(2,1)}, bf16[2,2,128,1024]{3,2,1,0:T(8,128)(2,1)}, u32[]{:S(2)}, u32[]{:S(2)}) collective-permute-start(bf16[2,2,128,1024]{3,2,1,0:T(8,128)(2,1)} %get-tuple-element.276), channel_id=1, source_target_pairs={{0,1},{1,0},{2,3},{3,2},{4,5},{5,4},{6,7},{7,6},{8,9},{9,8},{10,11... | collective-permute-start | bytes 3145736 | tf_op jit(solution)/shard_map/ppermute | solution.py:245
  286.9 22.7 %collective-permute-start.29 = (bf16[4,64,1024]{2,1,0:T(8,128)(2,1)}, bf16[4,64,1024]{2,1,0:T(8,128)(2,1)}, u32[]{:S(2)}, u32[]{:S(2)}) collective-permute-start(bf16[4,64,1024]{2,1,0:T(8,128)(2,1)} %dynamic-slice_bitcast_fusion), channel_id=1, source_target_pairs={{0,8},{2,10},{4,12},{6,14},{8,0},{10,2},{12,4},{14,6},{16,24},{18,... | collective-permute-start | bytes 1572872 | tf_op jit(solution)/shard_map/ppermute | solution.py:245
  313.1 26.9 %collective-permute-start.31 = (bf16[2,128,1024]{2,1,0:T(8,128)(2,1)S(1)}, bf16[2,128,1024]{2,1,0:T(8,128)(2,1)S(1)}, u32[]{:S(2)}, u32[]{:S(2)}) collective-permute-start(bf16[2,128,1024]{2,1,0:T(8,128)(2,1)S(1)} %get-tuple-element.345), channel_id=1, source_target_pairs={{0,4},{2,6},{4,0},{6,2},{8,12},{10,14},{12,8},{14,10},{16,20},{18,... | collective-permute-start | bytes 1572872 | tf_op jit(solution)/shard_map/ppermute | solution.py:245
  315.7 24.3 %collective-permute-start.30 = (bf16[4,32,1024]{2,1,0:T(8,128)(2,1)S(1)}, bf16[4,32,1024]{2,1,0:T(8,128)(2,1)S(1)}, u32[]{:S(2)}, u32[]{:S(2)}) collective-permute-start(bf16[4,32,1024]{2,1,0:T(8,128)(2,1)S(1)} %dynamic-slice_bitcast_fusion.4), channel_id=1, source_target_pairs={{0,16},{2,18},{4,20},{6,22},{8,24},{10,26},{12,28},{14,30},{16,0},... | collective-permute-start | bytes 786440 | tf_op jit(solution)/shard_map/ppermute | solution.py:245
  364.9 29.1 %collective-permute-start.38 = (bf16[2,32,1024]{2,1,0:T(8,128)(2,1)S(1)}, bf16[2,32,1024]{2,1,0:T(8,128)(2,1)S(1)}, u32[]{:S(2)}, u32[]{:S(2)}) collective-permute-start(bf16[2,32,1024]{2,1,0:T(8,128)(2,1)S(1)} %get-tuple-element.363), channel_id=1, source_target_pairs={{0,8},{2,10},{4,12},{6,14},{8,0},{10,2},{12,4},{14,6},{16,24},{18,... | collective-permute-start | bytes 393224 | tf_op jit(solution)/shard_map/ppermute | solution.py:245
  366.2 27.9 %collective-permute-start.39 = (bf16[2,32,1024]{2,1,0:T(8,128)(2,1)S(1)}, bf16[2,32,1024]{2,1,0:T(8,128)(2,1)S(1)}, u32[]{:S(2)}, u32[]{:S(2)}) collective-permute-start(bf16[2,32,1024]{2,1,0:T(8,128)(2,1)S(1)} %get-tuple-element.362), channel_id=1, source_target_pairs={{0,24},{2,26},{4,28},{6,30},{8,16},{10,18},{12,20},{14,22},{16,8},... | collective-permute-start | bytes 393224 | tf_op jit(solution)/shard_map/ppermute | solution.py:245
  369.3 24.8 %collective-permute-start.40 = (bf16[2,32,1024]{2,1,0:T(8,128)(2,1)S(1)}, bf16[2,32,1024]{2,1,0:T(8,128)(2,1)S(1)}, u32[]{:S(2)}, u32[]{:S(2)}) collective-permute-start(bf16[2,32,1024]{2,1,0:T(8,128)(2,1)S(1)} %get-tuple-element.342), channel_id=1, source_target_pairs={{0,16},{2,18},{4,20},{6,22},{8,24},{10,26},{12,28},{14,30},{16,0},... | collective-permute-start | bytes 393224 | tf_op jit(solution)/shard_map/ppermute | solution.py:245
  369.4 24.7 %collective-permute-start.41 = (bf16[2,32,1024]{2,1,0:T(8,128)(2,1)S(1)}, bf16[2,32,1024]{2,1,0:T(8,128)(2,1)S(1)}, u32[]{:S(2)}, u32[]{:S(2)}) collective-permute-start(bf16[2,32,1024]{2,1,0:T(8,128)(2,1)S(1)} %get-tuple-element.342), channel_id=1, source_target_pairs={{0,8},{2,10},{4,12},{6,14},{8,0},{10,2},{12,4},{14,6},{16,24},{18,... | collective-permute-start | bytes 393224 | tf_op jit(solution)/shard_map/ppermute | solution.py:245
  394.9 24.4 %collective-permute-start.43 = (bf16[2,32,1024]{2,1,0:T(8,128)(2,1)}, bf16[2,32,1024]{2,1,0:T(8,128)(2,1)S(1)}, u32[]{:S(2)}, u32[]{:S(2)}) collective-permute-start(bf16[2,32,1024]{2,1,0:T(8,128)(2,1)} %get-tuple-element.344), channel_id=1, source_target_pairs={{0,16},{2,18},{4,20},{6,22},{8,24},{10,26},{12,28},{14,30},{16,0},... | collective-permute-start | bytes 393224 | tf_op jit(solution)/shard_map/ppermute | solution.py:245
  (101 other events, 1024.1 us)
Sparse Core Ops, SparseCore 0:
  33.7 52.1 all-gather.6
  88.1 49.0 all-gather.8
  282.6 65.1 all-gather.10
  350.4 71.7 all-gather.12
